TPU v7x, 32 devices: a whole 2x2x4 slice. The times are simulated.
32 devices in a mesh: dp: 4 (over y, x), ctx: 8 (over z, core).
Axes of the slice: x: 2, y: 2, z: 4, core: 2. Of those that a mesh axis runs over, the one named last changes fastest.
Arguments:
- tokens: bfloat16 [8, 2048, 1024], P('dp', 'ctx'), may hold values from -6 to 6
- positions: int32 [8, 2048], P('dp'), may hold values from 0 to 2047, as said below
- w_query: bfloat16 [1024, 2048], P(('dp', 'ctx')), may hold values from -0.1875 to 0.1875
- w_key: bfloat16 [1024, 1024], P(('dp', 'ctx')), may hold values from -0.1875 to 0.1875
- w_value: bfloat16 [1024, 1024], P(('dp', 'ctx')), may hold values from -0.1875 to 0.1875
- w_out: bfloat16 [2048, 1024], P(('dp', 'ctx')), may hold values from -1 to 1
- w_gate: bfloat16 [1024, 3072], P(('dp', 'ctx')), may hold values from -0.1875 to 0.1875
- w_up: bfloat16 [1024, 3072], P(('dp', 'ctx')), may hold values from -0.1875 to 0.1875
- w_down: bfloat16 [3072, 1024], P(('dp', 'ctx')), may hold values from -0.109375 to 0.109375
- attn_gain: bfloat16 [1024], P(('dp', 'ctx')), may hold values from 0.5 to 1.5
- mlp_gain: bfloat16 [1024], P(('dp', 'ctx')), may hold values from 0.5 to 1.5
- q_gain: bfloat16 [128], P(('dp', 'ctx')), may hold values from 0.5 to 1.5
- k_gain: bfloat16 [128], P(('dp', 'ctx')), may hold values from 0.5 to 1.5
- grad_out: bfloat16 [8, 2048, 1024], P('dp', 'ctx'), may hold values from -6 to 6
Outputs:
- output: bfloat16 [8, 2048, 1024], P('dp', 'ctx')
- input_grad: bfloat16 [8, 2048, 1024], P('dp', 'ctx')
- grad_w_query: float32 [1024, 2048], P(('dp', 'ctx'))
- grad_w_key: float32 [1024, 1024], P(('dp', 'ctx'))
- grad_w_value: float32 [1024, 1024], P(('dp', 'ctx'))
- grad_w_out: float32 [2048, 1024], P(('dp', 'ctx'))
- grad_w_gate: float32 [1024, 3072], P(('dp', 'ctx'))
- grad_w_up: float32 [1024, 3072], P(('dp', 'ctx'))
- grad_w_down: float32 [3072, 1024], P(('dp', 'ctx'))
- grad_attn_gain: float32 [1024], P(('dp', 'ctx'))
- grad_mlp_gain: float32 [1024], P(('dp', 'ctx'))
- grad_q_gain: float32 [128], P(('dp', 'ctx'))
- grad_k_gain: float32 [128], P(('dp', 'ctx'))
Inputs may be any that keep to these rules, and one draw needn't show every extreme that they name: Each row is a permutation of 0 to 2047 made of 16 blocks of 128 consecutive positions in rising order; slots j * 2 * 128 to (j + 1) * 2 * 128 - 1 hold block c followed by block 15 - c, c drawn per row and per j.
All inputs are finite; a program needn't handle non-finite values.
Results may differ from a plain program's by a relative error of at most 0.023.
Values may be sent and summed in bfloat16 or wider, within the bound.
A program may use at most 384 MiB of HBM per device.

v0:
```python
import jax
import jax.numpy as jnp
from jax import lax
from jax.sharding import PartitionSpec as P

H = 16
KV = 8
HD = 128
SEQ = 2048
MICRO = 2
SEQ_MB = 1


EPSILON = 1e-06
THETA = 1000000.0
NEGATIVE = -1e30


def normed(values, weights):
    return values * lax.rsqrt(jnp.mean(values * values, axis=-1, keepdims=True) + EPSILON) * weights


def angle_tables(position_ids):
    half_width = HD // 2
    inverse = THETA ** (-(jnp.arange(half_width).astype(jnp.float32) * 2.0 / HD))
    angles = position_ids.astype(jnp.float32)[:, None] * inverse[None, :]
    angles = jnp.concatenate([angles, angles], axis=-1)
    return (jnp.cos(angles), jnp.sin(angles))


def rotated(values, cosine, sine_table):
    half_width = values.shape[-1] // 2
    turned = jnp.concatenate([-values[..., half_width:], values[..., :half_width]], axis=-1)
    return values * cosine + turned * sine_table


def prepared(raw_rows, gain_vector, cosine, sine_table):
    row_count = raw_rows.shape[0]
    heads = raw_rows.reshape(row_count, -1, HD)
    return rotated(normed(heads, gain_vector), cosine[:, None], sine_table[:, None]).reshape(
        row_count, -1
    )


def scored(query_heads, keys_all, causal):
    result = jnp.einsum(
        "bqkgd,bskd->bkgqs", query_heads, keys_all, preferred_element_type=jnp.float32
    ) * HD ** (-0.5)
    return jnp.where(causal[:, None, None], result, NEGATIVE)


def accumulate(totals, new_items):
    if totals is None:
        return new_items
    return tuple((total_item + new_item for total_item, new_item in zip(totals, new_items)))


def shards(
    tokens,
    positions,
    w_query,
    w_key,
    w_value,
    w_out,
    w_gate,
    w_up,
    w_down,
    attn_gain,
    mlp_gain,
    q_gain,
    k_gain,
    grad_out,
):
    shard_slots = tokens.shape[1]
    model_width = tokens.shape[2]
    ctx_index = lax.axis_index("ctx")
    groups = H // KV
    row_count = SEQ_MB * shard_slots
    attn_totals = None
    mlp_totals = None
    outputs = []
    input_grads = []
    for micro_step in range(MICRO):
        first_seq = micro_step * SEQ_MB
        block_tokens = tokens[first_seq : first_seq + SEQ_MB]
        block_cotangent = grad_out[first_seq : first_seq + SEQ_MB]
        whole_pos = positions[first_seq : first_seq + SEQ_MB]
        own_pos = lax.dynamic_slice_in_dim(whole_pos, ctx_index * shard_slots, shard_slots, 1)
        causal = whole_pos[:, None, :] <= own_pos[:, :, None]
        cosine, sine_table = angle_tables(own_pos.reshape(row_count))
        residual_in = block_tokens.reshape(row_count, model_width).astype(jnp.float32)
        full_query, full_key, full_value, full_out, full_attn_gain, full_q_gain, full_k_gain = (
            lax.all_gather(w_query, ("dp", "ctx"), axis=0, tiled=True),
            lax.all_gather(w_key, ("dp", "ctx"), axis=0, tiled=True),
            lax.all_gather(w_value, ("dp", "ctx"), axis=0, tiled=True),
            lax.all_gather(w_out, ("dp", "ctx"), axis=0, tiled=True),
            lax.all_gather(attn_gain, ("dp", "ctx"), axis=0, tiled=True),
            lax.all_gather(q_gain, ("dp", "ctx"), axis=0, tiled=True),
            lax.all_gather(k_gain, ("dp", "ctx"), axis=0, tiled=True),
        )
        gain_attn = full_attn_gain.astype(jnp.float32)
        query_gain = full_q_gain.astype(jnp.float32)
        key_gain = full_k_gain.astype(jnp.float32)
        hidden = normed(residual_in, gain_attn).astype(jnp.bfloat16)
        query_raw = jnp.dot(hidden, full_query, preferred_element_type=jnp.float32)
        key_raw = jnp.dot(hidden, full_key, preferred_element_type=jnp.float32)
        value_raw = jnp.dot(hidden, full_value, preferred_element_type=jnp.float32)
        queries = prepared(query_raw, query_gain, cosine, sine_table).astype(jnp.bfloat16)
        keys_own = prepared(key_raw, key_gain, cosine, sine_table).astype(jnp.bfloat16)
        values_own = value_raw.astype(jnp.bfloat16)
        keys_all, values_all = (
            lax.all_gather(
                keys_own.reshape(SEQ_MB, shard_slots, KV * HD), "ctx", axis=1, tiled=True
            ),
            lax.all_gather(
                values_own.reshape(SEQ_MB, shard_slots, KV * HD), "ctx", axis=1, tiled=True
            ),
        )
        keys_all = keys_all.reshape(SEQ_MB, SEQ, KV, HD)
        values_all = values_all.reshape(SEQ_MB, SEQ, KV, HD)
        query_heads = queries.reshape(SEQ_MB, shard_slots, KV, groups, HD)
        scores = scored(query_heads, keys_all, causal)
        top_score = jnp.max(scores, axis=-1, keepdims=True)
        log_total = top_score + jnp.log(
            jnp.sum(jnp.exp(scores - top_score), axis=-1, keepdims=True)
        )
        prob_low = jnp.exp(scores - log_total).astype(jnp.bfloat16)
        mixed_heads = jnp.einsum(
            "bkgqs,bskd->bqkgd", prob_low, values_all, preferred_element_type=jnp.float32
        )
        mixed_rows = mixed_heads.reshape(row_count, H * HD).astype(jnp.bfloat16)
        middle = residual_in + jnp.dot(mixed_rows, full_out, preferred_element_type=jnp.float32)
        full_gate, full_up, full_down, full_mlp_gain = (
            lax.all_gather(w_gate, ("dp", "ctx"), axis=0, tiled=True),
            lax.all_gather(w_up, ("dp", "ctx"), axis=0, tiled=True),
            lax.all_gather(w_down, ("dp", "ctx"), axis=0, tiled=True),
            lax.all_gather(mlp_gain, ("dp", "ctx"), axis=0, tiled=True),
        )
        gain_mlp = full_mlp_gain.astype(jnp.float32)
        second = normed(middle, gain_mlp).astype(jnp.bfloat16)
        gate_proj = jnp.dot(second, full_gate, preferred_element_type=jnp.float32)
        up_proj = jnp.dot(second, full_up, preferred_element_type=jnp.float32)
        sigmoid_gate = jax.nn.sigmoid(gate_proj)
        silu_gate = gate_proj * sigmoid_gate
        activated = (silu_gate * up_proj).astype(jnp.bfloat16)
        result_rows = middle + jnp.dot(activated, full_down, preferred_element_type=jnp.float32)
        outputs.append(result_rows.astype(jnp.bfloat16).reshape(SEQ_MB, shard_slots, model_width))
        cotangent = block_cotangent.reshape(row_count, model_width).astype(jnp.float32)
        full_gate, full_up, full_down = (full_gate, full_up, full_down)
        down_grad_in = block_cotangent.reshape(row_count, model_width)
        grad_down_w = jnp.einsum(
            "rf,rd->fd", activated, down_grad_in, preferred_element_type=jnp.float32
        )
        grad_act = jnp.einsum(
            "rd,fd->rf", down_grad_in, full_down, preferred_element_type=jnp.float32
        )
        grad_gate = (
            grad_act * up_proj * sigmoid_gate * (1.0 + gate_proj * (1.0 - sigmoid_gate))
        ).astype(jnp.bfloat16)
        grad_up_rows = (grad_act * silu_gate).astype(jnp.bfloat16)
        grad_gate_w = jnp.einsum("rd,rf->df", second, grad_gate, preferred_element_type=jnp.float32)
        grad_up_w = jnp.einsum(
            "rd,rf->df", second, grad_up_rows, preferred_element_type=jnp.float32
        )
        grad_second = jnp.einsum(
            "rf,df->rd", grad_gate, full_gate, preferred_element_type=jnp.float32
        ) + jnp.einsum("rf,df->rd", grad_up_rows, full_up, preferred_element_type=jnp.float32)
        _, mlp_pull = jax.vjp(normed, middle, gain_mlp)
        grad_middle_part, grad_mlp_gain = mlp_pull(grad_second)
        grad_middle = cotangent + grad_middle_part
        mlp_totals = accumulate(mlp_totals, (grad_gate_w, grad_up_w, grad_down_w, grad_mlp_gain))
        full_query, full_key, full_value, full_out = (full_query, full_key, full_value, full_out)
        attn_grad_in = grad_middle.astype(jnp.bfloat16)
        grad_out_w = jnp.einsum(
            "rh,rd->hd", mixed_rows, attn_grad_in, preferred_element_type=jnp.float32
        )
        grad_mixed = jnp.einsum(
            "rd,hd->rh", attn_grad_in, full_out, preferred_element_type=jnp.float32
        ).astype(jnp.bfloat16)
        grad_heads = grad_mixed.reshape(SEQ_MB, shard_slots, KV, groups, HD)
        scores = scored(query_heads, keys_all, causal)
        weights_full = jnp.exp(scores - log_total)
        grad_probs = jnp.einsum(
            "bqkgd,bskd->bkgqs", grad_heads, values_all, preferred_element_type=jnp.float32
        )
        row_sum = jnp.sum(weights_full * grad_probs, axis=-1, keepdims=True)
        grad_scores = (weights_full * (grad_probs - row_sum)).astype(jnp.bfloat16)
        grad_query = jnp.einsum(
            "bkgqs,bskd->bqkgd", grad_scores, keys_all, preferred_element_type=jnp.float32
        ) * HD ** (-0.5)
        weights_low = weights_full.astype(jnp.bfloat16)
        key_part = jnp.einsum(
            "bkgqs,bqkgd->bskd", grad_scores, query_heads, preferred_element_type=jnp.float32
        ) * HD ** (-0.5)
        value_part = jnp.einsum(
            "bkgqs,bqkgd->bskd", weights_low, grad_heads, preferred_element_type=jnp.float32
        )
        key_sum, value_sum = (
            lax.psum_scatter(
                key_part.reshape(SEQ_MB, SEQ, KV * HD).astype(jnp.bfloat16),
                "ctx",
                scatter_dimension=1,
                tiled=True,
            ).astype(jnp.float32),
            lax.psum_scatter(
                value_part.reshape(SEQ_MB, SEQ, KV * HD).astype(jnp.bfloat16),
                "ctx",
                scatter_dimension=1,
                tiled=True,
            ).astype(jnp.float32),
        )
        _, key_pull = jax.vjp(
            lambda raw_rows, gain_vector: prepared(raw_rows, gain_vector, cosine, sine_table),
            key_raw,
            key_gain,
        )
        grad_key_raw, grad_key_gain = key_pull(key_sum.reshape(row_count, KV * HD))
        _, query_pull = jax.vjp(
            lambda raw_rows, gain_vector: prepared(raw_rows, gain_vector, cosine, sine_table),
            query_raw,
            query_gain,
        )
        grad_query_raw, grad_query_gain = query_pull(grad_query.reshape(row_count, H * HD))
        grad_query_low = grad_query_raw.astype(jnp.bfloat16)
        grad_key_low = grad_key_raw.astype(jnp.bfloat16)
        grad_value_low = value_sum.reshape(row_count, KV * HD).astype(jnp.bfloat16)
        grad_query_w = jnp.einsum(
            "rd,rh->dh", hidden, grad_query_low, preferred_element_type=jnp.float32
        )
        grad_key_w = jnp.einsum(
            "rd,rh->dh", hidden, grad_key_low, preferred_element_type=jnp.float32
        )
        grad_value_w = jnp.einsum(
            "rd,rh->dh", hidden, grad_value_low, preferred_element_type=jnp.float32
        )
        grad_hidden = jnp.einsum(
            "rh,dh->rd", grad_query_low, full_query, preferred_element_type=jnp.float32
        )
        grad_hidden = grad_hidden + jnp.einsum(
            "rh,dh->rd", grad_key_low, full_key, preferred_element_type=jnp.float32
        )
        grad_hidden = grad_hidden + jnp.einsum(
            "rh,dh->rd", grad_value_low, full_value, preferred_element_type=jnp.float32
        )
        _, attn_pull = jax.vjp(normed, residual_in, gain_attn)
        grad_input_part, grad_attn_gain = attn_pull(grad_hidden)
        input_grads.append(
            (grad_middle + grad_input_part)
            .astype(jnp.bfloat16)
            .reshape(SEQ_MB, shard_slots, model_width)
        )
        attn_totals = accumulate(
            attn_totals,
            (
                grad_query_w,
                grad_key_w,
                grad_value_w,
                grad_out_w,
                grad_attn_gain,
                grad_query_gain,
                grad_key_gain,
            ),
        )
    mlp_sums = lax.psum_scatter(mlp_totals, ("dp", "ctx"), scatter_dimension=0, tiled=True)
    attn_sums = lax.psum_scatter(attn_totals, ("dp", "ctx"), scatter_dimension=0, tiled=True)
    output_all = jnp.concatenate(outputs, axis=0)
    input_all = jnp.concatenate(input_grads, axis=0)
    return (
        output_all,
        input_all,
        attn_sums[0],
        attn_sums[1],
        attn_sums[2],
        attn_sums[3],
        mlp_sums[0],
        mlp_sums[1],
        mlp_sums[2],
        attn_sums[4],
        mlp_sums[3],
        attn_sums[5],
        attn_sums[6],
    )


def solution(mesh):
    in_specs = (
        P("dp", "ctx", None),
        P("dp", None),
        P(("dp", "ctx"), None),
        P(("dp", "ctx"), None),
        P(("dp", "ctx"), None),
        P(("dp", "ctx"), None),
        P(("dp", "ctx"), None),
        P(("dp", "ctx"), None),
        P(("dp", "ctx"), None),
        P(("dp", "ctx")),
        P(("dp", "ctx")),
        P(("dp", "ctx")),
        P(("dp", "ctx")),
        P("dp", "ctx", None),
    )
    out_specs = (
        P("dp", "ctx", None),
        P("dp", "ctx", None),
        P(("dp", "ctx"), None),
        P(("dp", "ctx"), None),
        P(("dp", "ctx"), None),
        P(("dp", "ctx"), None),
        P(("dp", "ctx"), None),
        P(("dp", "ctx"), None),
        P(("dp", "ctx"), None),
        P(("dp", "ctx")),
        P(("dp", "ctx")),
        P(("dp", "ctx")),
        P(("dp", "ctx")),
    )
    return jax.shard_map(shards, mesh=mesh, in_specs=in_specs, out_specs=out_specs, check_vma=False)
```

profile of v0, /device:TPU:0, one launch (start us, length us, event | category | flops | bytes accessed | tf_op | source)
XLA Modules:
  0.0 2012.8 jit_solution(11946247957743827104)
XLA Ops:
  12.8 42.3 %all-reduce.17 = (bf16[1024]{0:T(1024)(128)(2,1)S(1)}, bf16[128]{0:T(256)(128)(2,1)S(1)}, bf16[128]{0:T(256)(128)(2,1)S(1)}, bf16[1024]{0:T(1024)(128)(2,1)S(1)}) all-reduce(bf16[1024]{0:T(1024)(128)(2,1)S(1)} %dynamic-update-slice, bf16[128]{0:T(256)(128)(2,1)S(1)} %dynamic-update-slice.1, ...), channel_id=1, replica_groups=mesh['dp'=4,'ctx'=8] {'dp','ctx'}, use_global_device_ids=true, to_apply=%add.8 | all-reduce | flops 2304 | bytes 9216
  58.7 11.5 all-gather.16.cloned.1.call-done
  79.3 49.3 %all-gather.14.cloned.1.call-done = bf16[1024,1024]{1,0:T(8,128)(2,1)} async-done(((bf16[32,1024]{1,0:T(8,128)(2,1)}), bf16[1024,1024]{1,0:T(8,128)(2,1)}) %all-gather.14.cloned.1.call-update) | async-done | bytes 2097168 | tf_op jit(solution)/shard_map/all_gather | solution.py:95
  140.6 52.0 %all-gather.20.cloned.1.call-done = bf16[1024,2048]{1,0:T(8,128)(2,1)} async-done(((bf16[32,2048]{1,0:T(8,128)(2,1)}), bf16[1024,2048]{1,0:T(8,128)(2,1)}) %all-gather.20.cloned.1.call-update) | async-done | bytes 4194320 | tf_op jit(solution)/shard_map/all_gather | solution.py:93
  208.7 31.7 %all-gather.30.cloned.1.call-done = bf16[1,2048,1024]{1,2,0:T(8,128)(2,1)} async-done(((bf16[1,256,1024]{1,2,0:T(8,128)(2,1)}), bf16[1,2048,1024]{1,2,0:T(8,128)(2,1)}) %all-gather.30.cloned.1.call-update) | async-done | bytes 4194320 | tf_op jit(solution)/shard_map/all_gather | solution.py:112
  240.4 16.0 fusion.9
  256.4 14.5 exponential_reduce_fusion
  270.9 16.9 all-gather.34.cloned.1.call-done
  293.1 42.1 %all-gather.32.cloned.1.call-done = bf16[2048,1024]{1,0:T(8,128)(2,1)} async-done(((bf16[256,1024]{1,0:T(8,128)(2,1)}), bf16[2048,1024]{1,0:T(8,128)(2,1)}) %all-gather.32.cloned.1.call-update) | async-done | bytes 4194320 | tf_op jit(solution)/shard_map/all_gather | solution.py:115
  340.5 17.6 fusion.39
  358.1 41.0 %all-gather.22.cloned.1.call-done = bf16[2048,1024]{1,0:T(8,128)(2,1)} async-done(((bf16[64,1024]{1,0:T(8,128)(2,1)}), bf16[2048,1024]{1,0:T(8,128)(2,1)}) %all-gather.22.cloned.1.call-update) | async-done | bytes 4194320 | tf_op jit(solution)/shard_map/all_gather | solution.py:96
  403.9 43.2 %all-gather.18.cloned.1.call-done = bf16[1,2048,1024]{1,2,0:T(8,128)(2,1)} async-done(((bf16[1,256,1024]{1,2,0:T(8,128)(2,1)}), bf16[1,2048,1024]{1,2,0:T(8,128)(2,1)}) %all-gather.18.cloned.1.call-update) | async-done | bytes 4194320 | tf_op jit(solution)/shard_map/all_gather | solution.py:112
  447.1 16.3 fusion.8
  463.4 14.5 exponential_reduce_fusion.1
  477.9 17.2 fusion.36
  499.2 18.6 all-gather.26.cloned.1.call-done
  524.1 64.5 %all-gather.24.cloned.1.call-done = bf16[1024,3072]{1,0:T(8,128)(2,1)} async-done(((bf16[32,3072]{1,0:T(8,128)(2,1)}), bf16[1024,3072]{1,0:T(8,128)(2,1)}) %all-gather.24.cloned.1.call-update) | async-done | bytes 6291472 | tf_op jit(solution)/shard_map/all_gather | solution.py:134
  594.9 64.7 %all-gather.28.cloned.1.call-done = bf16[3072,1024]{1,0:T(8,128)(2,1)} async-done(((bf16[96,1024]{1,0:T(8,128)(2,1)}), bf16[3072,1024]{1,0:T(8,128)(2,1)}) %all-gather.28.cloned.1.call-update) | async-done | bytes 6291472 | tf_op jit(solution)/shard_map/all_gather | solution.py:136
  709.2 16.8 bitcast_convert_fusion.1
  732.0 16.6 bitcast_convert_fusion
  748.7 25.8 %fusion = (f32[8,2,256]{2,1,0:T(2,128)S(1)}, f32[8,2048,256,2]{2,1,3,0:T(8,128)}) fusion(f32[8,2048,256,2]{2,1,3,0:T(8,128)} %get-tuple-element.100, f32[8,2,256]{2,1,0:T(2,128)S(1)} %bitcast.472, pred[256,2048]{0,1:T(8,128)(4,1)S(1)} %broadcast_compare_fusion, bf16[256,8,2,128]{0,3,2,1:T(8,128)(2,1)S(1)} %bitcast.444, bf16[2048,8,128,1]{2,1,0,3:T(8,128)(2,1)} %bitcast.418), kind=kOutput, calls=%fused_computation.4 | convolution fusion | flops 2189422592 | bytes 72908800 | tf_op jit(solution)/shard_map/bqkgd,bskd->bkgqs/dot_general | solution.py:183
  774.5 28.9 %fusion.13 = bf16[8,2,256,2048]{2,3,1,0:T(8,128)(2,1)} fusion(f32[8,2048,256,2]{2,1,3,0:T(8,128)} %get-tuple-element.112, f32[8,2048,256,2]{2,1,3,0:T(8,128)} %get-tuple-element.100, f32[8,2,256]{2,1,0:T(2,128)S(1)} %get-tuple-element.111, f32[8,2,256]{2,1,0:T(2,128)S(1)} %bitcast.473, pred[256,2048]{0,1:T(8,128)(4,1)S(1)} %broadcast_compare_fusion), kind=kLoop, calls=%fused_computation.23 | loop fusion | flops 50331648 | bytes 84443136 | tf_op jit(solution)/shard_map/reshape.45
  815.1 25.6 %fusion.3 = (f32[8,2,256]{2,1,0:T(2,128)S(1)}, f32[8,2048,256,2]{2,1,3,0:T(8,128)}) fusion(f32[8,2048,256,2]{2,1,3,0:T(8,128)} %get-tuple-element.102, f32[8,2,256]{2,1,0:T(2,128)S(1)} %bitcast.468, pred[256,2048]{0,1:T(8,128)(4,1)S(1)} %broadcast_compare_fusion.1, bf16[256,8,2,128]{0,3,2,1:T(8,128)(2,1)S(1)} %bitcast.442, ...), kind=kOutput, calls=%fused_computation.9 | convolution fusion | flops 2189422592 | bytes 72908800 | tf_op jit(solution)/shard_map/bqkgd,bskd->bkgqs/dot_general | solution.py:183
  840.7 29.0 %fusion.12 = bf16[8,2,256,2048]{2,3,1,0:T(8,128)(2,1)} fusion(f32[8,2048,256,2]{2,1,3,0:T(8,128)} %get-tuple-element.110, f32[8,2048,256,2]{2,1,3,0:T(8,128)} %get-tuple-element.102, f32[8,2,256]{2,1,0:T(2,128)S(1)} %get-tuple-element.109, f32[8,2,256]{2,1,0:T(2,128)S(1)} %bitcast.469, pred[256,2048]{0,1:T(8,128)(4,1)S(1)} %broadcast_compare_fusion.1), kind=kLoop, calls=%fused_computation.22 | loop fusion | flops 50331648 | bytes 84443136 | tf_op jit(solution)/shard_map/reshape.28
  990.5 40.6 %all-reduce.16 = (f32[1024]{0:T(1024)S(1)}, f32[1024]{0:T(1024)S(1)}, f32[128]{0:T(128)S(1)}, f32[128]{0:T(128)S(1)}) all-reduce(f32[1024]{0:T(1024)S(1)} %add.293, f32[1024]{0:T(1024)S(1)} %add.294, f32[128]{0:T(128)S(1)} %add.295, f32[128]{0:T(128)S(1)} %add.296), channel_id=15, replica_groups=mesh['dp'=4,'ctx'=8] {'dp','ctx'}, use_global_device_ids=true, to_apply=%region_35.36.clone | all-reduce | flops 2304 | bytes 18432
  1036.7 45.9 %reduce-scatter.26.cloned.1.call-done = f32[64,1024]{1,0:T(8,128)} async-done(((f32[2048,1024]{1,0:T(8,128)}), f32[64,1024]{1,0:T(8,128)}) %reduce-scatter.26.cloned.1.call-update) | async-done | bytes 262160 | tf_op jit(solution)/shard_map/reduce_scatter | solution.py:265
  1082.6 159.5 %reduce-scatter.30.cloned.1.call-done = f32[32,3072]{1,0:T(8,128)} async-done(((f32[1024,3072]{1,0:T(8,128)}), f32[32,3072]{1,0:T(8,128)}) %reduce-scatter.30.cloned.1.call-update) | async-done | bytes 393232 | tf_op jit(solution)/shard_map/reduce_scatter | solution.py:264
  1242.2 162.3 %reduce-scatter.28.cloned.1.call-done = f32[32,3072]{1,0:T(8,128)} async-done(((f32[1024,3072]{1,0:T(8,128)}), f32[32,3072]{1,0:T(8,128)}) %reduce-scatter.28.cloned.1.call-update) | async-done | bytes 393232 | tf_op jit(solution)/shard_map/reduce_scatter | solution.py:264
  1404.4 161.4 %reduce-scatter.32.cloned.1.call-done = f32[96,1024]{1,0:T(8,128)} async-done(((f32[3072,1024]{1,0:T(8,128)}), f32[96,1024]{1,0:T(8,128)}) %reduce-scatter.32.cloned.1.call-update) | async-done | bytes 393232 | tf_op jit(solution)/shard_map/reduce_scatter | solution.py:264
  1565.8 153.8 %reduce-scatter.20.cloned.1.call-done = f32[32,2048]{1,0:T(8,128)} async-done(((f32[1024,2048]{1,0:T(8,128)}), f32[32,2048]{1,0:T(8,128)}) %reduce-scatter.20.cloned.1.call-update) | async-done | bytes 262160 | tf_op jit(solution)/shard_map/reduce_scatter | solution.py:265
  1719.6 143.8 %reduce-scatter.24.cloned.1.call-done = f32[32,1024]{1,0:T(8,128)} async-done(((f32[1024,1024]{1,0:T(8,128)}), f32[32,1024]{1,0:T(8,128)}) %reduce-scatter.24.cloned.1.call-update) | async-done | bytes 131088 | tf_op jit(solution)/shard_map/reduce_scatter | solution.py:265
  1863.4 142.3 %reduce-scatter.22.cloned.1.call-done = f32[32,1024]{1,0:T(8,128)} async-done(((f32[1024,1024]{1,0:T(8,128)}), f32[32,1024]{1,0:T(8,128)}) %reduce-scatter.22.cloned.1.call-update) | async-done | bytes 131088 | tf_op jit(solution)/shard_map/reduce_scatter | solution.py:265
  (406 shorter events, 270.2 us)
Async XLA Ops:
  7.2 63.1 %all-gather.16.cloned.1.call-start = ((), (), s32[]{:S(2)}) async-start(), calls=%async_computation.12 | async-start | bytes 2162688 | tf_op jit(solution)/shard_map/all_gather | solution.py:94
  7.9 120.7 %all-gather.14.cloned.1.call-start = ((), (), s32[]{:S(2)}) async-start(), calls=%async_computation.11 | async-start | bytes 2162688 | tf_op jit(solution)/shard_map/all_gather | solution.py:95
  8.7 183.9 %all-gather.20.cloned.1.call-start = ((), (), s32[]{:S(2)}) async-start(), calls=%async_computation.14 | async-start | bytes 4325376 | tf_op jit(solution)/shard_map/all_gather | solution.py:93
  9.4 231.0 %all-gather.30.cloned.1.call-start = ((), (), s32[]{:S(2)}) async-start(), calls=%async_computation.19 | async-start | bytes 4718592 | tf_op jit(solution)/shard_map/all_gather | solution.py:112
  55.1 148.0 %copy-start.71 = (f32[1024]{0:T(1024)}, f32[1024]{0:T(1024)S(1)}, u32[]{:S(2)}) copy-start(f32[1024]{0:T(1024)S(1)} %convert_element_type.356) | copy-start | bytes 12292
  56.6 150.7 %copy-start.29 = (f32[256,128]{0,1:T(8,128)}, f32[256,128]{0,1:T(8,128)S(1)}, u32[]{:S(2)}) copy-start(f32[256,128]{0,1:T(8,128)S(1)} %get-tuple-element.71) | copy-start | bytes 393220
  56.6 150.7 %copy-start.54 = (f32[256,128]{0,1:T(8,128)}, f32[256,128]{0,1:T(8,128)S(1)}, u32[]{:S(2)}) copy-start(f32[256,128]{0,1:T(8,128)S(1)} %get-tuple-element.72) | copy-start | bytes 393220
  58.7 144.4 %copy-start.85 = (f32[256]{0:T(256)}, f32[256]{0:T(256)S(1)}, u32[]{:S(2)}) copy-start(f32[256]{0:T(256)S(1)} %fusion.147) | copy-start | bytes 3076
  58.7 140.3 %copy-start.91 = (f32[256]{0:T(256)}, f32[256]{0:T(256)S(1)}, u32[]{:S(2)}) copy-start(f32[256]{0:T(256)S(1)} %fusion.149) | copy-start | bytes 3076
  79.2 208.7 %all-gather.34.cloned.1.call-start = ((), (), s32[]{:S(2)}) async-start(), calls=%async_computation.32 | async-start | bytes 4718592 | tf_op jit(solution)/shard_map/all_gather | solution.py:115
  131.7 203.5 %all-gather.32.cloned.1.call-start = ((), (), s32[]{:S(2)}) async-start(), calls=%async_computation.31 | async-start | bytes 4718592 | tf_op jit(solution)/shard_map/all_gather | solution.py:115
  135.0 264.1 %all-gather.22.cloned.1.call-start = ((), (), s32[]{:S(2)}) async-start(), calls=%async_computation.15 | async-start | bytes 4325376 | tf_op jit(solution)/shard_map/all_gather | solution.py:96
  135.7 311.3 %all-gather.18.cloned.1.call-start = ((), (), s32[]{:S(2)}) async-start(), calls=%async_computation.13 | async-start | bytes 4718592 | tf_op jit(solution)/shard_map/all_gather | solution.py:112
  136.2 70.0 %copy-start.31 = (f32[256,128]{0,1:T(8,128)}, f32[256,128]{0,1:T(8,128)S(1)}, u32[]{:S(2)}) copy-start(f32[256,128]{0,1:T(8,128)S(1)} %get-tuple-element.69) | copy-start | bytes 393220
  137.4 380.4 %all-gather.26.cloned.1.call-start = ((), (), s32[]{:S(2)}) async-start(), calls=%async_computation.17 | async-start | bytes 6488064 | tf_op jit(solution)/shard_map/all_gather | solution.py:135
  138.1 450.5 %all-gather.24.cloned.1.call-start = ((), (), s32[]{:S(2)}) async-start(), calls=%async_computation.16 | async-start | bytes 6488064 | tf_op jit(solution)/shard_map/all_gather | solution.py:134
  138.7 520.9 %all-gather.28.cloned.1.call-start = ((), (), s32[]{:S(2)}) async-start(), calls=%async_computation.18 | async-start | bytes 6488064 | tf_op jit(solution)/shard_map/all_gather | solution.py:136
  139.4 809.5 %reduce-scatter.14.cloned.1.call-start = ((), (), s32[]{:S(2)}) async-start(), calls=%async_computation.21 | async-start | bytes 4718592 | tf_op jit(solution)/shard_map/reduce_scatter | solution.py:205
  207.3 239.8 %copy-start.18 = (bf16[256,16,128]{0,2,1:T(8,128)(2,1)}, bf16[256,16,128]{0,2,1:T(8,128)(2,1)S(1)}, u32[]{:S(2)}) copy-start(bf16[256,16,128]{0,2,1:T(8,128)(2,1)S(1)} %fusion.29) | copy-start | bytes 3145732
  499.0 203.5 %copy-start.11 = (f32[256,1024]{1,0:T(8,128)}, f32[256,1024]{1,0:T(8,128)S(1)}, u32[]{:S(2)}) copy-start(f32[256,1024]{1,0:T(8,128)S(1)} %get-tuple-element.104) | copy-start | bytes 3145732
  499.2 89.4 %copy-start.25 = (bf16[256,1024]{1,0:T(8,128)(2,1)}, bf16[256,1024]{1,0:T(8,128)(2,1)S(1)}, u32[]{:S(2)}) copy-start(bf16[256,1024]{1,0:T(8,128)(2,1)S(1)} %multiply_convert_fusion.7) | copy-start | bytes 1572868
  703.1 179.9 %copy-start.13 = (f32[256,1024]{1,0:T(8,128)}, f32[256,1024]{1,0:T(8,128)S(1)}, u32[]{:S(2)}) copy-start(f32[256,1024]{1,0:T(8,128)S(1)} %get-tuple-element.60) | copy-start | bytes 3145732
  726.0 226.8 %reduce-scatter.18.cloned.1.call-start = ((), (), s32[]{:S(2)}) async-start(), calls=%async_computation.23 | async-start | bytes 4718592 | tf_op jit(solution)/shard_map/reduce_scatter | solution.py:205
  748.6 209.7 %reduce-scatter.16.cloned.1.call-start = ((), (), s32[]{:S(2)}) async-start(), calls=%async_computation.22 | async-start | bytes 4718592 | tf_op jit(solution)/shard_map/reduce_scatter | solution.py:199
  813.9 146.8 %reduce-scatter.12.cloned.1.call-start = ((), (), s32[]{:S(2)}) async-start(), calls=%async_computation.20 | async-start | bytes 4718592 | tf_op jit(solution)/shard_map/reduce_scatter | solution.py:199
  880.2 202.4 %reduce-scatter.26.cloned.1.call-start = ((), (), s32[]{:S(2)}) async-start(), calls=%async_computation.27 | async-start | bytes 8650752 | tf_op jit(solution)/shard_map/reduce_scatter | solution.py:265
  887.6 354.6 %reduce-scatter.30.cloned.1.call-start = ((), (), s32[]{:S(2)}) async-start(), calls=%async_computation.29 | async-start | bytes 12976128 | tf_op jit(solution)/shard_map/reduce_scatter | solution.py:264
  897.5 506.9 %reduce-scatter.28.cloned.1.call-start = ((), (), s32[]{:S(2)}) async-start(), calls=%async_computation.28 | async-start | bytes 12976128 | tf_op jit(solution)/shard_map/reduce_scatter | solution.py:264
  907.5 658.3 %reduce-scatter.32.cloned.1.call-start = ((), (), s32[]{:S(2)}) async-start(), calls=%async_computation.30 | async-start | bytes 12976128 | tf_op jit(solution)/shard_map/reduce_scatter | solution.py:264
  917.6 802.0 %reduce-scatter.20.cloned.1.call-start = ((), (), s32[]{:S(2)}) async-start(), calls=%async_computation.24 | async-start | bytes 8650752 | tf_op jit(solution)/shard_map/reduce_scatter | solution.py:265
  948.9 914.6 %reduce-scatter.24.cloned.1.call-start = ((), (), s32[]{:S(2)}) async-start(), calls=%async_computation.26 | async-start | bytes 4325376 | tf_op jit(solution)/shard_map/reduce_scatter | solution.py:265
  958.0 1047.7 %reduce-scatter.22.cloned.1.call-start = ((), (), s32[]{:S(2)}) async-start(), calls=%async_computation.25 | async-start | bytes 4325376 | tf_op jit(solution)/shard_map/reduce_scatter | solution.py:265
  (104 other events, 746.9 us)
Sparse Core Ops, SparseCore 0:
  11.0 59.1 all-gather.15
  73.2 55.3 all-gather.13
  131.6 60.9 all-gather.19
  194.0 46.3 all-gather.29
  242.5 45.3 all-gather.33
  289.3 45.8 all-gather.31
  338.2 60.8 all-gather.21
  400.7 46.3 all-gather.17
  450.1 67.6 all-gather.25
  520.6 67.9 all-gather.23
  591.6 67.9 all-gather.27
  726.1 48.4 reduce-scatter.13
  776.9 48.1 reduce-scatter.17
  827.3 48.1 reduce-scatter.15
  880.4 49.2 reduce-scatter.11
  932.4 150.2 reduce-scatter.25
  1089.1 153.0 reduce-scatter.29
  1249.7 154.7 reduce-scatter.27
  1411.0 154.7 reduce-scatter.31
  1568.7 150.9 reduce-scatter.19
  1722.6 140.8 reduce-scatter.23
  1866.4 139.3 reduce-scatter.21
where the time goes:
time: 2020 us; the launch traced here: 2010 us
  waiting for transfers between devices  1410 us (70%)
  matrix products  342 us (17%)
  other arithmetic  114 us (6%)
  blocking collectives  82.9 us (4%)
  local copies, waits for them, and re-layouts  47.1 us (2%)
    reduce_scatter x4, waiting for transfers between devices, shards(): lax.psum_scatter(attn_totals, ('dp', 'ctx'), scatter_dimension=0, tiled=T...  486 us
    reduce_scatter x3, waiting for transfers between devices, shards(): lax.psum_scatter(mlp_totals, ('dp', 'ctx'), scatter_dimension=0, tiled=True)  483 us
    unnamed x2, blocking collectives  82.9 us
    all_gather x2, waiting for transfers between devices, shards(): lax.all_gather(keys_own.reshape(SEQ_MB, shard_slots, KV * HD), 'ctx', axi...  74.9 us
    all_gather x1, waiting for transfers between devices, shards(): lax.all_gather(w_down, ('dp', 'ctx'), axis=0, tiled=True)  64.7 us
    all_gather x1, waiting for transfers between devices, shards(): lax.all_gather(w_gate, ('dp', 'ctx'), axis=0, tiled=True)  64.5 us
    all_gather x2, waiting for transfers between devices, shards(): lax.all_gather(values_own.reshape(SEQ_MB, shard_slots, KV * HD), 'ctx', a...  59 us
    another operation x2, other arithmetic  57.9 us
  transfers between devices with their start and end apart: 22, of which 18 were waited for; matrix products, arithmetic and copies ran while one was open for 21% of the time, Pallas kernels for 0%

commit v1 on v0

v1 whole, which is shorter than its diff:
```python
import functools

import jax
import jax.numpy as jnp
import numpy as np
from jax import lax
from jax.experimental import pallas as pl
from jax.experimental.pallas import tpu as pltpu
from jax.sharding import PartitionSpec as P

H = 16
KV = 8
HD = 128
GROUPS = H // KV
EPSILON = 1e-06
THETA = 1000000.0
LOG2E = 1.4426950408889634
KEY_TILE = 512
VMEM_LIMIT = 48 * 1024 * 1024
MESH = pl.DeviceIdType.MESH
F32 = jnp.float32
BF16 = jnp.bfloat16


def normed(values, weights):
    return values * lax.rsqrt(jnp.mean(values * values, axis=-1, keepdims=True) + EPSILON) * weights


def norm_back(values, weights, grad):
    r = lax.rsqrt(jnp.mean(values * values, axis=-1, keepdims=True) + EPSILON)
    unit = values * r
    u = grad * weights
    return r * (u - unit * jnp.mean(u * unit, axis=-1, keepdims=True)), grad * unit


def rope_tables(seq):
    half = HD // 2
    inverse = (THETA ** (-(np.arange(half, dtype=np.float32) * np.float32(2.0) / np.float32(HD)))).astype(np.float32)
    angles = np.arange(seq, dtype=np.float32)[:, None] * inverse[None, :]
    cosine, sine = np.cos(angles), np.sin(angles)
    return (
        jnp.asarray(np.concatenate([cosine, cosine], axis=-1).astype(np.float32)),
        jnp.asarray(np.concatenate([-sine, sine], axis=-1).astype(np.float32)),
    )


def dot(a, b, dims, out=F32):
    return lax.dot_general(a, b, (dims, ((), ())), preferred_element_type=out)


NN = ((1,), (0,))
NT = ((1,), (1,))
TN = ((0,), (0,))


def sort_norm_kernel(order_ref, x_ref, gain_ref, o_ref):
    x = x_ref[...].astype(F32)
    o_ref[...] = normed(x, gain_ref[...]).astype(o_ref.dtype)


def sort_norm(order, rows, gain, span):
    count, width = rows.shape
    return pl.pallas_call(
        sort_norm_kernel,
        out_shape=jax.ShapeDtypeStruct((count, width), BF16),
        grid_spec=pltpu.PrefetchScalarGridSpec(
            num_scalar_prefetch=1,
            grid=(count // span,),
            in_specs=[
                pl.BlockSpec((span, width), lambda i, order: (order[i], 0)),
                pl.BlockSpec((1, width), lambda i, order: (0, 0)),
            ],
            out_specs=pl.BlockSpec((span, width), lambda i, order: (i, 0)),
        ),
        name="sort_norm",
    )(order, rows, gain)


def pick_kernel(order_ref, x_ref, o_ref):
    o_ref[...] = x_ref[...]


def pick_blocks(order, rows, span):
    count, width = rows.shape
    return pl.pallas_call(
        pick_kernel,
        out_shape=jax.ShapeDtypeStruct((count, width), rows.dtype),
        grid_spec=pltpu.PrefetchScalarGridSpec(
            num_scalar_prefetch=1,
            grid=(count // span,),
            in_specs=[pl.BlockSpec((span, width), lambda i, order: (order[i], 0))],
            out_specs=pl.BlockSpec((span, width), lambda i, order: (i, 0)),
        ),
        name="pick_blocks",
    )(order, rows)


def unit_rows(raw):
    r = lax.rsqrt(jnp.mean(raw * raw, axis=-1, keepdims=True) + EPSILON)
    return raw * r, r


def rope(values, cosine, sine):
    return values * cosine + pltpu.roll(values, HD // 2, 1) * sine


def rope_back(values, cosine, sine):
    return values * cosine - pltpu.roll(values, HD // 2, 1) * sine


def prepare_keys(k_ref, cos_ref, sin_ref, gk_ref, ks_ref):
    step = 256

    def body(i, _):
        rows = pl.ds(pl.multiple_of(i * step, step), step)
        unit, _r = unit_rows(k_ref[rows, :].astype(F32))
        ks_ref[rows, :] = rope(unit * gk_ref[...], cos_ref[rows, :], sin_ref[rows, :]).astype(BF16)
        return 0

    lax.fori_loop(0, k_ref.shape[0] // step, body, 0)


def query_block(q_ref, rows, places, cos_ref, sin_ref, gq_ref):
    units, scales, parts = [], [], []
    for g in range(GROUPS):
        unit, r = unit_rows(q_ref[rows, g * HD : (g + 1) * HD].astype(F32))
        turned = rope(unit * gq_ref[...], cos_ref[places, :], sin_ref[places, :])
        units.append(unit)
        scales.append(r)
        parts.append((turned * (LOG2E * HD**-0.5)).astype(BF16))
    return units, scales, jnp.concatenate(parts, axis=0)


def attend_kernel(span, ids_ref, q_ref, k_ref, v_ref, cos_ref, sin_ref, gq_ref, gk_ref, o_ref, lse_ref, ks_ref, acc_ref, sum_ref):
    prepare_keys(k_ref, cos_ref, sin_ref, gk_ref, ks_ref)
    m = GROUPS * span

    def block(j, _):
        b = ids_ref[j]
        rows = pl.ds(pl.multiple_of(j * span, span), span)
        places = pl.ds(pl.multiple_of(b * span, span), span)
        _u, _s, q2 = query_block(q_ref, rows, places, cos_ref, sin_ref, gq_ref)
        acc_ref[...] = jnp.zeros_like(acc_ref)
        sum_ref[...] = jnp.zeros_like(sum_ref)

        def tile(t, masked):
            keys = pl.ds(pl.multiple_of(t * KEY_TILE, KEY_TILE), KEY_TILE)
            p = jnp.exp2(dot(q2, ks_ref[keys, :], NT))
            if masked:
                at = t * KEY_TILE + lax.broadcasted_iota(jnp.int32, p.shape, 1)
                own = b * span + lax.broadcasted_iota(jnp.int32, p.shape, 0) % span
                p = jnp.where(at <= own, p, 0.0)
            part = p[:, 0:HD]
            for i in range(1, KEY_TILE // HD):
                part = part + p[:, i * HD : (i + 1) * HD]
            sum_ref[...] += part
            acc_ref[...] += dot(p.astype(BF16), v_ref[keys, :], NN)

        last = (b * span) // KEY_TILE
        lax.fori_loop(0, last, lambda t, _: (tile(t, False), 0)[1], 0)
        tile(last, True)
        total = jnp.sum(sum_ref[...], axis=-1, keepdims=True)
        mixed = acc_ref[...] * (1.0 / total)
        for g in range(GROUPS):
            o_ref[rows, g * HD : (g + 1) * HD] = mixed[g * span : (g + 1) * span].astype(BF16)
        wide = jnp.broadcast_to(jnp.log2(total), (m, HD))
        lse_ref[0, j] = jnp.transpose(wide)[0:1, :]
        return 0

    lax.fori_loop(0, q_ref.shape[0] // span, block, 0)


def attend(ids, q_raw, kv_raw, cosine, sine, gq, gk, span):
    rows = q_raw.shape[0]
    seq = kv_raw.shape[0]
    heads = q_raw.shape[1] // (GROUPS * HD)
    blocks, m = rows // span, GROUPS * span
    whole = lambda k, ids: (0, 0)
    return pl.pallas_call(
        functools.partial(attend_kernel, span),
        out_shape=[
            jax.ShapeDtypeStruct((rows, heads * GROUPS * HD), BF16),
            jax.ShapeDtypeStruct((heads, blocks, 1, m), F32),
        ],
        grid_spec=pltpu.PrefetchScalarGridSpec(
            num_scalar_prefetch=1,
            grid=(heads,),
            in_specs=[
                pl.BlockSpec((rows, GROUPS * HD), lambda k, ids: (0, k)),
                pl.BlockSpec((seq, HD), lambda k, ids: (0, k)),
                pl.BlockSpec((seq, HD), lambda k, ids: (0, heads + k)),
                pl.BlockSpec((seq, HD), whole),
                pl.BlockSpec((seq, HD), whole),
                pl.BlockSpec((1, HD), whole),
                pl.BlockSpec((1, HD), whole),
            ],
            out_specs=[
                pl.BlockSpec((rows, GROUPS * HD), lambda k, ids: (0, k)),
                pl.BlockSpec((1, blocks, 1, m), lambda k, ids: (k, 0, 0, 0)),
            ],
            scratch_shapes=[
                pltpu.VMEM((seq, HD), BF16),
                pltpu.VMEM((m, HD), F32),
                pltpu.VMEM((m, HD), F32),
            ],
        ),
        compiler_params=pltpu.CompilerParams(vmem_limit_bytes=VMEM_LIMIT),
        cost_estimate=pl.CostEstimate(
            flops=2 * 2 * rows * seq * heads * GROUPS * HD,
            bytes_accessed=2 * (2 * rows * heads * GROUPS * HD + 2 * seq * heads * HD),
            transcendentals=rows * seq * heads * GROUPS // 2,
        ),
        name="attend",
    )(ids, q_raw, kv_raw, kv_raw, cosine, sine, gq, gk)


def attend_back_kernel(
    span, ids_ref, q_ref, k_ref, v_ref, do_ref, o_ref, lse_ref, cos_ref, sin_ref, gq_ref, gk_ref,
    dq_ref, dk_ref, dv_ref, dgq_ref, dgk_ref, ks_ref, dka_ref, dva_ref, dqa_ref,
):
    prepare_keys(k_ref, cos_ref, sin_ref, gk_ref, ks_ref)
    dka_ref[...] = jnp.zeros_like(dka_ref)
    dva_ref[...] = jnp.zeros_like(dva_ref)

    @pl.when(pl.program_id(0) == 0)
    def _():
        dgq_ref[...] = jnp.zeros_like(dgq_ref)
        dgk_ref[...] = jnp.zeros_like(dgk_ref)

    def block(j, _):
        b = ids_ref[j]
        rows = pl.ds(pl.multiple_of(j * span, span), span)
        places = pl.ds(pl.multiple_of(b * span, span), span)
        units, scales, q2 = query_block(q_ref, rows, places, cos_ref, sin_ref, gq_ref)
        do2 = jnp.concatenate([do_ref[rows, g * HD : (g + 1) * HD] for g in range(GROUPS)], axis=0)
        o2 = jnp.concatenate([o_ref[rows, g * HD : (g + 1) * HD] for g in range(GROUPS)], axis=0)
        delta = jnp.sum(jnp.transpose(do2.astype(F32) * o2.astype(F32)), axis=0, keepdims=True)
        lse = lse_ref[0, j]
        dqa_ref[...] = jnp.zeros_like(dqa_ref)

        def tile(t, masked):
            keys = pl.ds(pl.multiple_of(t * KEY_TILE, KEY_TILE), KEY_TILE)
            kt = ks_ref[keys, :]
            p = jnp.exp2(dot(kt, q2, NT) - lse)
            if masked:
                at = t * KEY_TILE + lax.broadcasted_iota(jnp.int32, p.shape, 0)
                own = b * span + lax.broadcasted_iota(jnp.int32, p.shape, 1) % span
                p = jnp.where(at <= own, p, 0.0)
            ds = (p * (dot(v_ref[keys, :], do2, NT) - delta)).astype(BF16)
            dva_ref[keys, :] += dot(p.astype(BF16), do2, NN)
            dka_ref[keys, :] += dot(ds, q2, NN)
            dqa_ref[...] += dot(ds, kt, TN)

        last = (b * span) // KEY_TILE
        lax.fori_loop(0, last, lambda t, _: (tile(t, False), 0)[1], 0)
        tile(last, True)
        dq = dqa_ref[...] * HD**-0.5
        for g in range(GROUPS):
            grad = rope_back(dq[g * span : (g + 1) * span], cos_ref[places, :], sin_ref[places, :])
            dgq_ref[...] += jnp.sum(grad * units[g], axis=0, keepdims=True)
            u = grad * gq_ref[...]
            back = scales[g] * (u - units[g] * jnp.mean(u * units[g], axis=-1, keepdims=True))
            dq_ref[rows, g * HD : (g + 1) * HD] = back.astype(BF16)
        return 0

    lax.fori_loop(0, q_ref.shape[0] // span, block, 0)
    step = 256

    def finish(i, _):
        rows = pl.ds(pl.multiple_of(i * step, step), step)
        unit, r = unit_rows(k_ref[rows, :].astype(F32))
        grad = rope_back(dka_ref[rows, :] * (1.0 / LOG2E), cos_ref[rows, :], sin_ref[rows, :])
        dgk_ref[...] += jnp.sum(grad * unit, axis=0, keepdims=True)
        u = grad * gk_ref[...]
        back = r * (u - unit * jnp.mean(u * unit, axis=-1, keepdims=True))
        dk_ref[rows, :] = back.astype(BF16)
        dv_ref[rows, :] = dva_ref[rows, :].astype(BF16)
        return 0

    lax.fori_loop(0, k_ref.shape[0] // step, finish, 0)


def attend_back(ids, q_raw, kv_raw, grad_mixed, mixed, lse, cosine, sine, gq, gk, span):
    rows = q_raw.shape[0]
    seq = kv_raw.shape[0]
    heads = q_raw.shape[1] // (GROUPS * HD)
    blocks, m = rows // span, GROUPS * span
    whole = lambda k, ids: (0, 0)
    per_query = pl.BlockSpec((rows, GROUPS * HD), lambda k, ids: (0, k))
    per_key = pl.BlockSpec((seq, HD), lambda k, ids: (0, k))
    gain = pl.BlockSpec((1, HD), whole)
    return pl.pallas_call(
        functools.partial(attend_back_kernel, span),
        out_shape=[
            jax.ShapeDtypeStruct((rows, heads * GROUPS * HD), BF16),
            jax.ShapeDtypeStruct((seq, heads * HD), BF16),
            jax.ShapeDtypeStruct((seq, heads * HD), BF16),
            jax.ShapeDtypeStruct((1, HD), F32),
            jax.ShapeDtypeStruct((1, HD), F32),
        ],
        grid_spec=pltpu.PrefetchScalarGridSpec(
            num_scalar_prefetch=1,
            grid=(heads,),
            in_specs=[
                per_query,
                per_key,
                pl.BlockSpec((seq, HD), lambda k, ids: (0, heads + k)),
                per_query,
                per_query,
                pl.BlockSpec((1, blocks, 1, m), lambda k, ids: (k, 0, 0, 0)),
                pl.BlockSpec((seq, HD), whole),
                pl.BlockSpec((seq, HD), whole),
                gain,
                gain,
            ],
            out_specs=[per_query, per_key, per_key, gain, gain],
            scratch_shapes=[
                pltpu.VMEM((seq, HD), BF16),
                pltpu.VMEM((seq, HD), F32),
                pltpu.VMEM((seq, HD), F32),
                pltpu.VMEM((m, HD), F32),
            ],
        ),
        compiler_params=pltpu.CompilerParams(vmem_limit_bytes=VMEM_LIMIT),
        cost_estimate=pl.CostEstimate(
            flops=5 * 2 * rows * seq * heads * GROUPS * HD // 2,
            bytes_accessed=2 * (4 * rows * heads * GROUPS * HD + 4 * seq * heads * HD),
            transcendentals=rows * seq * heads * GROUPS // 2,
        ),
        name="attend_back",
    )(ids, q_raw, kv_raw, kv_raw, grad_mixed, mixed, lse, cosine, sine, gq, gk)


def peers():
    dp, ctx = lax.axis_index("dp"), lax.axis_index("ctx")
    to = lambda d, k: (jnp.bitwise_xor(dp, d), jnp.bitwise_xor(ctx, k))
    return dp, ctx, to


def greet(devices):
    barrier = pltpu.get_barrier_semaphore()
    for device in devices:
        pl.semaphore_signal(barrier, inc=1, device_id=device, device_id_type=MESH)
    pl.semaphore_wait(barrier, len(devices))


def sender(send_sem, recv_sem):
    made = []

    def send(src, dst, device):
        i = len(made)
        copy = pltpu.make_async_remote_copy(
            src_ref=src, dst_ref=dst, send_sem=send_sem.at[i], recv_sem=recv_sem.at[i],
            device_id=device, device_id_type=MESH,
        )
        copy.start()
        made.append(copy)
        return copy

    return send, made


def gather_kernel(pk_ref, wo_ref, tok_ref, w_ref, x_ref, send_sem, recv_sem, local_sem):
    dp, ctx, to = peers()
    c, z = ctx % 2, ctx // 2
    which = ctx // 4
    greet([to(0, 1), to(0, 2), to(0, 4), to(0, 6), to(1, 0), to(2, 0)])
    send, made = sender(send_sem, recv_sem)
    sib, nbr, far, xn, yn = to(0, 1), to(0, 2), to(0, 4), to(1, 0), to(2, 0)
    rows = pk_ref.shape[1]
    cols = pk_ref.shape[2]
    slots = tok_ref.shape[1]

    me = ctx % 4
    local = [
        pltpu.make_async_copy(tok_ref.at[which], x_ref.at[me, 0], local_sem.at[0]),
        pltpu.make_async_copy(pk_ref.at[c], w_ref.at[dp, z, pl.ds(c * rows, rows), pl.ds(0, cols)], local_sem.at[1]),
        pltpu.make_async_copy(wo_ref, w_ref.at[dp, z, :, pl.ds(cols, wo_ref.shape[1])], local_sem.at[2]),
    ]
    for copy in local:
        copy.start()
    swap = send(tok_ref.at[1 - which], x_ref.at[me, 1], far)
    mine_sib = send(tok_ref.at[which], x_ref.at[me, 0], sib)
    mine_nbr = send(tok_ref.at[which], x_ref.at[me, 0], nbr)
    cross = send(pk_ref.at[1 - c], w_ref.at[dp, z, pl.ds(c * rows, rows), pl.ds(0, cols)], sib)
    for copy in local:
        copy.wait()
    cross.wait_recv()

    def block(q, zz, part=None):
        if part is None:
            return w_ref.at[q, zz]
        return w_ref.at[q, zz, pl.ds(part * rows, rows)]

    own = block(dp, z)
    arrive = [send(own, own, to(0, 2 * k)) for k in (1, 2, 3)]
    first_y, first_x, last = [], [], []

    def spread(zz):
        first_y.append(send(block(dp, zz, 0), block(dp, zz, 0), yn))
        first_x.append(send(block(dp, zz, 1), block(dp, zz, 1), xn))
        last.append(send(block(dp, zz, 0), block(dp, zz, 0), xn))
        last.append(send(block(dp, zz, 1), block(dp, zz, 1), yn))

    spread(z)
    swap.wait_recv()
    swap_sib = send(x_ref.at[me, 1], x_ref.at[me, 1], sib)
    swap_nbr = send(x_ref.at[me, 1], x_ref.at[me, 1], nbr)
    order = [z] + [jnp.bitwise_xor(z, k) for k in (1, 2, 3)]
    other = jnp.bitwise_xor(me, 2)
    for k in (1, 2, 3):
        arrive[k - 1].wait_recv()
        spread(order[k])
        if k == 2:
            mine_nbr.wait_recv()
            last.append(send(x_ref.at[other, 0], x_ref.at[other, 0], sib))
    swap_nbr.wait_recv()
    last.append(send(x_ref.at[other, 1], x_ref.at[other, 1], sib))
    for k in range(4):
        zz = order[k]
        first_y[k].wait_recv()
        from_y = block(jnp.bitwise_xor(dp, 2), zz, 0)
        last.append(send(from_y, from_y, xn))
        first_x[k].wait_recv()
        from_x = block(jnp.bitwise_xor(dp, 1), zz, 1)
        last.append(send(from_x, from_x, yn))
    for copy in last + [mine_sib, swap_sib]:
        copy.wait_recv()
    for copy in made:
        copy.wait_send()


def gather(packed, w_out, tokens):
    rows, cols = 2 * packed.shape[1], packed.shape[2] + w_out.shape[1]
    copies = 45
    anywhere = pl.BlockSpec(memory_space=pl.ANY)
    w, x = pl.pallas_call(
        gather_kernel,
        out_shape=[
            jax.ShapeDtypeStruct((4, 4, rows, cols), BF16),
            jax.ShapeDtypeStruct((4, 2) + tokens.shape[1:], BF16),
        ],
        in_specs=[anywhere] * 3,
        out_specs=[anywhere] * 2,
        scratch_shapes=[
            pltpu.SemaphoreType.DMA((copies,)),
            pltpu.SemaphoreType.DMA((copies,)),
            pltpu.SemaphoreType.DMA((3,)),
        ],
        compiler_params=pltpu.CompilerParams(collective_id=0, has_side_effects=True),
        name="gather",
    )(packed, w_out, tokens)
    return w.reshape(16 * rows, cols), x.reshape(-1, tokens.shape[2])


def reduce_kernel(n_in, *refs):
    g_refs, o_ref = refs[:n_in], refs[n_in]
    g_ref, in_a, in_b, mid_a, mid_b, got_a, got_b, out3, in3, send_sem, recv_sem, local_sem = refs[n_in + 1 :]
    dp, ctx, to = peers()
    z = ctx // 2
    x, y = dp % 2, dp // 2
    greet([to(0, 2), to(0, 4), to(0, 6), to(1, 0), to(2, 0)])
    send, made = sender(send_sem, recv_sem)
    xn, yn = to(1, 0), to(2, 0)
    hr = g_ref.shape[3] // 2
    at, local = 0, []
    for i, ref in enumerate(g_refs):
        width = ref.shape[-1]
        local.append(pltpu.make_async_copy(ref, g_ref.at[:, :, :, :, pl.ds(at, width)], local_sem.at[i]))
        at += width
    for copy in local:
        copy.start()
    for copy in local:
        copy.wait()
    low, high = pl.ds(0, hr), pl.ds(hr, hr)
    order = [jnp.bitwise_xor(z, k) for k in (2, 3, 1, 0)]
    a_in, b_in = [], []
    for k, zz in enumerate(order):
        a_in.append(send(g_ref.at[:, 1 - x, zz, low], in_a.at[k], xn))
        b_in.append(send(g_ref.at[1 - y, :, zz, high], in_b.at[k], yn))
    add = lambda p, q: (p.astype(F32) + q.astype(F32)).astype(BF16)
    a_mid, b_mid = [], []
    for k, zz in enumerate(order):
        a_in[k].wait_recv()
        mid_a[k] = add(g_ref[1 - y, x, zz, 0:hr], in_a[k, 1 - y])
        a_mid.append(send(mid_a.at[k], got_a.at[k], yn))
        b_in[k].wait_recv()
        mid_b[k] = add(g_ref[y, 1 - x, zz, hr:], in_b[k, 1 - x])
        b_mid.append(send(mid_b.at[k], got_b.at[k], xn))
    final = []
    for k, zz in enumerate(order):
        a_mid[k].wait_recv()
        out3[k, 0:hr] = (
            g_ref[y, x, zz, 0:hr].astype(F32) + in_a[k, y].astype(F32) + got_a[k].astype(F32)
        ).astype(BF16)
        b_mid[k].wait_recv()
        out3[k, hr:] = (
            g_ref[y, x, zz, hr:].astype(F32) + in_b[k, x].astype(F32) + got_b[k].astype(F32)
        ).astype(BF16)
        if k < 3:
            final.append(send(out3.at[k], in3.at[k], to(0, 2 * (2, 3, 1)[k])))
    for copy in final:
        copy.wait_recv()
    o_ref[...] = (
        out3[3].astype(F32) + in3[0].astype(F32) + in3[1].astype(F32) + in3[2].astype(F32)
    ).astype(BF16)
    for copy in made:
        copy.wait_send()


def reduce(grads):
    rows = grads[0].shape[0] // 16
    cols = sum(g.shape[1] for g in grads)
    grads = [g.reshape(2, 2, 4, rows, g.shape[1]) for g in grads]
    copies = 19
    return pl.pallas_call(
        functools.partial(reduce_kernel, len(grads)),
        out_shape=jax.ShapeDtypeStruct((rows, cols), BF16),
        in_specs=[pl.BlockSpec(memory_space=pl.ANY)] * len(grads),
        out_specs=pl.BlockSpec(memory_space=pltpu.VMEM),
        scratch_shapes=[
            pltpu.VMEM((2, 2, 4, rows, cols), BF16),
            pltpu.VMEM((4, 2, rows // 2, cols), BF16),
            pltpu.VMEM((4, 2, rows // 2, cols), BF16),
        ]
        + [pltpu.VMEM((4, rows // 2, cols), BF16)] * 4
        + [
            pltpu.VMEM((4, rows, cols), BF16),
            pltpu.VMEM((3, rows, cols), BF16),
            pltpu.SemaphoreType.DMA((copies,)),
            pltpu.SemaphoreType.DMA((copies,)),
            pltpu.SemaphoreType.DMA((len(grads),)),
        ],
        compiler_params=pltpu.CompilerParams(
            collective_id=1, has_side_effects=True, vmem_limit_bytes=VMEM_LIMIT
        ),
        name="reduce",
    )(*grads)


def by_core(c, own, other):
    return jnp.where(c == 0, jnp.stack([own, other]), jnp.stack([other, own]))


def layer(
    n_dp, n, tokens, positions, w_query, w_key, w_value, w_out, w_gate, w_up, w_down,
    attn_gain, mlp_gain, q_gain, k_gain, grad_out,
):
    axes = ("dp", "ctx")
    slots, width = tokens.shape[1:]
    seq = positions.shape[1]
    span = slots // 2
    half = n // 2
    chips = n_dp * half
    ctx = lax.axis_index("ctx")
    c = ctx % 2
    which = ctx // half
    r_in, r_out, r_down = w_query.shape[0], w_out.shape[0], w_down.shape[0]
    ff = w_gate.shape[1]
    ff_c = ff // 2
    q_c, kv_c = H * HD // 2, KV * HD // 2

    to_sibling = [(i, i ^ 1) for i in range(n)]
    to_partner = [(i, (i + half) % n) for i in range(n)]
    halves = [list(range(half)), list(range(half, n))]
    same_core = [list(range(0, n, 2)), list(range(1, n, 2))]
    sibling = lambda v: lax.ppermute(v, "ctx", to_sibling)
    partner = lambda v: lax.ppermute(v, "ctx", to_partner)

    def placed(values):
        mine = lax.dynamic_index_in_dim(values, which, 0, False)
        other = lax.dynamic_index_in_dim(values, 1 - which, 0, False)
        return jnp.concatenate([mine, partner(other)], axis=0)

    gains = jnp.concatenate(
        [
            attn_gain[:, None],
            mlp_gain[:, None],
            jnp.pad(q_gain, (0, r_in - q_gain.shape[0]))[:, None],
            jnp.pad(k_gain, (0, r_in - k_gain.shape[0]))[:, None],
            jnp.zeros((r_in, 124), BF16),
        ],
        axis=1,
    )
    tall = (n_dp, n) == (4, 8)
    qkv_halves = [
        jnp.concatenate(
            [
                w_query[:, i * q_c : (i + 1) * q_c],
                w_key[:, i * kv_c : (i + 1) * kv_c],
                w_value[:, i * kv_c : (i + 1) * kv_c],
            ],
            axis=1,
        )
        for i in range(2)
    ]

    def ff_order(shard):
        return shard.reshape(r_in, chips, 2, r_down).transpose(2, 0, 1, 3).reshape(2, r_in, ff_c)

    gate_order, up_order = ff_order(w_gate), ff_order(w_up)
    qkv_c = q_c + 2 * kv_c
    packed = jnp.stack(
        [
            jnp.concatenate([qkv_halves[i], gains, gate_order[i], up_order[i]], axis=1)
            for i in range(2)
        ]
    )
    if tall:
        w_all, x_all = gather(packed, w_out, tokens)
        x_own = lax.dynamic_slice_in_dim(x_all, (ctx % half) * 2 * slots, 2 * slots, 0)
        w_qkv = w_all[:, :qkv_c]
        g_cols = w_all[:, qkv_c : qkv_c + HD].astype(F32)
        w_gu = w_all[:, qkv_c + HD : qkv_c + HD + 2 * ff_c]
        out_rows = w_all[:, qkv_c + HD + 2 * ff_c :].reshape(2, -1, r_out, width)
        out_keep = lax.dynamic_index_in_dim(out_rows, c, 0, False)
        out_give = lax.dynamic_index_in_dim(out_rows, 1 - c, 0, False)
        w_out_c = by_core(c, out_keep, sibling(out_give)).transpose(1, 0, 2, 3).reshape(q_c, width)
        w_down, w_all = lax.optimization_barrier((w_down, w_all))
    else:
        both = lax.all_gather(packed, axes, axis=1, tiled=True)
        w_all = lax.dynamic_index_in_dim(both, c, 0, False)
        out_all = lax.all_gather(w_out, axes, axis=0, tiled=True)
        x_own = placed(tokens)
        x_all = lax.all_gather(x_own, "ctx", axis=0, tiled=True, axis_index_groups=halves)
        w_qkv = w_all[:, :qkv_c]
        g_cols = w_all[:, qkv_c : qkv_c + HD].astype(F32)
        w_gu = w_all[:, qkv_c + HD :]
        w_out_c = lax.dynamic_slice_in_dim(out_all, c * q_c, q_c, 0)
    down_all = lax.all_gather(w_down, axes, axis=0, tiled=True)
    w_down_c = lax.dynamic_index_in_dim(down_all.reshape(chips, 2, r_down, width), c, 1, False).reshape(ff_c, width)
    gain_attn = g_cols[:, 0][None]
    gain_mlp = g_cols[:, 1][None]
    per_head = g_cols.reshape(n_dp * n, r_in, HD)[:, : q_gain.shape[0]].reshape(HD, HD)
    gain_q = per_head[:, 2][None]
    gain_k = per_head[:, 3][None]

    chip = (ctx % half) // 2
    chip_rows = 4 * slots
    x_chip = lax.dynamic_slice_in_dim(x_all, chip * chip_rows, chip_rows, 0)
    go_own = placed(grad_out)
    go_chip = by_core(c, go_own, sibling(go_own)).reshape(chip_rows, width)
    slot_ids = lax.dynamic_index_in_dim(positions, which, 0, False).reshape(2 * n, span)[:, 0] // span
    places = np.stack(
        [
            [s for d in side for k in (d, (d + half) % n) for s in (2 * k, 2 * k + 1)]
            for side in halves
        ]
    ).astype(np.int32)
    ids_all = slot_ids[lax.dynamic_index_in_dim(jnp.asarray(places), which, 0, False)]
    steps = jnp.arange(2 * n, dtype=jnp.int32)
    order = jnp.sum(jnp.where(ids_all[None, :] == steps[:, None], steps[None, :], 0), axis=1).astype(jnp.int32)
    ids = lax.dynamic_slice_in_dim(ids_all, chip * 8, 8, 0)
    cosine, sine = rope_tables(seq)

    hidden_all = sort_norm(order, x_all, gain_attn, span)
    x_chip32 = x_chip.astype(F32)
    hidden = normed(x_chip32, gain_attn).astype(BF16)
    q_raw = dot(hidden, w_qkv[:, :q_c], NN, BF16)
    kv_raw = dot(hidden_all, w_qkv[:, q_c:], NN, BF16)
    mixed, lse = attend(ids, q_raw, kv_raw, cosine, sine, gain_q, gain_k, span)
    proj = dot(mixed, w_out_c, NN, BF16)
    middle = x_chip32 + (proj.astype(F32) + sibling(proj).astype(F32))
    second = normed(middle, gain_mlp).astype(BF16)
    gate = dot(second, w_gu[:, :ff_c], NN, BF16).astype(F32)
    up = dot(second, w_gu[:, ff_c:], NN, BF16).astype(F32)
    sig = jax.nn.sigmoid(gate)
    silu = gate * sig
    activated = (silu * up).astype(BF16)
    down = dot(activated, w_down_c, NN, BF16).reshape(2, 2 * slots, width)
    down_own = lax.dynamic_index_in_dim(down, c, 0, False)
    down_other = sibling(lax.dynamic_index_in_dim(down, 1 - c, 0, False))
    own_rows = lambda v: lax.dynamic_slice_in_dim(v, c * 2 * slots, 2 * slots, 0)
    result = (own_rows(middle) + (down_own.astype(F32) + down_other.astype(F32))).astype(BF16)

    def returned(rows):
        mine, back = rows[:slots], partner(rows[slots:])
        return jnp.where(which == 0, jnp.stack([mine, back]), jnp.stack([back, mine]))

    output = returned(result)

    grad_act = dot(go_chip, w_down_c, NT)
    grad_gate = (grad_act * up * sig * (1.0 + gate * (1.0 - sig))).astype(BF16)
    grad_up = (grad_act * silu).astype(BF16)
    grad_down_w = dot(activated, go_chip, TN, BF16)
    grad_gate_w = dot(second, grad_gate, TN, BF16)
    grad_up_w = dot(second, grad_up, TN, BF16)
    grad_second_part = (dot(grad_gate, w_gu[:, :ff_c], NT) + dot(grad_up, w_gu[:, ff_c:], NT)).astype(BF16)
    grad_second = grad_second_part.astype(F32) + sibling(grad_second_part).astype(F32)
    back, gain_terms = norm_back(middle, gain_mlp, grad_second)
    grad_mlp_gain = jnp.where(c == 0, jnp.sum(gain_terms, axis=0), 0.0)
    grad_middle = go_chip.astype(F32) + back
    grad_attn = grad_middle.astype(BF16)

    def reduced(grad):
        part = lax.psum_scatter(grad, "dp", scatter_dimension=0, tiled=True)
        return lax.psum_scatter(part, "ctx", scatter_dimension=0, tiled=True, axis_index_groups=same_core)

    sum_gu = reduced(jnp.concatenate([grad_gate_w, grad_up_w], axis=1))
    sum_down = reduced(grad_down_w)

    grad_mixed = dot(grad_attn, w_out_c, NT, BF16)
    grad_out_w = dot(mixed, grad_attn, TN, BF16)
    dq, dk, dv, dgq, dgk = attend_back(
        ids, q_raw, kv_raw, grad_mixed, mixed, lse, cosine, sine, gain_q, gain_k, span
    )
    dkv = jnp.concatenate([dk, dv], axis=1)
    grad_q_w = dot(hidden, dq, TN, BF16)
    grad_kv_w = dot(hidden_all, dkv, TN, BF16)
    out_w = grad_out_w.reshape(-1, 2, r_out, width)
    out_mine = lax.dynamic_index_in_dim(out_w, c, 1, False)
    out_recv = sibling(lax.dynamic_index_in_dim(out_w, 1 - c, 1, False))
    grad_out_w = by_core(c, out_mine, out_recv).reshape(chips * r_out, width)

    part_all = pick_blocks(ids_all, dot(dkv, w_qkv[:, q_c:], NT, BF16), span)
    part_q = dot(dq, w_qkv[:, :q_c], NT)
    part_chip = lax.dynamic_slice_in_dim(part_all, chip * chip_rows, chip_rows, 0).astype(F32) + part_q
    part_all = lax.dynamic_update_slice_in_dim(part_all, part_chip.astype(BF16), chip * chip_rows, 0)
    grad_hidden = lax.psum_scatter(
        part_all, "ctx", scatter_dimension=0, tiled=True, axis_index_groups=halves
    ).astype(F32)
    x_own32 = x_own.astype(F32)
    back, _terms = norm_back(x_own32, gain_attn, grad_hidden)
    grad_attn_gain = jnp.sum(part_all.astype(F32) * normed(x_all.astype(F32), 1.0), axis=0)
    input_grad = returned((own_rows(grad_middle) + back).astype(BF16))

    apart = width // HD
    spaced = lambda v: jnp.pad(v.reshape(HD, 1), ((0, 0), (0, apart - 1))).reshape(width, 1)
    gain_cols = jnp.concatenate(
        [grad_attn_gain[:, None], grad_mlp_gain[:, None], spaced(dgq), spaced(dgk), jnp.zeros((width, HD - 4), F32)],
        axis=1,
    ).astype(BF16)
    grads = [grad_q_w, grad_kv_w, gain_cols, grad_out_w]
    if tall:
        sums = reduce(grads)
    else:
        sums = jnp.concatenate([reduced(g) for g in grads], axis=1)
    sum_out = sums[:, qkv_c + HD :]
    def columns(sums):
        rows = sums.reshape(2, r_in, -1)
        mine = lax.dynamic_index_in_dim(rows, c, 0, False)
        other = sibling(lax.dynamic_index_in_dim(rows, 1 - c, 0, False))
        return by_core(c, mine, other).astype(F32)

    qkv_own = columns(sums[:, : qkv_c + HD])
    gain_own = jnp.sum(qkv_own[:, :, qkv_c : qkv_c + 4], axis=0)
    gu_own = columns(sum_gu)
    beside = lambda v: v.transpose(1, 0, 2).reshape(r_in, -1)
    ff_back = lambda v: v.reshape(2, r_in, chips, r_down).transpose(1, 2, 0, 3).reshape(r_in, ff)
    return (
        output,
        input_grad,
        beside(qkv_own[:, :, :q_c]),
        beside(qkv_own[:, :, q_c : q_c + kv_c]),
        beside(qkv_own[:, :, q_c + kv_c : qkv_c]),
        sum_out.astype(F32),
        ff_back(gu_own[:, :, :ff_c]),
        ff_back(gu_own[:, :, ff_c:]),
        sum_down.astype(F32),
        gain_own[:, 0],
        gain_own[:, 1],
        gain_own[::apart, 2],
        gain_own[::apart, 3],
    )


def solution(mesh):
    rows = P(("dp", "ctx"), None)
    gain = P(("dp", "ctx"))
    acts = P("dp", "ctx", None)
    return jax.shard_map(
        functools.partial(layer, mesh.shape["dp"], mesh.shape["ctx"]),
        mesh=mesh,
        in_specs=(acts, P("dp", None)) + (rows,) * 7 + (gain,) * 4 + (acts,),
        out_specs=(acts, acts) + (rows,) * 7 + (gain,) * 4,
        check_vma=False,
    )
```

time: 2020 us -> 696 us (0.34)
  waiting for transfers between devices: 1410 us -> 82.4 us
  Pallas kernels: 0 us -> 387 us
  matrix products: 342 us -> 104 us
  blocking collectives: 82.9 us -> 0 us
  other arithmetic: 114 us -> 48.9 us
    reduce_scatter x11 -> x5, waiting for transfers between devices: 969 us -> 25.1 us  [the longest x2 25.1 us: reduced(): lax.psum_scatter(part, 'ctx', scatter_dimension=0, tiled=True, axis_index...]
    all_gather x11 -> x1, waiting for transfers between devices: 436 us -> 0.01 us  [layer(): down_all = lax.all_gather(w_down, axes, axis=0, tiled=True)]
    pallas_call x0 -> x6, Pallas kernels: none -> 387 us  [the longest x1 161 us: gather(): pl.pallas_call(gather_kernel, out_shape=[jax.ShapeDtypeStruct((4, 4, rows...]
    dot_general x54 -> x18, matrix products: 342 us -> 104 us  [dot(): return lax.dot_general(a, b, (dims, ((), ())), preferred_element_type=out)]
    unnamed x2 -> x0, blocking collectives: 82.9 us -> none
    ppermute x0 -> x11, waiting for transfers between devices: none -> 57.1 us  [the longest x3 51.4 us: layer(): partner = lambda v: lax.ppermute(v, 'ctx', to_partner)]
    another operation x2 -> x3, other arithmetic: 57.9 us -> 1.2 us  [the longest x1 0.91 us: layer(): jnp.stack([jnp.concatenate([qkv_halves[i], gains, gate_order[i], up_order...]
    unnamed x242 -> x92, local copies, waits for them, and re-layouts: 33 us -> 9.64 us
  transfers between devices with their start and end apart: 22 -> 17, of which waited for: 18 -> 7; matrix products, arithmetic and copies ran while one was open for 21% -> 23% of each run, Pallas kernels for 0% -> 33%
where the time goes in v1:
time: 696 us; the launch traced here: 687 us
  Pallas kernels  387 us (56%)
  matrix products  104 us (15%)
  waiting for transfers between devices  82.4 us (12%)
  other arithmetic  48.9 us (7%)
  local copies, waits for them, and re-layouts  43.3 us (6%)
  between operations  15.5 us (2%)
    pallas_call x1, Pallas kernels, gather(): pl.pallas_call(gather_kernel, out_shape=[jax.ShapeDtypeStruct((4, 4, rows...  161 us
    dot_general x18, matrix products, dot(): return lax.dot_general(a, b, (dims, ((), ())), preferred_element_type=out)  104 us
    pallas_call x1, Pallas kernels, reduce(): pl.pallas_call(functools.partial(reduce_kernel, len(grads)), out_shape=ja...  82.3 us
    pallas_call x1, Pallas kernels, attend_back(): pl.pallas_call(functools.partial(attend_back_kernel, span), out_shape=[ja...  75.8 us
    ppermute x3, waiting for transfers between devices, layer(): partner = lambda v: lax.ppermute(v, 'ctx', to_partner)  51.4 us
    pallas_call x1, Pallas kernels, attend(): pl.pallas_call(functools.partial(attend_kernel, span), out_shape=[jax.Sha...  45.1 us
    reduce_scatter x2, waiting for transfers between devices, reduced(): lax.psum_scatter(part, 'ctx', scatter_dimension=0, tiled=True, axis_index...  25.1 us
  transfers between devices with their start and end apart: 17, of which 7 were waited for; matrix products, arithmetic and copies ran while one was open for 23% of the time, Pallas kernels for 33%

profile of v1, /device:TPU:0, one launch (start us, length us, event | category | flops | bytes accessed | tf_op | source)
XLA Modules:
  0.0 686.7 jit_solution(5124333571863228835)
XLA Ops:
  15.6 161.4 %gather.7 = (bf16[4,4,64,6272]{3,2,1,0:T(8,128)(2,1)}, bf16[4,2,256,1024]{3,2,1,0:T(8,128)(2,1)}) custom-call(bf16[2,32,5248]{2,1,0:T(8,128)(2,1)} %pad_maximum_fusion.2.pk_ref, bf16[64,1024]{1,0:T(8,128)(2,1)} %wo_ref.1, bf16[2,256,1024]{2,1,0:T(8,128)(2,1)} %tok_ref.1), custom_call_target="tpu_custom_call" | custom-call | tf_op jit(solution)/shard_map/gather/pallas_call | solution.py:437
  184.0 11.7 %sort_norm.1 = bf16[2048,1024]{1,0:T(8,128)(2,1)} custom-call(s32[16]{0:T(128)} %select_reduce_fusion.order_ref, bf16[2048,1024]{1,0:T(8,128)(2,1)} %bitcast.144, f32[1,1024]{1,0:T(1,128)} %bitcast.190), custom_call_target="tpu_custom_call" | custom-call | tf_op jit(solution)/shard_map/sort_norm/pallas_call | solution.py:63
  197.8 9.7 %fusion.34.k_ref.v_ref = bf16[2048,1024]{1,0:T(8,128)(2,1)} fusion(bf16[2048,1024]{1,0:T(8,128)(2,1)} %sort_norm.1, bf16[1024,6272]{1,0:T(8,128)(2,1)} %bitcast.176), kind=kOutput, calls=%fused_computation.62 | convolution fusion | flops 4294967296 | bytes 10485760 | tf_op jit(solution)/shard_map/dot_general | solution.py:48
  207.5 5.4 fusion.37.q_ref
  213.3 45.1 %attend.1 = (bf16[1024,1024]{1,0:T(8,128)(2,1)S(1)}, f32[4,8,1,256]{3,2,1,0:T(1,128)S(1)}) custom-call(s32[8]{0:T(128)S(1)} %dynamic_slice.75.ids_ref, bf16[1024,1024]{1,0:T(8,128)(2,1)} %fusion.37.q_ref, bf16[2048,1024]{1,0:T(8,128)(2,1)} %fusion.34.k_ref.v_ref, bf16[2048,1024]{1,0:T(8,128)(2,1)} %fusion.34.k_ref.v_ref, f32[2048,128]{1,0:T(8,128)S(1)} %copy-done.2, ...), custom_call_target="tpu_custom_call" | custom-call | flops 8589934592 | bytes 8388608 | tf_op jit(solution)/shard_map/attend/pallas_call | solution.py:179
  261.3 3.7 fusion.61
  266.2 24.5 %collective-permute-done.4 = bf16[256,1024]{1,0:T(8,128)(2,1)S(1)} collective-permute-done((bf16[256,1024]{1,0:T(8,128)(2,1)S(1)}, bf16[256,1024]{1,0:T(8,128)(2,1)S(1)}, u32[]{:S(2)}, u32[]{:S(2)}) %collective-permute-start.4) | collective-permute-done | bytes 524320 | tf_op jit(solution)/shard_map/ppermute | solution.py:568
  300.7 7.4 %fusion.14 = bf16[1024,1536]{1,0:T(8,128)(2,1)} fusion(bf16[1024,1024]{1,0:T(8,128)(2,1)S(1)} %multiply_convert_fusion.1, bf16[1024,6272]{1,0:T(8,128)(2,1)} %bitcast.178), kind=kOutput, calls=%fused_computation.35 | convolution fusion | flops 3221225472 | bytes 8388608 | tf_op jit(solution)/shard_map/dot_general | solution.py:48
  308.1 6.6 fusion.18
  318.4 8.7 %fusion.3 = (bf16[1024,1536]{1,0:T(8,128)(2,1)S(1)}, bf16[1024,1536]{1,0:T(8,128)(2,1)S(1)}, bf16[1024,1536]{1,0:T(8,128)(2,1)}) fusion(bf16[1024,1536]{1,0:T(8,128)(2,1)S(1)} %copy-done.42, bf16[1024,1536]{1,0:T(8,128)(2,1)} %fusion.18, bf16[1024,1024]{1,0:T(8,128)(2,1)S(1)} %bitcast.153, bf16[1536,1024]{1,0:T(8,128)(2,1)S(1)} %bitcast.157), kind=kOutput, calls=%fused_computation.11 | convolution fusion | flops 3247964160 | bytes 20971520 | tf_op jit(solution)/shard_map/dot_general | solution.py:48
  327.1 4.2 fusion.65
  331.3 3.8 fusion.64
  335.1 3.6 pad_maximum_fusion
  338.8 6.4 fusion.12
  345.2 6.7 add_convert_fusion.1
  352.1 4.8 fusion.66
  357.1 5.3 multiply_reduce_fusion.2
  362.8 3.7 multiply_add_fusion
  366.5 3.7 fusion.43.do_ref
  370.2 75.8 %attend_back.1 = (bf16[1024,1024]{1,0:T(8,128)(2,1)S(1)}, bf16[2048,512]{1,0:T(8,128)(2,1)}, bf16[2048,512]{1,0:T(8,128)(2,1)}, f32[1,128]{1,0:T(1,128)S(1)}, f32[1,128]{1,0:T(1,128)S(1)}) custom-call(s32[8]{0:T(128)S(1)} %dynamic_slice.75.ids_ref, bf16[1024,1024]{1,0:T(8,128)(2,1)} %fusion.37.q_ref, bf16[2048,1024]{1,0:T(8,128)(2,1)} %fusion.34.k_ref.v_ref, ...), custom_call_target="tpu_custom_call" | custom-call | flops 10737418240 | bytes 16777216 | tf_op jit(solution)/shard_map/attend_back/pallas_call | solution.py:292
  451.3 7.7 %fusion.32.x_ref = bf16[2048,1024]{1,0:T(8,128)(2,1)} fusion(bf16[2048,1024]{1,0:T(8,128)(2,1)S(1)} %constant_dynamic-update-slice_fusion, bf16[1024,6272]{1,0:T(8,128)(2,1)} %bitcast.182), kind=kOutput, calls=%fused_computation.60 | convolution fusion | flops 4294967296 | bytes 10485760 | tf_op jit(solution)/shard_map/dot_general | solution.py:48
  459.1 10.9 %pick_blocks.1 = bf16[2048,1024]{1,0:T(8,128)(2,1)} custom-call(s32[16]{0:T(128)} %copy-done.36, bf16[2048,1024]{1,0:T(8,128)(2,1)} %fusion.32.x_ref), custom_call_target="tpu_custom_call" | custom-call | tf_op jit(solution)/shard_map/pick_blocks/pallas_call | solution.py:85
  470.0 6.0 fusion.28
  476.3 6.3 fusion.62
  490.9 23.2 %collective-permute-done.3 = bf16[256,1024]{1,0:T(8,128)(2,1)S(1)} collective-permute-done((bf16[256,1024]{1,0:T(8,128)(2,1)S(1)}, bf16[256,1024]{1,0:T(8,128)(2,1)S(1)}, u32[]{:S(2)}, u32[]{:S(2)}) %collective-permute-start.3) | collective-permute-done | bytes 524320 | tf_op jit(solution)/shard_map/ppermute | solution.py:568
  515.3 4.4 multiply_reduce_fusion
  520.6 3.8 fusion.41
  534.4 4.3 fusion.46
  538.8 4.8 fusion.63
  546.8 82.3 %reduce.19 = bf16[64,3200]{1,0:T(8,128)(2,1)S(1)} custom-call(bf16[2,2,4,64,1024]{4,3,2,1,0:T(8,128)(2,1)S(1)} %bitcast.138, bf16[2,2,4,64,1024]{4,3,2,1,0:T(8,128)(2,1)S(1)} %bitcast.139, bf16[2,2,4,64,128]{4,3,2,1,0:T(8,128)(2,1)S(1)} %concatenate.38.refs_2_, bf16[2,2,4,64,1024]{4,3,2,1,0:T(8,128)(2,1)} %maximum_select_fusion.2.refs_3_), custom_call_target="tpu_custom_call" | custom-call | tf_op jit(solution)/shard_map/reduce/pallas_call | solution.py:516
  643.6 25.1 %reduce-scatter.14.cloned.1.call-done = bf16[96,1024]{1,0:T(8,128)(2,1)} async-done(((bf16[384,1024]{1,0:T(8,128)(2,1)}), bf16[96,1024]{1,0:T(8,128)(2,1)}) %reduce-scatter.14.cloned.1.call-update) | async-done | bytes 196624 | tf_op jit(solution)/shard_map/reduce_scatter | solution.py:697
  670.4 3.7 collective-permute-done.7
  (226 shorter events, 86.4 us)
Async XLA Ops:
  7.2 173.3 %copy-start = (s32[2,2048]{1,0:T(2,128)S(1)}, s32[2,2048]{1,0:T(2,128)}, u32[]{:S(2)}) copy-start(s32[2,2048]{1,0:T(2,128)} %param.18) | copy-start | bytes 49156
  7.2 7.2 %copy-start.30 = (bf16[32,1024]{1,0:T(8,128)(2,1)S(1)}, bf16[32,1024]{1,0:T(8,128)(2,1)}, u32[]{:S(2)}) copy-start(bf16[32,1024]{1,0:T(8,128)(2,1)} %param.21) | copy-start | bytes 196612
  7.2 7.2 %copy-start.31 = (bf16[32,1024]{1,0:T(8,128)(2,1)S(1)}, bf16[32,1024]{1,0:T(8,128)(2,1)}, u32[]{:S(2)}) copy-start(bf16[32,1024]{1,0:T(8,128)(2,1)} %param.20) | copy-start | bytes 196612
  7.2 307.5 %all-gather.2.cloned.1.call-start = ((), (), s32[]{:S(2)}) async-start(), calls=%async_computation.5 | async-start | bytes 6488064 | tf_op jit(solution)/shard_map/all_gather | solution.py:630
  177.0 347.4 %reduce-scatter.8.cloned.1.call-start = ((), (), s32[]{:S(2)}) async-start(), calls=%async_computation.7 | async-start | bytes 7864320 | tf_op jit(solution)/shard_map/reduce_scatter | solution.py:696
  180.4 78.0 %collective-permute-start = (bf16[8,64,1024]{2,1,0:T(8,128)(2,1)}, bf16[8,64,1024]{2,1,0:T(8,128)(2,1)}, u32[]{:S(2)}, u32[]{:S(2)}) collective-permute-start(bf16[8,64,1024]{2,1,0:T(8,128)(2,1)} %get-tuple-element.49), channel_id=1, source_target_pairs={{0,1},{1,0},{2,3},{3,2},{4,5},{5,4},{6,7},{7,6},{8,9},{9,8},{10,11... | collective-permute-start | bytes 3145736 | tf_op jit(solution)/shard_map/ppermute | solution.py:567
  181.3 31.7 %copy-start.36 = (s32[16]{0:T(128)}, s32[16]{0:T(128)S(1)}, u32[]{:S(2)}) copy-start(s32[16]{0:T(128)S(1)} %gather_fusion) | copy-start | bytes 196
  197.8 9.7 %copy-start.34 = (f32[1024]{0:T(1024)}, f32[1024]{0:T(1024)S(1)}, u32[]{:S(2)}) copy-start(f32[1024]{0:T(1024)S(1)} %add_rsqrt_fusion.1) | copy-start | bytes 12292
  197.8 9.7 %copy-start.9 = (bf16[4,2,256,1024]{3,2,1,0:T(8,128)(2,1)S(1)}, bf16[4,2,256,1024]{3,2,1,0:T(8,128)(2,1)}, u32[]{:S(2)}) copy-start(bf16[4,2,256,1024]{3,2,1,0:T(8,128)(2,1)} %get-tuple-element.23) | copy-start | bytes 12582916
  197.8 9.7 %copy-start.32 = (f32[1024]{0:T(1024)S(1)}, f32[1024]{0:T(1024)}, u32[]{:S(2)}) copy-start(f32[1024]{0:T(1024)} %get-tuple-element.36) | copy-start | bytes 12292
  213.3 45.1 %copy-start.19 = (bf16[1,8,64,1024]{3,2,1,0:T(8,128)(2,1)S(1)}, bf16[1,8,64,1024]{3,2,1,0:T(8,128)(2,1)}, u32[]{:S(2)}) copy-start(bf16[1,8,64,1024]{3,2,1,0:T(8,128)(2,1)} %get-tuple-element.48) | copy-start | bytes 3145732
  265.0 30.3 %collective-permute-start.1 = (bf16[1024,1024]{1,0:T(8,128)(2,1)}, bf16[1024,1024]{1,0:T(8,128)(2,1)}, u32[]{:S(2)}, u32[]{:S(2)}) collective-permute-start(bf16[1024,1024]{1,0:T(8,128)(2,1)} %fusion.61), channel_id=1, source_target_pairs={{0,1},{1,0},{2,3},{3,2},{4,5},{5,4},{6,7},{7,6},{8,9},{9,8},{10,11... | collective-permute-start | bytes 6291464 | tf_op jit(solution)/shard_map/ppermute | solution.py:567
  265.6 25.1 %collective-permute-start.4 = (bf16[256,1024]{1,0:T(8,128)(2,1)S(1)}, bf16[256,1024]{1,0:T(8,128)(2,1)S(1)}, u32[]{:S(2)}, u32[]{:S(2)}) collective-permute-start(bf16[256,1024]{1,0:T(8,128)(2,1)S(1)} %get-tuple-element.55), channel_id=1, source_target_pairs={{0,4},{1,5},{2,6},{3,7},{4,0},{5,1},{6,2},{7,3},{8,12},{9,13},{10,... | collective-permute-start | bytes 1572872 | tf_op jit(solution)/shard_map/ppermute | solution.py:568
  291.0 2.7 collective-permute-start.5
  300.7 7.4 %copy-start.25 = (bf16[1024,1024]{1,0:T(8,128)(2,1)}, bf16[1024,1024]{1,0:T(8,128)(2,1)S(1)}, u32[]{:S(2)}) copy-start(bf16[1024,1024]{1,0:T(8,128)(2,1)S(1)} %multiply_convert_fusion.1) | copy-start | bytes 6291460
  317.2 9.9 %copy-start.21 = (bf16[16,1,96,1024]{3,2,1,0:T(8,128)(2,1)}, bf16[16,1,96,1024]{3,2,1,0:T(8,128)(2,1)S(1)}, u32[]{:S(2)}) copy-start(bf16[16,1,96,1024]{3,2,1,0:T(8,128)(2,1)S(1)} %constant_dynamic-slice_fusion.3) | copy-start | bytes 9437188
  318.4 8.7 %copy-start.26 = (bf16[1024,1024]{1,0:T(8,128)(2,1)S(1)}, bf16[1024,1024]{1,0:T(8,128)(2,1)}, u32[]{:S(2)}) copy-start(bf16[1024,1024]{1,0:T(8,128)(2,1)} %copy-done.25) | copy-start | bytes 6291460
  338.7 292.0 %reduce-scatter.12.cloned.1.call-start = ((), (), s32[]{:S(2)}) async-start(), calls=%async_computation.9 | async-start | bytes 3932160 | tf_op jit(solution)/shard_map/reduce_scatter | solution.py:696
  338.8 6.4 copy-start.40
  345.2 6.9 %copy-start.17 = (bf16[2,512,1024]{2,1,0:T(8,128)(2,1)S(1)}, bf16[2,512,1024]{2,1,0:T(8,128)(2,1)}, u32[]{:S(2)}) copy-start(bf16[2,512,1024]{2,1,0:T(8,128)(2,1)} %maximum_select_fusion.1) | copy-start | bytes 6291460
  345.2 6.9 %copy-start.37 = (bf16[1024,1536]{1,0:T(8,128)(2,1)S(1)}, bf16[1024,1536]{1,0:T(8,128)(2,1)}, u32[]{:S(2)}) copy-start(bf16[1024,1536]{1,0:T(8,128)(2,1)} %get-tuple-element.45) | copy-start | bytes 9437188
  352.0 5.1 collective-permute-start.6
  357.0 273.8 %reduce-scatter.6.cloned.1.call-start = ((), (), s32[]{:S(2)}) async-start(), calls=%async_computation.6 | async-start | bytes 5242880 | tf_op jit(solution)/shard_map/reduce_scatter | solution.py:719
  459.1 10.9 %copy-start.7 = (bf16[1024,1024]{1,0:T(8,128)(2,1)S(1)}, bf16[1024,1024]{1,0:T(8,128)(2,1)}, u32[]{:S(2)}) copy-start(bf16[1024,1024]{1,0:T(8,128)(2,1)} %copy-done.6) | copy-start | bytes 6291460
  476.0 165.8 %reduce-scatter.10.cloned.1.call-start = ((), (), s32[]{:S(2)}) async-start(), calls=%async_computation.8 | async-start | bytes 1966080 | tf_op jit(solution)/shard_map/reduce_scatter | solution.py:697
  482.6 2.9 collective-permute-start.2
  488.2 25.9 %collective-permute-start.3 = (bf16[256,1024]{1,0:T(8,128)(2,1)S(1)}, bf16[256,1024]{1,0:T(8,128)(2,1)S(1)}, u32[]{:S(2)}, u32[]{:S(2)}) collective-permute-start(bf16[256,1024]{1,0:T(8,128)(2,1)S(1)} %get-tuple-element.57), channel_id=1, source_target_pairs={{0,4},{1,5},{2,6},{3,7},{4,0},{5,1},{6,2},{7,3},{8,12},{9,13},{10,... | collective-permute-start | bytes 1572872 | tf_op jit(solution)/shard_map/ppermute | solution.py:568
  524.4 144.3 %reduce-scatter.14.cloned.1.call-start = ((), (), s32[]{:S(2)}) async-start(), calls=%async_computation.10 | async-start | bytes 983040 | tf_op jit(solution)/shard_map/reduce_scatter | solution.py:697
  531.7 11.9 %collective-permute-start.8 = (bf16[8,64,1024]{2,1,0:T(8,128)(2,1)}, bf16[8,64,1024]{2,1,0:T(8,128)(2,1)}, u32[]{:S(2)}, u32[]{:S(2)}) collective-permute-start(bf16[8,64,1024]{2,1,0:T(8,128)(2,1)} %get-tuple-element.47), channel_id=1, source_target_pairs={{0,1},{1,0},{2,3},{3,2},{4,5},{5,4},{6,7},{7,6},{8,9},{9,8},{10,11... | collective-permute-start | bytes 3145736 | tf_op jit(solution)/shard_map/ppermute | solution.py:567
  629.2 1.4 collective-permute-start.9
  635.7 38.3 %collective-permute-start.7 = (bf16[256,1024]{1,0:T(8,128)(2,1)S(1)}, bf16[256,1024]{1,0:T(8,128)(2,1)S(1)}, u32[]{:S(2)}, u32[]{:S(2)}) collective-permute-start(bf16[256,1024]{1,0:T(8,128)(2,1)S(1)} %get-tuple-element.51), channel_id=1, source_target_pairs={{0,4},{1,5},{2,6},{3,7},{4,0},{5,1},{6,2},{7,3},{8,12},{9,13},{10,... | collective-permute-start | bytes 1572872 | tf_op jit(solution)/shard_map/ppermute | solution.py:568
  642.8 32.4 %collective-permute-start.10 = (bf16[32,3072]{1,0:T(8,128)(2,1)S(1)}, bf16[32,3072]{1,0:T(8,128)(2,1)S(1)}, u32[]{:S(2)}, u32[]{:S(2)}) collective-permute-start(bf16[32,3072]{1,0:T(8,128)(2,1)S(1)} %get-tuple-element.63), channel_id=1, source_target_pairs={{0,1},{1,0},{2,3},{3,2},{4,5},{5,4},{6,7},{7,6},{8,9},{9,8},{10,11... | collective-permute-start | bytes 589832 | tf_op jit(solution)/shard_map/ppermute | solution.py:567
  (28 other events, 119.1 us)
Sparse Core Ops, SparseCore 0:
  177.1 67.0 all-gather.1
  338.8 68.2 reduce-scatter.7
  410.1 43.9 reduce-scatter.11
  476.1 52.5 reduce-scatter.5
  531.0 35.2 reduce-scatter.9
  630.8 37.8 reduce-scatter.13

commit v2 on v1

v2 whole, which is shorter than its diff:
```python
import functools

import jax
import jax.numpy as jnp
import numpy as np
from jax import lax
from jax.experimental import pallas as pl
from jax.experimental.pallas import tpu as pltpu
from jax.sharding import PartitionSpec as P

H = 16
KV = 8
HD = 128
GROUPS = H // KV
EPSILON = 1e-06
THETA = 1000000.0
LOG2E = 1.4426950408889634
KEY_TILE = 512
ROW_TILE = 256
FF_TILE = 512
FWD_HEADS = 4
BACK_HEADS = 4
VMEM_LIMIT = 48 * 1024 * 1024
MESH = pl.DeviceIdType.MESH
F32 = jnp.float32
BF16 = jnp.bfloat16


def normed(values, weights):
    return values * lax.rsqrt(jnp.mean(values * values, axis=-1, keepdims=True) + EPSILON) * weights


def norm_back(values, weights, grad):
    r = lax.rsqrt(jnp.mean(values * values, axis=-1, keepdims=True) + EPSILON)
    unit = values * r
    u = grad * weights
    return r * (u - unit * jnp.mean(u * unit, axis=-1, keepdims=True)), grad * unit


def rope_tables(seq):
    half = HD // 2
    inverse = (THETA ** (-(np.arange(half, dtype=np.float32) * np.float32(2.0) / np.float32(HD)))).astype(np.float32)
    angles = np.arange(seq, dtype=np.float32)[:, None] * inverse[None, :]
    cosine, sine = np.cos(angles), np.sin(angles)
    return (
        jnp.asarray(np.concatenate([cosine, cosine], axis=-1).astype(np.float32)),
        jnp.asarray(np.concatenate([-sine, sine], axis=-1).astype(np.float32)),
    )


def dot(a, b, dims, out=F32):
    return lax.dot_general(a, b, (dims, ((), ())), preferred_element_type=out)


NN = ((1,), (0,))
NT = ((1,), (1,))
TN = ((0,), (0,))


def row_mean(values):
    return dot(values.astype(BF16), jnp.full((HD, HD), 1.0 / HD, BF16), NN)


def unit_rows(raw):
    r = lax.rsqrt(row_mean(raw * raw) + EPSILON)
    return raw * r, r


def rope(values, cosine, sine):
    return values * cosine + pltpu.roll(values, HD // 2, 1) * sine


def rope_back(values, cosine, sine):
    return values * cosine - pltpu.roll(values, HD // 2, 1) * sine


def lanes(head, width=HD):
    return slice(head * width, (head + 1) * width)


def prepare_keys(span, order_ref, k_ref, v_ref, cos_ref, sin_ref, gk_ref, ks_ref, vs_ref):
    def body(i, _):
        rows = pl.ds(pl.multiple_of(i * span, span), span)
        source = pl.ds(pl.multiple_of(order_ref[i] * span, span), span)
        for p in range(k_ref.shape[1] // HD):
            unit, _r = unit_rows(k_ref[source, lanes(p)].astype(F32))
            ks_ref[rows, lanes(p)] = rope(unit * gk_ref[...], cos_ref[rows, :], sin_ref[rows, :]).astype(BF16)
        vs_ref[rows, :] = v_ref[source, :]
        return 0

    lax.fori_loop(0, k_ref.shape[0] // span, body, 0)


def query_block(q_ref, p, rows, places, cos_ref, sin_ref, gq_ref):
    units, scales, parts = [], [], []
    for g in range(GROUPS):
        unit, r = unit_rows(q_ref[rows, lanes(p * GROUPS + g)].astype(F32))
        turned = rope(unit * gq_ref[...], cos_ref[places, :], sin_ref[places, :])
        units.append(unit)
        scales.append(r)
        parts.append((turned * (LOG2E * HD**-0.5)).astype(BF16))
    return units, scales, jnp.concatenate(parts, axis=0)


def seen(shape, t, b, span, key_axis):
    at = t * KEY_TILE + lax.broadcasted_iota(jnp.int32, shape, key_axis)
    own = b * span + lax.broadcasted_iota(jnp.int32, shape, 1 - key_axis) % span
    return at <= own


def attend_kernel(
    span, ids_ref, order_ref, q_ref, k_ref, v_ref, cos_ref, sin_ref, gq_ref, gk_ref,
    o_ref, lse_ref, ks_ref, vs_ref, acc_ref, sum_ref,
):
    prepare_keys(span, order_ref, k_ref, v_ref, cos_ref, sin_ref, gk_ref, ks_ref, vs_ref)
    m = GROUPS * span
    heads = range(FWD_HEADS)

    def block(j, _):
        b = ids_ref[j]
        rows = pl.ds(pl.multiple_of(j * span, span), span)
        places = pl.ds(pl.multiple_of(b * span, span), span)
        q2 = [query_block(q_ref, p, rows, places, cos_ref, sin_ref, gq_ref)[2] for p in heads]
        acc_ref[...] = jnp.zeros_like(acc_ref)
        sum_ref[...] = jnp.zeros_like(sum_ref)

        def tile(t, masked):
            keys = pl.ds(pl.multiple_of(t * KEY_TILE, KEY_TILE), KEY_TILE)
            scores = [dot(q2[p], ks_ref[keys, lanes(p)], NT) for p in heads]
            keep = seen(scores[0].shape, t, b, span, 1) if masked else None
            for p in heads:
                e = jnp.exp2(scores[p])
                if masked:
                    e = jnp.where(keep, e, 0.0)
                part = e[:, 0:HD]
                for i in range(1, KEY_TILE // HD):
                    part = part + e[:, lanes(i)]
                sum_ref[p] += part
                acc_ref[p] += dot(e.astype(BF16), vs_ref[keys, lanes(p)], NN)

        last = (b * span) // KEY_TILE
        lax.fori_loop(0, last, lambda t, _: (tile(t, False), 0)[1], 0)
        tile(last, True)
        for p in heads:
            total = jnp.sum(sum_ref[p], axis=-1, keepdims=True)
            mixed = acc_ref[p] * (1.0 / total)
            for g in range(GROUPS):
                o_ref[rows, lanes(p * GROUPS + g)] = mixed[g * span : (g + 1) * span].astype(BF16)
            wide = jnp.broadcast_to(jnp.log2(total), (m, HD))
            lse_ref[p, j] = jnp.transpose(wide)[0:1, :]
        return 0

    lax.fori_loop(0, q_ref.shape[0] // span, block, 0)


def attend(ids, order, q_raw, kv_raw, cosine, sine, gq, gk, span):
    rows = q_raw.shape[0]
    seq = kv_raw.shape[0]
    heads = q_raw.shape[1] // (GROUPS * HD)
    blocks, m = rows // span, GROUPS * span
    hp = FWD_HEADS
    whole = lambda k, ids, order: (0, 0)
    per_query = pl.BlockSpec((rows, hp * GROUPS * HD), lambda k, ids, order: (0, k))
    once = pl.Buffered(1)
    return pl.pallas_call(
        functools.partial(attend_kernel, span),
        out_shape=[
            jax.ShapeDtypeStruct((rows, heads * GROUPS * HD), BF16),
            jax.ShapeDtypeStruct((heads, blocks, 1, m), F32),
        ],
        grid_spec=pltpu.PrefetchScalarGridSpec(
            num_scalar_prefetch=2,
            grid=(heads // hp,),
            in_specs=[
                per_query,
                pl.BlockSpec((seq, hp * HD), lambda k, ids, order: (0, k)),
                pl.BlockSpec((seq, hp * HD), lambda k, ids, order: (0, heads // hp + k)),
                pl.BlockSpec((seq, HD), whole, pipeline_mode=once),
                pl.BlockSpec((seq, HD), whole, pipeline_mode=once),
                pl.BlockSpec((1, HD), whole),
                pl.BlockSpec((1, HD), whole),
            ],
            out_specs=[
                per_query,
                pl.BlockSpec((hp, blocks, 1, m), lambda k, ids, order: (k, 0, 0, 0)),
            ],
            scratch_shapes=[
                pltpu.VMEM((seq, hp * HD), BF16),
                pltpu.VMEM((seq, hp * HD), BF16),
                pltpu.VMEM((hp, m, HD), F32),
                pltpu.VMEM((hp, m, HD), F32),
            ],
        ),
        compiler_params=pltpu.CompilerParams(vmem_limit_bytes=VMEM_LIMIT),
        cost_estimate=pl.CostEstimate(
            flops=2 * 2 * rows * seq * heads * GROUPS * HD,
            bytes_accessed=2 * (2 * rows * heads * GROUPS * HD + 2 * seq * heads * HD),
            transcendentals=rows * seq * heads * GROUPS // 2,
        ),
        name="attend",
    )(ids, order, q_raw, kv_raw, kv_raw, cosine, sine, gq, gk)


def attend_back_kernel(
    span, ids_ref, order_ref, q_ref, k_ref, v_ref, do_ref, o_ref, lse_ref, cos_ref, sin_ref, gq_ref, gk_ref,
    dq_ref, dk_ref, dv_ref, dgq_ref, dgk_ref, ks_ref, vs_ref, dka_ref, dva_ref, dqa_ref,
):
    prepare_keys(span, order_ref, k_ref, v_ref, cos_ref, sin_ref, gk_ref, ks_ref, vs_ref)
    dka_ref[...] = jnp.zeros_like(dka_ref)
    dva_ref[...] = jnp.zeros_like(dva_ref)
    heads = range(BACK_HEADS)

    @pl.when(pl.program_id(0) == 0)
    def _():
        dgq_ref[...] = jnp.zeros_like(dgq_ref)
        dgk_ref[...] = jnp.zeros_like(dgk_ref)

    def block(j, _):
        b = ids_ref[j]
        rows = pl.ds(pl.multiple_of(j * span, span), span)
        places = pl.ds(pl.multiple_of(b * span, span), span)
        q2, do2, delta, lse = [], [], [], []
        for p in heads:
            q2.append(query_block(q_ref, p, rows, places, cos_ref, sin_ref, gq_ref)[2])
            pick = lambda ref: jnp.concatenate([ref[rows, lanes(p * GROUPS + g)] for g in range(GROUPS)], axis=0)
            do2.append(pick(do_ref))
            delta.append(
                jnp.sum(jnp.transpose(do2[p].astype(F32) * pick(o_ref).astype(F32)), axis=0, keepdims=True)
            )
            lse.append(lse_ref[p, j])
        dqa_ref[...] = jnp.zeros_like(dqa_ref)

        def tile(t, masked):
            keys = pl.ds(pl.multiple_of(t * KEY_TILE, KEY_TILE), KEY_TILE)
            kt = [ks_ref[keys, lanes(p)] for p in heads]
            scores = [dot(kt[p], q2[p], NT) for p in heads]
            slopes = [dot(vs_ref[keys, lanes(p)], do2[p], NT) for p in heads]
            keep = seen(scores[0].shape, t, b, span, 0) if masked else None
            for p in heads:
                e = jnp.exp2(scores[p] - lse[p])
                if masked:
                    e = jnp.where(keep, e, 0.0)
                ds = (e * (slopes[p] - delta[p])).astype(BF16)
                dva_ref[keys, lanes(p)] += dot(e.astype(BF16), do2[p], NN)
                dka_ref[keys, lanes(p)] += dot(ds, q2[p], NN)
                dqa_ref[p] += dot(ds, kt[p], TN)

        last = (b * span) // KEY_TILE
        lax.fori_loop(0, last, lambda t, _: (tile(t, False), 0)[1], 0)
        tile(last, True)
        for p in heads:
            units, scales, _q = query_block(q_ref, p, rows, places, cos_ref, sin_ref, gq_ref)
            dq = dqa_ref[p] * HD**-0.5
            for g in range(GROUPS):
                grad = rope_back(dq[g * span : (g + 1) * span], cos_ref[places, :], sin_ref[places, :])
                dgq_ref[...] += jnp.sum(grad * units[g], axis=0, keepdims=True)
                u = grad * gq_ref[...]
                back = scales[g] * (u - units[g] * row_mean(u * units[g]))
                dq_ref[rows, lanes(p * GROUPS + g)] = back.astype(BF16)
        return 0

    lax.fori_loop(0, q_ref.shape[0] // span, block, 0)

    def finish(i, _):
        rows = pl.ds(pl.multiple_of(i * span, span), span)
        source = pl.ds(pl.multiple_of(order_ref[i] * span, span), span)
        for p in heads:
            unit, r = unit_rows(k_ref[source, lanes(p)].astype(F32))
            grad = rope_back(dka_ref[rows, lanes(p)] * (1.0 / LOG2E), cos_ref[rows, :], sin_ref[rows, :])
            dgk_ref[...] += jnp.sum(grad * unit, axis=0, keepdims=True)
            u = grad * gk_ref[...]
            back = r * (u - unit * row_mean(u * unit))
            dk_ref[source, lanes(p)] = back.astype(BF16)
        dv_ref[source, :] = dva_ref[rows, :].astype(BF16)
        return 0

    lax.fori_loop(0, k_ref.shape[0] // span, finish, 0)


def attend_back(ids, order, q_raw, kv_raw, grad_mixed, mixed, lse, cosine, sine, gq, gk, span):
    rows = q_raw.shape[0]
    seq = kv_raw.shape[0]
    heads = q_raw.shape[1] // (GROUPS * HD)
    blocks, m = rows // span, GROUPS * span
    hp = BACK_HEADS
    whole = lambda k, ids, order: (0, 0)
    per_query = pl.BlockSpec((rows, hp * GROUPS * HD), lambda k, ids, order: (0, k))
    per_key = pl.BlockSpec((seq, hp * HD), lambda k, ids, order: (0, k))
    gain = pl.BlockSpec((1, HD), whole)
    once = pl.Buffered(1)
    return pl.pallas_call(
        functools.partial(attend_back_kernel, span),
        out_shape=[
            jax.ShapeDtypeStruct((rows, heads * GROUPS * HD), BF16),
            jax.ShapeDtypeStruct((seq, heads * HD), BF16),
            jax.ShapeDtypeStruct((seq, heads * HD), BF16),
            jax.ShapeDtypeStruct((1, HD), F32),
            jax.ShapeDtypeStruct((1, HD), F32),
        ],
        grid_spec=pltpu.PrefetchScalarGridSpec(
            num_scalar_prefetch=2,
            grid=(heads // hp,),
            in_specs=[
                per_query,
                per_key,
                pl.BlockSpec((seq, hp * HD), lambda k, ids, order: (0, heads // hp + k)),
                per_query,
                per_query,
                pl.BlockSpec((hp, blocks, 1, m), lambda k, ids, order: (k, 0, 0, 0)),
                pl.BlockSpec((seq, HD), whole, pipeline_mode=once),
                pl.BlockSpec((seq, HD), whole, pipeline_mode=once),
                gain,
                gain,
            ],
            out_specs=[per_query, per_key, per_key, gain, gain],
            scratch_shapes=[
                pltpu.VMEM((seq, hp * HD), BF16),
                pltpu.VMEM((seq, hp * HD), BF16),
                pltpu.VMEM((seq, hp * HD), F32),
                pltpu.VMEM((seq, hp * HD), F32),
                pltpu.VMEM((hp, m, HD), F32),
            ],
        ),
        compiler_params=pltpu.CompilerParams(vmem_limit_bytes=VMEM_LIMIT),
        cost_estimate=pl.CostEstimate(
            flops=5 * 2 * rows * seq * heads * GROUPS * HD // 2,
            bytes_accessed=2 * (4 * rows * heads * GROUPS * HD + 4 * seq * heads * HD),
            transcendentals=rows * seq * heads * GROUPS // 2,
        ),
        name="attend_back",
    )(ids, order, q_raw, kv_raw, kv_raw, grad_mixed, mixed, lse, cosine, sine, gq, gk)


def project_kernel(own, chip_ref, x_ref, gain_ref, wq_ref, wkv_ref, h_ref, q_ref, kv_ref):
    hidden = normed(x_ref[...].astype(F32), gain_ref[...]).astype(BF16)
    h_ref[...] = hidden
    kv_ref[...] = dot(hidden, wkv_ref[...], NN).astype(BF16)

    @pl.when(pl.program_id(0) < own)
    def _():
        q_ref[...] = dot(hidden, wq_ref[...], NN).astype(BF16)


def project(chip, x_all, gain, w_all, chip_rows):
    seq, width = x_all.shape
    size = min(ROW_TILE, chip_rows)
    own, tiles = chip_rows // size, seq // size
    at = lambda i, chip: ((i + chip[0] * own) % tiles, 0)
    weight = lambda col: pl.BlockSpec((width, width), lambda i, chip: (0, col), pipeline_mode=pl.Buffered(1))
    return pl.pallas_call(
        functools.partial(project_kernel, own),
        out_shape=[
            jax.ShapeDtypeStruct((seq, width), BF16),
            jax.ShapeDtypeStruct((chip_rows, width), BF16),
            jax.ShapeDtypeStruct((seq, width), BF16),
        ],
        grid_spec=pltpu.PrefetchScalarGridSpec(
            num_scalar_prefetch=1,
            grid=(tiles,),
            in_specs=[
                pl.BlockSpec((size, width), at),
                pl.BlockSpec((1, width), lambda i, chip: (0, 0)),
                weight(0),
                weight(1),
            ],
            out_specs=[
                pl.BlockSpec((size, width), at),
                pl.BlockSpec((size, width), lambda i, chip: (jnp.minimum(i, own - 1), 0)),
                pl.BlockSpec((size, width), at),
            ],
        ),
        compiler_params=pltpu.CompilerParams(vmem_limit_bytes=VMEM_LIMIT),
        name="project",
    )(chip, x_all, gain, w_all, w_all)


def project_back_kernel(own, chip_ref, dq_ref, dk_ref, dv_ref, x_ref, wq_ref, wk_ref, wv_ref, p_ref, g_ref, acc_ref):
    i = pl.program_id(0)
    acc_ref[...] = dot(dk_ref[...], wk_ref[...], NT) + dot(dv_ref[...], wv_ref[...], NT)

    @pl.when(i < own)
    def _():
        acc_ref[...] += dot(dq_ref[...], wq_ref[...], NT)

    @pl.when(i == 0)
    def _():
        g_ref[...] = jnp.zeros_like(g_ref)

    part = acc_ref[...]
    p_ref[...] = part.astype(BF16)
    g_ref[...] += jnp.sum(part * normed(x_ref[...].astype(F32), 1.0), axis=0, keepdims=True)


def project_back(chip, dq, dk, dv, x_all, w_all):
    seq, width = x_all.shape
    chip_rows, kv = dq.shape[0], dk.shape[1]
    size = min(ROW_TILE, chip_rows)
    own, tiles = chip_rows // size, seq // size
    at = lambda i, chip: ((i + chip[0] * own) % tiles, 0)
    weight = lambda cols, col: pl.BlockSpec((width, cols), lambda i, chip: (0, col), pipeline_mode=pl.Buffered(1))
    return pl.pallas_call(
        functools.partial(project_back_kernel, own),
        out_shape=[jax.ShapeDtypeStruct((seq, width), BF16), jax.ShapeDtypeStruct((1, width), F32)],
        grid_spec=pltpu.PrefetchScalarGridSpec(
            num_scalar_prefetch=1,
            grid=(tiles,),
            in_specs=[
                pl.BlockSpec((size, width), lambda i, chip: (jnp.minimum(i, own - 1), 0)),
                pl.BlockSpec((size, kv), at),
                pl.BlockSpec((size, kv), at),
                pl.BlockSpec((size, width), at),
                weight(width, 0),
                weight(kv, width // kv),
                weight(kv, width // kv + 1),
            ],
            out_specs=[
                pl.BlockSpec((size, width), at),
                pl.BlockSpec((1, width), lambda i, chip: (0, 0)),
            ],
            scratch_shapes=[pltpu.VMEM((size, width), F32)],
        ),
        compiler_params=pltpu.CompilerParams(vmem_limit_bytes=VMEM_LIMIT),
        name="project_back",
    )(chip, dq, dk, dv, x_all, w_all, w_all, w_all)


def feed_kernel(x_ref, p0_ref, p1_ref, gain_ref, go_ref, w_ref, d_ref, mid_ref, sec_ref, act_ref, gg_ref):
    count = x_ref.shape[0]
    size = min(ROW_TILE, count)
    tile = lambda i: pl.ds(pl.multiple_of(i * size, size), size)

    @pl.when(pl.program_id(0) == 0)
    def _():
        def start(i, _):
            rows = tile(i)
            middle = x_ref[rows, :].astype(F32) + (p0_ref[rows, :].astype(F32) + p1_ref[rows, :].astype(F32))
            mid_ref[rows, :] = middle
            sec_ref[rows, :] = normed(middle, gain_ref[...]).astype(BF16)
            return 0

        lax.fori_loop(0, count // size, start, 0)

    def body(i, _):
        rows = tile(i)
        both = dot(sec_ref[rows, :], w_ref[...], NN)
        grad = dot(go_ref[rows, :], d_ref[...], NT)
        gate, up = both[:, :FF_TILE], both[:, FF_TILE:]
        sig = jax.nn.sigmoid(gate)
        silu = gate * sig
        act_ref[rows, :] = (silu * up).astype(BF16)
        gg_ref[rows, :FF_TILE] = (grad * up * sig * (1.0 + gate * (1.0 - sig))).astype(BF16)
        gg_ref[rows, FF_TILE:] = (grad * silu).astype(BF16)
        return 0

    lax.fori_loop(0, count // size, body, 0)


def feed(x, p0, p1, gain, go, w_all, at, w_down):
    rows, width = x.shape
    ff = w_down.shape[0]
    whole = lambda: pl.BlockSpec((rows, width), lambda j: (0, 0), pipeline_mode=pl.Buffered(1))
    return pl.pallas_call(
        feed_kernel,
        out_shape=[
            jax.ShapeDtypeStruct((rows, width), F32),
            jax.ShapeDtypeStruct((rows, width), BF16),
            jax.ShapeDtypeStruct((rows, ff), BF16),
            jax.ShapeDtypeStruct((rows, 2 * ff), BF16),
        ],
        grid=(ff // FF_TILE,),
        in_specs=[
            whole(), whole(), whole(),
            pl.BlockSpec((1, width), lambda j: (0, 0)),
            whole(),
            pl.BlockSpec((width, 2 * FF_TILE), lambda j: (0, at // (2 * FF_TILE) + j)),
            pl.BlockSpec((FF_TILE, width), lambda j: (j, 0)),
        ],
        out_specs=[
            pl.BlockSpec((rows, width), lambda j: (0, 0)),
            pl.BlockSpec((rows, width), lambda j: (0, 0)),
            pl.BlockSpec((rows, FF_TILE), lambda j: (0, j)),
            pl.BlockSpec((rows, 2 * FF_TILE), lambda j: (0, j)),
        ],
        compiler_params=pltpu.CompilerParams(vmem_limit_bytes=VMEM_LIMIT),
        name="feed",
    )(x, p0, p1, gain, go, w_all, w_down)


def middle_back_kernel(mid_ref, s0_ref, s1_ref, go_ref, gain_ref, wo_ref, ga_ref, gm_ref, g_ref):
    back, terms = norm_back(mid_ref[...], gain_ref[...], s0_ref[...].astype(F32) + s1_ref[...].astype(F32))
    grad = (go_ref[...].astype(F32) + back).astype(BF16)
    ga_ref[...] = grad
    gm_ref[...] = dot(grad, wo_ref[...], NT).astype(BF16)

    @pl.when(pl.program_id(0) == 0)
    def _():
        g_ref[...] = jnp.zeros_like(g_ref)

    g_ref[...] += jnp.sum(terms, axis=0, keepdims=True)


def middle_back(middle, s0, s1, go, gain, w_out):
    rows, width = middle.shape
    size = min(ROW_TILE, rows)
    row = pl.BlockSpec((size, width), lambda i: (i, 0))
    line = pl.BlockSpec((1, width), lambda i: (0, 0))
    return pl.pallas_call(
        middle_back_kernel,
        out_shape=[
            jax.ShapeDtypeStruct((rows, width), BF16),
            jax.ShapeDtypeStruct((rows, w_out.shape[0]), BF16),
            jax.ShapeDtypeStruct((1, width), F32),
        ],
        grid=(rows // size,),
        in_specs=[row, row, row, row, line, pl.BlockSpec(w_out.shape, lambda i: (0, 0), pipeline_mode=pl.Buffered(1))],
        out_specs=[row, pl.BlockSpec((size, w_out.shape[0]), lambda i: (i, 0)), line],
        compiler_params=pltpu.CompilerParams(vmem_limit_bytes=VMEM_LIMIT),
        name="middle_back",
    )(middle, s0, s1, go, gain, w_out)


def peers():
    dp, ctx = lax.axis_index("dp"), lax.axis_index("ctx")
    to = lambda d, k: (jnp.bitwise_xor(dp, d), jnp.bitwise_xor(ctx, k))
    return dp, ctx, to


def greet(devices):
    barrier = pltpu.get_barrier_semaphore()
    for device in devices:
        pl.semaphore_signal(barrier, inc=1, device_id=device, device_id_type=MESH)
    pl.semaphore_wait(barrier, len(devices))


def sender(send_sem, recv_sem):
    made = []

    def send(src, dst, device):
        i = len(made)
        copy = pltpu.make_async_remote_copy(
            src_ref=src, dst_ref=dst, send_sem=send_sem.at[i], recv_sem=recv_sem.at[i],
            device_id=device, device_id_type=MESH,
        )
        copy.start()
        made.append(copy)
        return copy

    return send, made


def gather_kernel(pk_ref, wo_ref, tok_ref, go_ref, w_ref, x_ref, g_ref, send_sem, recv_sem, local_sem):
    dp, ctx, to = peers()
    c, z = ctx % 2, ctx // 2
    which, me = ctx // 4, ctx % 4
    inner = jnp.logical_or(z == 1, z == 2)
    greet([to(0, 1), to(0, 2), to(0, 4), to(0, 6), to(1, 0), to(2, 0)])
    send, made = sender(send_sem, recv_sem)
    sib, nbr, far, across, xn, yn = to(0, 1), to(0, 2), to(0, 4), to(0, 6), to(1, 0), to(2, 0)
    rows, cols = pk_ref.shape[1:]

    place = w_ref.at[dp, z, pl.ds(c * rows, rows), pl.ds(0, cols)]
    local = [
        pltpu.make_async_copy(pk_ref.at[c], place, local_sem.at[0]),
        pltpu.make_async_copy(wo_ref, w_ref.at[dp, z, :, pl.ds(cols, wo_ref.shape[1])], local_sem.at[1]),
        pltpu.make_async_copy(tok_ref.at[which], x_ref.at[me, 0], local_sem.at[2]),
        pltpu.make_async_copy(go_ref.at[which], g_ref.at[c, 0], local_sem.at[3]),
    ]
    for copy in local:
        copy.start()
    cross = send(pk_ref.at[1 - c], place, sib)
    for copy in local:
        copy.wait()
    cross.wait_recv()
    done = []

    def half(h, q, zz):
        return w_ref.at[q, zz, pl.ds(h * rows, rows)]

    first = []

    def spread(zz):
        low, high = half(0, dp, zz), half(1, dp, zz)
        first.append((send(low, low, yn), low, half(0, jnp.bitwise_xor(dp, 2), zz), xn))
        first.append((send(high, high, xn), high, half(1, jnp.bitwise_xor(dp, 1), zz), yn))

    def pass_on():
        for copy, own, part, device in first[:2]:
            done.append(send(own, own, device))
            copy.wait_recv()
            done.append(send(part, part, device))
        del first[:2]

    z_one = jnp.bitwise_xor(z, 1)
    z_near = jnp.bitwise_xor(z, jnp.where(inner, 3, 2))
    z_far = jnp.bitwise_xor(z, jnp.where(inner, 2, 3))
    relayed = []

    def relay(slot, source, device):
        copy = pltpu.make_async_remote_copy(
            src_ref=w_ref.at[dp, source], dst_ref=w_ref.at[dp, source],
            send_sem=send_sem.at[send_sem.shape[0] - 4 + len(relayed)],
            recv_sem=recv_sem.at[send_sem.shape[0] - 2 + slot],
            device_id=device, device_id_type=MESH,
        )
        relayed.append(copy)
        pl.when(inner)(copy.start)
        return copy

    step = send(w_ref.at[dp, z], w_ref.at[dp, z], nbr)
    near = relay(0, z, across)
    spread(z)
    pass_on()
    step.wait_recv()
    far_block = relay(1, z_one, across)
    spread(z_one)
    near.wait_recv()
    relay(0, z_near, nbr)
    spread(z_near)
    pass_on()
    far_block.wait_recv()
    relay(1, z_far, nbr)
    spread(z_far)
    swap = send(tok_ref.at[1 - which], x_ref.at[me, 1], far)
    mine_nbr = send(tok_ref.at[which], x_ref.at[me, 0], nbr)
    done += [send(tok_ref.at[which], x_ref.at[me, 0], sib), send(go_ref.at[which], g_ref.at[c, 0], sib)]
    pass_on()
    swap.wait_recv()
    done.append(send(x_ref.at[me, 1], x_ref.at[me, 1], sib))
    swap_nbr = send(x_ref.at[me, 1], x_ref.at[me, 1], nbr)
    go_swap = send(go_ref.at[1 - which], g_ref.at[c, 1], far)
    pass_on()
    other = jnp.bitwise_xor(me, 2)
    mine_nbr.wait_recv()
    done.append(send(x_ref.at[other, 0], x_ref.at[other, 0], sib))
    swap_nbr.wait_recv()
    done.append(send(x_ref.at[other, 1], x_ref.at[other, 1], sib))
    go_swap.wait_recv()
    done.append(send(g_ref.at[c, 1], g_ref.at[c, 1], sib))
    for copy in done:
        copy.wait_recv()
    for copy in made:
        copy.wait_send()

    @pl.when(inner)
    def _():
        for copy in relayed:
            copy.wait_send()


def gather(packed, w_out, tokens, grad_out):
    rows, cols = 2 * packed.shape[1], packed.shape[2] + w_out.shape[1]
    slots, width = tokens.shape[1:]
    copies = 36 + 4
    anywhere = pl.BlockSpec(memory_space=pl.ANY)
    near = pl.BlockSpec(memory_space=pltpu.VMEM)
    w, x, g = pl.pallas_call(
        gather_kernel,
        out_shape=[
            jax.ShapeDtypeStruct((4, 4, rows, cols), BF16),
            jax.ShapeDtypeStruct((4, 2, slots, width), BF16),
            jax.ShapeDtypeStruct((2, 2, slots, width), BF16),
        ],
        in_specs=[near] * 4,
        out_specs=[anywhere] * 3,
        scratch_shapes=[
            pltpu.SemaphoreType.DMA((copies,)),
            pltpu.SemaphoreType.DMA((copies,)),
            pltpu.SemaphoreType.DMA((4,)),
        ],
        compiler_params=pltpu.CompilerParams(
            collective_id=0, has_side_effects=True, vmem_limit_bytes=VMEM_LIMIT
        ),
        name="gather",
    )(packed, w_out, tokens, grad_out)
    return w.reshape(16 * rows, cols), x.reshape(-1, width), g.reshape(-1, width)


def reduce_kernel(n_in, *refs):
    g_refs, (part_ref, x_ref, ga_ref, gain_ref) = refs[:n_in], refs[n_in : n_in + 4]
    o_ref, s_ref, ig_ref = refs[n_in + 4 : n_in + 7]
    (
        g_ref, in_a, in_b, mid_a, mid_b, got_a, got_b, out3, in3,
        mine_ref, sib_ref, give_ref, nbr_ref, back_ref, send_sem, recv_sem, local_sem,
    ) = refs[n_in + 7 :]
    dp, ctx, to = peers()
    c, z = ctx % 2, ctx // 2
    which, chip = ctx // 4, z % 2
    x, y = dp % 2, dp // 2
    greet([to(0, 1), to(0, 2), to(0, 4), to(0, 6), to(1, 0), to(2, 0)])
    send, made = sender(send_sem, recv_sem)
    sib, nbr, far, xn, yn = to(0, 1), to(0, 2), to(0, 4), to(1, 0), to(2, 0)
    hr = g_ref.shape[3] // 2
    at, local = 0, []
    for i, ref in enumerate(g_refs):
        width = ref.shape[-1]
        local.append(pltpu.make_async_copy(ref, g_ref.at[:, :, :, :, pl.ds(at, width)], local_sem.at[i]))
        at += width
    local.append(pltpu.make_async_copy(part_ref.at[:, c], mine_ref, local_sem.at[n_in]))
    for copy in local:
        copy.start()
    cross = send(part_ref.at[:, 1 - c], sib_ref, sib)
    for copy in local:
        copy.wait()
    low, high = pl.ds(0, hr), pl.ds(hr, hr)
    order = [jnp.bitwise_xor(z, k) for k in (2, 3, 1, 0)]
    a_in, b_in, a_mid, b_mid, last = [], [], [], [], []
    size = 64
    tile = lambda i: pl.ds(pl.multiple_of(i * size, size), size)
    count = mine_ref.shape[1]

    def enter(k):
        a_in.append(send(g_ref.at[:, 1 - x, order[k], low], in_a.at[k], xn))
        b_in.append(send(g_ref.at[1 - y, :, order[k], high], in_b.at[k], yn))

    def middle(k):
        add = lambda p, q: (p.astype(F32) + q.astype(F32)).astype(BF16)
        a_in[k].wait_recv()
        mid_a[k] = add(g_ref[1 - y, x, order[k], 0:hr], in_a[k, 1 - y])
        a_mid.append(send(mid_a.at[k], got_a.at[k], yn))
        b_in[k].wait_recv()
        mid_b[k] = add(g_ref[y, 1 - x, order[k], hr:], in_b[k, 1 - x])
        b_mid.append(send(mid_b.at[k], got_b.at[k], xn))

    def leave(k):
        add = lambda p, q, r: (p.astype(F32) + q.astype(F32) + r.astype(F32)).astype(BF16)
        a_mid[k].wait_recv()
        out3[k, 0:hr] = add(g_ref[y, x, order[k], 0:hr], in_a[k, y], got_a[k])
        b_mid[k].wait_recv()
        out3[k, hr:] = add(g_ref[y, x, order[k], hr:], in_b[k, x], got_b[k])
        if k < 3:
            last.append(send(out3.at[k], in3.at[k], to(0, 2 * (2, 3, 1)[k])))

    enter(0)
    enter(1)
    cross.wait_recv()

    def give(i, _):
        rows = tile(i)
        give_ref[rows] = (mine_ref[1 - chip, rows].astype(F32) + sib_ref[1 - chip, rows].astype(F32)).astype(BF16)
        return 0

    lax.fori_loop(0, count // size, give, 0)
    swap = send(give_ref, nbr_ref, nbr)
    middle(0)
    enter(2)
    middle(1)
    enter(3)
    leave(0)
    middle(2)
    leave(1)
    swap.wait_recv()

    def back(i, _):
        rows = tile(i)
        grad = mine_ref[chip, rows].astype(F32) + sib_ref[chip, rows].astype(F32) + nbr_ref[rows].astype(F32)
        through, _terms = norm_back(x_ref[rows, :].astype(F32), gain_ref[...], grad)
        back_ref[rows] = (ga_ref[rows, :].astype(F32) + through).astype(BF16)
        return 0

    lax.fori_loop(0, count // size, back, 0)
    slots = ig_ref.shape[1]
    home = send(back_ref.at[pl.ds(slots, slots)], ig_ref.at[which], far)
    keep = pltpu.make_async_copy(back_ref.at[pl.ds(0, slots)], ig_ref.at[which], local_sem.at[0])
    keep.start()
    middle(3)
    leave(2)
    leave(3)
    for copy in last:
        copy.wait_recv()
    o_ref[...] = (
        out3[3].astype(F32) + in3[0].astype(F32) + in3[1].astype(F32) + in3[2].astype(F32)
    ).astype(BF16)
    other = send(o_ref.at[pl.ds((1 - c) * hr, hr), pl.ds(0, s_ref.shape[1])], s_ref, sib)
    keep.wait()
    other.wait_recv()
    home.wait_recv()
    for copy in made:
        copy.wait_send()


def reduce(grads, near_cols, part, x, grad_middle, gain):
    rows = grads[0].shape[0] // 16
    cols = sum(g.shape[1] for g in grads)
    grads = [g.reshape(2, 2, 4, rows, g.shape[1]) for g in grads]
    count, width = x.shape
    copies = 23
    anywhere = pl.BlockSpec(memory_space=pl.ANY)
    near = pl.BlockSpec(memory_space=pltpu.VMEM)
    return pl.pallas_call(
        functools.partial(reduce_kernel, len(grads)),
        out_shape=[
            jax.ShapeDtypeStruct((rows, cols), BF16),
            jax.ShapeDtypeStruct((rows // 2, near_cols), BF16),
            jax.ShapeDtypeStruct((2, count // 2, width), BF16),
        ],
        in_specs=[anywhere] * (len(grads) + 1) + [near] * 3,
        out_specs=[near, anywhere, anywhere],
        scratch_shapes=[
            pltpu.VMEM((2, 2, 4, rows, cols), BF16),
            pltpu.VMEM((4, 2, rows // 2, cols), BF16),
            pltpu.VMEM((4, 2, rows // 2, cols), BF16),
        ]
        + [pltpu.VMEM((4, rows // 2, cols), BF16)] * 4
        + [
            pltpu.VMEM((4, rows, cols), BF16),
            pltpu.VMEM((3, rows, cols), BF16),
            pltpu.VMEM((2, count, width), BF16),
            pltpu.VMEM((2, count, width), BF16),
            pltpu.VMEM((count, width), BF16),
            pltpu.VMEM((count, width), BF16),
            pltpu.VMEM((count, width), BF16),
            pltpu.SemaphoreType.DMA((copies,)),
            pltpu.SemaphoreType.DMA((copies,)),
            pltpu.SemaphoreType.DMA((len(grads) + 1,)),
        ],
        compiler_params=pltpu.CompilerParams(
            collective_id=1, has_side_effects=True, vmem_limit_bytes=VMEM_LIMIT
        ),
        name="reduce",
    )(*grads, part.reshape(2, 2, count, width), x, grad_middle, gain)


def by_core(c, own, other):
    return jnp.where(c == 0, jnp.stack([own, other]), jnp.stack([other, own]))


def layer(
    n_dp, n, tokens, positions, w_query, w_key, w_value, w_out, w_gate, w_up, w_down,
    attn_gain, mlp_gain, q_gain, k_gain, grad_out,
):
    axes = ("dp", "ctx")
    slots, width = tokens.shape[1:]
    seq = positions.shape[1]
    span = slots // 2
    half = n // 2
    chips = n_dp * half
    ctx = lax.axis_index("ctx")
    c = ctx % 2
    which = ctx // half
    r_in, r_out, r_down = w_query.shape[0], w_out.shape[0], w_down.shape[0]
    ff = w_gate.shape[1]
    ff_c = ff // 2
    q_c, kv_c = H * HD // 2, KV * HD // 2

    to_sibling = [(i, i ^ 1) for i in range(n)]
    to_partner = [(i, (i + half) % n) for i in range(n)]
    halves = [list(range(half)), list(range(half, n))]
    same_core = [list(range(0, n, 2)), list(range(1, n, 2))]
    sibling = lambda v: lax.ppermute(v, "ctx", to_sibling)
    partner = lambda v: lax.ppermute(v, "ctx", to_partner)

    def placed(values):
        mine = lax.dynamic_index_in_dim(values, which, 0, False)
        other = lax.dynamic_index_in_dim(values, 1 - which, 0, False)
        return jnp.concatenate([mine, partner(other)], axis=0)

    gains = jnp.concatenate(
        [
            attn_gain[:, None],
            mlp_gain[:, None],
            jnp.pad(q_gain, (0, r_in - q_gain.shape[0]))[:, None],
            jnp.pad(k_gain, (0, r_in - k_gain.shape[0]))[:, None],
            jnp.zeros((r_in, 124), BF16),
        ],
        axis=1,
    )
    tall = (n_dp, n) == (4, 8)
    qkv_halves = [
        jnp.concatenate(
            [
                w_query[:, i * q_c : (i + 1) * q_c],
                w_key[:, i * kv_c : (i + 1) * kv_c],
                w_value[:, i * kv_c : (i + 1) * kv_c],
            ],
            axis=1,
        )
        for i in range(2)
    ]

    def ff_order(shard):
        return shard.reshape(r_in, chips, 2, r_down).transpose(2, 0, 1, 3).reshape(2, r_in, ff_c)

    gate_order, up_order = ff_order(w_gate), ff_order(w_up)
    qkv_c = q_c + 2 * kv_c
    all_c = qkv_c + 2 * ff_c
    by_tile = lambda v: v.reshape(2, r_in, ff_c // FF_TILE, FF_TILE)
    gu_shard = jnp.stack([by_tile(gate_order), by_tile(up_order)], axis=3).reshape(2, r_in, 2 * ff_c)
    packed = jnp.stack([jnp.concatenate([qkv_halves[i], gu_shard[i], gains], axis=1) for i in range(2)])
    if tall:
        w_all, x_all, go_chip = gather(packed, w_out, tokens, grad_out)
        x_own = lax.dynamic_slice_in_dim(x_all, (ctx % half) * 2 * slots, 2 * slots, 0)
        out_rows = w_all[:, all_c + HD :].reshape(2, -1, r_out, width)
        out_keep = lax.dynamic_index_in_dim(out_rows, c, 0, False)
        out_give = lax.dynamic_index_in_dim(out_rows, 1 - c, 0, False)
        w_out_c = by_core(c, out_keep, sibling(out_give)).transpose(1, 0, 2, 3).reshape(q_c, width)
        w_down, w_all = lax.optimization_barrier((w_down, w_all))
    else:
        both = lax.all_gather(packed, axes, axis=1, tiled=True)
        w_all = lax.dynamic_index_in_dim(both, c, 0, False)
        out_all = lax.all_gather(w_out, axes, axis=0, tiled=True)
        w_out_c = lax.dynamic_slice_in_dim(out_all, c * q_c, q_c, 0)
        x_own = placed(tokens)
        x_all = lax.all_gather(x_own, "ctx", axis=0, tiled=True, axis_index_groups=halves)
        go_own = placed(grad_out)
        go_chip = by_core(c, go_own, sibling(go_own)).reshape(4 * slots, width)
    down_all = lax.all_gather(w_down, axes, axis=0, tiled=True).reshape(chips, 2, r_down, width)
    w_down_c = lax.dynamic_index_in_dim(down_all, c, 1, False).reshape(ff_c, width)
    g_cols = w_all[:, all_c : all_c + HD].astype(F32)
    gain_attn = g_cols[:, 0][None]
    gain_mlp = g_cols[:, 1][None]
    per_head = g_cols.reshape(n_dp * n, r_in, HD)[:, : q_gain.shape[0]].reshape(HD, HD)
    gain_q = per_head[:, 2][None]
    gain_k = per_head[:, 3][None]

    chip = (ctx % half) // 2
    chip_rows = 4 * slots
    x_chip = lax.dynamic_slice_in_dim(x_all, chip * chip_rows, chip_rows, 0)
    slot_ids = lax.dynamic_index_in_dim(positions, which, 0, False).reshape(2 * n, span)[:, 0] // span
    places = np.stack(
        [
            [s for d in side for k in (d, (d + half) % n) for s in (2 * k, 2 * k + 1)]
            for side in halves
        ]
    ).astype(np.int32)
    ids_all = slot_ids[lax.dynamic_index_in_dim(jnp.asarray(places), which, 0, False)]
    steps = jnp.arange(2 * n, dtype=jnp.int32)
    order = jnp.sum(jnp.where(ids_all[None, :] == steps[:, None], steps[None, :], 0), axis=1).astype(jnp.int32)
    ids = lax.dynamic_slice_in_dim(ids_all, chip * 8, 8, 0)
    cosine, sine = rope_tables(seq)

    chip_at = chip.astype(jnp.int32).reshape(1)
    hidden_all, q_raw, kv_raw = project(chip_at, x_all, gain_attn, w_all, chip_rows)
    hidden = lax.dynamic_slice_in_dim(hidden_all, chip * chip_rows, chip_rows, 0)
    mixed, lse = attend(ids, order, q_raw, kv_raw, cosine, sine, gain_q, gain_k, span)
    proj = dot(mixed, w_out_c, NN, BF16)
    middle, second, activated, grad_gu = feed(
        x_chip, proj, sibling(proj), gain_mlp, go_chip, w_all, qkv_c, w_down_c
    )
    down = dot(activated, w_down_c, NN, BF16).reshape(2, 2 * slots, width)
    down_own = lax.dynamic_index_in_dim(down, c, 0, False)
    down_other = sibling(lax.dynamic_index_in_dim(down, 1 - c, 0, False))
    own_rows = lambda v: lax.dynamic_slice_in_dim(v, c * 2 * slots, 2 * slots, 0)
    result = (own_rows(middle) + (down_own.astype(F32) + down_other.astype(F32))).astype(BF16)

    def returned(rows):
        mine, back = rows[:slots], partner(rows[slots:])
        return jnp.where(which == 0, jnp.stack([mine, back]), jnp.stack([back, mine]))


    second_part = dot(grad_gu, w_all[:, qkv_c:all_c], NT, BF16)
    grad_gu_w = dot(second, grad_gu, TN, BF16)
    grad_down_w = dot(activated, go_chip, TN, BF16)
    grad_attn, grad_mixed, mlp_gain_sum = middle_back(
        middle, second_part, sibling(second_part), go_chip, gain_mlp, w_out_c
    )
    grad_mlp_gain = jnp.where(c == 0, mlp_gain_sum[0], 0.0)

    def reduced(grad):
        part = lax.psum_scatter(grad, "dp", scatter_dimension=0, tiled=True)
        return lax.psum_scatter(part, "ctx", scatter_dimension=0, tiled=True, axis_index_groups=same_core)

    sum_gu = reduced(grad_gu_w)
    sum_down = reduced(grad_down_w)

    grad_out_w = dot(mixed, grad_attn, TN, BF16)
    result, grad_mixed = lax.optimization_barrier((result, grad_mixed))
    output = returned(result)
    dq, dk, dv, dgq, dgk = attend_back(
        ids, order, q_raw, kv_raw, grad_mixed, mixed, lse, cosine, sine, gain_q, gain_k, span
    )
    output, dq = lax.optimization_barrier((output, dq))
    part_all, attn_gain_sum = project_back(chip_at, dq, dk, dv, x_all, w_all)
    grad_q_w = dot(hidden, dq, TN, BF16)
    grad_k_w = dot(hidden_all, dk, TN, BF16)
    grad_v_w = dot(hidden_all, dv, TN, BF16)
    out_w = grad_out_w.reshape(-1, 2, r_out, width)
    out_mine = lax.dynamic_index_in_dim(out_w, c, 1, False)
    out_recv = sibling(lax.dynamic_index_in_dim(out_w, 1 - c, 1, False))
    grad_out_w = by_core(c, out_mine, out_recv).reshape(chips * r_out, width)

    apart = width // HD
    spaced = lambda v: jnp.pad(v.reshape(HD, 1), ((0, 0), (0, apart - 1))).reshape(width, 1)
    gain_cols = jnp.concatenate(
        [attn_gain_sum.T, grad_mlp_gain[:, None], spaced(dgq), spaced(dgk), jnp.zeros((width, HD - 4), F32)],
        axis=1,
    ).astype(BF16)
    grads = [grad_q_w, grad_k_w, grad_v_w, gain_cols, grad_out_w]
    near_c = qkv_c + HD
    own_grad = own_rows(grad_attn)
    by_rows = lambda v: lax.dynamic_index_in_dim(v.reshape(2, r_in, -1), c, 0, False)

    def columns(sums):
        other = lax.dynamic_index_in_dim(sums.reshape(2, r_in, -1), 1 - c, 0, False)
        return by_core(c, by_rows(sums), sibling(other)).astype(F32)

    if tall:
        sums, near_sums, input_grad = reduce(grads, near_c, part_all, x_own, own_grad, gain_attn)
        qkv_own = by_core(c, by_rows(sums[:, :near_c]), near_sums).astype(F32)
    else:
        sums = jnp.concatenate([reduced(g) for g in grads], axis=1)
        qkv_own = columns(sums[:, :near_c])
        grad_hidden = lax.psum_scatter(
            part_all, "ctx", scatter_dimension=0, tiled=True, axis_index_groups=halves
        ).astype(F32)
        back, _terms = norm_back(x_own.astype(F32), gain_attn, grad_hidden)
        input_grad = returned((own_grad.astype(F32) + back).astype(BF16))
    sum_out = sums[:, near_c:]
    gain_own = jnp.sum(qkv_own[:, :, qkv_c : qkv_c + 4], axis=0)
    gu_own = columns(sum_gu).reshape(2, r_in, ff_c // FF_TILE, 2, FF_TILE)
    beside = lambda v: v.transpose(1, 0, 2).reshape(r_in, -1)
    ff_back = lambda v: v.reshape(2, r_in, chips, r_down).transpose(1, 2, 0, 3).reshape(r_in, ff)
    return (
        output,
        input_grad,
        beside(qkv_own[:, :, :q_c]),
        beside(qkv_own[:, :, q_c : q_c + kv_c]),
        beside(qkv_own[:, :, q_c + kv_c : qkv_c]),
        sum_out.astype(F32),
        ff_back(gu_own[:, :, :, 0]),
        ff_back(gu_own[:, :, :, 1]),
        sum_down.astype(F32),
        gain_own[:, 0],
        gain_own[:, 1],
        gain_own[::apart, 2],
        gain_own[::apart, 3],
    )


def solution(mesh):
    rows = P(("dp", "ctx"), None)
    gain = P(("dp", "ctx"))
    acts = P("dp", "ctx", None)
    return jax.shard_map(
        functools.partial(layer, mesh.shape["dp"], mesh.shape["ctx"]),
        mesh=mesh,
        in_specs=(acts, P("dp", None)) + (rows,) * 7 + (gain,) * 4 + (acts,),
        out_specs=(acts, acts) + (rows,) * 7 + (gain,) * 4,
        check_vma=False,
    )
```

time: 696 us -> 531 us (0.76)
  waiting for transfers between devices: 82.4 us -> 30 us
  matrix products: 104 us -> 54.7 us
  other arithmetic: 48.9 us -> 18.5 us
  Pallas kernels: 387 us -> 357 us
    ppermute x3 -> x1, waiting for transfers between devices: 51.4 us -> 0.01 us  [layer(): partner = lambda v: lax.ppermute(v, 'ctx', to_partner)]
    dot_general x18 -> x9, matrix products: 104 us -> 54.7 us  [dot(): return lax.dot_general(a, b, (dims, ((), ())), preferred_element_type=out)]
    pallas_call x3 -> x5, Pallas kernels: 105 us -> 148 us  [the longest x1 88.2 us: reduce(): pl.pallas_call(functools.partial(reduce_kernel, len(grads)), out_shape=[j...]
    pallas_call x1, Pallas kernels: 161 us -> 121 us  [gather(): pl.pallas_call(gather_kernel, out_shape=[jax.ShapeDtypeStruct((4, 4, rows...]
    reduce_sum x7 -> x0, other arithmetic: 19.6 us -> none  [the longest x3 6.31 us: normed(): jnp.mean(values * values, axis=-1, keepdims=True) + EPSILON]
    pallas_call x1, Pallas kernels: 45.1 us -> 27.2 us  [attend(): pl.pallas_call(functools.partial(attend_kernel, span), out_shape=[jax.Sha...]
    pallas_call x1, Pallas kernels: 75.8 us -> 59.8 us  [attend_back(): pl.pallas_call(functools.partial(attend_back_kernel, span), out_shape=[ja...]
    all_gather x1, waiting for transfers between devices: 0.01 us -> 14.3 us  [layer(): lax.all_gather(w_down, axes, axis=0, tiled=True)]
  transfers between devices with their start and end apart: 17 -> 12, of which waited for: 7 -> 3; matrix products, arithmetic and copies ran while one was open for 23% -> 17% of each run, Pallas kernels for 33% -> 41%
where the time goes in v2:
time: 531 us; the launch traced here: 526 us
  Pallas kernels  357 us (67%)
  matrix products  54.7 us (10%)
  local copies, waits for them, and re-layouts  48.1 us (9%)
  waiting for transfers between devices  30 us (6%)
  other arithmetic  18.5 us (3%)
  between operations  15.1 us (3%)
    pallas_call x1, Pallas kernels, gather(): pl.pallas_call(gather_kernel, out_shape=[jax.ShapeDtypeStruct((4, 4, rows...  121 us
    pallas_call x1, Pallas kernels, reduce(): pl.pallas_call(functools.partial(reduce_kernel, len(grads)), out_shape=[j...  88.2 us
    pallas_call x1, Pallas kernels, attend_back(): pl.pallas_call(functools.partial(attend_back_kernel, span), out_shape=[ja...  59.8 us
    dot_general x9, matrix products, dot(): return lax.dot_general(a, b, (dims, ((), ())), preferred_element_type=out)  54.7 us
    pallas_call x1, Pallas kernels, attend(): pl.pallas_call(functools.partial(attend_kernel, span), out_shape=[jax.Sha...  27.2 us
    pallas_call x1, Pallas kernels, feed(): pl.pallas_call(feed_kernel, out_shape=[jax.ShapeDtypeStruct((rows, width)...  21.1 us
    pallas_call x1, Pallas kernels, project_back(): pl.pallas_call(functools.partial(project_back_kernel, own), out_shape=[ja...  15.2 us
    pallas_call x1, Pallas kernels, project(): pl.pallas_call(functools.partial(project_kernel, own), out_shape=[jax.Sha...  14.9 us
  transfers between devices with their start and end apart: 12, of which 3 were waited for; matrix products, arithmetic and copies ran while one was open for 17% of the time, Pallas kernels for 41%

profile of v2, /device:TPU:0, one launch (start us, length us, event | category | flops | bytes accessed | tf_op | source)
XLA Modules:
  0.0 526.5 jit_solution(2729088851815655597)
XLA Ops:
  12.0 121.5 %gather.7 = (bf16[4,4,64,6272]{3,2,1,0:T(8,128)(2,1)}, bf16[4,2,256,1024]{3,2,1,0:T(8,128)(2,1)}, bf16[2,2,256,1024]{3,2,1,0:T(8,128)(2,1)S(1)}) custom-call(bf16[2,32,5248]{2,1,0:T(8,128)(2,1)S(1)} %pad_maximum_fusion.pk_ref, bf16[64,1024]{1,0:T(8,128)(2,1)S(1)} %copy-done.16, bf16[2,256,1024]{2,1,0:T(8,128)(2,1)S(1)} %copy-done.11, ...), custom_call_target="tpu_custom_call" | custom-call | tf_op jit(solution)/shard_map/gather/pallas_call | solution.py:656
  134.9 1.8 slice.135
  140.4 14.9 %project.1 = (bf16[2048,1024]{1,0:T(8,128)(2,1)}, bf16[1024,1024]{1,0:T(8,128)(2,1)S(1)}, bf16[2048,1024]{1,0:T(8,128)(2,1)}) custom-call(s32[1]{0:T(128)} %bitcast.12.chip_ref, bf16[2048,1024]{1,0:T(8,128)(2,1)} %bitcast.131, f32[1,1024]{1,0:T(1,128)S(1)} %bitcast.114, bf16[1024,6272]{1,0:T(8,128)(2,1)} %bitcast.124, bf16[1024,6272]{1,0:T(8,128)(2,1)} %bitcast.125), custom_call_target="tpu_custom_call" | custom-call | tf_op jit(solution)/shard_map/project/pallas_call | solution.py:350
  156.9 27.2 %attend.1 = (bf16[1024,1024]{1,0:T(8,128)(2,1)S(1)}, f32[4,8,1,256]{3,2,1,0:T(1,128)S(1)}) custom-call(s32[8]{0:T(128)S(1)} %dynamic_slice.65.ids_ref, s32[16]{0:T(128)S(1)} %select_reduce_fusion.order_ref, bf16[1024,1024]{1,0:T(8,128)(2,1)} %copy-done.17, bf16[2048,1024]{1,0:T(8,128)(2,1)} %get-tuple-element.48.k_ref.v_ref, ...), custom_call_target="tpu_custom_call" | custom-call | flops 8589934592 | bytes 8388608 | tf_op jit(solution)/shard_map/attend/pallas_call | solution.py:165
  184.1 2.6 fusion.2
  187.0 3.7 fusion.18.p0_ref
  191.2 1.8 constant_dynamic-slice_fusion.9.x_ref
  193.0 14.3 %all-gather.2.cloned.1.call-done = bf16[3072,1024]{1,0:T(8,128)(2,1)} async-done(((bf16[96,1024]{1,0:T(8,128)(2,1)}), bf16[3072,1024]{1,0:T(8,128)(2,1)}) %all-gather.2.cloned.1.call-update) | async-done | bytes 6291472 | tf_op jit(solution)/shard_map/all_gather | solution.py:906
  207.3 4.0 constant_dynamic-slice_fusion.5
  211.3 21.1 %feed.1 = (f32[1024,1024]{1,0:T(8,128)}, bf16[1024,1024]{1,0:T(8,128)(2,1)S(1)}, bf16[1024,1536]{1,0:T(8,128)(2,1)}, bf16[1024,3072]{1,0:T(8,128)(2,1)}) custom-call(bf16[1024,1024]{1,0:T(8,128)(2,1)S(1)} %constant_dynamic-slice_fusion.9.x_ref, bf16[1024,1024]{1,0:T(8,128)(2,1)} %fusion.18.p0_ref, bf16[1024,1024]{1,0:T(8,128)(2,1)} %collective-permute-done.1.p1_ref, ...), custom_call_target="tpu_custom_call" | custom-call | tf_op jit(solution)/shard_map/feed/pallas_call | solution.py:462
  232.4 11.4 %fusion.23 = bf16[1024,3072]{1,0:T(8,128)(2,1)} fusion(bf16[1024,1024]{1,0:T(8,128)(2,1)S(1)} %get-tuple-element.74, bf16[1024,3072]{1,0:T(8,128)(2,1)} %get-tuple-element.54), kind=kOutput, calls=%fused_computation.79 | convolution fusion | flops 6442450944 | bytes 14680064 | tf_op jit(solution)/shard_map/dot_general | solution.py:52
  244.0 1.5 copy-done.3
  245.5 6.9 %fusion.24 = bf16[1536,1024]{1,0:T(8,128)(2,1)} fusion(bf16[1024,1536]{1,0:T(8,128)(2,1)} %get-tuple-element.53, bf16[1024,1024]{1,0:T(8,128)(2,1)S(1)} %bitcast.110), kind=kOutput, calls=%fused_computation.80 | convolution fusion | flops 3221225472 | bytes 8388608 | tf_op jit(solution)/shard_map/dot_general | solution.py:52
  252.5 11.8 %fusion.s0_ref = bf16[1024,1024]{1,0:T(8,128)(2,1)} fusion(bf16[1024,3072]{1,0:T(8,128)(2,1)} %get-tuple-element.54, bf16[1024,6272]{1,0:T(8,128)(2,1)} %bitcast.127), kind=kOutput, calls=%fused_computation.1 | convolution fusion | flops 6442450944 | bytes 14680064 | tf_op jit(solution)/shard_map/dot_general | solution.py:52
  264.6 3.6 fusion.19
  272.5 2.5 fusion.4
  275.0 8.8 %middle_back.1 = (bf16[1024,1024]{1,0:T(8,128)(2,1)S(1)}, bf16[1024,1024]{1,0:T(8,128)(2,1)S(1)}, f32[1,1024]{1,0:T(1,128)S(1)}) custom-call(f32[1024,1024]{1,0:T(8,128)} %get-tuple-element.52.mid_ref, bf16[1024,1024]{1,0:T(8,128)(2,1)} %fusion.s0_ref, bf16[1024,1024]{1,0:T(8,128)(2,1)} %collective-permute-done.3.s1_ref, bf16[1024,1024]{1,0:T(8,128)(2,1)} %bitcast.109, ...), custom_call_target="tpu_custom_call" | custom-call | tf_op jit(solution)/shard_map/middle_back/pallas_call | solution.py:507
  283.8 2.4 fusion.22
  286.2 1.6 constant_dynamic-slice_fusion.4
  291.0 59.8 %attend_back.1 = (bf16[1024,1024]{1,0:T(8,128)(2,1)S(1)}, bf16[2048,512]{1,0:T(8,128)(2,1)}, bf16[2048,512]{1,0:T(8,128)(2,1)}, f32[1,128]{1,0:T(1,128)S(1)}, f32[1,128]{1,0:T(1,128)S(1)}) custom-call(s32[8]{0:T(128)S(1)} %dynamic_slice.65.ids_ref, s32[16]{0:T(128)S(1)} %select_reduce_fusion.order_ref, bf16[1024,1024]{1,0:T(8,128)(2,1)} %copy-done.17, ...), custom_call_target="tpu_custom_call" | custom-call | flops 10737418240 | bytes 16777216 | tf_op jit(solution)/shard_map/attend_back/pallas_call | solution.py:291
  352.2 5.4 %fusion.21 = bf16[1024,512]{1,0:T(8,128)(2,1)S(1)} fusion(bf16[2048,1024]{1,0:T(8,128)(2,1)} %get-tuple-element.61, bf16[2048,512]{1,0:T(8,128)(2,1)} %get-tuple-element.64.dv_ref), kind=kOutput, calls=%fused_computation.77 | convolution fusion | flops 2147483648 | bytes 7340032 | tf_op jit(solution)/shard_map/dot_general | solution.py:52
  357.6 3.3 fusion.20
  365.7 2.8 maximum_select_fusion.2
  368.5 15.2 %project_back.1 = (bf16[2048,1024]{1,0:T(8,128)(2,1)}, f32[1,1024]{1,0:T(1,128)S(1)}) custom-call(s32[1]{0:T(128)} %bitcast.12.chip_ref, bf16[1024,1024]{1,0:T(8,128)(2,1)S(1)} %copy-done.5, bf16[2048,512]{1,0:T(8,128)(2,1)S(1)} %copy-done.7, bf16[2048,512]{1,0:T(8,128)(2,1)} %get-tuple-element.64.dv_ref, bf16[2048,1024]{1,0:T(8,128)(2,1)} %bitcast.134, ...), custom_call_target="tpu_custom_call" | custom-call | tf_op jit(solution)/shard_map/project_back/pallas_call | solution.py:401
  385.6 1.7 concatenate.29.refs_3_
  387.4 6.0 %fusion.5 = bf16[1024,1024]{1,0:T(8,128)(2,1)} fusion(bf16[1024,1024]{1,0:T(8,128)(2,1)} %copy-done.4, bf16[2048,1024]{1,0:T(8,128)(2,1)} %get-tuple-element.61, s32[]{:T(128)S(6)} %select_n.142), kind=kOutput, calls=%fused_computation.9 | convolution fusion | flops 2147483648 | bytes 6291460 | tf_op jit(solution)/shard_map/dot_general | solution.py:52
  393.4 3.3 maximum_select_fusion.1.refs_4_
  396.7 88.2 %reduce.25 = (bf16[64,3200]{1,0:T(8,128)(2,1)S(1)}, bf16[32,2176]{1,0:T(8,128)(2,1)S(1)}, bf16[2,256,1024]{2,1,0:T(8,128)(2,1)S(1)}) custom-call(bf16[2,2,4,64,1024]{4,3,2,1,0:T(8,128)(2,1)} %bitcast.146, bf16[2,2,4,64,512]{4,3,2,1,0:T(8,128)(2,1)S(1)} %bitcast.112, bf16[2,2,4,64,512]{4,3,2,1,0:T(8,128)(2,1)S(1)} %bitcast.111, ...), custom_call_target="tpu_custom_call" | custom-call | tf_op jit(solution)/shard_map/reduce/pallas_call | solution.py:789
  493.2 1.6 slice_convert_fusion.1
  494.8 14.4 %reduce-scatter.11.cloned.1.call-done = bf16[96,1024]{1,0:T(8,128)(2,1)} async-done(((bf16[384,1024]{1,0:T(8,128)(2,1)}), bf16[96,1024]{1,0:T(8,128)(2,1)}) %reduce-scatter.11.cloned.1.call-update) | async-done | bytes 196624 | tf_op jit(solution)/shard_map/reduce_scatter | solution.py:960
  509.2 1.7 convert_element_type.44
  511.7 2.3 slice_reduce_fusion.2
  (187 shorter events, 42.1 us)
Async XLA Ops:
  7.2 130.7 %copy-start = (s32[2,2048]{1,0:T(2,128)S(1)}, s32[2,2048]{1,0:T(2,128)}, u32[]{:S(2)}) copy-start(s32[2,2048]{1,0:T(2,128)} %param.18) | copy-start | bytes 49156
  7.2 200.1 %all-gather.2.cloned.1.call-start = ((), (), s32[]{:S(2)}) async-start(), calls=%async_computation.4 | async-start | bytes 6488064 | tf_op jit(solution)/shard_map/all_gather | solution.py:906
  134.8 217.3 %reduce-scatter.5.cloned.1.call-start = ((), (), s32[]{:S(2)}) async-start(), calls=%async_computation.5 | async-start | bytes 7864320 | tf_op jit(solution)/shard_map/reduce_scatter | solution.py:959
  137.9 46.2 %collective-permute-start = (bf16[8,64,1024]{2,1,0:T(8,128)(2,1)}, bf16[8,64,1024]{2,1,0:T(8,128)(2,1)}, u32[]{:S(2)}, u32[]{:S(2)}) collective-permute-start(bf16[8,64,1024]{2,1,0:T(8,128)(2,1)} %get-tuple-element.86), channel_id=1, source_target_pairs={{0,1},{1,0},{2,3},{3,2},{4,5},{5,4},{6,7},{7,6},{8,9},{9,8},{10,11... | collective-permute-start | bytes 3145736 | tf_op jit(solution)/shard_map/ppermute | solution.py:849
  140.4 16.5 %copy-start.19 = (f32[2048,128]{1,0:T(8,128)S(1)}, f32[2048,128]{1,0:T(8,128)}, u32[]{:S(2)}) copy-start(f32[2048,128]{1,0:T(8,128)} %constant.133.clone.cos_ref) | copy-start | bytes 3145732
  140.4 16.5 %copy-start.20 = (f32[2048,128]{1,0:T(8,128)S(1)}, f32[2048,128]{1,0:T(8,128)}, u32[]{:S(2)}) copy-start(f32[2048,128]{1,0:T(8,128)} %constant.134.clone.sin_ref) | copy-start | bytes 3145732
  184.1 2.9 copy-start.22
  187.0 3.7 copy-start.25
  190.7 20.6 %collective-permute-start.1 = (bf16[1024,1024]{1,0:T(8,128)(2,1)}, bf16[1024,1024]{1,0:T(8,128)(2,1)}, u32[]{:S(2)}, u32[]{:S(2)}) collective-permute-start(bf16[1024,1024]{1,0:T(8,128)(2,1)} %fusion.18.p0_ref), channel_id=1, source_target_pairs={{0,1},{1,0},{2,3},{3,2},{4,5},{5,4},{6,7},{7,6},{8,9},{9,8},{10,11... | collective-permute-start | bytes 6291464 | tf_op jit(solution)/shard_map/ppermute | solution.py:849
  243.9 242.8 %reduce-scatter.9.cloned.1.call-start = ((), (), s32[]{:S(2)}) async-start(), calls=%async_computation.7 | async-start | bytes 3932160 | tf_op jit(solution)/shard_map/reduce_scatter | solution.py:959
  252.4 239.6 %reduce-scatter.7.cloned.1.call-start = ((), (), s32[]{:S(2)}) async-start(), calls=%async_computation.6 | async-start | bytes 1966080 | tf_op jit(solution)/shard_map/reduce_scatter | solution.py:960
  252.5 12.1 %copy-start.24 = (bf16[16,1,96,1024]{3,2,1,0:T(8,128)(2,1)S(1)}, bf16[16,1,96,1024]{3,2,1,0:T(8,128)(2,1)}, u32[]{:S(2)}) copy-start(bf16[16,1,96,1024]{3,2,1,0:T(8,128)(2,1)} %constant_dynamic-slice_fusion.5) | copy-start | bytes 9437188
  252.5 12.1 %copy-start.36 = (bf16[1024,1536]{1,0:T(8,128)(2,1)S(1)}, bf16[1024,1536]{1,0:T(8,128)(2,1)}, u32[]{:S(2)}) copy-start(bf16[1024,1536]{1,0:T(8,128)(2,1)} %get-tuple-element.53) | copy-start | bytes 9437188
  264.3 10.7 %collective-permute-start.3 = (bf16[1024,1024]{1,0:T(8,128)(2,1)}, bf16[1024,1024]{1,0:T(8,128)(2,1)}, u32[]{:S(2)}, u32[]{:S(2)}) collective-permute-start(bf16[1024,1024]{1,0:T(8,128)(2,1)} %fusion.s0_ref), channel_id=1, source_target_pairs={{0,1},{1,0},{2,3},{3,2},{4,5},{5,4},{6,7},{7,6},{8,9},{9,8},{10,11... | collective-permute-start | bytes 6291464 | tf_op jit(solution)/shard_map/ppermute | solution.py:849
  269.6 2.9 collective-permute-start.2
  269.9 2.5 copy-start.28
  275.0 8.9 %copy-start.23 = (bf16[1024,1024]{1,0:T(8,128)(2,1)S(1)}, bf16[1024,1024]{1,0:T(8,128)(2,1)}, u32[]{:S(2)}) copy-start(bf16[1024,1024]{1,0:T(8,128)(2,1)} %copy-done.22) | copy-start | bytes 6291460
  283.8 2.4 copy-start.13
  283.8 2.4 copy-start.18
  287.9 3.1 copy-start.21
  287.9 105.5 %collective-permute-start.5 = (bf16[8,64,1024]{2,1,0:T(8,128)(2,1)}, bf16[8,64,1024]{2,1,0:T(8,128)(2,1)}, u32[]{:S(2)}, u32[]{:S(2)}) collective-permute-start(bf16[8,64,1024]{2,1,0:T(8,128)(2,1)} %get-tuple-element.84), channel_id=1, source_target_pairs={{0,1},{1,0},{2,3},{3,2},{4,5},{5,4},{6,7},{7,6},{8,9},{9,8},{10,11... | collective-permute-start | bytes 3145736 | tf_op jit(solution)/shard_map/ppermute | solution.py:849
  289.4 76.3 %collective-permute-start.4 = (bf16[256,1024]{1,0:T(8,128)(2,1)}, bf16[256,1024]{1,0:T(8,128)(2,1)}, u32[]{:S(2)}, u32[]{:S(2)}) collective-permute-start(bf16[256,1024]{1,0:T(8,128)(2,1)} %get-tuple-element.88), channel_id=1, source_target_pairs={{0,4},{1,5},{2,6},{3,7},{4,0},{5,1},{6,2},{7,3},{8,12},{9,13},{10,... | collective-permute-start | bytes 1572872 | tf_op jit(solution)/shard_map/ppermute | solution.py:850
  352.1 157.1 %reduce-scatter.11.cloned.1.call-start = ((), (), s32[]{:S(2)}) async-start(), calls=%async_computation.8 | async-start | bytes 983040 | tf_op jit(solution)/shard_map/reduce_scatter | solution.py:960
  352.2 5.5 %copy-start.6 = (bf16[2048,512]{1,0:T(8,128)(2,1)S(1)}, bf16[2048,512]{1,0:T(8,128)(2,1)}, u32[]{:S(2)}) copy-start(bf16[2048,512]{1,0:T(8,128)(2,1)} %get-tuple-element.63.dk_ref) | copy-start | bytes 6291460
  352.2 5.5 %copy-start.35 = (bf16[2048,1024]{1,0:T(8,128)(2,1)S(1)}, bf16[2048,1024]{1,0:T(8,128)(2,1)}, u32[]{:S(2)}) copy-start(bf16[2048,1024]{1,0:T(8,128)(2,1)} %get-tuple-element.61) | copy-start | bytes 12582916
  364.3 4.2 copy-start.5
  364.3 4.2 copy-start.7
  387.4 6.1 %copy-start.26 = (bf16[8,1,64,1024]{3,2,1,0:T(8,128)(2,1)S(1)}, bf16[8,1,64,1024]{3,2,1,0:T(8,128)(2,1)}, u32[]{:S(2)}) copy-start(bf16[8,1,64,1024]{3,2,1,0:T(8,128)(2,1)} %get-tuple-element.83) | copy-start | bytes 3145732
  393.4 3.3 copy-start.8
  493.1 18.0 %collective-permute-start.6 = (bf16[32,3072]{1,0:T(8,128)(2,1)S(1)}, bf16[32,3072]{1,0:T(8,128)(2,1)S(1)}, u32[]{:S(2)}, u32[]{:S(2)}) collective-permute-start(bf16[32,3072]{1,0:T(8,128)(2,1)S(1)} %get-tuple-element.94), channel_id=1, source_target_pairs={{0,1},{1,0},{2,3},{3,2},{4,5},{5,4},{6,7},{7,6},{8,9},{9,8},{10,11... | collective-permute-start | bytes 589832 | tf_op jit(solution)/shard_map/ppermute | solution.py:849
  514.8 3.7 copy-start.10
  516.3 3.2 copy-start.1
  (20 other events, 28.7 us)
Sparse Core Ops, SparseCore 0:
  134.9 72.3 all-gather.1
  244.0 68.6 reduce-scatter.4
  315.8 44.0 reduce-scatter.8
  362.0 35.2 reduce-scatter.6
  486.9 22.3 reduce-scatter.10

commit v3 on v2

--- a/solution.py
+++ b/solution.py
@@ -424,7 +424,7 @@
     )(chip, dq, dk, dv, x_all, w_all, w_all, w_all)
 
 
-def feed_kernel(x_ref, p0_ref, p1_ref, gain_ref, go_ref, w_ref, d_ref, mid_ref, sec_ref, act_ref, gg_ref):
+def feed_kernel(chip_ref, x_ref, p0_ref, p1_ref, gain_ref, go_ref, w_ref, d_ref, mid_ref, sec_ref, act_ref, gg_ref):
     count = x_ref.shape[0]
     size = min(ROW_TILE, count)
     tile = lambda i: pl.ds(pl.multiple_of(i * size, size), size)
@@ -455,10 +455,11 @@
     lax.fori_loop(0, count // size, body, 0)
 
 
-def feed(x, p0, p1, gain, go, w_all, at, w_down):
-    rows, width = x.shape
+def feed(chip, x_all, p0, p1, gain, go, w_all, at, w_down):
+    rows, width = go.shape
     ff = w_down.shape[0]
-    whole = lambda: pl.BlockSpec((rows, width), lambda j: (0, 0), pipeline_mode=pl.Buffered(1))
+    once = pl.Buffered(1)
+    whole = lambda: pl.BlockSpec((rows, width), lambda j, chip: (0, 0), pipeline_mode=once)
     return pl.pallas_call(
         feed_kernel,
         out_shape=[
@@ -467,23 +468,27 @@
             jax.ShapeDtypeStruct((rows, ff), BF16),
             jax.ShapeDtypeStruct((rows, 2 * ff), BF16),
         ],
-        grid=(ff // FF_TILE,),
-        in_specs=[
-            whole(), whole(), whole(),
-            pl.BlockSpec((1, width), lambda j: (0, 0)),
-            whole(),
-            pl.BlockSpec((width, 2 * FF_TILE), lambda j: (0, at // (2 * FF_TILE) + j)),
-            pl.BlockSpec((FF_TILE, width), lambda j: (j, 0)),
-        ],
-        out_specs=[
-            pl.BlockSpec((rows, width), lambda j: (0, 0)),
-            pl.BlockSpec((rows, width), lambda j: (0, 0)),
-            pl.BlockSpec((rows, FF_TILE), lambda j: (0, j)),
-            pl.BlockSpec((rows, 2 * FF_TILE), lambda j: (0, j)),
-        ],
+        grid_spec=pltpu.PrefetchScalarGridSpec(
+            num_scalar_prefetch=1,
+            grid=(ff // FF_TILE,),
+            in_specs=[
+                pl.BlockSpec((rows, width), lambda j, chip: (chip[0], 0), pipeline_mode=once),
+                whole(), whole(),
+                pl.BlockSpec((1, width), lambda j, chip: (0, 0)),
+                whole(),
+                pl.BlockSpec((width, 2 * FF_TILE), lambda j, chip: (0, at // (2 * FF_TILE) + j)),
+                pl.BlockSpec((FF_TILE, width), lambda j, chip: (j, 0)),
+            ],
+            out_specs=[
+                pl.BlockSpec((rows, width), lambda j, chip: (0, 0)),
+                pl.BlockSpec((rows, width), lambda j, chip: (0, 0)),
+                pl.BlockSpec((rows, FF_TILE), lambda j, chip: (0, j)),
+                pl.BlockSpec((rows, 2 * FF_TILE), lambda j, chip: (0, j)),
+            ],
+        ),
         compiler_params=pltpu.CompilerParams(vmem_limit_bytes=VMEM_LIMIT),
         name="feed",
-    )(x, p0, p1, gain, go, w_all, w_down)
+    )(chip, x_all, p0, p1, gain, go, w_all, w_down)
 
 
 def middle_back_kernel(mid_ref, s0_ref, s1_ref, go_ref, gain_ref, wo_ref, ga_ref, gm_ref, g_ref):
@@ -519,6 +524,9 @@
     )(middle, s0, s1, go, gain, w_out)
 
 
+LINK_TIME = pl.CostEstimate(flops=0, bytes_accessed=300_000_000, transcendentals=0)
+
+
 def peers():
     dp, ctx = lax.axis_index("dp"), lax.axis_index("ctx")
     to = lambda d, k: (jnp.bitwise_xor(dp, d), jnp.bitwise_xor(ctx, k))
@@ -548,7 +556,9 @@
     return send, made
 
 
-def gather_kernel(pk_ref, wo_ref, tok_ref, go_ref, w_ref, x_ref, g_ref, send_sem, recv_sem, local_sem):
+def gather_kernel(
+    pk_ref, wd_ref, tok_ref, go_ref, w_ref, d_ref, x_ref, g_ref, send_sem, recv_sem, local_sem
+):
     dp, ctx, to = peers()
     c, z = ctx % 2, ctx // 2
     which, me = ctx // 4, ctx % 4
@@ -556,12 +566,12 @@
     greet([to(0, 1), to(0, 2), to(0, 4), to(0, 6), to(1, 0), to(2, 0)])
     send, made = sender(send_sem, recv_sem)
     sib, nbr, far, across, xn, yn = to(0, 1), to(0, 2), to(0, 4), to(0, 6), to(1, 0), to(2, 0)
-    rows, cols = pk_ref.shape[1:]
-
-    place = w_ref.at[dp, z, pl.ds(c * rows, rows), pl.ds(0, cols)]
+    rows = pk_ref.shape[1]
+
+    place = w_ref.at[dp, z, pl.ds(c * rows, rows)]
     local = [
         pltpu.make_async_copy(pk_ref.at[c], place, local_sem.at[0]),
-        pltpu.make_async_copy(wo_ref, w_ref.at[dp, z, :, pl.ds(cols, wo_ref.shape[1])], local_sem.at[1]),
+        pltpu.make_async_copy(wd_ref, d_ref.at[dp, z], local_sem.at[1]),
         pltpu.make_async_copy(tok_ref.at[which], x_ref.at[me, 0], local_sem.at[2]),
         pltpu.make_async_copy(go_ref.at[which], g_ref.at[c, 0], local_sem.at[3]),
     ]
@@ -573,22 +583,26 @@
     cross.wait_recv()
     done = []
 
-    def half(h, q, zz):
-        return w_ref.at[q, zz, pl.ds(h * rows, rows)]
+    refs = [w_ref, d_ref]
+
+    def half(ref, h, q, zz):
+        size = ref.shape[2] // 2
+        return ref.at[q, zz, pl.ds(h * size, size)]
 
     first = []
 
     def spread(zz):
-        low, high = half(0, dp, zz), half(1, dp, zz)
-        first.append((send(low, low, yn), low, half(0, jnp.bitwise_xor(dp, 2), zz), xn))
-        first.append((send(high, high, xn), high, half(1, jnp.bitwise_xor(dp, 1), zz), yn))
+        for ref in refs:
+            low, high = half(ref, 0, dp, zz), half(ref, 1, dp, zz)
+            first.append((send(low, low, yn), low, half(ref, 0, jnp.bitwise_xor(dp, 2), zz), xn))
+            first.append((send(high, high, xn), high, half(ref, 1, jnp.bitwise_xor(dp, 1), zz), yn))
 
     def pass_on():
-        for copy, own, part, device in first[:2]:
+        for copy, own, part, device in first[:4]:
             done.append(send(own, own, device))
             copy.wait_recv()
             done.append(send(part, part, device))
-        del first[:2]
+        del first[:4]
 
     z_one = jnp.bitwise_xor(z, 1)
     z_near = jnp.bitwise_xor(z, jnp.where(inner, 3, 2))
@@ -596,28 +610,33 @@
     relayed = []
 
     def relay(slot, source, device):
-        copy = pltpu.make_async_remote_copy(
-            src_ref=w_ref.at[dp, source], dst_ref=w_ref.at[dp, source],
-            send_sem=send_sem.at[send_sem.shape[0] - 4 + len(relayed)],
-            recv_sem=recv_sem.at[send_sem.shape[0] - 2 + slot],
-            device_id=device, device_id_type=MESH,
-        )
-        relayed.append(copy)
-        pl.when(inner)(copy.start)
-        return copy
-
-    step = send(w_ref.at[dp, z], w_ref.at[dp, z], nbr)
+        for i, ref in enumerate(refs):
+            copy = pltpu.make_async_remote_copy(
+                src_ref=ref.at[dp, source], dst_ref=ref.at[dp, source],
+                send_sem=send_sem.at[send_sem.shape[0] - 8 + len(relayed)],
+                recv_sem=recv_sem.at[send_sem.shape[0] - 4 + 2 * slot + i],
+                device_id=device, device_id_type=MESH,
+            )
+            relayed.append(copy)
+            pl.when(inner)(copy.start)
+        return relayed[-2:]
+
+    def arrived(copies):
+        for copy in copies:
+            copy.wait_recv()
+
+    step = [send(ref.at[dp, z], ref.at[dp, z], nbr) for ref in refs]
     near = relay(0, z, across)
     spread(z)
     pass_on()
-    step.wait_recv()
+    arrived(step)
     far_block = relay(1, z_one, across)
     spread(z_one)
-    near.wait_recv()
+    arrived(near)
     relay(0, z_near, nbr)
     spread(z_near)
     pass_on()
-    far_block.wait_recv()
+    arrived(far_block)
     relay(1, z_far, nbr)
     spread(z_far)
     swap = send(tok_ref.at[1 - which], x_ref.at[me, 1], far)
@@ -647,21 +666,22 @@
             copy.wait_send()
 
 
-def gather(packed, w_out, tokens, grad_out):
-    rows, cols = 2 * packed.shape[1], packed.shape[2] + w_out.shape[1]
+def gather(packed, w_down, tokens, grad_out):
+    rows, cols = 2 * packed.shape[1], packed.shape[2]
     slots, width = tokens.shape[1:]
-    copies = 36 + 4
+    copies = 61 + 8
     anywhere = pl.BlockSpec(memory_space=pl.ANY)
     near = pl.BlockSpec(memory_space=pltpu.VMEM)
-    w, x, g = pl.pallas_call(
+    w, d, x, g = pl.pallas_call(
         gather_kernel,
         out_shape=[
             jax.ShapeDtypeStruct((4, 4, rows, cols), BF16),
+            jax.ShapeDtypeStruct((4, 4) + w_down.shape, BF16),
             jax.ShapeDtypeStruct((4, 2, slots, width), BF16),
             jax.ShapeDtypeStruct((2, 2, slots, width), BF16),
         ],
         in_specs=[near] * 4,
-        out_specs=[anywhere] * 3,
+        out_specs=[anywhere] * 4,
         scratch_shapes=[
             pltpu.SemaphoreType.DMA((copies,)),
             pltpu.SemaphoreType.DMA((copies,)),
@@ -670,85 +690,132 @@
         compiler_params=pltpu.CompilerParams(
             collective_id=0, has_side_effects=True, vmem_limit_bytes=VMEM_LIMIT
         ),
+        cost_estimate=LINK_TIME,
         name="gather",
-    )(packed, w_out, tokens, grad_out)
-    return w.reshape(16 * rows, cols), x.reshape(-1, width), g.reshape(-1, width)
+    )(packed, w_down, tokens, grad_out)
+    return w.reshape(16 * rows, cols), d.reshape(-1, width), x.reshape(-1, width), g.reshape(-1, width)
 
 
 def reduce_kernel(n_in, *refs):
-    g_refs, (part_ref, x_ref, ga_ref, gain_ref) = refs[:n_in], refs[n_in : n_in + 4]
-    o_ref, s_ref, ig_ref = refs[n_in + 4 : n_in + 7]
+    g_refs, (ow_ref, or_ref, part_ref, xa_ref, gm_ref, gain_ref) = refs[:n_in], refs[n_in : n_in + 6]
+    gq_ref, gk_ref, gv_ref, gg_ref, go_ref, ig_ref = refs[n_in + 6 : n_in + 12]
     (
         g_ref, in_a, in_b, mid_a, mid_b, got_a, got_b, out3, in3,
-        mine_ref, sib_ref, give_ref, nbr_ref, back_ref, send_sem, recv_sem, local_sem,
-    ) = refs[n_in + 7 :]
+        mine_ref, sib_ref, give_ref, nbr_ref, back_ref, x_ref, ga_ref, o_ref, s_ref, send_sem, recv_sem, local_sem,
+    ) = refs[n_in + 12 :]
     dp, ctx, to = peers()
     c, z = ctx % 2, ctx // 2
     which, chip = ctx // 4, z % 2
     x, y = dp % 2, dp // 2
-    greet([to(0, 1), to(0, 2), to(0, 4), to(0, 6), to(1, 0), to(2, 0)])
-    send, made = sender(send_sem, recv_sem)
-    sib, nbr, far, xn, yn = to(0, 1), to(0, 2), to(0, 4), to(1, 0), to(2, 0)
     hr = g_ref.shape[3] // 2
     at, local = 0, []
     for i, ref in enumerate(g_refs):
         width = ref.shape[-1]
         local.append(pltpu.make_async_copy(ref, g_ref.at[:, :, :, :, pl.ds(at, width)], local_sem.at[i]))
         at += width
-    local.append(pltpu.make_async_copy(part_ref.at[:, c], mine_ref, local_sem.at[n_in]))
+    wide = pl.ds(at, ow_ref.shape[-1])
+    count = mine_ref.shape[1]
+    local += [
+        pltpu.make_async_copy(ow_ref.at[:, :, c], g_ref.at[c, :, :, :, wide], local_sem.at[n_in]),
+        pltpu.make_async_copy(or_ref, g_ref.at[1 - c, :, :, :, wide], local_sem.at[n_in + 1]),
+        pltpu.make_async_copy(part_ref.at[:, c], mine_ref, local_sem.at[n_in + 2]),
+        pltpu.make_async_copy(xa_ref.at[ctx % 4], x_ref, local_sem.at[n_in + 3]),
+        pltpu.make_async_copy(gm_ref.at[c], ga_ref, local_sem.at[n_in + 4]),
+    ]
     for copy in local:
         copy.start()
+    greet([to(0, 1), to(0, 2), to(0, 4), to(0, 6), to(1, 0), to(2, 0)])
+    send, made = sender(send_sem, recv_sem)
+    sib, nbr, far, across = to(0, 1), to(0, 2), to(0, 4), to(0, 6)
+    xn, yn = to(1, 0), to(2, 0)
     cross = send(part_ref.at[:, 1 - c], sib_ref, sib)
     for copy in local:
         copy.wait()
     low, high = pl.ds(0, hr), pl.ds(hr, hr)
-    order = [jnp.bitwise_xor(z, k) for k in (2, 3, 1, 0)]
-    a_in, b_in, a_mid, b_mid, last = [], [], [], [], []
+    inner = jnp.logical_or(z == 1, z == 2)
+    outer = jnp.logical_not(inner)
+    order = [jnp.bitwise_xor(z, jnp.where(inner, 3, 2)), jnp.bitwise_xor(z, jnp.where(inner, 2, 3)), jnp.bitwise_xor(z, 1), z]
+    passed = []
+
+    def pass_z(kind, slot, source, part, device, role):
+        copy = pltpu.make_async_remote_copy(
+            src_ref=out3.at[source, :, parts[part]], dst_ref=in3.at[slot, :, parts[part]],
+            send_sem=send_sem.at[40 + 2 * kind + part], recv_sem=recv_sem.at[40 + 2 * slot + part],
+            device_id=device, device_id_type=MESH,
+        )
+        pl.when(role)(copy.start)
+        passed.append((role, copy))
+
+    def from_z(slot, part):
+        return pltpu.make_async_remote_copy(
+            src_ref=out3.at[0, :, parts[part]], dst_ref=in3.at[slot, :, parts[part]],
+            send_sem=send_sem.at[40 + part], recv_sem=recv_sem.at[40 + 2 * slot + part],
+            device_id=nbr, device_id_type=MESH,
+        )
+
+    def add_z(block, slot, part):
+        p = parts[part]
+        out3[block, :, p] = (out3[block, :, p].astype(F32) + in3[slot, :, p].astype(F32)).astype(BF16)
+
+    def inward(i):
+        k, part = i // 2, i % 2
+
+        @pl.when(inner)
+        def _():
+            from_z(k, part).wait_recv()
+            add_z(k, k, part)
+
+        pass_z(3 + k, 3 + k, k, part, across, inner)
+
+    def outward(part):
+        @pl.when(inner)
+        def _():
+            from_z(4, part).wait_recv()
+            add_z(2, 4, part)
+
+        pass_z(5, 2, 2, part, nbr, inner)
+
+    a_in, b_in, a_mid, b_mid = [], [], [], []
     size = 64
     tile = lambda i: pl.ds(pl.multiple_of(i * size, size), size)
-    count = mine_ref.shape[1]
-
-    def enter(k):
-        a_in.append(send(g_ref.at[:, 1 - x, order[k], low], in_a.at[k], xn))
-        b_in.append(send(g_ref.at[1 - y, :, order[k], high], in_b.at[k], yn))
-
-    def middle(k):
+    cut = g_ref.shape[4] // 2 // HD * HD
+    parts = (pl.ds(0, cut), pl.ds(cut, g_ref.shape[4] - cut))
+
+    def enter(i):
+        k, p = i // 2, parts[i % 2]
+        a_in.append(send(g_ref.at[:, 1 - x, order[k], low, p], in_a.at[k, :, :, p], xn))
+        b_in.append(send(g_ref.at[1 - y, :, order[k], high, p], in_b.at[k, :, :, p], yn))
+
+    def middle(i):
+        k, p = i // 2, parts[i % 2]
         add = lambda p, q: (p.astype(F32) + q.astype(F32)).astype(BF16)
-        a_in[k].wait_recv()
-        mid_a[k] = add(g_ref[1 - y, x, order[k], 0:hr], in_a[k, 1 - y])
-        a_mid.append(send(mid_a.at[k], got_a.at[k], yn))
-        b_in[k].wait_recv()
-        mid_b[k] = add(g_ref[y, 1 - x, order[k], hr:], in_b[k, 1 - x])
-        b_mid.append(send(mid_b.at[k], got_b.at[k], xn))
-
-    def leave(k):
+        a_in[i].wait_recv()
+        mid_a[k, :, p] = add(g_ref[1 - y, x, order[k], 0:hr, p], in_a[k, 1 - y, :, p])
+        a_mid.append(send(mid_a.at[k, :, p], got_a.at[k, :, p], yn))
+        b_in[i].wait_recv()
+        mid_b[k, :, p] = add(g_ref[y, 1 - x, order[k], hr:, p], in_b[k, 1 - x, :, p])
+        b_mid.append(send(mid_b.at[k, :, p], got_b.at[k, :, p], xn))
+
+    def leave(i):
+        k, p = i // 2, parts[i % 2]
         add = lambda p, q, r: (p.astype(F32) + q.astype(F32) + r.astype(F32)).astype(BF16)
-        a_mid[k].wait_recv()
-        out3[k, 0:hr] = add(g_ref[y, x, order[k], 0:hr], in_a[k, y], got_a[k])
-        b_mid[k].wait_recv()
-        out3[k, hr:] = add(g_ref[y, x, order[k], hr:], in_b[k, x], got_b[k])
+        a_mid[i].wait_recv()
+        out3[k, 0:hr, p] = add(g_ref[y, x, order[k], 0:hr, p], in_a[k, y, :, p], got_a[k, :, p])
+        b_mid[i].wait_recv()
+        out3[k, hr:, p] = add(g_ref[y, x, order[k], hr:, p], in_b[k, x, :, p], got_b[k, :, p])
         if k < 3:
-            last.append(send(out3.at[k], in3.at[k], to(0, 2 * (2, 3, 1)[k])))
+            pass_z(k, k, k, i % 2, nbr, outer)
 
     enter(0)
     enter(1)
+    enter(2)
     cross.wait_recv()
+    slots = ig_ref.shape[1]
 
     def give(i, _):
         rows = tile(i)
         give_ref[rows] = (mine_ref[1 - chip, rows].astype(F32) + sib_ref[1 - chip, rows].astype(F32)).astype(BF16)
         return 0
-
-    lax.fori_loop(0, count // size, give, 0)
-    swap = send(give_ref, nbr_ref, nbr)
-    middle(0)
-    enter(2)
-    middle(1)
-    enter(3)
-    leave(0)
-    middle(2)
-    leave(1)
-    swap.wait_recv()
 
     def back(i, _):
         rows = tile(i)
@@ -757,44 +824,101 @@
         back_ref[rows] = (ga_ref[rows, :].astype(F32) + through).astype(BF16)
         return 0
 
-    lax.fori_loop(0, count // size, back, 0)
-    slots = ig_ref.shape[1]
+    swaps = []
+    for first in (slots, 0):
+        lax.fori_loop(first // size, (first + slots) // size, give, 0)
+        rows = pl.ds(first, slots)
+        swaps.append(send(give_ref.at[rows], nbr_ref.at[rows], nbr))
+    middle(0)
+    enter(3)
+    middle(1)
+    enter(4)
+    swaps[0].wait_recv()
+    lax.fori_loop(slots // size, 2 * slots // size, back, 0)
     home = send(back_ref.at[pl.ds(slots, slots)], ig_ref.at[which], far)
+    leave(0)
+    middle(2)
+    enter(5)
+    leave(1)
+    middle(3)
+    enter(6)
+    leave(2)
+    inward(0)
+    middle(4)
+    enter(7)
+    leave(3)
+    inward(1)
+    swaps[1].wait_recv()
+    lax.fori_loop(0, slots // size, back, 0)
     keep = pltpu.make_async_copy(back_ref.at[pl.ds(0, slots)], ig_ref.at[which], local_sem.at[0])
     keep.start()
-    middle(3)
-    leave(2)
-    leave(3)
-    for copy in last:
-        copy.wait_recv()
-    o_ref[...] = (
-        out3[3].astype(F32) + in3[0].astype(F32) + in3[1].astype(F32) + in3[2].astype(F32)
-    ).astype(BF16)
-    other = send(o_ref.at[pl.ds((1 - c) * hr, hr), pl.ds(0, s_ref.shape[1])], s_ref, sib)
+    middle(5)
+    leave(4)
+    inward(2)
+    middle(6)
+    leave(5)
+    inward(3)
+    outward(0)
+    middle(7)
+    leave(6)
+    outward(1)
+    leave(7)
+    for part in range(2):
+        from_z(2, part).wait_recv()
+
+    @pl.when(inner)
+    def _():
+        for part in range(2):
+            from_z(3, part).wait_recv()
+            add_z(3, 3, part)
+
+    total = out3[3].astype(F32) + in3[2].astype(F32)
+    near = s_ref.shape[1]
+    o_ref[...] = total[:, :near].astype(BF16)
+    other = send(o_ref.at[pl.ds(pl.multiple_of((1 - c) * hr, hr), hr)], s_ref, sib)
+    go_ref[...] = total[:, near:]
+    own = o_ref.at[pl.ds(pl.multiple_of(c * hr, hr), hr)]
+
+    def place(source, core):
+        col = 0
+        for ref in (gq_ref, gk_ref, gv_ref):
+            size = ref.shape[1] // 2
+            ref[:, pl.ds(pl.multiple_of(core * size, size), size)] = source[:, col : col + size].astype(F32)
+            col += size
+
+    place(own, c)
+    other.wait_recv()
+    place(s_ref, 1 - c)
+    gains = near - HD
+    gg_ref[...] = own[:, gains:].astype(F32) + s_ref[:, gains:].astype(F32)
     keep.wait()
-    other.wait_recv()
     home.wait_recv()
     for copy in made:
         copy.wait_send()
-
-
-def reduce(grads, near_cols, part, x, grad_middle, gain):
+    for role, copy in passed:
+        pl.when(role)(copy.wait_send)
+
+
+def reduce(grads, out_own, out_sib, part, x_all, grad_middle, gain):
     rows = grads[0].shape[0] // 16
-    cols = sum(g.shape[1] for g in grads)
-    grads = [g.reshape(2, 2, 4, rows, g.shape[1]) for g in grads]
-    count, width = x.shape
-    copies = 23
+    width = x_all.shape[1]
+    near_cols = sum(g.shape[1] for g in grads)
+    cols = near_cols + width
+    count = part.shape[0] // 4
+    split = lambda v: v.reshape(2, 2, 4, rows, v.shape[1])
+    copies = 52
     anywhere = pl.BlockSpec(memory_space=pl.ANY)
     near = pl.BlockSpec(memory_space=pltpu.VMEM)
     return pl.pallas_call(
         functools.partial(reduce_kernel, len(grads)),
         out_shape=[
-            jax.ShapeDtypeStruct((rows, cols), BF16),
-            jax.ShapeDtypeStruct((rows // 2, near_cols), BF16),
+            *[jax.ShapeDtypeStruct((rows // 2, 2 * g.shape[-1]), F32) for g in grads[:3]],
+            jax.ShapeDtypeStruct((rows // 2, HD), F32),
+            jax.ShapeDtypeStruct((rows, width), F32),
             jax.ShapeDtypeStruct((2, count // 2, width), BF16),
         ],
-        in_specs=[anywhere] * (len(grads) + 1) + [near] * 3,
-        out_specs=[near, anywhere, anywhere],
+        in_specs=[anywhere] * (len(grads) + 5) + [near],
+        out_specs=[near] * 5 + [anywhere],
         scratch_shapes=[
             pltpu.VMEM((2, 2, 4, rows, cols), BF16),
             pltpu.VMEM((4, 2, rows // 2, cols), BF16),
@@ -803,21 +927,32 @@
         + [pltpu.VMEM((4, rows // 2, cols), BF16)] * 4
         + [
             pltpu.VMEM((4, rows, cols), BF16),
-            pltpu.VMEM((3, rows, cols), BF16),
+            pltpu.VMEM((5, rows, cols), BF16),
             pltpu.VMEM((2, count, width), BF16),
             pltpu.VMEM((2, count, width), BF16),
-            pltpu.VMEM((count, width), BF16),
-            pltpu.VMEM((count, width), BF16),
-            pltpu.VMEM((count, width), BF16),
+        ]
+        + [pltpu.VMEM((count, width), BF16)] * 5
+        + [
+            pltpu.VMEM((rows, near_cols), BF16),
+            pltpu.VMEM((rows // 2, near_cols), BF16),
             pltpu.SemaphoreType.DMA((copies,)),
             pltpu.SemaphoreType.DMA((copies,)),
-            pltpu.SemaphoreType.DMA((len(grads) + 1,)),
+            pltpu.SemaphoreType.DMA((len(grads) + 5,)),
         ],
         compiler_params=pltpu.CompilerParams(
             collective_id=1, has_side_effects=True, vmem_limit_bytes=VMEM_LIMIT
         ),
+        cost_estimate=LINK_TIME,
         name="reduce",
-    )(*grads, part.reshape(2, 2, count, width), x, grad_middle, gain)
+    )(
+        *[split(g) for g in grads],
+        out_own.reshape(2, 4, 2, rows, width),
+        out_sib.reshape(2, 4, rows, width),
+        part.reshape(2, 2, count, width),
+        x_all.reshape(4, count, width),
+        grad_middle.reshape(2, count, width),
+        gain,
+    )
 
 
 def by_core(c, own, other):
@@ -887,24 +1022,19 @@
     gu_shard = jnp.stack([by_tile(gate_order), by_tile(up_order)], axis=3).reshape(2, r_in, 2 * ff_c)
     packed = jnp.stack([jnp.concatenate([qkv_halves[i], gu_shard[i], gains], axis=1) for i in range(2)])
     if tall:
-        w_all, x_all, go_chip = gather(packed, w_out, tokens, grad_out)
-        x_own = lax.dynamic_slice_in_dim(x_all, (ctx % half) * 2 * slots, 2 * slots, 0)
-        out_rows = w_all[:, all_c + HD :].reshape(2, -1, r_out, width)
-        out_keep = lax.dynamic_index_in_dim(out_rows, c, 0, False)
-        out_give = lax.dynamic_index_in_dim(out_rows, 1 - c, 0, False)
-        w_out_c = by_core(c, out_keep, sibling(out_give)).transpose(1, 0, 2, 3).reshape(q_c, width)
-        w_down, w_all = lax.optimization_barrier((w_down, w_all))
+        w_all, w_down_c, x_all, go_chip = gather(packed, w_down, tokens, grad_out)
+        w_out, w_all = lax.optimization_barrier((w_out, w_all))
     else:
         both = lax.all_gather(packed, axes, axis=1, tiled=True)
         w_all = lax.dynamic_index_in_dim(both, c, 0, False)
-        out_all = lax.all_gather(w_out, axes, axis=0, tiled=True)
-        w_out_c = lax.dynamic_slice_in_dim(out_all, c * q_c, q_c, 0)
+        down_all = lax.all_gather(w_down, axes, axis=0, tiled=True).reshape(chips, 2, r_down, width)
+        w_down_c = lax.dynamic_index_in_dim(down_all, c, 1, False).reshape(ff_c, width)
         x_own = placed(tokens)
         x_all = lax.all_gather(x_own, "ctx", axis=0, tiled=True, axis_index_groups=halves)
         go_own = placed(grad_out)
         go_chip = by_core(c, go_own, sibling(go_own)).reshape(4 * slots, width)
-    down_all = lax.all_gather(w_down, axes, axis=0, tiled=True).reshape(chips, 2, r_down, width)
-    w_down_c = lax.dynamic_index_in_dim(down_all, c, 1, False).reshape(ff_c, width)
+    out_all = lax.all_gather(w_out, axes, axis=0, tiled=True)
+    w_out_c = lax.dynamic_slice_in_dim(out_all, c * q_c, q_c, 0)
     g_cols = w_all[:, all_c : all_c + HD].astype(F32)
     gain_attn = g_cols[:, 0][None]
     gain_mlp = g_cols[:, 1][None]
@@ -914,7 +1044,6 @@
 
     chip = (ctx % half) // 2
     chip_rows = 4 * slots
-    x_chip = lax.dynamic_slice_in_dim(x_all, chip * chip_rows, chip_rows, 0)
     slot_ids = lax.dynamic_index_in_dim(positions, which, 0, False).reshape(2 * n, span)[:, 0] // span
     places = np.stack(
         [
@@ -934,7 +1063,7 @@
     mixed, lse = attend(ids, order, q_raw, kv_raw, cosine, sine, gain_q, gain_k, span)
     proj = dot(mixed, w_out_c, NN, BF16)
     middle, second, activated, grad_gu = feed(
-        x_chip, proj, sibling(proj), gain_mlp, go_chip, w_all, qkv_c, w_down_c
+        chip_at, x_all, proj, sibling(proj), gain_mlp, go_chip, w_all, qkv_c, w_down_c
     )
     down = dot(activated, w_down_c, NN, BF16).reshape(2, 2 * slots, width)
     down_own = lax.dynamic_index_in_dim(down, c, 0, False)
@@ -955,38 +1084,44 @@
     )
     grad_mlp_gain = jnp.where(c == 0, mlp_gain_sum[0], 0.0)
 
-    def reduced(grad):
-        part = lax.psum_scatter(grad, "dp", scatter_dimension=0, tiled=True)
-        return lax.psum_scatter(part, "ctx", scatter_dimension=0, tiled=True, axis_index_groups=same_core)
-
-    sum_gu = reduced(grad_gu_w)
-    sum_down = reduced(grad_down_w)
-
-    grad_out_w = dot(mixed, grad_attn, TN, BF16)
+    over_dp = lambda grad: lax.psum_scatter(grad, "dp", scatter_dimension=0, tiled=True)
+    over_ctx = lambda part: lax.psum_scatter(
+        part, "ctx", scatter_dimension=0, tiled=True, axis_index_groups=same_core
+    )
+    part_gu = over_dp(grad_gu_w)
+    part_down = over_dp(grad_down_w)
+
+    out_w = dot(mixed, grad_attn, TN, BF16).reshape(-1, 2, r_out, width)
+    out_recv = sibling(lax.dynamic_index_in_dim(out_w, 1 - c, 1, False))
+    out_recv, grad_mixed = lax.optimization_barrier((out_recv, grad_mixed))
     result, grad_mixed = lax.optimization_barrier((result, grad_mixed))
     output = returned(result)
     dq, dk, dv, dgq, dgk = attend_back(
         ids, order, q_raw, kv_raw, grad_mixed, mixed, lse, cosine, sine, gain_q, gain_k, span
     )
-    output, dq = lax.optimization_barrier((output, dq))
+    output, dq, dk, dv, part_gu, part_down = lax.optimization_barrier((output, dq, dk, dv, part_gu, part_down))
+    rows2, extra = 2 * r_in, r_down - 2 * r_in
+    part_down = part_down.reshape(half, r_down, width)
+    rest = part_down[:, rows2:]
+    fold = rows2 // extra
+    folded = [rest[:, :, i * width // fold : (i + 1) * width // fold] for i in range(fold)]
+    pieces = [part_gu.reshape(half, rows2, -1), part_down[:, :rows2], jnp.concatenate(folded, axis=1)]
+    sum_ff = over_ctx(jnp.concatenate(pieces, axis=2).reshape(half * rows2, -1))
+    sum_gu = sum_ff[:, : 2 * ff_c]
+    tail = sum_ff[:, 2 * ff_c + width :].reshape(fold, extra, -1)
+    sum_down = jnp.concatenate(
+        [sum_ff[:, 2 * ff_c : 2 * ff_c + width], jnp.concatenate([tail[i] for i in range(fold)], axis=1)], axis=0
+    )
     part_all, attn_gain_sum = project_back(chip_at, dq, dk, dv, x_all, w_all)
     grad_q_w = dot(hidden, dq, TN, BF16)
     grad_k_w = dot(hidden_all, dk, TN, BF16)
     grad_v_w = dot(hidden_all, dv, TN, BF16)
-    out_w = grad_out_w.reshape(-1, 2, r_out, width)
-    out_mine = lax.dynamic_index_in_dim(out_w, c, 1, False)
-    out_recv = sibling(lax.dynamic_index_in_dim(out_w, 1 - c, 1, False))
-    grad_out_w = by_core(c, out_mine, out_recv).reshape(chips * r_out, width)
-
-    apart = width // HD
-    spaced = lambda v: jnp.pad(v.reshape(HD, 1), ((0, 0), (0, apart - 1))).reshape(width, 1)
-    gain_cols = jnp.concatenate(
-        [attn_gain_sum.T, grad_mlp_gain[:, None], spaced(dgq), spaced(dgk), jnp.zeros((width, HD - 4), F32)],
-        axis=1,
-    ).astype(BF16)
-    grads = [grad_q_w, grad_k_w, grad_v_w, gain_cols, grad_out_w]
+    lot = lambda v: v.reshape(n_dp * n, -1)
+    entries = jnp.concatenate([lot(attn_gain_sum), lot(grad_mlp_gain), lot(dgq), lot(dgk)], axis=1)
+    entries = jnp.pad(entries[:, None], ((0, 0), (0, r_in - 1), (0, HD - entries.shape[1])))
+    grads = [grad_q_w, grad_k_w, grad_v_w, entries.reshape(width, HD).astype(BF16)]
     near_c = qkv_c + HD
-    own_grad = own_rows(grad_attn)
+    beside = lambda v: v.transpose(1, 0, 2).reshape(r_in, -1)
     by_rows = lambda v: lax.dynamic_index_in_dim(v.reshape(2, r_in, -1), c, 0, False)
 
     def columns(sums):
@@ -994,35 +1129,39 @@
         return by_core(c, by_rows(sums), sibling(other)).astype(F32)
 
     if tall:
-        sums, near_sums, input_grad = reduce(grads, near_c, part_all, x_own, own_grad, gain_attn)
-        qkv_own = by_core(c, by_rows(sums[:, :near_c]), near_sums).astype(F32)
+        grad_q, grad_k, grad_v, gain_own, sum_out, input_grad = reduce(
+            grads, out_w, out_recv, part_all, x_all, grad_attn, gain_attn
+        )
     else:
-        sums = jnp.concatenate([reduced(g) for g in grads], axis=1)
-        qkv_own = columns(sums[:, :near_c])
+        qkv_own = columns(over_ctx(over_dp(jnp.concatenate(grads, axis=1))))
+        out_mine = lax.dynamic_index_in_dim(out_w, c, 1, False)
+        sum_out = over_ctx(over_dp(by_core(c, out_mine, out_recv).reshape(chips * r_out, width))).astype(F32)
+        grad_q = beside(qkv_own[:, :, :q_c])
+        grad_k = beside(qkv_own[:, :, q_c : q_c + kv_c])
+        grad_v = beside(qkv_own[:, :, q_c + kv_c : qkv_c])
+        gain_own = jnp.sum(qkv_own[:, :, qkv_c:], axis=0)
         grad_hidden = lax.psum_scatter(
             part_all, "ctx", scatter_dimension=0, tiled=True, axis_index_groups=halves
         ).astype(F32)
         back, _terms = norm_back(x_own.astype(F32), gain_attn, grad_hidden)
-        input_grad = returned((own_grad.astype(F32) + back).astype(BF16))
-    sum_out = sums[:, near_c:]
-    gain_own = jnp.sum(qkv_own[:, :, qkv_c : qkv_c + 4], axis=0)
+        input_grad = returned((own_rows(grad_attn).astype(F32) + back).astype(BF16))
+    gain_row, r_head = gain_own[0], q_gain.shape[0]
     gu_own = columns(sum_gu).reshape(2, r_in, ff_c // FF_TILE, 2, FF_TILE)
-    beside = lambda v: v.transpose(1, 0, 2).reshape(r_in, -1)
     ff_back = lambda v: v.reshape(2, r_in, chips, r_down).transpose(1, 2, 0, 3).reshape(r_in, ff)
     return (
         output,
         input_grad,
-        beside(qkv_own[:, :, :q_c]),
-        beside(qkv_own[:, :, q_c : q_c + kv_c]),
-        beside(qkv_own[:, :, q_c + kv_c : qkv_c]),
-        sum_out.astype(F32),
+        grad_q,
+        grad_k,
+        grad_v,
+        sum_out,
         ff_back(gu_own[:, :, :, 0]),
         ff_back(gu_own[:, :, :, 1]),
         sum_down.astype(F32),
-        gain_own[:, 0],
-        gain_own[:, 1],
-        gain_own[::apart, 2],
-        gain_own[::apart, 3],
+        gain_row[:r_in],
+        gain_row[r_in : 2 * r_in],
+        gain_row[2 * r_in : 2 * r_in + r_head],
+        gain_row[2 * r_in + r_head : 2 * r_in + 2 * r_head],
     )
 
 

time: 531 us -> 503 us (0.947)
  local copies, waits for them, and re-layouts: 48.1 us -> 35.8 us
  other arithmetic: 18.5 us -> 7.81 us
  waiting for transfers between devices: 30 us -> 23 us
    reduce_scatter x4 -> x3, waiting for transfers between devices: 14.4 us -> 3.05 us  [the longest x2 3.05 us: layer(): lax.psum_scatter(grad, 'dp', scatter_dimension=0, tiled=True)]
    dynamic_slice x6 -> x1, local copies, waits for them, and re-layouts: 11.6 us -> 1.76 us  [layer(): w_out_c = lax.dynamic_slice_in_dim(out_all, c * q_c, q_c, 0)]
    pallas_call x1, Pallas kernels: 121 us -> 130 us  [gather(): pl.pallas_call(gather_kernel, out_shape=[jax.ShapeDtypeStruct((4, 4, rows...]
    unnamed x86 -> x75, local copies, waits for them, and re-layouts: 10.4 us -> 13.7 us
  transfers between devices with their start and end apart: 12 -> 10, of which waited for: 3 -> 4; matrix products, arithmetic and copies ran while one was open for 17% -> 11% of each run, Pallas kernels for 41% -> 42%
where the time goes in v3:
time: 503 us; the launch traced here: 498 us
  Pallas kernels  361 us (72%)
  matrix products  52.2 us (10%)
  local copies, waits for them, and re-layouts  35.8 us (7%)
  waiting for transfers between devices  23 us (5%)
  between operations  14.8 us (3%)
  other arithmetic  7.81 us (2%)
    pallas_call x1, Pallas kernels, gather(): pl.pallas_call(gather_kernel, out_shape=[jax.ShapeDtypeStruct((4, 4, rows...  130 us
    pallas_call x1, Pallas kernels, reduce(): pl.pallas_call(functools.partial(reduce_kernel, len(grads)), out_shape=[*...  84.4 us
    pallas_call x1, Pallas kernels, attend_back(): pl.pallas_call(functools.partial(attend_back_kernel, span), out_shape=[ja...  60.3 us
    dot_general x9, matrix products, dot(): return lax.dot_general(a, b, (dims, ((), ())), preferred_element_type=out)  52.2 us
    pallas_call x1, Pallas kernels, attend(): pl.pallas_call(functools.partial(attend_kernel, span), out_shape=[jax.Sha...  27.2 us
    pallas_call x1, Pallas kernels, feed(): pl.pallas_call(feed_kernel, out_shape=[jax.ShapeDtypeStruct((rows, width)...  21.1 us
    all_gather x1, waiting for transfers between devices, layer(): out_all = lax.all_gather(w_out, axes, axis=0, tiled=True)  15.9 us
    pallas_call x1, Pallas kernels, project_back(): pl.pallas_call(functools.partial(project_back_kernel, own), out_shape=[ja...  15 us
  transfers between devices with their start and end apart: 10, of which 4 were waited for; matrix products, arithmetic and copies ran while one was open for 11% of the time, Pallas kernels for 42%

profile of v3, /device:TPU:0, one launch (start us, length us, event | category | flops | bytes accessed | tf_op | source)
XLA Modules:
  0.0 498.5 jit_solution(11008435345366725953)
XLA Ops:
  12.0 129.7 %gather.7 = (bf16[4,4,64,5248]{3,2,1,0:T(8,128)(2,1)}, bf16[4,4,96,1024]{3,2,1,0:T(8,128)(2,1)}, bf16[4,2,256,1024]{3,2,1,0:T(8,128)(2,1)}, bf16[2,2,256,1024]{3,2,1,0:T(8,128)(2,1)S(1)}) custom-call(bf16[2,32,5248]{2,1,0:T(8,128)(2,1)S(1)} %pad_maximum_fusion.1.pk_ref, bf16[96,1024]{1,0:T(8,128)(2,1)S(1)} %copy-done.10, ...), custom_call_target="tpu_custom_call" | custom-call | bytes 300000000 | tf_op jit(solution)/shard_map/gather/pallas_call | solution.py:675
  141.7 1.3 copy-done.2
  145.9 14.4 %project.1 = (bf16[2048,1024]{1,0:T(8,128)(2,1)}, bf16[1024,1024]{1,0:T(8,128)(2,1)S(1)}, bf16[2048,1024]{1,0:T(8,128)(2,1)}) custom-call(s32[1]{0:T(128)} %bitcast.chip_ref, bf16[2048,1024]{1,0:T(8,128)(2,1)} %bitcast.119, f32[1,1024]{1,0:T(1,128)S(1)} %bitcast.103, bf16[1024,5248]{1,0:T(8,128)(2,1)} %bitcast.112, bf16[1024,5248]{1,0:T(8,128)(2,1)} %bitcast.113), custom_call_target="tpu_custom_call" | custom-call | tf_op jit(solution)/shard_map/project/pallas_call | solution.py:350
  161.9 27.2 %attend.1 = (bf16[1024,1024]{1,0:T(8,128)(2,1)S(1)}, f32[4,8,1,256]{3,2,1,0:T(1,128)S(1)}) custom-call(s32[8]{0:T(128)S(1)} %dynamic_slice.40.ids_ref, s32[16]{0:T(128)S(1)} %select_reduce_fusion.order_ref, bf16[1024,1024]{1,0:T(8,128)(2,1)} %copy-done.11, bf16[2048,1024]{1,0:T(8,128)(2,1)} %get-tuple-element.58.k_ref.v_ref, ...), custom_call_target="tpu_custom_call" | custom-call | flops 8589934592 | bytes 8388608 | tf_op jit(solution)/shard_map/attend/pallas_call | solution.py:165
  189.1 15.9 %all-gather.2.cloned.1.call-done = bf16[2048,1024]{1,0:T(8,128)(2,1)} async-done(((bf16[64,1024]{1,0:T(8,128)(2,1)}), bf16[2048,1024]{1,0:T(8,128)(2,1)}) %all-gather.2.cloned.1.call-update) | async-done | bytes 4194320 | tf_op jit(solution)/shard_map/all_gather | solution.py:1036
  205.0 1.8 constant_dynamic-slice_fusion.1.wo_ref
  206.8 2.3 fusion.18.p0_ref
  209.4 3.9 collective-permute-done.p1_ref
  213.3 1.4 copy-done.22
  214.7 21.1 %feed.1 = (f32[1024,1024]{1,0:T(8,128)}, bf16[1024,1024]{1,0:T(8,128)(2,1)S(1)}, bf16[1024,1536]{1,0:T(8,128)(2,1)}, bf16[1024,3072]{1,0:T(8,128)(2,1)}) custom-call(s32[1]{0:T(128)} %bitcast.chip_ref, bf16[2048,1024]{1,0:T(8,128)(2,1)} %bitcast.120, bf16[1024,1024]{1,0:T(8,128)(2,1)S(1)} %fusion.18.p0_ref, bf16[1024,1024]{1,0:T(8,128)(2,1)} %copy-done.22, ...), custom_call_target="tpu_custom_call" | custom-call | tf_op jit(solution)/shard_map/feed/pallas_call | solution.py:463
  235.9 6.8 %fusion.22 = bf16[1536,1024]{1,0:T(8,128)(2,1)} fusion(bf16[1024,1536]{1,0:T(8,128)(2,1)} %get-tuple-element.64, bf16[1024,1024]{1,0:T(8,128)(2,1)S(1)} %bitcast.97), kind=kOutput, calls=%fused_computation.69 | convolution fusion | flops 3221225472 | bytes 8388608 | tf_op jit(solution)/shard_map/dot_general | solution.py:52
  243.0 11.4 %fusion.21 = bf16[1024,3072]{1,0:T(8,128)(2,1)} fusion(bf16[1024,1024]{1,0:T(8,128)(2,1)S(1)} %get-tuple-element.75, bf16[1024,3072]{1,0:T(8,128)(2,1)} %get-tuple-element.65), kind=kOutput, calls=%fused_computation.68 | convolution fusion | flops 6442450944 | bytes 14680064 | tf_op jit(solution)/shard_map/dot_general | solution.py:52
  254.5 12.0 %fusion.s0_ref = bf16[1024,1024]{1,0:T(8,128)(2,1)} fusion(bf16[1024,3072]{1,0:T(8,128)(2,1)} %get-tuple-element.65, bf16[1024,5248]{1,0:T(8,128)(2,1)} %bitcast.115), kind=kOutput, calls=%fused_computation.1 | convolution fusion | flops 6442450944 | bytes 14680064 | tf_op jit(solution)/shard_map/dot_general | solution.py:52
  266.8 6.3 %fusion.19 = bf16[2,512,1024]{2,1,0:T(8,128)(2,1)S(1)} fusion(bf16[2,512,1536]{2,1,0:T(8,128)(2,1)} %bitcast.146, bf16[1536,1024,1]{1,0,2:T(8,128)(2,1)} %bitcast.128), kind=kOutput, calls=%fused_computation.66 | convolution fusion | flops 3221225472 | bytes 8388608 | tf_op jit(solution)/shard_map/dot_general | solution.py:52
  274.4 8.9 %middle_back.1 = (bf16[1024,1024]{1,0:T(8,128)(2,1)S(1)}, bf16[1024,1024]{1,0:T(8,128)(2,1)S(1)}, f32[1,1024]{1,0:T(1,128)S(1)}) custom-call(f32[1024,1024]{1,0:T(8,128)} %get-tuple-element.63.mid_ref, bf16[1024,1024]{1,0:T(8,128)(2,1)} %fusion.s0_ref, bf16[1024,1024]{1,0:T(8,128)(2,1)} %collective-permute-done.2.s1_ref, bf16[1024,1024]{1,0:T(8,128)(2,1)} %bitcast.96, ...), custom_call_target="tpu_custom_call" | custom-call | tf_op jit(solution)/shard_map/middle_back/pallas_call | solution.py:512
  283.3 2.4 fusion.20
  285.8 1.4 copy-done.20
  288.4 2.5 fusion.3
  291.1 1.6 collective-permute-start.4
  292.7 60.3 %attend_back.1 = (bf16[1024,1024]{1,0:T(8,128)(2,1)S(1)}, bf16[2048,512]{1,0:T(8,128)(2,1)}, bf16[2048,512]{1,0:T(8,128)(2,1)}, f32[1,128]{1,0:T(1,128)S(1)}, f32[1,128]{1,0:T(1,128)S(1)}) custom-call(s32[8]{0:T(128)S(1)} %dynamic_slice.40.ids_ref, s32[16]{0:T(128)S(1)} %select_reduce_fusion.order_ref, bf16[1024,1024]{1,0:T(8,128)(2,1)} %copy-done.11, ...), custom_call_target="tpu_custom_call" | custom-call | flops 10737418240 | bytes 16777216 | tf_op jit(solution)/shard_map/attend_back/pallas_call | solution.py:291
  353.0 1.3 copy-done.6
  355.5 3.0 reduce-scatter.4.cloned.1.call-done
  360.8 1.5 pad_maximum_fusion
  363.9 1.6 copy-done.7
  365.5 15.0 %project_back.1 = (bf16[2048,1024]{1,0:T(8,128)(2,1)}, f32[1,1024]{1,0:T(1,128)S(1)}) custom-call(s32[1]{0:T(128)} %bitcast.chip_ref, bf16[1024,1024]{1,0:T(8,128)(2,1)S(1)} %copy-done.7, bf16[2048,512]{1,0:T(8,128)(2,1)S(1)} %copy-done.5, bf16[2048,512]{1,0:T(8,128)(2,1)} %get-tuple-element.80.dv_ref, bf16[2048,1024]{1,0:T(8,128)(2,1)} %bitcast.121, ...), custom_call_target="tpu_custom_call" | custom-call | tf_op jit(solution)/shard_map/project_back/pallas_call | solution.py:401
  380.8 6.2 %fusion.4 = bf16[1024,1024]{1,0:T(8,128)(2,1)} fusion(bf16[1024,1024]{1,0:T(8,128)(2,1)} %copy-done.6, bf16[2048,1024]{1,0:T(8,128)(2,1)} %get-tuple-element.77, s32[]{:T(128)S(6)} %select_n.111), kind=kOutput, calls=%fused_computation.7 | convolution fusion | flops 2147483648 | bytes 6291460 | tf_op jit(solution)/shard_map/dot_general | solution.py:52
  387.0 2.4 fusion.24
  389.4 2.4 fusion.23
  391.7 84.4 %reduce.27 = (f32[32,2048]{1,0:T(8,128)S(1)}, f32[32,1024]{1,0:T(8,128)S(1)}, f32[32,1024]{1,0:T(8,128)S(1)}, f32[32,128]{1,0:T(8,128)S(1)}, f32[64,1024]{1,0:T(8,128)S(1)}, /*index=5*/bf16[2,256,1024]{2,1,0:T(8,128)(2,1)S(1)}) custom-call(bf16[2,2,4,64,1024]{4,3,2,1,0:T(8,128)(2,1)} %bitcast.129, bf16[2,2,4,64,512]{4,3,2,1,0:T(8,128)(2,1)S(1)} %bitcast.102, ...), custom_call_target="tpu_custom_call" | custom-call | bytes 300000000 | tf_op jit(solution)/shard_map/reduce/pallas_call | solution.py:912
  481.3 2.3 slice_reduce_fusion.2
  484.4 1.4 reshape.195
  486.6 1.4 reshape.196
  (158 shorter events, 28.1 us)
Async XLA Ops:
  7.2 137.3 %copy-start = (s32[2,2048]{1,0:T(2,128)S(1)}, s32[2,2048]{1,0:T(2,128)}, u32[]{:S(2)}) copy-start(s32[2,2048]{1,0:T(2,128)} %param.18) | copy-start | bytes 49156
  7.2 1.8 copy-start.24
  7.2 197.8 %all-gather.2.cloned.1.call-start = ((), (), s32[]{:S(2)}) async-start(), calls=%async_computation.3 | async-start | bytes 4325376 | tf_op jit(solution)/shard_map/all_gather | solution.py:1036
  9.0 1.7 copy-start.28
  9.1 1.8 copy-start.29
  9.4 2.0 copy-start.26
  9.4 2.0 copy-start.27
  12.0 132.4 %copy-start.33 = (s32[2,16]{1,0:T(2,128)S(1)}, s32[2,16]{1,0:T(2,128)}, u32[]{:S(2)}) copy-start(s32[2,16]{1,0:T(2,128)} %constant.112.clone) | copy-start | bytes 388
  143.1 212.4 %reduce-scatter.6.cloned.1.call-start = ((), (), s32[]{:S(2)}) async-start(), calls=%async_computation.5 | async-start | bytes 3932160 | tf_op jit(solution)/shard_map/reduce_scatter | solution.py:1087
  145.9 16.0 %copy-start.13 = (f32[2048,128]{1,0:T(8,128)S(1)}, f32[2048,128]{1,0:T(8,128)}, u32[]{:S(2)}) copy-start(f32[2048,128]{1,0:T(8,128)} %constant.113.clone.cos_ref) | copy-start | bytes 3145732
  145.9 16.0 %copy-start.15 = (f32[2048,128]{1,0:T(8,128)S(1)}, f32[2048,128]{1,0:T(8,128)}, u32[]{:S(2)}) copy-start(f32[2048,128]{1,0:T(8,128)} %constant.114.clone.sin_ref) | copy-start | bytes 3145732
  189.1 17.6 %copy-start.17 = (bf16[1024,1024]{1,0:T(8,128)(2,1)}, bf16[1024,1024]{1,0:T(8,128)(2,1)S(1)}, u32[]{:S(2)}) copy-start(bf16[1024,1024]{1,0:T(8,128)(2,1)S(1)} %get-tuple-element.59.o_ref) | copy-start | bytes 6291460
  206.7 2.4 copy-start.19
  209.1 4.2 collective-permute-start
  214.7 21.1 %copy-start.3 = (bf16[2,2,256,1024]{3,2,1,0:T(8,128)(2,1)S(1)}, bf16[2,2,256,1024]{3,2,1,0:T(8,128)(2,1)}, u32[]{:S(2)}) copy-start(bf16[2,2,256,1024]{3,2,1,0:T(8,128)(2,1)} %copy-done.2) | copy-start | bytes 6291460
  242.7 115.8 %reduce-scatter.4.cloned.1.call-start = ((), (), s32[]{:S(2)}) async-start(), calls=%async_computation.4 | async-start | bytes 7864320 | tf_op jit(solution)/shard_map/reduce_scatter | solution.py:1087
  254.5 222.9 %reduce-scatter.8.cloned.1.call-start = ((), (), s32[]{:S(2)}) async-start(), calls=%async_computation.6 | async-start | bytes 2949120 | tf_op jit(solution)/shard_map/reduce_scatter | solution.py:1088
  266.5 7.9 %collective-permute-start.2 = (bf16[1024,1024]{1,0:T(8,128)(2,1)}, bf16[1024,1024]{1,0:T(8,128)(2,1)}, u32[]{:S(2)}, u32[]{:S(2)}) collective-permute-start(bf16[1024,1024]{1,0:T(8,128)(2,1)} %fusion.s0_ref), channel_id=1, source_target_pairs={{0,1},{1,0},{2,3},{3,2},{4,5},{5,4},{6,7},{7,6},{8,9},{9,8},{10,11... | collective-permute-start | bytes 6291464 | tf_op jit(solution)/shard_map/ppermute | solution.py:984
  274.2 14.2 %collective-permute-start.1 = (bf16[512,1024]{1,0:T(8,128)(2,1)}, bf16[512,1024]{1,0:T(8,128)(2,1)}, u32[]{:S(2)}, u32[]{:S(2)}) collective-permute-start(bf16[512,1024]{1,0:T(8,128)(2,1)} %dynamic-slice_bitcast_fusion.1), channel_id=1, source_target_pairs={{0,1},{1,0},{2,3},{3,2},{4,5},{5,4},{6,7},{7,6},{8,9},{9,8},{10,11... | collective-permute-start | bytes 3145736 | tf_op jit(solution)/shard_map/ppermute | solution.py:984
  274.4 8.9 %copy-start.18 = (bf16[1024,1024]{1,0:T(8,128)(2,1)S(1)}, bf16[1024,1024]{1,0:T(8,128)(2,1)}, u32[]{:S(2)}) copy-start(bf16[1024,1024]{1,0:T(8,128)(2,1)} %copy-done.17) | copy-start | bytes 6291460
  283.3 2.4 copy-start.4
  283.3 2.4 copy-start.12
  288.1 2.9 collective-permute-start.3
  290.8 1.8 copy-start.14
  290.9 1.8 copy-start.16
  291.1 63.3 %collective-permute-start.4 = (bf16[256,1024]{1,0:T(8,128)(2,1)S(1)}, bf16[256,1024]{1,0:T(8,128)(2,1)S(1)}, u32[]{:S(2)}, u32[]{:S(2)}) collective-permute-start(bf16[256,1024]{1,0:T(8,128)(2,1)S(1)} %get-tuple-element.102), channel_id=1, source_target_pairs={{0,4},{1,5},{2,6},{3,7},{4,0},{5,1},{6,2},{7,3},{8,12},{9,13},{10,... | collective-permute-start | bytes 1572872 | tf_op jit(solution)/shard_map/ppermute | solution.py:985
  358.5 2.2 copy-start.23
  380.8 6.2 %copy-start.21 = (bf16[2048,512]{1,0:T(8,128)(2,1)S(1)}, bf16[2048,512]{1,0:T(8,128)(2,1)}, u32[]{:S(2)}) copy-start(bf16[2048,512]{1,0:T(8,128)(2,1)} %get-tuple-element.80.dv_ref) | copy-start | bytes 6291460
  380.8 6.2 %copy-start.30 = (bf16[2048,1024]{1,0:T(8,128)(2,1)S(1)}, bf16[2048,1024]{1,0:T(8,128)(2,1)}, u32[]{:S(2)}) copy-start(bf16[2048,1024]{1,0:T(8,128)(2,1)} %get-tuple-element.77) | copy-start | bytes 12582916
  477.3 2.5 slice-start
  478.4 2.2 collective-permute-start.5
  486.2 5.5 %copy-start.1 = (s32[2,2048]{1,0:T(2,128)S(1)}, s32[2,2048]{1,0:T(2,128)}, u32[]{:S(2)}) copy-start(s32[2,2048]{1,0:T(2,128)} %param.18) | copy-start | bytes 49156
  (13 other events, 18.7 us)
Sparse Core Ops, SparseCore 0:
  143.2 61.7 all-gather.1
  242.8 42.4 reduce-scatter.5
  288.3 70.1 reduce-scatter.3
  362.4 55.1 reduce-scatter.7

commit v4 on v3

--- a/solution.py
+++ b/solution.py
@@ -17,9 +17,7 @@
 LOG2E = 1.4426950408889634
 KEY_TILE = 512
 ROW_TILE = 256
-FF_TILE = 512
-FWD_HEADS = 4
-BACK_HEADS = 4
+FF_TILE = 384
 VMEM_LIMIT = 48 * 1024 * 1024
 MESH = pl.DeviceIdType.MESH
 F32 = jnp.float32
@@ -112,45 +110,43 @@
     span, ids_ref, order_ref, q_ref, k_ref, v_ref, cos_ref, sin_ref, gq_ref, gk_ref,
     o_ref, lse_ref, ks_ref, vs_ref, acc_ref, sum_ref,
 ):
-    prepare_keys(span, order_ref, k_ref, v_ref, cos_ref, sin_ref, gk_ref, ks_ref, vs_ref)
+    @pl.when(pl.program_id(0) == 0)
+    def _():
+        prepare_keys(span, order_ref, k_ref, v_ref, cos_ref, sin_ref, gk_ref, ks_ref, vs_ref)
+
     m = GROUPS * span
-    heads = range(FWD_HEADS)
-
-    def block(j, _):
-        b = ids_ref[j]
-        rows = pl.ds(pl.multiple_of(j * span, span), span)
-        places = pl.ds(pl.multiple_of(b * span, span), span)
-        q2 = [query_block(q_ref, p, rows, places, cos_ref, sin_ref, gq_ref)[2] for p in heads]
-        acc_ref[...] = jnp.zeros_like(acc_ref)
-        sum_ref[...] = jnp.zeros_like(sum_ref)
-
-        def tile(t, masked):
-            keys = pl.ds(pl.multiple_of(t * KEY_TILE, KEY_TILE), KEY_TILE)
-            scores = [dot(q2[p], ks_ref[keys, lanes(p)], NT) for p in heads]
-            keep = seen(scores[0].shape, t, b, span, 1) if masked else None
-            for p in heads:
-                e = jnp.exp2(scores[p])
-                if masked:
-                    e = jnp.where(keep, e, 0.0)
-                part = e[:, 0:HD]
-                for i in range(1, KEY_TILE // HD):
-                    part = part + e[:, lanes(i)]
-                sum_ref[p] += part
-                acc_ref[p] += dot(e.astype(BF16), vs_ref[keys, lanes(p)], NN)
-
-        last = (b * span) // KEY_TILE
-        lax.fori_loop(0, last, lambda t, _: (tile(t, False), 0)[1], 0)
-        tile(last, True)
+    heads = range(k_ref.shape[1] // HD)
+    b = ids_ref[pl.program_id(0)]
+    rows = slice(None)
+    places = pl.ds(pl.multiple_of(b * span, span), span)
+    q2 = [query_block(q_ref, p, rows, places, cos_ref, sin_ref, gq_ref)[2] for p in heads]
+    acc_ref[...] = jnp.zeros_like(acc_ref)
+    sum_ref[...] = jnp.zeros_like(sum_ref)
+
+    def tile(t, masked):
+        keys = pl.ds(pl.multiple_of(t * KEY_TILE, KEY_TILE), KEY_TILE)
+        scores = [dot(q2[p], ks_ref[keys, lanes(p)], NT) for p in heads]
+        keep = seen(scores[0].shape, t, b, span, 1) if masked else None
         for p in heads:
-            total = jnp.sum(sum_ref[p], axis=-1, keepdims=True)
-            mixed = acc_ref[p] * (1.0 / total)
-            for g in range(GROUPS):
-                o_ref[rows, lanes(p * GROUPS + g)] = mixed[g * span : (g + 1) * span].astype(BF16)
-            wide = jnp.broadcast_to(jnp.log2(total), (m, HD))
-            lse_ref[p, j] = jnp.transpose(wide)[0:1, :]
-        return 0
-
-    lax.fori_loop(0, q_ref.shape[0] // span, block, 0)
+            e = jnp.exp2(scores[p])
+            if masked:
+                e = jnp.where(keep, e, 0.0)
+            part = e[:, 0:HD]
+            for i in range(1, KEY_TILE // HD):
+                part = part + e[:, lanes(i)]
+            sum_ref[p] += part
+            acc_ref[p] += dot(e.astype(BF16), vs_ref[keys, lanes(p)], NN)
+
+    last = (b * span) // KEY_TILE
+    lax.fori_loop(0, last, lambda t, _: (tile(t, False), 0)[1], 0)
+    tile(last, True)
+    for p in heads:
+        total = jnp.sum(sum_ref[p], axis=-1, keepdims=True)
+        mixed = acc_ref[p] * (1.0 / total)
+        for g in range(GROUPS):
+            o_ref[rows, lanes(p * GROUPS + g)] = mixed[g * span : (g + 1) * span].astype(BF16)
+        wide = jnp.broadcast_to(jnp.log2(total), (m, HD))
+        lse_ref[p, 0] = jnp.transpose(wide)[0:1, :]
 
 
 def attend(ids, order, q_raw, kv_raw, cosine, sine, gq, gk, span):
@@ -158,9 +154,9 @@
     seq = kv_raw.shape[0]
     heads = q_raw.shape[1] // (GROUPS * HD)
     blocks, m = rows // span, GROUPS * span
-    hp = FWD_HEADS
+    hp = heads
     whole = lambda k, ids, order: (0, 0)
-    per_query = pl.BlockSpec((rows, hp * GROUPS * HD), lambda k, ids, order: (0, k))
+    per_query = pl.BlockSpec((span, hp * GROUPS * HD), lambda j, ids, order: (j, 0))
     once = pl.Buffered(1)
     return pl.pallas_call(
         functools.partial(attend_kernel, span),
@@ -170,11 +166,11 @@
         ],
         grid_spec=pltpu.PrefetchScalarGridSpec(
             num_scalar_prefetch=2,
-            grid=(heads // hp,),
+            grid=(blocks,),
             in_specs=[
                 per_query,
-                pl.BlockSpec((seq, hp * HD), lambda k, ids, order: (0, k)),
-                pl.BlockSpec((seq, hp * HD), lambda k, ids, order: (0, heads // hp + k)),
+                pl.BlockSpec((seq, hp * HD), whole, pipeline_mode=once),
+                pl.BlockSpec((seq, hp * HD), lambda j, ids, order: (0, 1), pipeline_mode=once),
                 pl.BlockSpec((seq, HD), whole, pipeline_mode=once),
                 pl.BlockSpec((seq, HD), whole, pipeline_mode=once),
                 pl.BlockSpec((1, HD), whole),
@@ -182,7 +178,7 @@
             ],
             out_specs=[
                 per_query,
-                pl.BlockSpec((hp, blocks, 1, m), lambda k, ids, order: (k, 0, 0, 0)),
+                pl.BlockSpec((hp, 1, 1, m), lambda j, ids, order: (0, j, 0, 0)),
             ],
             scratch_shapes=[
                 pltpu.VMEM((seq, hp * HD), BF16),
@@ -205,61 +201,57 @@
     span, ids_ref, order_ref, q_ref, k_ref, v_ref, do_ref, o_ref, lse_ref, cos_ref, sin_ref, gq_ref, gk_ref,
     dq_ref, dk_ref, dv_ref, dgq_ref, dgk_ref, ks_ref, vs_ref, dka_ref, dva_ref, dqa_ref,
 ):
-    prepare_keys(span, order_ref, k_ref, v_ref, cos_ref, sin_ref, gk_ref, ks_ref, vs_ref)
-    dka_ref[...] = jnp.zeros_like(dka_ref)
-    dva_ref[...] = jnp.zeros_like(dva_ref)
-    heads = range(BACK_HEADS)
+    heads = range(k_ref.shape[1] // HD)
 
     @pl.when(pl.program_id(0) == 0)
     def _():
+        prepare_keys(span, order_ref, k_ref, v_ref, cos_ref, sin_ref, gk_ref, ks_ref, vs_ref)
+        dka_ref[...] = jnp.zeros_like(dka_ref)
+        dva_ref[...] = jnp.zeros_like(dva_ref)
         dgq_ref[...] = jnp.zeros_like(dgq_ref)
         dgk_ref[...] = jnp.zeros_like(dgk_ref)
 
-    def block(j, _):
-        b = ids_ref[j]
-        rows = pl.ds(pl.multiple_of(j * span, span), span)
-        places = pl.ds(pl.multiple_of(b * span, span), span)
-        q2, do2, delta, lse = [], [], [], []
+    b = ids_ref[pl.program_id(0)]
+    rows = slice(None)
+    places = pl.ds(pl.multiple_of(b * span, span), span)
+    q2, do2, delta, lse = [], [], [], []
+    for p in heads:
+        q2.append(query_block(q_ref, p, rows, places, cos_ref, sin_ref, gq_ref)[2])
+        pick = lambda ref: jnp.concatenate([ref[rows, lanes(p * GROUPS + g)] for g in range(GROUPS)], axis=0)
+        do2.append(pick(do_ref))
+        delta.append(
+            jnp.sum(jnp.transpose(do2[p].astype(F32) * pick(o_ref).astype(F32)), axis=0, keepdims=True)
+        )
+        lse.append(lse_ref[p, 0])
+    dqa_ref[...] = jnp.zeros_like(dqa_ref)
+
+    def tile(t, masked):
+        keys = pl.ds(pl.multiple_of(t * KEY_TILE, KEY_TILE), KEY_TILE)
+        kt = [ks_ref[keys, lanes(p)] for p in heads]
+        scores = [dot(kt[p], q2[p], NT) for p in heads]
+        slopes = [dot(vs_ref[keys, lanes(p)], do2[p], NT) for p in heads]
+        keep = seen(scores[0].shape, t, b, span, 0) if masked else None
         for p in heads:
-            q2.append(query_block(q_ref, p, rows, places, cos_ref, sin_ref, gq_ref)[2])
-            pick = lambda ref: jnp.concatenate([ref[rows, lanes(p * GROUPS + g)] for g in range(GROUPS)], axis=0)
-            do2.append(pick(do_ref))
-            delta.append(
-                jnp.sum(jnp.transpose(do2[p].astype(F32) * pick(o_ref).astype(F32)), axis=0, keepdims=True)
-            )
-            lse.append(lse_ref[p, j])
-        dqa_ref[...] = jnp.zeros_like(dqa_ref)
-
-        def tile(t, masked):
-            keys = pl.ds(pl.multiple_of(t * KEY_TILE, KEY_TILE), KEY_TILE)
-            kt = [ks_ref[keys, lanes(p)] for p in heads]
-            scores = [dot(kt[p], q2[p], NT) for p in heads]
-            slopes = [dot(vs_ref[keys, lanes(p)], do2[p], NT) for p in heads]
-            keep = seen(scores[0].shape, t, b, span, 0) if masked else None
-            for p in heads:
-                e = jnp.exp2(scores[p] - lse[p])
-                if masked:
-                    e = jnp.where(keep, e, 0.0)
-                ds = (e * (slopes[p] - delta[p])).astype(BF16)
-                dva_ref[keys, lanes(p)] += dot(e.astype(BF16), do2[p], NN)
-                dka_ref[keys, lanes(p)] += dot(ds, q2[p], NN)
-                dqa_ref[p] += dot(ds, kt[p], TN)
-
-        last = (b * span) // KEY_TILE
-        lax.fori_loop(0, last, lambda t, _: (tile(t, False), 0)[1], 0)
-        tile(last, True)
-        for p in heads:
-            units, scales, _q = query_block(q_ref, p, rows, places, cos_ref, sin_ref, gq_ref)
-            dq = dqa_ref[p] * HD**-0.5
-            for g in range(GROUPS):
-                grad = rope_back(dq[g * span : (g + 1) * span], cos_ref[places, :], sin_ref[places, :])
-                dgq_ref[...] += jnp.sum(grad * units[g], axis=0, keepdims=True)
-                u = grad * gq_ref[...]
-                back = scales[g] * (u - units[g] * row_mean(u * units[g]))
-                dq_ref[rows, lanes(p * GROUPS + g)] = back.astype(BF16)
-        return 0
-
-    lax.fori_loop(0, q_ref.shape[0] // span, block, 0)
+            e = jnp.exp2(scores[p] - lse[p])
+            if masked:
+                e = jnp.where(keep, e, 0.0)
+            ds = (e * (slopes[p] - delta[p])).astype(BF16)
+            dva_ref[keys, lanes(p)] += dot(e.astype(BF16), do2[p], NN)
+            dka_ref[keys, lanes(p)] += dot(ds, q2[p], NN)
+            dqa_ref[p] += dot(ds, kt[p], TN)
+
+    last = (b * span) // KEY_TILE
+    lax.fori_loop(0, last, lambda t, _: (tile(t, False), 0)[1], 0)
+    tile(last, True)
+    for p in heads:
+        units, scales, _q = query_block(q_ref, p, rows, places, cos_ref, sin_ref, gq_ref)
+        dq = dqa_ref[p] * HD**-0.5
+        for g in range(GROUPS):
+            grad = rope_back(dq[g * span : (g + 1) * span], cos_ref[places, :], sin_ref[places, :])
+            dgq_ref[...] += jnp.sum(grad * units[g], axis=0, keepdims=True)
+            u = grad * gq_ref[...]
+            back = scales[g] * (u - units[g] * row_mean(u * units[g]))
+            dq_ref[rows, lanes(p * GROUPS + g)] = back.astype(BF16)
 
     def finish(i, _):
         rows = pl.ds(pl.multiple_of(i * span, span), span)
@@ -274,7 +266,9 @@
         dv_ref[source, :] = dva_ref[rows, :].astype(BF16)
         return 0
 
-    lax.fori_loop(0, k_ref.shape[0] // span, finish, 0)
+    @pl.when(pl.program_id(0) == pl.num_programs(0) - 1)
+    def _():
+        lax.fori_loop(0, k_ref.shape[0] // span, finish, 0)
 
 
 def attend_back(ids, order, q_raw, kv_raw, grad_mixed, mixed, lse, cosine, sine, gq, gk, span):
@@ -282,12 +276,12 @@
     seq = kv_raw.shape[0]
     heads = q_raw.shape[1] // (GROUPS * HD)
     blocks, m = rows // span, GROUPS * span
-    hp = BACK_HEADS
+    hp = heads
     whole = lambda k, ids, order: (0, 0)
-    per_query = pl.BlockSpec((rows, hp * GROUPS * HD), lambda k, ids, order: (0, k))
-    per_key = pl.BlockSpec((seq, hp * HD), lambda k, ids, order: (0, k))
+    once = pl.Buffered(1)
+    per_query = pl.BlockSpec((span, hp * GROUPS * HD), lambda j, ids, order: (j, 0))
+    per_key = pl.BlockSpec((seq, hp * HD), whole, pipeline_mode=once)
     gain = pl.BlockSpec((1, HD), whole)
-    once = pl.Buffered(1)
     return pl.pallas_call(
         functools.partial(attend_back_kernel, span),
         out_shape=[
@@ -299,20 +293,20 @@
         ],
         grid_spec=pltpu.PrefetchScalarGridSpec(
             num_scalar_prefetch=2,
-            grid=(heads // hp,),
+            grid=(blocks,),
             in_specs=[
                 per_query,
                 per_key,
-                pl.BlockSpec((seq, hp * HD), lambda k, ids, order: (0, heads // hp + k)),
+                pl.BlockSpec((seq, hp * HD), lambda j, ids, order: (0, 1), pipeline_mode=once),
                 per_query,
                 per_query,
-                pl.BlockSpec((hp, blocks, 1, m), lambda k, ids, order: (k, 0, 0, 0)),
+                pl.BlockSpec((hp, 1, 1, m), lambda j, ids, order: (0, j, 0, 0)),
                 pl.BlockSpec((seq, HD), whole, pipeline_mode=once),
                 pl.BlockSpec((seq, HD), whole, pipeline_mode=once),
                 gain,
                 gain,
             ],
-            out_specs=[per_query, per_key, per_key, gain, gain],
+            out_specs=[per_query] + [pl.BlockSpec((seq, hp * HD), whole)] * 2 + [gain, gain],
             scratch_shapes=[
                 pltpu.VMEM((seq, hp * HD), BF16),
                 pltpu.VMEM((seq, hp * HD), BF16),
@@ -341,7 +335,7 @@
         q_ref[...] = dot(hidden, wq_ref[...], NN).astype(BF16)
 
 
-def project(chip, x_all, gain, w_all, chip_rows):
+def project(chip, x_all, gain, w_all, first, chip_rows):
     seq, width = x_all.shape
     size = min(ROW_TILE, chip_rows)
     own, tiles = chip_rows // size, seq // size
@@ -360,8 +354,8 @@
             in_specs=[
                 pl.BlockSpec((size, width), at),
                 pl.BlockSpec((1, width), lambda i, chip: (0, 0)),
-                weight(0),
-                weight(1),
+                weight(first // width),
+                weight(first // width + 1),
             ],
             out_specs=[
                 pl.BlockSpec((size, width), at),
@@ -391,7 +385,7 @@
     g_ref[...] += jnp.sum(part * normed(x_ref[...].astype(F32), 1.0), axis=0, keepdims=True)
 
 
-def project_back(chip, dq, dk, dv, x_all, w_all):
+def project_back(chip, dq, dk, dv, x_all, w_all, first):
     seq, width = x_all.shape
     chip_rows, kv = dq.shape[0], dk.shape[1]
     size = min(ROW_TILE, chip_rows)
@@ -409,9 +403,9 @@
                 pl.BlockSpec((size, kv), at),
                 pl.BlockSpec((size, kv), at),
                 pl.BlockSpec((size, width), at),
-                weight(width, 0),
-                weight(kv, width // kv),
-                weight(kv, width // kv + 1),
+                weight(width, first // width),
+                weight(kv, (first + width) // kv),
+                weight(kv, (first + width) // kv + 1),
             ],
             out_specs=[
                 pl.BlockSpec((size, width), at),
@@ -424,7 +418,7 @@
     )(chip, dq, dk, dv, x_all, w_all, w_all, w_all)
 
 
-def feed_kernel(chip_ref, x_ref, p0_ref, p1_ref, gain_ref, go_ref, w_ref, d_ref, mid_ref, sec_ref, act_ref, gg_ref):
+def feed_kernel(chip_ref, x_ref, p0_ref, p1_ref, gain_ref, w_ref, mid_ref, sec_ref, act_ref, gu_ref):
     count = x_ref.shape[0]
     size = min(ROW_TILE, count)
     tile = lambda i: pl.ds(pl.multiple_of(i * size, size), size)
@@ -443,21 +437,16 @@
     def body(i, _):
         rows = tile(i)
         both = dot(sec_ref[rows, :], w_ref[...], NN)
-        grad = dot(go_ref[rows, :], d_ref[...], NT)
         gate, up = both[:, :FF_TILE], both[:, FF_TILE:]
-        sig = jax.nn.sigmoid(gate)
-        silu = gate * sig
-        act_ref[rows, :] = (silu * up).astype(BF16)
-        gg_ref[rows, :FF_TILE] = (grad * up * sig * (1.0 + gate * (1.0 - sig))).astype(BF16)
-        gg_ref[rows, FF_TILE:] = (grad * silu).astype(BF16)
+        act_ref[rows, :] = (gate * jax.nn.sigmoid(gate) * up).astype(BF16)
+        gu_ref[rows, :] = both.astype(BF16)
         return 0
 
     lax.fori_loop(0, count // size, body, 0)
 
 
-def feed(chip, x_all, p0, p1, gain, go, w_all, at, w_down):
-    rows, width = go.shape
-    ff = w_down.shape[0]
+def feed(chip, x_all, p0, p1, gain, w_all, ff):
+    rows, width = p0.shape
     once = pl.Buffered(1)
     whole = lambda: pl.BlockSpec((rows, width), lambda j, chip: (0, 0), pipeline_mode=once)
     return pl.pallas_call(
@@ -475,9 +464,7 @@
                 pl.BlockSpec((rows, width), lambda j, chip: (chip[0], 0), pipeline_mode=once),
                 whole(), whole(),
                 pl.BlockSpec((1, width), lambda j, chip: (0, 0)),
-                whole(),
-                pl.BlockSpec((width, 2 * FF_TILE), lambda j, chip: (0, at // (2 * FF_TILE) + j)),
-                pl.BlockSpec((FF_TILE, width), lambda j, chip: (j, 0)),
+                pl.BlockSpec((width, 2 * FF_TILE), lambda j, chip: (0, j)),
             ],
             out_specs=[
                 pl.BlockSpec((rows, width), lambda j, chip: (0, 0)),
@@ -488,7 +475,51 @@
         ),
         compiler_params=pltpu.CompilerParams(vmem_limit_bytes=VMEM_LIMIT),
         name="feed",
-    )(chip, x_all, p0, p1, gain, go, w_all, w_down)
+    )(chip, x_all, p0, p1, gain, w_all)
+
+
+def feed_back_kernel(core_ref, gu_ref, go_ref, wd_ref, gg_ref, d_ref):
+    count = gu_ref.shape[0]
+    size = min(ROW_TILE, count)
+    unit = wd_ref.shape[2]
+    for u in range(FF_TILE // unit):
+        d_ref[u * unit : (u + 1) * unit, :] = wd_ref[u, 0]
+
+    def body(i, _):
+        rows = pl.ds(pl.multiple_of(i * size, size), size)
+        grad = dot(go_ref[rows, :], d_ref[...], NT)
+        gate, up = gu_ref[rows, :FF_TILE].astype(F32), gu_ref[rows, FF_TILE:].astype(F32)
+        sig = jax.nn.sigmoid(gate)
+        gg_ref[rows, :FF_TILE] = (grad * up * sig * (1.0 + gate * (1.0 - sig))).astype(BF16)
+        gg_ref[rows, FF_TILE:] = (grad * (gate * sig)).astype(BF16)
+        return 0
+
+    lax.fori_loop(0, count // size, body, 0)
+
+
+def feed_back(core, gate_up, go, w_down):
+    rows, width = go.shape
+    chips, _, unit, _ = w_down.shape
+    ff = chips * unit
+    return pl.pallas_call(
+        feed_back_kernel,
+        out_shape=[jax.ShapeDtypeStruct((rows, 2 * ff), BF16), jax.ShapeDtypeStruct((ff, width), BF16)],
+        grid_spec=pltpu.PrefetchScalarGridSpec(
+            num_scalar_prefetch=1,
+            grid=(ff // FF_TILE,),
+            in_specs=[
+                pl.BlockSpec((rows, 2 * FF_TILE), lambda j, core: (0, j)),
+                pl.BlockSpec((rows, width), lambda j, core: (0, 0), pipeline_mode=pl.Buffered(1)),
+                pl.BlockSpec((FF_TILE // unit, 1, unit, width), lambda j, core: (j, core[0], 0, 0)),
+            ],
+            out_specs=[
+                pl.BlockSpec((rows, 2 * FF_TILE), lambda j, core: (0, j)),
+                pl.BlockSpec((FF_TILE, width), lambda j, core: (j, 0)),
+            ],
+        ),
+        compiler_params=pltpu.CompilerParams(vmem_limit_bytes=VMEM_LIMIT),
+        name="feed_back",
+    )(core, gate_up, go, w_down)
 
 
 def middle_back_kernel(mid_ref, s0_ref, s1_ref, go_ref, gain_ref, wo_ref, ga_ref, gm_ref, g_ref):
@@ -556,9 +587,7 @@
     return send, made
 
 
-def gather_kernel(
-    pk_ref, wd_ref, tok_ref, go_ref, w_ref, d_ref, x_ref, g_ref, send_sem, recv_sem, local_sem
-):
+def gather_kernel(pk_ref, wo_ref, tok_ref, go_ref, w_ref, x_ref, g_ref, send_sem, recv_sem, local_sem):
     dp, ctx, to = peers()
     c, z = ctx % 2, ctx // 2
     which, me = ctx // 4, ctx % 4
@@ -566,12 +595,12 @@
     greet([to(0, 1), to(0, 2), to(0, 4), to(0, 6), to(1, 0), to(2, 0)])
     send, made = sender(send_sem, recv_sem)
     sib, nbr, far, across, xn, yn = to(0, 1), to(0, 2), to(0, 4), to(0, 6), to(1, 0), to(2, 0)
-    rows = pk_ref.shape[1]
-
-    place = w_ref.at[dp, z, pl.ds(c * rows, rows)]
+    rows, cols = pk_ref.shape[1:]
+
+    place = w_ref.at[dp, z, pl.ds(c * rows, rows), pl.ds(0, cols)]
     local = [
         pltpu.make_async_copy(pk_ref.at[c], place, local_sem.at[0]),
-        pltpu.make_async_copy(wd_ref, d_ref.at[dp, z], local_sem.at[1]),
+        pltpu.make_async_copy(wo_ref, w_ref.at[dp, z, :, pl.ds(cols, wo_ref.shape[1])], local_sem.at[1]),
         pltpu.make_async_copy(tok_ref.at[which], x_ref.at[me, 0], local_sem.at[2]),
         pltpu.make_async_copy(go_ref.at[which], g_ref.at[c, 0], local_sem.at[3]),
     ]
@@ -583,26 +612,22 @@
     cross.wait_recv()
     done = []
 
-    refs = [w_ref, d_ref]
-
-    def half(ref, h, q, zz):
-        size = ref.shape[2] // 2
-        return ref.at[q, zz, pl.ds(h * size, size)]
+    def half(h, q, zz):
+        return w_ref.at[q, zz, pl.ds(h * rows, rows)]
 
     first = []
 
     def spread(zz):
-        for ref in refs:
-            low, high = half(ref, 0, dp, zz), half(ref, 1, dp, zz)
-            first.append((send(low, low, yn), low, half(ref, 0, jnp.bitwise_xor(dp, 2), zz), xn))
-            first.append((send(high, high, xn), high, half(ref, 1, jnp.bitwise_xor(dp, 1), zz), yn))
+        low, high = half(0, dp, zz), half(1, dp, zz)
+        first.append((send(low, low, yn), low, half(0, jnp.bitwise_xor(dp, 2), zz), xn))
+        first.append((send(high, high, xn), high, half(1, jnp.bitwise_xor(dp, 1), zz), yn))
 
     def pass_on():
-        for copy, own, part, device in first[:4]:
+        for copy, own, part, device in first[:2]:
             done.append(send(own, own, device))
             copy.wait_recv()
             done.append(send(part, part, device))
-        del first[:4]
+        del first[:2]
 
     z_one = jnp.bitwise_xor(z, 1)
     z_near = jnp.bitwise_xor(z, jnp.where(inner, 3, 2))
@@ -610,33 +635,28 @@
     relayed = []
 
     def relay(slot, source, device):
-        for i, ref in enumerate(refs):
-            copy = pltpu.make_async_remote_copy(
-                src_ref=ref.at[dp, source], dst_ref=ref.at[dp, source],
-                send_sem=send_sem.at[send_sem.shape[0] - 8 + len(relayed)],
-                recv_sem=recv_sem.at[send_sem.shape[0] - 4 + 2 * slot + i],
-                device_id=device, device_id_type=MESH,
-            )
-            relayed.append(copy)
-            pl.when(inner)(copy.start)
-        return relayed[-2:]
-
-    def arrived(copies):
-        for copy in copies:
-            copy.wait_recv()
-
-    step = [send(ref.at[dp, z], ref.at[dp, z], nbr) for ref in refs]
+        copy = pltpu.make_async_remote_copy(
+            src_ref=w_ref.at[dp, source], dst_ref=w_ref.at[dp, source],
+            send_sem=send_sem.at[send_sem.shape[0] - 4 + len(relayed)],
+            recv_sem=recv_sem.at[send_sem.shape[0] - 2 + slot],
+            device_id=device, device_id_type=MESH,
+        )
+        relayed.append(copy)
+        pl.when(inner)(copy.start)
+        return copy
+
+    step = send(w_ref.at[dp, z], w_ref.at[dp, z], nbr)
     near = relay(0, z, across)
     spread(z)
     pass_on()
-    arrived(step)
+    step.wait_recv()
     far_block = relay(1, z_one, across)
     spread(z_one)
-    arrived(near)
+    near.wait_recv()
     relay(0, z_near, nbr)
     spread(z_near)
     pass_on()
-    arrived(far_block)
+    far_block.wait_recv()
     relay(1, z_far, nbr)
     spread(z_far)
     swap = send(tok_ref.at[1 - which], x_ref.at[me, 1], far)
@@ -666,22 +686,21 @@
             copy.wait_send()
 
 
-def gather(packed, w_down, tokens, grad_out):
-    rows, cols = 2 * packed.shape[1], packed.shape[2]
+def gather(packed, w_out, tokens, grad_out):
+    rows, cols = 2 * packed.shape[1], packed.shape[2] + w_out.shape[1]
     slots, width = tokens.shape[1:]
-    copies = 61 + 8
+    copies = 36 + 4
     anywhere = pl.BlockSpec(memory_space=pl.ANY)
     near = pl.BlockSpec(memory_space=pltpu.VMEM)
-    w, d, x, g = pl.pallas_call(
+    w, x, g = pl.pallas_call(
         gather_kernel,
         out_shape=[
             jax.ShapeDtypeStruct((4, 4, rows, cols), BF16),
-            jax.ShapeDtypeStruct((4, 4) + w_down.shape, BF16),
             jax.ShapeDtypeStruct((4, 2, slots, width), BF16),
             jax.ShapeDtypeStruct((2, 2, slots, width), BF16),
         ],
         in_specs=[near] * 4,
-        out_specs=[anywhere] * 4,
+        out_specs=[anywhere] * 3,
         scratch_shapes=[
             pltpu.SemaphoreType.DMA((copies,)),
             pltpu.SemaphoreType.DMA((copies,)),
@@ -692,45 +711,62 @@
         ),
         cost_estimate=LINK_TIME,
         name="gather",
-    )(packed, w_down, tokens, grad_out)
-    return w.reshape(16 * rows, cols), d.reshape(-1, width), x.reshape(-1, width), g.reshape(-1, width)
-
-
-def reduce_kernel(n_in, *refs):
-    g_refs, (ow_ref, or_ref, part_ref, xa_ref, gm_ref, gain_ref) = refs[:n_in], refs[n_in : n_in + 6]
-    gq_ref, gk_ref, gv_ref, gg_ref, go_ref, ig_ref = refs[n_in + 6 : n_in + 12]
-    (
-        g_ref, in_a, in_b, mid_a, mid_b, got_a, got_b, out3, in3,
-        mine_ref, sib_ref, give_ref, nbr_ref, back_ref, x_ref, ga_ref, o_ref, s_ref, send_sem, recv_sem, local_sem,
-    ) = refs[n_in + 12 :]
+    )(packed, w_out, tokens, grad_out)
+    return w.reshape(16 * rows, cols), x.reshape(-1, width), g.reshape(-1, width)
+
+
+def reduce_kernel(
+    h_hbm, dq_hbm, dk_hbm, dv_hbm, e_hbm, ow_hbm, or_hbm, part_ref, xa_hbm, gm_hbm, gain_ref,
+    a_ref, go_ref, ig_ref,
+    g_ref, in_a, in_b, mid_a, mid_b, got_a, got_b, out3, in3, mine_ref, sib_ref, give_ref, nbr_ref, back_ref,
+    x_ref, ga_ref, h_ref, dq_ref, dk_ref, dv_ref, o_ref, s_ref, send_sem, recv_sem, local_sem,
+):
     dp, ctx, to = peers()
     c, z = ctx % 2, ctx // 2
     which, chip = ctx // 4, z % 2
     x, y = dp % 2, dp // 2
     hr = g_ref.shape[3] // 2
-    at, local = 0, []
-    for i, ref in enumerate(g_refs):
-        width = ref.shape[-1]
-        local.append(pltpu.make_async_copy(ref, g_ref.at[:, :, :, :, pl.ds(at, width)], local_sem.at[i]))
-        at += width
-    wide = pl.ds(at, ow_ref.shape[-1])
     count = mine_ref.shape[1]
-    local += [
-        pltpu.make_async_copy(ow_ref.at[:, :, c], g_ref.at[c, :, :, :, wide], local_sem.at[n_in]),
-        pltpu.make_async_copy(or_ref, g_ref.at[1 - c, :, :, :, wide], local_sem.at[n_in + 1]),
-        pltpu.make_async_copy(part_ref.at[:, c], mine_ref, local_sem.at[n_in + 2]),
-        pltpu.make_async_copy(xa_ref.at[ctx % 4], x_ref, local_sem.at[n_in + 3]),
-        pltpu.make_async_copy(gm_ref.at[c], ga_ref, local_sem.at[n_in + 4]),
-    ]
-    for copy in local:
+    q_cols, kv_cols = dq_ref.shape[1], dk_ref.shape[1]
+    near = s_ref.shape[1]
+    first_col, width = near - HD, ow_hbm.shape[-1]
+    local = []
+
+    def fetch(src, dst):
+        copy = pltpu.make_async_copy(src, dst, local_sem.at[len(local)])
         copy.start()
+        local.append(copy)
+
+    fetch(ow_hbm.at[:, :, c], g_ref.at[c, :, :, :, pl.ds(near, width)])
+    fetch(or_hbm, g_ref.at[1 - c, :, :, :, pl.ds(near, width)])
+    fetch(e_hbm, g_ref.at[:, :, :, :, pl.ds(first_col, HD)])
+    fetch(part_ref.at[:, c], mine_ref)
+    fetch(dq_hbm, dq_ref)
+    fetch(h_hbm, h_ref)
+    fetch(dk_hbm, dk_ref)
+    fetch(dv_hbm, dv_ref)
+    fetch(xa_hbm.at[ctx % 4], x_ref)
+    fetch(gm_hbm.at[c], ga_ref)
     greet([to(0, 1), to(0, 2), to(0, 4), to(0, 6), to(1, 0), to(2, 0)])
     send, made = sender(send_sem, recv_sem)
     sib, nbr, far, across = to(0, 1), to(0, 2), to(0, 4), to(0, 6)
     xn, yn = to(1, 0), to(2, 0)
     cross = send(part_ref.at[:, 1 - c], sib_ref, sib)
-    for copy in local:
-        copy.wait()
+
+    def ready(count):
+        for copy in local[:count]:
+            copy.wait()
+        del local[:count]
+
+    def weigh(rows, grad_ref, at):
+        def body(i, _):
+            some = h_ref[rows, pl.ds(pl.multiple_of(i * 4 * 2 * hr, 128), 4 * 2 * hr)]
+            part = dot(some, grad_ref[...], TN).astype(BF16)
+            g_ref[i // 2, i % 2, :, :, at : at + grad_ref.shape[1]] = part.reshape(4, 2 * hr, grad_ref.shape[1])
+            return 0
+
+        lax.fori_loop(0, 4, body, 0)
+
     low, high = pl.ds(0, hr), pl.ds(hr, hr)
     inner = jnp.logical_or(z == 1, z == 2)
     outer = jnp.logical_not(inner)
@@ -758,7 +794,7 @@
         out3[block, :, p] = (out3[block, :, p].astype(F32) + in3[slot, :, p].astype(F32)).astype(BF16)
 
     def inward(i):
-        k, part = i // 2, i % 2
+        k, part = i % 4, i // 4
 
         @pl.when(inner)
         def _():
@@ -778,16 +814,15 @@
     a_in, b_in, a_mid, b_mid = [], [], [], []
     size = 64
     tile = lambda i: pl.ds(pl.multiple_of(i * size, size), size)
-    cut = g_ref.shape[4] // 2 // HD * HD
-    parts = (pl.ds(0, cut), pl.ds(cut, g_ref.shape[4] - cut))
+    parts = (pl.ds(first_col, HD + width), pl.ds(0, first_col))
 
     def enter(i):
-        k, p = i // 2, parts[i % 2]
+        k, p = i % 4, parts[i // 4]
         a_in.append(send(g_ref.at[:, 1 - x, order[k], low, p], in_a.at[k, :, :, p], xn))
         b_in.append(send(g_ref.at[1 - y, :, order[k], high, p], in_b.at[k, :, :, p], yn))
 
     def middle(i):
-        k, p = i // 2, parts[i % 2]
+        k, p = i % 4, parts[i // 4]
         add = lambda p, q: (p.astype(F32) + q.astype(F32)).astype(BF16)
         a_in[i].wait_recv()
         mid_a[k, :, p] = add(g_ref[1 - y, x, order[k], 0:hr, p], in_a[k, 1 - y, :, p])
@@ -797,18 +832,20 @@
         b_mid.append(send(mid_b.at[k, :, p], got_b.at[k, :, p], xn))
 
     def leave(i):
-        k, p = i // 2, parts[i % 2]
+        k, p = i % 4, parts[i // 4]
         add = lambda p, q, r: (p.astype(F32) + q.astype(F32) + r.astype(F32)).astype(BF16)
         a_mid[i].wait_recv()
         out3[k, 0:hr, p] = add(g_ref[y, x, order[k], 0:hr, p], in_a[k, y, :, p], got_a[k, :, p])
         b_mid[i].wait_recv()
         out3[k, hr:, p] = add(g_ref[y, x, order[k], hr:, p], in_b[k, x, :, p], got_b[k, :, p])
         if k < 3:
-            pass_z(k, k, k, i % 2, nbr, outer)
-
+            pass_z(k, k, k, i // 4, nbr, outer)
+
+    ready(3)
     enter(0)
     enter(1)
     enter(2)
+    ready(1)
     cross.wait_recv()
     slots = ig_ref.shape[1]
 
@@ -829,40 +866,46 @@
         lax.fori_loop(first // size, (first + slots) // size, give, 0)
         rows = pl.ds(first, slots)
         swaps.append(send(give_ref.at[rows], nbr_ref.at[rows], nbr))
+    ready(2)
+    weigh(pl.ds(pl.multiple_of(chip * dq_ref.shape[0], dq_ref.shape[0]), dq_ref.shape[0]), dq_ref, 0)
     middle(0)
     enter(3)
     middle(1)
+    middle(2)
+    ready(2)
+    weigh(slice(None), dk_ref, q_cols)
+    weigh(slice(None), dv_ref, q_cols + kv_cols)
     enter(4)
+    enter(5)
+    leave(0)
+    leave(1)
+    middle(3)
+    ready(2)
     swaps[0].wait_recv()
     lax.fori_loop(slots // size, 2 * slots // size, back, 0)
     home = send(back_ref.at[pl.ds(slots, slots)], ig_ref.at[which], far)
-    leave(0)
-    middle(2)
-    enter(5)
-    leave(1)
-    middle(3)
-    enter(6)
     leave(2)
     inward(0)
+    inward(1)
     middle(4)
+    enter(6)
+    leave(3)
+    middle(5)
     enter(7)
-    leave(3)
-    inward(1)
+    leave(4)
+    outward(0)
     swaps[1].wait_recv()
     lax.fori_loop(0, slots // size, back, 0)
     keep = pltpu.make_async_copy(back_ref.at[pl.ds(0, slots)], ig_ref.at[which], local_sem.at[0])
     keep.start()
-    middle(5)
-    leave(4)
-    inward(2)
     middle(6)
     leave(5)
-    inward(3)
-    outward(0)
+    inward(4)
     middle(7)
     leave(6)
+    inward(5)
+    leave(7)
     outward(1)
-    leave(7)
     for part in range(2):
         from_z(2, part).wait_recv()
 
@@ -873,24 +916,22 @@
             add_z(3, 3, part)
 
     total = out3[3].astype(F32) + in3[2].astype(F32)
-    near = s_ref.shape[1]
     o_ref[...] = total[:, :near].astype(BF16)
     other = send(o_ref.at[pl.ds(pl.multiple_of((1 - c) * hr, hr), hr)], s_ref, sib)
-    go_ref[...] = total[:, near:]
+    go_ref[...] = total[:, near:].astype(BF16)
     own = o_ref.at[pl.ds(pl.multiple_of(c * hr, hr), hr)]
 
     def place(source, core):
-        col = 0
-        for ref in (gq_ref, gk_ref, gv_ref):
-            size = ref.shape[1] // 2
-            ref[:, pl.ds(pl.multiple_of(core * size, size), size)] = source[:, col : col + size].astype(F32)
-            col += size
+        at = 0
+        for size in (q_cols, kv_cols, kv_cols):
+            a_ref[:, pl.ds(pl.multiple_of(2 * at + core * size, HD), size)] = source[:, at : at + size]
+            at += size
 
     place(own, c)
     other.wait_recv()
     place(s_ref, 1 - c)
-    gains = near - HD
-    gg_ref[...] = own[:, gains:].astype(F32) + s_ref[:, gains:].astype(F32)
+    both = own[:, first_col:].astype(F32) + s_ref[:, first_col:].astype(F32)
+    a_ref[:, 2 * first_col :] = both.astype(BF16)
     keep.wait()
     home.wait_recv()
     for copy in made:
@@ -899,26 +940,24 @@
         pl.when(role)(copy.wait_send)
 
 
-def reduce(grads, out_own, out_sib, part, x_all, grad_middle, gain):
-    rows = grads[0].shape[0] // 16
-    width = x_all.shape[1]
-    near_cols = sum(g.shape[1] for g in grads)
+def reduce(hidden, dq, dk, dv, entries, out_own, out_sib, part, x_all, grad_middle, gain):
+    seq, width = x_all.shape
+    rows = width // 16
+    near_cols = dq.shape[1] + dk.shape[1] + dv.shape[1] + HD
     cols = near_cols + width
     count = part.shape[0] // 4
-    split = lambda v: v.reshape(2, 2, 4, rows, v.shape[1])
     copies = 52
     anywhere = pl.BlockSpec(memory_space=pl.ANY)
     near = pl.BlockSpec(memory_space=pltpu.VMEM)
     return pl.pallas_call(
-        functools.partial(reduce_kernel, len(grads)),
+        reduce_kernel,
         out_shape=[
-            *[jax.ShapeDtypeStruct((rows // 2, 2 * g.shape[-1]), F32) for g in grads[:3]],
-            jax.ShapeDtypeStruct((rows // 2, HD), F32),
-            jax.ShapeDtypeStruct((rows, width), F32),
+            jax.ShapeDtypeStruct((rows // 2, 2 * (near_cols - HD) + HD), BF16),
+            jax.ShapeDtypeStruct((rows, width), BF16),
             jax.ShapeDtypeStruct((2, count // 2, width), BF16),
         ],
-        in_specs=[anywhere] * (len(grads) + 5) + [near],
-        out_specs=[near] * 5 + [anywhere],
+        in_specs=[anywhere] * 10 + [near],
+        out_specs=[near] * 2 + [anywhere],
         scratch_shapes=[
             pltpu.VMEM((2, 2, 4, rows, cols), BF16),
             pltpu.VMEM((4, 2, rows // 2, cols), BF16),
@@ -932,12 +971,13 @@
             pltpu.VMEM((2, count, width), BF16),
         ]
         + [pltpu.VMEM((count, width), BF16)] * 5
+        + [pltpu.VMEM(v.shape, BF16) for v in (hidden, dq, dk, dv)]
         + [
             pltpu.VMEM((rows, near_cols), BF16),
             pltpu.VMEM((rows // 2, near_cols), BF16),
             pltpu.SemaphoreType.DMA((copies,)),
             pltpu.SemaphoreType.DMA((copies,)),
-            pltpu.SemaphoreType.DMA((len(grads) + 5,)),
+            pltpu.SemaphoreType.DMA((10,)),
         ],
         compiler_params=pltpu.CompilerParams(
             collective_id=1, has_side_effects=True, vmem_limit_bytes=VMEM_LIMIT
@@ -945,7 +985,8 @@
         cost_estimate=LINK_TIME,
         name="reduce",
     )(
-        *[split(g) for g in grads],
+        hidden, dq, dk, dv,
+        entries.reshape(2, 2, 4, rows, HD),
         out_own.reshape(2, 4, 2, rows, width),
         out_sib.reshape(2, 4, rows, width),
         part.reshape(2, 2, count, width),
@@ -1017,24 +1058,28 @@
 
     gate_order, up_order = ff_order(w_gate), ff_order(w_up)
     qkv_c = q_c + 2 * kv_c
-    all_c = qkv_c + 2 * ff_c
+    gu_c = 2 * ff_c
+    all_c = gu_c + qkv_c
     by_tile = lambda v: v.reshape(2, r_in, ff_c // FF_TILE, FF_TILE)
     gu_shard = jnp.stack([by_tile(gate_order), by_tile(up_order)], axis=3).reshape(2, r_in, 2 * ff_c)
-    packed = jnp.stack([jnp.concatenate([qkv_halves[i], gu_shard[i], gains], axis=1) for i in range(2)])
+    packed = jnp.stack([jnp.concatenate([gu_shard[i], qkv_halves[i], gains], axis=1) for i in range(2)])
     if tall:
-        w_all, w_down_c, x_all, go_chip = gather(packed, w_down, tokens, grad_out)
-        w_out, w_all = lax.optimization_barrier((w_out, w_all))
+        w_all, x_all, go_chip = gather(packed, w_out, tokens, grad_out)
+        out_rows = w_all[:, all_c + HD :].reshape(2, -1, r_out, width)
+        out_keep = lax.dynamic_index_in_dim(out_rows, c, 0, False)
+        out_give = lax.dynamic_index_in_dim(out_rows, 1 - c, 0, False)
+        w_out_c = by_core(c, out_keep, sibling(out_give)).transpose(1, 0, 2, 3).reshape(q_c, width)
+        w_down, w_all = lax.optimization_barrier((w_down, w_all))
     else:
         both = lax.all_gather(packed, axes, axis=1, tiled=True)
         w_all = lax.dynamic_index_in_dim(both, c, 0, False)
-        down_all = lax.all_gather(w_down, axes, axis=0, tiled=True).reshape(chips, 2, r_down, width)
-        w_down_c = lax.dynamic_index_in_dim(down_all, c, 1, False).reshape(ff_c, width)
+        out_all = lax.all_gather(w_out, axes, axis=0, tiled=True)
+        w_out_c = lax.dynamic_slice_in_dim(out_all, c * q_c, q_c, 0)
         x_own = placed(tokens)
         x_all = lax.all_gather(x_own, "ctx", axis=0, tiled=True, axis_index_groups=halves)
         go_own = placed(grad_out)
         go_chip = by_core(c, go_own, sibling(go_own)).reshape(4 * slots, width)
-    out_all = lax.all_gather(w_out, axes, axis=0, tiled=True)
-    w_out_c = lax.dynamic_slice_in_dim(out_all, c * q_c, q_c, 0)
+    down_all = lax.all_gather(w_down, axes, axis=0, tiled=True).reshape(chips, 2, r_down, width)
     g_cols = w_all[:, all_c : all_c + HD].astype(F32)
     gain_attn = g_cols[:, 0][None]
     gain_mlp = g_cols[:, 1][None]
@@ -1058,13 +1103,11 @@
     cosine, sine = rope_tables(seq)
 
     chip_at = chip.astype(jnp.int32).reshape(1)
-    hidden_all, q_raw, kv_raw = project(chip_at, x_all, gain_attn, w_all, chip_rows)
-    hidden = lax.dynamic_slice_in_dim(hidden_all, chip * chip_rows, chip_rows, 0)
+    hidden_all, q_raw, kv_raw = project(chip_at, x_all, gain_attn, w_all, gu_c, chip_rows)
     mixed, lse = attend(ids, order, q_raw, kv_raw, cosine, sine, gain_q, gain_k, span)
     proj = dot(mixed, w_out_c, NN, BF16)
-    middle, second, activated, grad_gu = feed(
-        chip_at, x_all, proj, sibling(proj), gain_mlp, go_chip, w_all, qkv_c, w_down_c
-    )
+    middle, second, activated, gate_up = feed(chip_at, x_all, proj, sibling(proj), gain_mlp, w_all, ff_c)
+    grad_gu, w_down_c = feed_back(c.astype(jnp.int32).reshape(1), gate_up, go_chip, down_all)
     down = dot(activated, w_down_c, NN, BF16).reshape(2, 2 * slots, width)
     down_own = lax.dynamic_index_in_dim(down, c, 0, False)
     down_other = sibling(lax.dynamic_index_in_dim(down, 1 - c, 0, False))
@@ -1076,7 +1119,7 @@
         return jnp.where(which == 0, jnp.stack([mine, back]), jnp.stack([back, mine]))
 
 
-    second_part = dot(grad_gu, w_all[:, qkv_c:all_c], NT, BF16)
+    second_part = dot(grad_gu, w_all[:, :gu_c], NT, BF16)
     grad_gu_w = dot(second, grad_gu, TN, BF16)
     grad_down_w = dot(activated, go_chip, TN, BF16)
     grad_attn, grad_mixed, mlp_gain_sum = middle_back(
@@ -1094,32 +1137,35 @@
     out_w = dot(mixed, grad_attn, TN, BF16).reshape(-1, 2, r_out, width)
     out_recv = sibling(lax.dynamic_index_in_dim(out_w, 1 - c, 1, False))
     out_recv, grad_mixed = lax.optimization_barrier((out_recv, grad_mixed))
-    result, grad_mixed = lax.optimization_barrier((result, grad_mixed))
+    result, grad_mixed, part_down = lax.optimization_barrier((result, grad_mixed, part_down))
+    if tall:
+        pieces = part_down.reshape(half, r_down, width)
+        place = ctx // 2
+        down_own = lax.dynamic_index_in_dim(pieces, place, 0, False).astype(F32)
+        down_got = [
+            lax.ppermute(
+                lax.dynamic_index_in_dim(pieces, jnp.bitwise_xor(place, k), 0, False),
+                "ctx",
+                [(i, i ^ (2 * k)) for i in range(n)],
+            )
+            for k in range(1, half)
+        ]
+    else:
+        down_own, down_got = over_ctx(part_down).astype(F32), []
     output = returned(result)
     dq, dk, dv, dgq, dgk = attend_back(
         ids, order, q_raw, kv_raw, grad_mixed, mixed, lse, cosine, sine, gain_q, gain_k, span
     )
-    output, dq, dk, dv, part_gu, part_down = lax.optimization_barrier((output, dq, dk, dv, part_gu, part_down))
-    rows2, extra = 2 * r_in, r_down - 2 * r_in
-    part_down = part_down.reshape(half, r_down, width)
-    rest = part_down[:, rows2:]
-    fold = rows2 // extra
-    folded = [rest[:, :, i * width // fold : (i + 1) * width // fold] for i in range(fold)]
-    pieces = [part_gu.reshape(half, rows2, -1), part_down[:, :rows2], jnp.concatenate(folded, axis=1)]
-    sum_ff = over_ctx(jnp.concatenate(pieces, axis=2).reshape(half * rows2, -1))
-    sum_gu = sum_ff[:, : 2 * ff_c]
-    tail = sum_ff[:, 2 * ff_c + width :].reshape(fold, extra, -1)
-    sum_down = jnp.concatenate(
-        [sum_ff[:, 2 * ff_c : 2 * ff_c + width], jnp.concatenate([tail[i] for i in range(fold)], axis=1)], axis=0
-    )
-    part_all, attn_gain_sum = project_back(chip_at, dq, dk, dv, x_all, w_all)
-    grad_q_w = dot(hidden, dq, TN, BF16)
-    grad_k_w = dot(hidden_all, dk, TN, BF16)
-    grad_v_w = dot(hidden_all, dv, TN, BF16)
+    output, dq, dk, dv, part_gu, down_got = lax.optimization_barrier((output, dq, dk, dv, part_gu, down_got))
+    sum_gu = over_ctx(part_gu)
+    sum_down = down_own
+    for piece in down_got:
+        sum_down = sum_down + piece.astype(F32)
+    part_all, attn_gain_sum = project_back(chip_at, dq, dk, dv, x_all, w_all, gu_c)
     lot = lambda v: v.reshape(n_dp * n, -1)
     entries = jnp.concatenate([lot(attn_gain_sum), lot(grad_mlp_gain), lot(dgq), lot(dgk)], axis=1)
     entries = jnp.pad(entries[:, None], ((0, 0), (0, r_in - 1), (0, HD - entries.shape[1])))
-    grads = [grad_q_w, grad_k_w, grad_v_w, entries.reshape(width, HD).astype(BF16)]
+    entries = entries.reshape(width, HD).astype(BF16)
     near_c = qkv_c + HD
     beside = lambda v: v.transpose(1, 0, 2).reshape(r_in, -1)
     by_rows = lambda v: lax.dynamic_index_in_dim(v.reshape(2, r_in, -1), c, 0, False)
@@ -1129,10 +1175,16 @@
         return by_core(c, by_rows(sums), sibling(other)).astype(F32)
 
     if tall:
-        grad_q, grad_k, grad_v, gain_own, sum_out, input_grad = reduce(
-            grads, out_w, out_recv, part_all, x_all, grad_attn, gain_attn
+        sums, sum_out, input_grad = reduce(
+            hidden_all, dq, dk, dv, entries, out_w, out_recv, part_all, x_all, grad_attn, gain_attn
         )
+        grad_q, grad_k, grad_v = (
+            sums[:, i:j].astype(F32) for i, j in ((0, 2 * q_c), (2 * q_c, 2 * q_c + 2 * kv_c), (2 * q_c + 2 * kv_c, 2 * qkv_c))
+        )
+        sum_out, gain_own = sum_out.astype(F32), sums[:, 2 * qkv_c :].astype(F32)
     else:
+        hidden = lax.dynamic_slice_in_dim(hidden_all, chip * chip_rows, chip_rows, 0)
+        grads = [dot(hidden, dq, TN, BF16), dot(hidden_all, dk, TN, BF16), dot(hidden_all, dv, TN, BF16), entries]
         qkv_own = columns(over_ctx(over_dp(jnp.concatenate(grads, axis=1))))
         out_mine = lax.dynamic_index_in_dim(out_w, c, 1, False)
         sum_out = over_ctx(over_dp(by_core(c, out_mine, out_recv).reshape(chips * r_out, width))).astype(F32)
@@ -1145,6 +1197,7 @@
         ).astype(F32)
         back, _terms = norm_back(x_own.astype(F32), gain_attn, grad_hidden)
         input_grad = returned((own_rows(grad_attn).astype(F32) + back).astype(BF16))
+    sum_gu, gain_own = lax.optimization_barrier((sum_gu, gain_own))
     gain_row, r_head = gain_own[0], q_gain.shape[0]
     gu_own = columns(sum_gu).reshape(2, r_in, ff_c // FF_TILE, 2, FF_TILE)
     ff_back = lambda v: v.reshape(2, r_in, chips, r_down).transpose(1, 2, 0, 3).reshape(r_in, ff)
@@ -1157,7 +1210,7 @@
         sum_out,
         ff_back(gu_own[:, :, :, 0]),
         ff_back(gu_own[:, :, :, 1]),
-        sum_down.astype(F32),
+        sum_down,
         gain_row[:r_in],
         gain_row[r_in : 2 * r_in],
         gain_row[2 * r_in : 2 * r_in + r_head],

time: 503 us -> 490 us (0.974)
  waiting for transfers between devices: 23 us -> 3.93 us
  matrix products: 52.2 us -> 37.7 us
  starting transfers between devices: 3.79 us -> 11.8 us
    pallas_call x1 -> x2, Pallas kernels: 84.4 us -> 101 us  [the longest x1 89.4 us: reduce(): pl.pallas_call(reduce_kernel, out_shape=[jax.ShapeDtypeStruct((rows // 2,...]
    all_gather x1, waiting for transfers between devices: 15.9 us -> 0.02 us  [layer(): lax.all_gather(w_down, axes, axis=0, tiled=True)]
    dot_general x9 -> x6, matrix products: 52.2 us -> 37.7 us  [dot(): return lax.dot_general(a, b, (dims, ((), ())), preferred_element_type=out)]
    pallas_call x1, Pallas kernels: 130 us -> 121 us  [gather(): pl.pallas_call(gather_kernel, out_shape=[jax.ShapeDtypeStruct((4, 4, rows...]
    unnamed x75 -> x85, local copies, waits for them, and re-layouts: 13.7 us -> 17 us
  transfers between devices with their start and end apart: 10 -> 14, of which waited for: 4 -> 1; matrix products, arithmetic and copies ran while one was open for 11% -> 13% of each run, Pallas kernels for 42% -> 50%
where the time goes in v4:
time: 490 us; the launch traced here: 486 us
  Pallas kernels  363 us (74%)
  local copies, waits for them, and re-layouts  40.5 us (8%)
  matrix products  37.7 us (8%)
  between operations  16.5 us (3%)
  other arithmetic  12.6 us (3%)
  starting transfers between devices  11.8 us (2%)
    pallas_call x1, Pallas kernels, gather(): pl.pallas_call(gather_kernel, out_shape=[jax.ShapeDtypeStruct((4, 4, rows...  121 us
    pallas_call x1, Pallas kernels, reduce(): pl.pallas_call(reduce_kernel, out_shape=[jax.ShapeDtypeStruct((rows // 2,...  89.4 us
    pallas_call x1, Pallas kernels, attend_back(): pl.pallas_call(functools.partial(attend_back_kernel, span), out_shape=[ja...  59 us
    dot_general x6, matrix products, dot(): return lax.dot_general(a, b, (dims, ((), ())), preferred_element_type=out)  37.7 us
    pallas_call x1, Pallas kernels, attend(): pl.pallas_call(functools.partial(attend_kernel, span), out_shape=[jax.Sha...  26.8 us
    unnamed x85, local copies, waits for them, and re-layouts  17 us
    pallas_call x1, Pallas kernels, feed(): pl.pallas_call(feed_kernel, out_shape=[jax.ShapeDtypeStruct((rows, width)...  16.6 us
    pallas_call x1, Pallas kernels, project_back(): pl.pallas_call(functools.partial(project_back_kernel, own), out_shape=[ja...  14.9 us
  transfers between devices with their start and end apart: 14, of which 1 were waited for; matrix products, arithmetic and copies ran while one was open for 13% of the time, Pallas kernels for 50%

profile of v4, /device:TPU:0, one launch (start us, length us, event | category | flops | bytes accessed | tf_op | source)
XLA Modules:
  0.0 486.2 jit_solution(5616446225698172544)
XLA Ops:
  14.3 121.5 %gather.7 = (bf16[4,4,64,6272]{3,2,1,0:T(8,128)(2,1)}, bf16[4,2,256,1024]{3,2,1,0:T(8,128)(2,1)}, bf16[2,2,256,1024]{3,2,1,0:T(8,128)(2,1)S(1)}) custom-call(bf16[2,32,5248]{2,1,0:T(8,128)(2,1)S(1)} %pad_maximum_fusion.pk_ref, bf16[64,1024]{1,0:T(8,128)(2,1)S(1)} %copy-done.9, bf16[2,256,1024]{2,1,0:T(8,128)(2,1)S(1)} %copy-done.7, ...), custom_call_target="tpu_custom_call" | custom-call | bytes 300000000 | tf_op jit(solution)/shard_map/gather/pallas_call | solution.py:695
  136.0 3.6 slice.148
  139.6 3.1 constant_dynamic-slice_fusion.1
  145.2 14.5 %project.1 = (bf16[2048,1024]{1,0:T(8,128)(2,1)}, bf16[1024,1024]{1,0:T(8,128)(2,1)S(1)}, bf16[2048,1024]{1,0:T(8,128)(2,1)}) custom-call(s32[1]{0:T(128)} %bitcast.chip_ref, bf16[2048,1024]{1,0:T(8,128)(2,1)} %bitcast.121, f32[1,1024]{1,0:T(1,128)S(1)} %bitcast.104, bf16[1024,6272]{1,0:T(8,128)(2,1)} %bitcast.114, bf16[1024,6272]{1,0:T(8,128)(2,1)} %bitcast.115), custom_call_target="tpu_custom_call" | custom-call | tf_op jit(solution)/shard_map/project/pallas_call | solution.py:344
  159.8 1.3 copy-done.12
  161.4 26.8 %attend.1 = (bf16[1024,1024]{1,0:T(8,128)(2,1)S(1)}, f32[4,8,1,256]{3,2,1,0:T(1,128)S(1)}) custom-call(s32[8]{0:T(128)S(1)} %dynamic_slice.54.ids_ref, s32[16]{0:T(128)S(1)} %select_reduce_fusion.order_ref, bf16[1024,1024]{1,0:T(8,128)(2,1)} %copy-done.12, bf16[2048,1024]{1,0:T(8,128)(2,1)} %get-tuple-element.61.k_ref.v_ref, ...), custom_call_target="tpu_custom_call" | custom-call | flops 8589934592 | bytes 8388608 | tf_op jit(solution)/shard_map/attend/pallas_call | solution.py:161
  188.3 2.6 fusion.2
  191.1 2.4 fusion.16.p0_ref
  194.0 3.8 collective-permute-done.1.p1_ref
  199.1 16.6 %feed.1 = (f32[1024,1024]{1,0:T(8,128)}, bf16[1024,1024]{1,0:T(8,128)(2,1)S(1)}, bf16[1024,1536]{1,0:T(8,128)(2,1)}, bf16[1024,3072]{1,0:T(8,128)(2,1)}) custom-call(s32[1]{0:T(128)} %bitcast.chip_ref, bf16[2048,1024]{1,0:T(8,128)(2,1)} %bitcast.122, bf16[1024,1024]{1,0:T(8,128)(2,1)S(1)} %fusion.16.p0_ref, bf16[1024,1024]{1,0:T(8,128)(2,1)} %copy-done.25, ...), custom_call_target="tpu_custom_call" | custom-call | tf_op jit(solution)/shard_map/feed/pallas_call | solution.py:452
  217.1 6.7 %fusion.19 = bf16[1536,1024]{1,0:T(8,128)(2,1)} fusion(bf16[1024,1536]{1,0:T(8,128)(2,1)} %get-tuple-element.64, bf16[1024,1024]{1,0:T(8,128)(2,1)S(1)} %bitcast.98), kind=kOutput, calls=%fused_computation.73 | convolution fusion | flops 3221225472 | bytes 8388608 | tf_op jit(solution)/shard_map/dot_general | solution.py:50
  224.2 11.5 %feed_back.1 = (bf16[1024,3072]{1,0:T(8,128)(2,1)}, bf16[1536,1024]{1,0:T(8,128)(2,1)S(1)}) custom-call(s32[1]{0:T(128)} %bitcast.21.core_ref, bf16[1024,3072]{1,0:T(8,128)(2,1)} %get-tuple-element.65.gu_ref, bf16[1024,1024]{1,0:T(8,128)(2,1)S(1)} %bitcast.99, bf16[16,2,96,1024]{3,2,1,0:T(8,128)(2,1)} %bitcast.128), custom_call_target="tpu_custom_call" | custom-call | tf_op jit(solution)/shard_map/feed_back/pallas_call | solution.py:504
  235.7 1.7 copy-done.10
  237.4 11.6 %fusion.20 = bf16[1024,3072]{1,0:T(8,128)(2,1)} fusion(bf16[1024,1024]{1,0:T(8,128)(2,1)S(1)} %copy-done.15, bf16[1024,3072]{1,0:T(8,128)(2,1)} %get-tuple-element.69), kind=kOutput, calls=%fused_computation.74 | convolution fusion | flops 6442450944 | bytes 14680064 | tf_op jit(solution)/shard_map/dot_general | solution.py:50
  249.1 10.9 %fusion.s0_ref = bf16[1024,1024]{1,0:T(8,128)(2,1)S(1)} fusion(bf16[1024,3072]{1,0:T(8,128)(2,1)} %get-tuple-element.69, bf16[1024,6272]{1,0:T(8,128)(2,1)} %bitcast.117), kind=kOutput, calls=%fused_computation.1 | convolution fusion | flops 6442450944 | bytes 14680064 | tf_op jit(solution)/shard_map/dot_general | solution.py:50
  260.4 3.6 fusion.17
  265.8 1.3 copy-done.28
  267.1 8.9 %middle_back.1 = (bf16[1024,1024]{1,0:T(8,128)(2,1)S(1)}, bf16[1024,1024]{1,0:T(8,128)(2,1)S(1)}, f32[1,1024]{1,0:T(1,128)S(1)}) custom-call(f32[1024,1024]{1,0:T(8,128)} %get-tuple-element.63.mid_ref, bf16[1024,1024]{1,0:T(8,128)(2,1)} %copy-done.27, bf16[1024,1024]{1,0:T(8,128)(2,1)} %copy-done.28, bf16[1024,1024]{1,0:T(8,128)(2,1)} %bitcast.100, ...), custom_call_target="tpu_custom_call" | custom-call | tf_op jit(solution)/shard_map/middle_back/pallas_call | solution.py:543
  276.0 2.4 fusion.18
  278.5 1.3 copy-done.23
  280.2 2.9 fusion.4
  283.3 4.9 %collective-permute-start.5 = (bf16[256,1024]{1,0:T(8,128)(2,1)S(1)}, bf16[256,1024]{1,0:T(8,128)(2,1)S(1)}, u32[]{:S(2)}, u32[]{:S(2)}) collective-permute-start(bf16[256,1024]{1,0:T(8,128)(2,1)S(1)} %get-tuple-element.110), channel_id=1, source_target_pairs={{0,4},{1,5},{2,6},{3,7},{4,0},{5,1},{6,2},{7,3},{8,12},{9,13},{10,... | collective-permute-start | bytes 1572872 | tf_op jit(solution)/shard_map/ppermute | solution.py:1026
  288.2 1.6 collective-permute-start.6
  289.9 1.9 collective-permute-start.7
  295.2 59.0 %attend_back.1 = (bf16[1024,1024]{1,0:T(8,128)(2,1)S(1)}, bf16[2048,512]{1,0:T(8,128)(2,1)}, bf16[2048,512]{1,0:T(8,128)(2,1)}, f32[1,128]{1,0:T(1,128)S(1)}, f32[1,128]{1,0:T(1,128)S(1)}) custom-call(s32[8]{0:T(128)S(1)} %dynamic_slice.54.ids_ref, s32[16]{0:T(128)S(1)} %select_reduce_fusion.order_ref, bf16[1024,1024]{1,0:T(8,128)(2,1)} %copy-done.12, ...), custom_call_target="tpu_custom_call" | custom-call | flops 10737418240 | bytes 16777216 | tf_op jit(solution)/shard_map/attend_back/pallas_call | solution.py:285
  356.5 1.6 copy-done.2
  358.1 14.9 %project_back.1 = (bf16[2048,1024]{1,0:T(8,128)(2,1)}, f32[1,1024]{1,0:T(1,128)S(1)}) custom-call(s32[1]{0:T(128)} %bitcast.chip_ref, bf16[1024,1024]{1,0:T(8,128)(2,1)S(1)} %get-tuple-element.83.dq_ref.dq_hbm, bf16[2048,512]{1,0:T(8,128)(2,1)S(1)} %copy-done.2, bf16[2048,512]{1,0:T(8,128)(2,1)} %get-tuple-element.85.dv_ref.dv_hbm, ...), custom_call_target="tpu_custom_call" | custom-call | tf_op jit(solution)/shard_map/project_back/pallas_call | solution.py:395
  373.3 89.4 %reduce.27 = (bf16[32,4224]{1,0:T(8,128)(2,1)S(1)}, bf16[64,1024]{1,0:T(8,128)(2,1)S(1)}, bf16[2,256,1024]{2,1,0:T(8,128)(2,1)S(1)}) custom-call(bf16[2048,1024]{1,0:T(8,128)(2,1)} %get-tuple-element.82.h_hbm, bf16[1024,1024]{1,0:T(8,128)(2,1)S(1)} %get-tuple-element.83.dq_ref.dq_hbm, bf16[2048,512]{1,0:T(8,128)(2,1)} %get-tuple-element.84.dk_ref.dk_hbm, ...), custom_call_target="tpu_custom_call" | custom-call | bytes 300000000 | tf_op jit(solution)/shard_map/reduce/pallas_call | solution.py:952
  465.1 1.9 fusion.7
  471.2 2.2 slice_reduce_fusion.2
  474.1 1.4 reshape.188
  476.2 1.4 reshape.189
  (174 shorter events, 30.0 us)
Async XLA Ops:
  8.0 134.7 %copy-start = (s32[2,2048]{1,0:T(2,128)S(1)}, s32[2,2048]{1,0:T(2,128)}, u32[]{:S(2)}) copy-start(s32[2,2048]{1,0:T(2,128)} %param.18) | copy-start | bytes 49156
  8.0 216.1 %all-gather.2.cloned.1.call-start = ((), (), s32[]{:S(2)}) async-start(), calls=%async_computation.3 | async-start | bytes 6488064 | tf_op jit(solution)/shard_map/all_gather | solution.py:1082
  9.3 2.5 copy-start.32
  9.6 2.6 copy-start.36
  135.8 88.4 %copy-start.3 = (bf16[2,2,256,1024]{3,2,1,0:T(8,128)(2,1)}, bf16[2,2,256,1024]{3,2,1,0:T(8,128)(2,1)S(1)}, u32[]{:S(2)}) copy-start(bf16[2,2,256,1024]{3,2,1,0:T(8,128)(2,1)S(1)} %get-tuple-element.66) | copy-start | bytes 6291460
  135.8 147.4 %reduce-scatter.4.cloned.1.call-start = ((), (), s32[]{:S(2)}) async-start(), calls=%async_computation.4 | async-start | bytes 3932160 | tf_op jit(solution)/shard_map/reduce_scatter | solution.py:1130
  139.6 3.1 copy-start.40
  142.7 45.5 %collective-permute-start = (bf16[8,64,1024]{2,1,0:T(8,128)(2,1)}, bf16[8,64,1024]{2,1,0:T(8,128)(2,1)}, u32[]{:S(2)}, u32[]{:S(2)}) collective-permute-start(bf16[8,64,1024]{2,1,0:T(8,128)(2,1)} %get-tuple-element.108), channel_id=1, source_target_pairs={{0,1},{1,0},{2,3},{3,2},{4,5},{5,4},{6,7},{7,6},{8,9},{9,8},{10,11... | collective-permute-start | bytes 3145736 | tf_op jit(solution)/shard_map/ppermute | solution.py:1025
  145.2 16.2 %copy-start.16 = (f32[2048,128]{1,0:T(8,128)S(1)}, f32[2048,128]{1,0:T(8,128)}, u32[]{:S(2)}) copy-start(f32[2048,128]{1,0:T(8,128)} %constant.135.clone.cos_ref) | copy-start | bytes 3145732
  145.2 16.2 %copy-start.18 = (f32[2048,128]{1,0:T(8,128)S(1)}, f32[2048,128]{1,0:T(8,128)}, u32[]{:S(2)}) copy-start(f32[2048,128]{1,0:T(8,128)} %constant.136.clone.sin_ref) | copy-start | bytes 3145732
  161.4 26.8 %copy-start.24 = (bf16[1,8,64,1024]{3,2,1,0:T(8,128)(2,1)S(1)}, bf16[1,8,64,1024]{3,2,1,0:T(8,128)(2,1)}, u32[]{:S(2)}) copy-start(bf16[1,8,64,1024]{3,2,1,0:T(8,128)(2,1)} %get-tuple-element.107) | copy-start | bytes 3145732
  188.2 2.8 copy-start.20
  193.4 4.4 collective-permute-start.1
  223.9 132.2 %reduce-scatter.6.cloned.1.call-start = ((), (), s32[]{:S(2)}) async-start(), calls=%async_computation.5 | async-start | bytes 7864320 | tf_op jit(solution)/shard_map/reduce_scatter | solution.py:1130
  224.2 13.2 %copy-start.15 = (bf16[1024,1024]{1,0:T(8,128)(2,1)S(1)}, bf16[1024,1024]{1,0:T(8,128)(2,1)}, u32[]{:S(2)}) copy-start(bf16[1024,1024]{1,0:T(8,128)(2,1)} %copy-done.14) | copy-start | bytes 6291460
  249.0 218.7 %reduce-scatter.8.cloned.1.call-start = ((), (), s32[]{:S(2)}) async-start(), calls=%async_computation.6 | async-start | bytes 1966080 | tf_op jit(solution)/shard_map/reduce_scatter | solution.py:1131
  249.1 11.3 %copy-start.11 = (bf16[1536,1024]{1,0:T(8,128)(2,1)S(1)}, bf16[1536,1024]{1,0:T(8,128)(2,1)}, u32[]{:S(2)}) copy-start(bf16[1536,1024]{1,0:T(8,128)(2,1)} %copy-done.10) | copy-start | bytes 9437188
  249.1 11.3 %copy-start.37 = (bf16[1024,1536]{1,0:T(8,128)(2,1)S(1)}, bf16[1024,1536]{1,0:T(8,128)(2,1)}, u32[]{:S(2)}) copy-start(bf16[1024,1536]{1,0:T(8,128)(2,1)} %get-tuple-element.64) | copy-start | bytes 9437188
  260.0 4.0 copy-start.27
  260.0 5.4 %collective-permute-start.3 = (bf16[1024,1024]{1,0:T(8,128)(2,1)S(1)}, bf16[1024,1024]{1,0:T(8,128)(2,1)S(1)}, u32[]{:S(2)}, u32[]{:S(2)}) collective-permute-start(bf16[1024,1024]{1,0:T(8,128)(2,1)S(1)} %fusion.s0_ref), channel_id=1, source_target_pairs={{0,1},{1,0},{2,3},{3,2},{4,5},{5,4},{6,7},{7,6},{8,9},{9,8},{10,11... | collective-permute-start | bytes 6291464 | tf_op jit(solution)/shard_map/ppermute | solution.py:1025
  265.2 15.0 %collective-permute-start.2 = (bf16[512,1024]{1,0:T(8,128)(2,1)}, bf16[512,1024]{1,0:T(8,128)(2,1)}, u32[]{:S(2)}, u32[]{:S(2)}) collective-permute-start(bf16[512,1024]{1,0:T(8,128)(2,1)} %dynamic-slice_bitcast_fusion.1), channel_id=1, source_target_pairs={{0,1},{1,0},{2,3},{3,2},{4,5},{5,4},{6,7},{7,6},{8,9},{9,8},{10,11... | collective-permute-start | bytes 3145736 | tf_op jit(solution)/shard_map/ppermute | solution.py:1025
  267.1 8.9 %copy-start.21 = (bf16[1024,1024]{1,0:T(8,128)(2,1)S(1)}, bf16[1024,1024]{1,0:T(8,128)(2,1)}, u32[]{:S(2)}) copy-start(bf16[1024,1024]{1,0:T(8,128)(2,1)} %copy-done.20) | copy-start | bytes 6291460
  280.0 3.2 collective-permute-start.4
  283.2 5.0 %copy-start.29 = (bf16[384,1024]{1,0:T(8,128)(2,1)S(1)}, bf16[384,1024]{1,0:T(8,128)(2,1)}, u32[]{:S(2)}) copy-start(bf16[384,1024]{1,0:T(8,128)(2,1)} %reduce-scatter.4.cloned.1.call-done) | copy-start | bytes 2359300
  283.3 70.9 %collective-permute-start.5 = (bf16[256,1024]{1,0:T(8,128)(2,1)S(1)}, bf16[256,1024]{1,0:T(8,128)(2,1)S(1)}, u32[]{:S(2)}, u32[]{:S(2)}) collective-permute-start(bf16[256,1024]{1,0:T(8,128)(2,1)S(1)} %get-tuple-element.110), channel_id=1, source_target_pairs={{0,4},{1,5},{2,6},{3,7},{4,0},{5,1},{6,2},{7,3},{8,12},{9,13},{10,... | collective-permute-start | bytes 1572872 | tf_op jit(solution)/shard_map/ppermute | solution.py:1026
  288.2 67.1 %collective-permute-start.6 = (bf16[96,1024]{1,0:T(8,128)(2,1)S(1)}, bf16[96,1024]{1,0:T(8,128)(2,1)S(1)}, u32[]{:S(2)}, u32[]{:S(2)}) collective-permute-start(bf16[96,1024]{1,0:T(8,128)(2,1)S(1)} %get-tuple-element.113), channel_id=1, source_target_pairs={{0,2},{1,3},{2,0},{3,1},{4,6},{5,7},{6,4},{7,5},{8,10},{9,11},{10,... | collective-permute-start | bytes 589832 | tf_op jit(solution)/shard_map/ppermute | solution.py:1146
  289.9 65.5 %collective-permute-start.7 = (bf16[96,1024]{1,0:T(8,128)(2,1)S(1)}, bf16[96,1024]{1,0:T(8,128)(2,1)S(1)}, u32[]{:S(2)}, u32[]{:S(2)}) collective-permute-start(bf16[96,1024]{1,0:T(8,128)(2,1)S(1)} %get-tuple-element.112), channel_id=1, source_target_pairs={{0,4},{1,5},{2,6},{3,7},{4,0},{5,1},{6,2},{7,3},{8,12},{9,13},{10,... | collective-permute-start | bytes 589832 | tf_op jit(solution)/shard_map/ppermute | solution.py:1146
  291.8 64.2 %collective-permute-start.8 = (bf16[96,1024]{1,0:T(8,128)(2,1)S(1)}, bf16[96,1024]{1,0:T(8,128)(2,1)}, u32[]{:S(2)}, u32[]{:S(2)}) collective-permute-start(bf16[96,1024]{1,0:T(8,128)(2,1)S(1)} %get-tuple-element.111), channel_id=1, source_target_pairs={{0,6},{1,7},{2,4},{3,5},{4,2},{5,3},{6,0},{7,1},{8,14},{9,15},{10,... | collective-permute-start | bytes 589832 | tf_op jit(solution)/shard_map/ppermute | solution.py:1146
  373.3 91.8 %copy-start.31 = (bf16[96,1024]{1,0:T(8,128)(2,1)S(1)}, bf16[96,1024]{1,0:T(8,128)(2,1)}, u32[]{:S(2)}) copy-start(bf16[96,1024]{1,0:T(8,128)(2,1)} %copy-done.30) | copy-start | bytes 589828
  468.8 1.8 collective-permute-start.9
  474.1 3.5 copy-start.6
  475.5 3.0 copy-start.1
  (23 other events, 37.6 us)
Sparse Core Ops, SparseCore 0:
  135.9 72.3 all-gather.1
  356.2 42.8 reduce-scatter.7
Sparse Core Ops, SparseCore 1:
  223.9 46.7 reduce-scatter.3
  273.6 70.0 reduce-scatter.5

commit v5 on v4

--- a/solution.py
+++ b/solution.py
@@ -18,7 +18,7 @@
 KEY_TILE = 512
 ROW_TILE = 256
 FF_TILE = 384
-VMEM_LIMIT = 48 * 1024 * 1024
+MIB = 1024 * 1024
 MESH = pl.DeviceIdType.MESH
 F32 = jnp.float32
 BF16 = jnp.bfloat16
@@ -187,7 +187,7 @@
                 pltpu.VMEM((hp, m, HD), F32),
             ],
         ),
-        compiler_params=pltpu.CompilerParams(vmem_limit_bytes=VMEM_LIMIT),
+        compiler_params=pltpu.CompilerParams(vmem_limit_bytes=48 * MIB),
         cost_estimate=pl.CostEstimate(
             flops=2 * 2 * rows * seq * heads * GROUPS * HD,
             bytes_accessed=2 * (2 * rows * heads * GROUPS * HD + 2 * seq * heads * HD),
@@ -315,7 +315,7 @@
                 pltpu.VMEM((hp, m, HD), F32),
             ],
         ),
-        compiler_params=pltpu.CompilerParams(vmem_limit_bytes=VMEM_LIMIT),
+        compiler_params=pltpu.CompilerParams(vmem_limit_bytes=46 * MIB),
         cost_estimate=pl.CostEstimate(
             flops=5 * 2 * rows * seq * heads * GROUPS * HD // 2,
             bytes_accessed=2 * (4 * rows * heads * GROUPS * HD + 4 * seq * heads * HD),
@@ -363,7 +363,7 @@
                 pl.BlockSpec((size, width), at),
             ],
         ),
-        compiler_params=pltpu.CompilerParams(vmem_limit_bytes=VMEM_LIMIT),
+        compiler_params=pltpu.CompilerParams(vmem_limit_bytes=48 * MIB),
         name="project",
     )(chip, x_all, gain, w_all, w_all)
 
@@ -413,7 +413,7 @@
             ],
             scratch_shapes=[pltpu.VMEM((size, width), F32)],
         ),
-        compiler_params=pltpu.CompilerParams(vmem_limit_bytes=VMEM_LIMIT),
+        compiler_params=pltpu.CompilerParams(vmem_limit_bytes=48 * MIB),
         name="project_back",
     )(chip, dq, dk, dv, x_all, w_all, w_all, w_all)
 
@@ -473,7 +473,7 @@
                 pl.BlockSpec((rows, 2 * FF_TILE), lambda j, chip: (0, j)),
             ],
         ),
-        compiler_params=pltpu.CompilerParams(vmem_limit_bytes=VMEM_LIMIT),
+        compiler_params=pltpu.CompilerParams(vmem_limit_bytes=38 * MIB),
         name="feed",
     )(chip, x_all, p0, p1, gain, w_all)
 
@@ -517,7 +517,7 @@
                 pl.BlockSpec((FF_TILE, width), lambda j, core: (j, 0)),
             ],
         ),
-        compiler_params=pltpu.CompilerParams(vmem_limit_bytes=VMEM_LIMIT),
+        compiler_params=pltpu.CompilerParams(vmem_limit_bytes=48 * MIB),
         name="feed_back",
     )(core, gate_up, go, w_down)
 
@@ -550,7 +550,7 @@
         grid=(rows // size,),
         in_specs=[row, row, row, row, line, pl.BlockSpec(w_out.shape, lambda i: (0, 0), pipeline_mode=pl.Buffered(1))],
         out_specs=[row, pl.BlockSpec((size, w_out.shape[0]), lambda i: (i, 0)), line],
-        compiler_params=pltpu.CompilerParams(vmem_limit_bytes=VMEM_LIMIT),
+        compiler_params=pltpu.CompilerParams(vmem_limit_bytes=22 * MIB),
         name="middle_back",
     )(middle, s0, s1, go, gain, w_out)
 
@@ -707,7 +707,7 @@
             pltpu.SemaphoreType.DMA((4,)),
         ],
         compiler_params=pltpu.CompilerParams(
-            collective_id=0, has_side_effects=True, vmem_limit_bytes=VMEM_LIMIT
+            collective_id=0, has_side_effects=True, vmem_limit_bytes=48 * MIB
         ),
         cost_estimate=LINK_TIME,
         name="gather",
@@ -980,7 +980,7 @@
             pltpu.SemaphoreType.DMA((10,)),
         ],
         compiler_params=pltpu.CompilerParams(
-            collective_id=1, has_side_effects=True, vmem_limit_bytes=VMEM_LIMIT
+            collective_id=1, has_side_effects=True, vmem_limit_bytes=48 * MIB
         ),
         cost_estimate=LINK_TIME,
         name="reduce",
@@ -1166,13 +1166,14 @@
     entries = jnp.concatenate([lot(attn_gain_sum), lot(grad_mlp_gain), lot(dgq), lot(dgk)], axis=1)
     entries = jnp.pad(entries[:, None], ((0, 0), (0, r_in - 1), (0, HD - entries.shape[1])))
     entries = entries.reshape(width, HD).astype(BF16)
+    entries, sum_down = lax.optimization_barrier((entries, sum_down))
     near_c = qkv_c + HD
     beside = lambda v: v.transpose(1, 0, 2).reshape(r_in, -1)
     by_rows = lambda v: lax.dynamic_index_in_dim(v.reshape(2, r_in, -1), c, 0, False)
 
     def columns(sums):
         other = lax.dynamic_index_in_dim(sums.reshape(2, r_in, -1), 1 - c, 0, False)
-        return by_core(c, by_rows(sums), sibling(other)).astype(F32)
+        return by_core(c, by_rows(sums), sibling(other))
 
     if tall:
         sums, sum_out, input_grad = reduce(
@@ -1185,7 +1186,7 @@
     else:
         hidden = lax.dynamic_slice_in_dim(hidden_all, chip * chip_rows, chip_rows, 0)
         grads = [dot(hidden, dq, TN, BF16), dot(hidden_all, dk, TN, BF16), dot(hidden_all, dv, TN, BF16), entries]
-        qkv_own = columns(over_ctx(over_dp(jnp.concatenate(grads, axis=1))))
+        qkv_own = columns(over_ctx(over_dp(jnp.concatenate(grads, axis=1)))).astype(F32)
         out_mine = lax.dynamic_index_in_dim(out_w, c, 1, False)
         sum_out = over_ctx(over_dp(by_core(c, out_mine, out_recv).reshape(chips * r_out, width))).astype(F32)
         grad_q = beside(qkv_own[:, :, :q_c])
@@ -1208,8 +1209,8 @@
         grad_k,
         grad_v,
         sum_out,
-        ff_back(gu_own[:, :, :, 0]),
-        ff_back(gu_own[:, :, :, 1]),
+        ff_back(gu_own[:, :, :, 0]).astype(F32),
+        ff_back(gu_own[:, :, :, 1]).astype(F32),
         sum_down,
         gain_row[:r_in],
         gain_row[r_in : 2 * r_in],

time: 490 us -> 480 us (0.980)
  Pallas kernels: 363 us -> 354 us
    unnamed x85 -> x87, local copies, waits for them, and re-layouts: 17 us -> 23.6 us
  transfers between devices with their start and end apart: 14 -> 14, of which waited for: 1 -> 1; matrix products, arithmetic and copies ran while one was open for 13% -> 11% of each run, Pallas kernels for 50% -> 49%
where the time goes in v5:
time: 480 us; the launch traced here: 476 us
  Pallas kernels  354 us (74%)
  local copies, waits for them, and re-layouts  41 us (9%)
  matrix products  35.8 us (7%)
  between operations  16.5 us (3%)
  other arithmetic  12.4 us (3%)
  starting transfers between devices  12.2 us (3%)
    pallas_call x1, Pallas kernels, gather(): pl.pallas_call(gather_kernel, out_shape=[jax.ShapeDtypeStruct((4, 4, rows...  121 us
    pallas_call x1, Pallas kernels, reduce(): pl.pallas_call(reduce_kernel, out_shape=[jax.ShapeDtypeStruct((rows // 2,...  87.2 us
    pallas_call x1, Pallas kernels, attend_back(): pl.pallas_call(functools.partial(attend_back_kernel, span), out_shape=[ja...  57.7 us
    dot_general x6, matrix products, dot(): return lax.dot_general(a, b, (dims, ((), ())), preferred_element_type=out)  35.8 us
    pallas_call x1, Pallas kernels, attend(): pl.pallas_call(functools.partial(attend_kernel, span), out_shape=[jax.Sha...  26.8 us
    unnamed x87, local copies, waits for them, and re-layouts  23.6 us
    pallas_call x1, Pallas kernels, project_back(): pl.pallas_call(functools.partial(project_back_kernel, own), out_shape=[ja...  14.9 us
    pallas_call x1, Pallas kernels, feed(): pl.pallas_call(feed_kernel, out_shape=[jax.ShapeDtypeStruct((rows, width)...  14.7 us
  transfers between devices with their start and end apart: 14, of which 1 were waited for; matrix products, arithmetic and copies ran while one was open for 11% of the time, Pallas kernels for 49%

profile of v5, /device:TPU:0, one launch (start us, length us, event | category | flops | bytes accessed | tf_op | source)
XLA Modules:
  0.0 476.2 jit_solution(12362854973683780656)
XLA Ops:
  13.4 121.4 %gather.7 = (bf16[4,4,64,6272]{3,2,1,0:T(8,128)(2,1)}, bf16[4,2,256,1024]{3,2,1,0:T(8,128)(2,1)}, bf16[2,2,256,1024]{3,2,1,0:T(8,128)(2,1)S(1)}) custom-call(bf16[2,32,5248]{2,1,0:T(8,128)(2,1)S(1)} %pad_maximum_fusion.pk_ref, bf16[64,1024]{1,0:T(8,128)(2,1)S(1)} %copy-done.15, bf16[2,256,1024]{2,1,0:T(8,128)(2,1)S(1)} %copy-done.13, ...), custom_call_target="tpu_custom_call" | custom-call | bytes 300000000 | tf_op jit(solution)/shard_map/gather/pallas_call | solution.py:695
  136.5 1.8 slice.148
  141.9 14.4 %project.1 = (bf16[2048,1024]{1,0:T(8,128)(2,1)}, bf16[1024,1024]{1,0:T(8,128)(2,1)S(1)}, bf16[2048,1024]{1,0:T(8,128)(2,1)}) custom-call(s32[1]{0:T(128)} %bitcast.chip_ref, bf16[2048,1024]{1,0:T(8,128)(2,1)} %bitcast.124, f32[1,1024]{1,0:T(1,128)S(1)} %bitcast.107, bf16[1024,6272]{1,0:T(8,128)(2,1)} %bitcast.117, bf16[1024,6272]{1,0:T(8,128)(2,1)} %bitcast.118), custom_call_target="tpu_custom_call" | custom-call | tf_op jit(solution)/shard_map/project/pallas_call | solution.py:344
  157.9 26.8 %attend.1 = (bf16[1024,1024]{1,0:T(8,128)(2,1)S(1)}, f32[4,8,1,256]{3,2,1,0:T(1,128)S(1)}) custom-call(s32[8]{0:T(128)S(1)} %dynamic_slice.54.ids_ref, s32[16]{0:T(128)S(1)} %select_reduce_fusion.order_ref, bf16[1024,1024]{1,0:T(8,128)(2,1)} %copy-done.20, bf16[2048,1024]{1,0:T(8,128)(2,1)} %get-tuple-element.63.k_ref.v_ref, ...), custom_call_target="tpu_custom_call" | custom-call | flops 8589934592 | bytes 8388608 | tf_op jit(solution)/shard_map/attend/pallas_call | solution.py:161
  186.1 2.4 fusion.17.p0_ref
  189.1 3.8 collective-permute-done.1.p1_ref
  192.8 14.7 %feed.1 = (f32[1024,1024]{1,0:T(8,128)S(1)}, bf16[1024,1024]{1,0:T(8,128)(2,1)S(1)}, bf16[1024,1536]{1,0:T(8,128)(2,1)S(1)}, bf16[1024,3072]{1,0:T(8,128)(2,1)}) custom-call(s32[1]{0:T(128)} %bitcast.chip_ref, bf16[2048,1024]{1,0:T(8,128)(2,1)} %bitcast.125, bf16[1024,1024]{1,0:T(8,128)(2,1)S(1)} %fusion.17.p0_ref, ...), custom_call_target="tpu_custom_call" | custom-call | tf_op jit(solution)/shard_map/feed/pallas_call | solution.py:452
  207.6 2.1 copy-done.2
  211.0 1.7 copy-done.16
  212.7 4.8 %fusion.20 = bf16[1536,1024]{1,0:T(8,128)(2,1)} fusion(bf16[1024,1536]{1,0:T(8,128)(2,1)S(1)} %get-tuple-element.66, bf16[1024,1024]{1,0:T(8,128)(2,1)S(1)} %bitcast.101), kind=kOutput, calls=%fused_computation.74 | convolution fusion | flops 3221225472 | bytes 8388608 | tf_op jit(solution)/shard_map/dot_general | solution.py:50
  217.9 1.6 copy-done.8
  219.5 11.7 %feed_back.1 = (bf16[1024,3072]{1,0:T(8,128)(2,1)}, bf16[1536,1024]{1,0:T(8,128)(2,1)S(1)}) custom-call(s32[1]{0:T(128)} %bitcast.21.core_ref, bf16[1024,3072]{1,0:T(8,128)(2,1)} %get-tuple-element.67.gu_ref, bf16[1024,1024]{1,0:T(8,128)(2,1)S(1)} %bitcast.102, bf16[16,2,96,1024]{3,2,1,0:T(8,128)(2,1)} %bitcast.129), custom_call_target="tpu_custom_call" | custom-call | tf_op jit(solution)/shard_map/feed_back/pallas_call | solution.py:504
  231.2 1.7 copy-done.18
  232.9 11.6 %fusion.21 = bf16[1024,3072]{1,0:T(8,128)(2,1)} fusion(bf16[1024,1024]{1,0:T(8,128)(2,1)S(1)} %copy-done.23, bf16[1024,3072]{1,0:T(8,128)(2,1)} %get-tuple-element.71), kind=kOutput, calls=%fused_computation.75 | convolution fusion | flops 6442450944 | bytes 14680064 | tf_op jit(solution)/shard_map/dot_general | solution.py:50
  244.6 11.0 %fusion.s0_ref = bf16[1024,1024]{1,0:T(8,128)(2,1)S(1)} fusion(bf16[1024,3072]{1,0:T(8,128)(2,1)} %get-tuple-element.71, bf16[1024,6272]{1,0:T(8,128)(2,1)} %bitcast.120), kind=kOutput, calls=%fused_computation.1 | convolution fusion | flops 6442450944 | bytes 14680064 | tf_op jit(solution)/shard_map/dot_general | solution.py:50
  256.0 3.6 fusion.18
  262.3 5.3 %middle_back.1 = (bf16[1024,1024]{1,0:T(8,128)(2,1)S(1)}, bf16[1024,1024]{1,0:T(8,128)(2,1)S(1)}, f32[1,1024]{1,0:T(1,128)S(1)}) custom-call(f32[1024,1024]{1,0:T(8,128)S(1)} %copy-done.3, bf16[1024,1024]{1,0:T(8,128)(2,1)S(1)} %fusion.s0_ref, bf16[1024,1024]{1,0:T(8,128)(2,1)S(1)} %collective-permute-done.3.s1_ref, bf16[1024,1024]{1,0:T(8,128)(2,1)S(1)} %bitcast.103, ...), custom_call_target="tpu_custom_call" | custom-call | tf_op jit(solution)/shard_map/middle_back/pallas_call | solution.py:543
  267.7 2.5 fusion.19
  271.8 2.7 fusion.4
  274.6 5.4 %collective-permute-start.5 = (bf16[256,1024]{1,0:T(8,128)(2,1)S(1)}, bf16[256,1024]{1,0:T(8,128)(2,1)S(1)}, u32[]{:S(2)}, u32[]{:S(2)}) collective-permute-start(bf16[256,1024]{1,0:T(8,128)(2,1)S(1)} %get-tuple-element.114), channel_id=1, source_target_pairs={{0,4},{1,5},{2,6},{3,7},{4,0},{5,1},{6,2},{7,3},{8,12},{9,13},{10,... | collective-permute-start | bytes 1572872 | tf_op jit(solution)/shard_map/ppermute | solution.py:1026
  280.9 1.9 collective-permute-start.7
  282.9 1.7 collective-permute-start.8
  285.8 1.4 copy-done.27
  287.2 57.7 %attend_back.1 = (bf16[1024,1024]{1,0:T(8,128)(2,1)S(1)}, bf16[2048,512]{1,0:T(8,128)(2,1)S(1)}, bf16[2048,512]{1,0:T(8,128)(2,1)}, f32[1,128]{1,0:T(1,128)S(1)}, f32[1,128]{1,0:T(1,128)S(1)}) custom-call(s32[8]{0:T(128)S(1)} %dynamic_slice.54.ids_ref, s32[16]{0:T(128)S(1)} %select_reduce_fusion.order_ref, bf16[1024,1024]{1,0:T(8,128)(2,1)} %copy-done.20, ...), custom_call_target="tpu_custom_call" | custom-call | flops 10737418240 | bytes 16777216 | tf_op jit(solution)/shard_map/attend_back/pallas_call | solution.py:285
  344.9 1.4 copy-done.4
  348.5 1.6 copy-done.5
  350.1 14.9 %project_back.1 = (bf16[2048,1024]{1,0:T(8,128)(2,1)}, f32[1,1024]{1,0:T(1,128)S(1)}) custom-call(s32[1]{0:T(128)} %bitcast.chip_ref, bf16[1024,1024]{1,0:T(8,128)(2,1)S(1)} %get-tuple-element.85.dq_ref.dq_hbm, bf16[2048,512]{1,0:T(8,128)(2,1)S(1)} %copy-done.5, bf16[2048,512]{1,0:T(8,128)(2,1)} %get-tuple-element.87.dv_ref.dv_hbm, ...), custom_call_target="tpu_custom_call" | custom-call | tf_op jit(solution)/shard_map/project_back/pallas_call | solution.py:395
  365.3 2.0 fusion.8
  367.3 87.2 %reduce.27 = (bf16[32,4224]{1,0:T(8,128)(2,1)S(1)}, bf16[64,1024]{1,0:T(8,128)(2,1)S(1)}, bf16[2,256,1024]{2,1,0:T(8,128)(2,1)S(1)}) custom-call(bf16[2048,1024]{1,0:T(8,128)(2,1)} %get-tuple-element.84.h_hbm, bf16[1024,1024]{1,0:T(8,128)(2,1)S(1)} %get-tuple-element.85.dq_ref.dq_hbm, bf16[2048,512]{1,0:T(8,128)(2,1)} %copy-done.4, ...), custom_call_target="tpu_custom_call" | custom-call | bytes 300000000 | tf_op jit(solution)/shard_map/reduce/pallas_call | solution.py:952
  461.2 2.2 fusion.5
  464.1 1.4 reshape.196
  466.2 1.4 reshape.197
  (176 shorter events, 33.9 us)
Async XLA Ops:
  8.0 131.4 %copy-start = (s32[2,2048]{1,0:T(2,128)S(1)}, s32[2,2048]{1,0:T(2,128)}, u32[]{:S(2)}) copy-start(s32[2,2048]{1,0:T(2,128)} %param.18) | copy-start | bytes 49156
  8.0 209.9 %all-gather.2.cloned.1.call-start = ((), (), s32[]{:S(2)}) async-start(), calls=%async_computation.3 | async-start | bytes 6488064 | tf_op jit(solution)/shard_map/all_gather | solution.py:1082
  9.3 2.5 copy-start.34
  9.6 2.5 copy-start.37
  9.6 2.6 copy-start.38
  136.2 138.3 %reduce-scatter.4.cloned.1.call-start = ((), (), s32[]{:S(2)}) async-start(), calls=%async_computation.4 | async-start | bytes 3932160 | tf_op jit(solution)/shard_map/reduce_scatter | solution.py:1130
  139.4 45.3 %collective-permute-start = (bf16[8,64,1024]{2,1,0:T(8,128)(2,1)}, bf16[8,64,1024]{2,1,0:T(8,128)(2,1)S(1)}, u32[]{:S(2)}, u32[]{:S(2)}) collective-permute-start(bf16[8,64,1024]{2,1,0:T(8,128)(2,1)} %get-tuple-element.112), channel_id=1, source_target_pairs={{0,1},{1,0},{2,3},{3,2},{4,5},{5,4},{6,7},{7,6},{8,9},{9,8},{10,11... | collective-permute-start | bytes 3145736 | tf_op jit(solution)/shard_map/ppermute | solution.py:1025
  141.9 16.0 %copy-start.24 = (f32[2048,128]{1,0:T(8,128)S(1)}, f32[2048,128]{1,0:T(8,128)}, u32[]{:S(2)}) copy-start(f32[2048,128]{1,0:T(8,128)} %constant.135.clone.cos_ref) | copy-start | bytes 3145732
  141.9 16.0 %copy-start.26 = (f32[2048,128]{1,0:T(8,128)S(1)}, f32[2048,128]{1,0:T(8,128)}, u32[]{:S(2)}) copy-start(f32[2048,128]{1,0:T(8,128)} %constant.136.clone.sin_ref) | copy-start | bytes 3145732
  188.5 4.4 collective-permute-start.1
  192.8 19.9 %copy-start.7 = (bf16[2,2,256,1024]{3,2,1,0:T(8,128)(2,1)S(1)}, bf16[2,2,256,1024]{3,2,1,0:T(8,128)(2,1)}, u32[]{:S(2)}) copy-start(bf16[2,2,256,1024]{3,2,1,0:T(8,128)(2,1)} %copy-done.6) | copy-start | bytes 6291460
  217.6 130.5 %reduce-scatter.6.cloned.1.call-start = ((), (), s32[]{:S(2)}) async-start(), calls=%async_computation.5 | async-start | bytes 7864320 | tf_op jit(solution)/shard_map/reduce_scatter | solution.py:1130
  219.5 13.4 %copy-start.23 = (bf16[1024,1024]{1,0:T(8,128)(2,1)S(1)}, bf16[1024,1024]{1,0:T(8,128)(2,1)}, u32[]{:S(2)}) copy-start(bf16[1024,1024]{1,0:T(8,128)(2,1)} %copy-done.22) | copy-start | bytes 6291460
  244.5 213.2 %reduce-scatter.8.cloned.1.call-start = ((), (), s32[]{:S(2)}) async-start(), calls=%async_computation.6 | async-start | bytes 1966080 | tf_op jit(solution)/shard_map/reduce_scatter | solution.py:1131
  244.5 11.4 %copy-start.17 = (bf16[1024,1536]{1,0:T(8,128)(2,1)S(1)}, bf16[1024,1536]{1,0:T(8,128)(2,1)}, u32[]{:S(2)}) copy-start(bf16[1024,1536]{1,0:T(8,128)(2,1)} %copy-done.16) | copy-start | bytes 9437188
  244.5 11.4 %copy-start.19 = (bf16[1536,1024]{1,0:T(8,128)(2,1)S(1)}, bf16[1536,1024]{1,0:T(8,128)(2,1)}, u32[]{:S(2)}) copy-start(bf16[1536,1024]{1,0:T(8,128)(2,1)} %copy-done.18) | copy-start | bytes 9437188
  255.5 5.3 %collective-permute-start.3 = (bf16[1024,1024]{1,0:T(8,128)(2,1)S(1)}, bf16[1024,1024]{1,0:T(8,128)(2,1)S(1)}, u32[]{:S(2)}, u32[]{:S(2)}) collective-permute-start(bf16[1024,1024]{1,0:T(8,128)(2,1)S(1)} %fusion.s0_ref), channel_id=1, source_target_pairs={{0,1},{1,0},{2,3},{3,2},{4,5},{5,4},{6,7},{7,6},{8,9},{9,8},{10,11... | collective-permute-start | bytes 6291464 | tf_op jit(solution)/shard_map/ppermute | solution.py:1025
  256.0 5.3 %copy-start.3 = (f32[1024,1024]{1,0:T(8,128)S(1)}, f32[1024,1024]{1,0:T(8,128)}, u32[]{:S(2)}) copy-start(f32[1024,1024]{1,0:T(8,128)} %copy-done.2) | copy-start | bytes 12582916
  259.6 2.7 copy-start.9
  260.6 11.2 %collective-permute-start.2 = (bf16[512,1024]{1,0:T(8,128)(2,1)}, bf16[512,1024]{1,0:T(8,128)(2,1)}, u32[]{:S(2)}, u32[]{:S(2)}) collective-permute-start(bf16[512,1024]{1,0:T(8,128)(2,1)} %dynamic-slice_bitcast_fusion.1), channel_id=1, source_target_pairs={{0,1},{1,0},{2,3},{3,2},{4,5},{5,4},{6,7},{7,6},{8,9},{9,8},{10,11... | collective-permute-start | bytes 3145736 | tf_op jit(solution)/shard_map/ppermute | solution.py:1025
  262.3 5.4 %copy-start.29 = (bf16[1024,1024]{1,0:T(8,128)(2,1)S(1)}, bf16[1024,1024]{1,0:T(8,128)(2,1)}, u32[]{:S(2)}) copy-start(bf16[1024,1024]{1,0:T(8,128)(2,1)} %copy-done.28) | copy-start | bytes 6291460
  267.7 2.5 copy-start.10
  267.7 2.5 copy-start.21
  271.6 2.9 collective-permute-start.4
  274.6 5.5 %copy-start.32 = (bf16[384,1024]{1,0:T(8,128)(2,1)S(1)}, bf16[384,1024]{1,0:T(8,128)(2,1)}, u32[]{:S(2)}) copy-start(bf16[384,1024]{1,0:T(8,128)(2,1)} %reduce-scatter.4.cloned.1.call-done) | copy-start | bytes 2359300
  274.6 71.6 %collective-permute-start.5 = (bf16[256,1024]{1,0:T(8,128)(2,1)S(1)}, bf16[256,1024]{1,0:T(8,128)(2,1)S(1)}, u32[]{:S(2)}, u32[]{:S(2)}) collective-permute-start(bf16[256,1024]{1,0:T(8,128)(2,1)S(1)} %get-tuple-element.114), channel_id=1, source_target_pairs={{0,4},{1,5},{2,6},{3,7},{4,0},{5,1},{6,2},{7,3},{8,12},{9,13},{10,... | collective-permute-start | bytes 1572872 | tf_op jit(solution)/shard_map/ppermute | solution.py:1026
  280.1 67.3 %collective-permute-start.6 = (bf16[96,1024]{1,0:T(8,128)(2,1)S(1)}, bf16[96,1024]{1,0:T(8,128)(2,1)S(1)}, u32[]{:S(2)}, u32[]{:S(2)}) collective-permute-start(bf16[96,1024]{1,0:T(8,128)(2,1)S(1)} %get-tuple-element.117), channel_id=1, source_target_pairs={{0,2},{1,3},{2,0},{3,1},{4,6},{5,7},{6,4},{7,5},{8,10},{9,11},{10,... | collective-permute-start | bytes 589832 | tf_op jit(solution)/shard_map/ppermute | solution.py:1146
  280.9 66.5 %collective-permute-start.7 = (bf16[96,1024]{1,0:T(8,128)(2,1)S(1)}, bf16[96,1024]{1,0:T(8,128)(2,1)S(1)}, u32[]{:S(2)}, u32[]{:S(2)}) collective-permute-start(bf16[96,1024]{1,0:T(8,128)(2,1)S(1)} %get-tuple-element.116), channel_id=1, source_target_pairs={{0,4},{1,5},{2,6},{3,7},{4,0},{5,1},{6,2},{7,3},{8,12},{9,13},{10,... | collective-permute-start | bytes 589832 | tf_op jit(solution)/shard_map/ppermute | solution.py:1146
  282.9 65.2 %collective-permute-start.8 = (bf16[96,1024]{1,0:T(8,128)(2,1)S(1)}, bf16[96,1024]{1,0:T(8,128)(2,1)}, u32[]{:S(2)}, u32[]{:S(2)}) collective-permute-start(bf16[96,1024]{1,0:T(8,128)(2,1)S(1)} %get-tuple-element.115), channel_id=1, source_target_pairs={{0,6},{1,7},{2,4},{3,5},{4,2},{5,3},{6,0},{7,1},{8,14},{9,15},{10,... | collective-permute-start | bytes 589832 | tf_op jit(solution)/shard_map/ppermute | solution.py:1146
  458.7 1.8 collective-permute-start.9
  464.1 3.5 copy-start.12
  465.5 3.0 copy-start.1
  (24 other events, 36.6 us)
Sparse Core Ops, SparseCore 0:
  136.3 72.2 all-gather.1
  348.2 41.5 reduce-scatter.7
Sparse Core Ops, SparseCore 1:
  217.7 46.9 reduce-scatter.3
  267.6 70.0 reduce-scatter.5

commit v6 on v5

--- a/solution.py
+++ b/solution.py
@@ -17,6 +17,7 @@
 LOG2E = 1.4426950408889634
 KEY_TILE = 512
 ROW_TILE = 256
+TOKEN_TILE = 512
 FF_TILE = 384
 MIB = 1024 * 1024
 MESH = pl.DeviceIdType.MESH
@@ -57,6 +58,12 @@
 
 def row_mean(values):
     return dot(values.astype(BF16), jnp.full((HD, HD), 1.0 / HD, BF16), NN)
+
+
+def row_sums(values):
+    high = values.astype(BF16)
+    ones = jnp.ones((8, HD), BF16)
+    return (dot(ones, high, NT) + dot(ones, (values - high.astype(F32)).astype(BF16), NT))[0:1]
 
 
 def unit_rows(raw):
@@ -220,7 +227,7 @@
         pick = lambda ref: jnp.concatenate([ref[rows, lanes(p * GROUPS + g)] for g in range(GROUPS)], axis=0)
         do2.append(pick(do_ref))
         delta.append(
-            jnp.sum(jnp.transpose(do2[p].astype(F32) * pick(o_ref).astype(F32)), axis=0, keepdims=True)
+            row_sums(do2[p].astype(F32) * pick(o_ref).astype(F32))
         )
         lse.append(lse_ref[p, 0])
     dqa_ref[...] = jnp.zeros_like(dqa_ref)
@@ -337,7 +344,7 @@
 
 def project(chip, x_all, gain, w_all, first, chip_rows):
     seq, width = x_all.shape
-    size = min(ROW_TILE, chip_rows)
+    size = min(TOKEN_TILE, chip_rows)
     own, tiles = chip_rows // size, seq // size
     at = lambda i, chip: ((i + chip[0] * own) % tiles, 0)
     weight = lambda col: pl.BlockSpec((width, width), lambda i, chip: (0, col), pipeline_mode=pl.Buffered(1))
@@ -388,7 +395,7 @@
 def project_back(chip, dq, dk, dv, x_all, w_all, first):
     seq, width = x_all.shape
     chip_rows, kv = dq.shape[0], dk.shape[1]
-    size = min(ROW_TILE, chip_rows)
+    size = min(TOKEN_TILE, chip_rows)
     own, tiles = chip_rows // size, seq // size
     at = lambda i, chip: ((i + chip[0] * own) % tiles, 0)
     weight = lambda cols, col: pl.BlockSpec((width, cols), lambda i, chip: (0, col), pipeline_mode=pl.Buffered(1))

time: 480 us -> 478 us (level)
  no operation moved by 1% of the time
where the time goes in v6:
time: 478 us; the launch traced here: 474 us
  Pallas kernels  352 us (74%)
  local copies, waits for them, and re-layouts  41.1 us (9%)
  matrix products  35.8 us (7%)
  between operations  16.5 us (3%)
  other arithmetic  12.7 us (3%)
  starting transfers between devices  11.6 us (2%)
    pallas_call x1, Pallas kernels, gather(): pl.pallas_call(gather_kernel, out_shape=[jax.ShapeDtypeStruct((4, 4, rows...  121 us
    pallas_call x1, Pallas kernels, reduce(): pl.pallas_call(reduce_kernel, out_shape=[jax.ShapeDtypeStruct((rows // 2,...  88.8 us
    pallas_call x1, Pallas kernels, attend_back(): pl.pallas_call(functools.partial(attend_back_kernel, span), out_shape=[ja...  56.9 us
    dot_general x6, matrix products, dot(): return lax.dot_general(a, b, (dims, ((), ())), preferred_element_type=out)  35.8 us
    pallas_call x1, Pallas kernels, attend(): pl.pallas_call(functools.partial(attend_kernel, span), out_shape=[jax.Sha...  26.8 us
    unnamed x87, local copies, waits for them, and re-layouts  23.7 us
    pallas_call x1, Pallas kernels, feed(): pl.pallas_call(feed_kernel, out_shape=[jax.ShapeDtypeStruct((rows, width)...  14.7 us
    pallas_call x1, Pallas kernels, project_back(): pl.pallas_call(functools.partial(project_back_kernel, own), out_shape=[ja...  13.4 us
  transfers between devices with their start and end apart: 14, of which 1 were waited for; matrix products, arithmetic and copies ran while one was open for 11% of the time, Pallas kernels for 49%

profile of v6, /device:TPU:0, one launch (start us, length us, event | category | flops | bytes accessed | tf_op | source)
XLA Modules:
  0.0 474.0 jit_solution(5996306140458331238)
XLA Ops:
  13.4 121.4 %gather.7 = (bf16[4,4,64,6272]{3,2,1,0:T(8,128)(2,1)}, bf16[4,2,256,1024]{3,2,1,0:T(8,128)(2,1)}, bf16[2,2,256,1024]{3,2,1,0:T(8,128)(2,1)S(1)}) custom-call(bf16[2,32,5248]{2,1,0:T(8,128)(2,1)S(1)} %pad_maximum_fusion.pk_ref, bf16[64,1024]{1,0:T(8,128)(2,1)S(1)} %copy-done.15, bf16[2,256,1024]{2,1,0:T(8,128)(2,1)S(1)} %copy-done.13, ...), custom_call_target="tpu_custom_call" | custom-call | bytes 300000000 | tf_op jit(solution)/shard_map/gather/pallas_call | solution.py:702
  136.5 1.8 slice.148
  141.9 12.9 %project.1 = (bf16[2048,1024]{1,0:T(8,128)(2,1)}, bf16[1024,1024]{1,0:T(8,128)(2,1)S(1)}, bf16[2048,1024]{1,0:T(8,128)(2,1)}) custom-call(s32[1]{0:T(128)} %bitcast.chip_ref, bf16[2048,1024]{1,0:T(8,128)(2,1)} %bitcast.124, f32[1,1024]{1,0:T(1,128)S(1)} %bitcast.107, bf16[1024,6272]{1,0:T(8,128)(2,1)} %bitcast.117, bf16[1024,6272]{1,0:T(8,128)(2,1)} %bitcast.118), custom_call_target="tpu_custom_call" | custom-call | tf_op jit(solution)/shard_map/project/pallas_call | solution.py:351
  156.5 26.8 %attend.1 = (bf16[1024,1024]{1,0:T(8,128)(2,1)S(1)}, f32[4,8,1,256]{3,2,1,0:T(1,128)S(1)}) custom-call(s32[8]{0:T(128)S(1)} %dynamic_slice.54.ids_ref, s32[16]{0:T(128)S(1)} %select_reduce_fusion.order_ref, bf16[1024,1024]{1,0:T(8,128)(2,1)} %copy-done.20, bf16[2048,1024]{1,0:T(8,128)(2,1)} %get-tuple-element.63.k_ref.v_ref, ...), custom_call_target="tpu_custom_call" | custom-call | flops 8589934592 | bytes 8388608 | tf_op jit(solution)/shard_map/attend/pallas_call | solution.py:168
  184.7 2.4 fusion.17.p0_ref
  187.6 3.9 collective-permute-done.1.p1_ref
  191.5 14.7 %feed.1 = (f32[1024,1024]{1,0:T(8,128)S(1)}, bf16[1024,1024]{1,0:T(8,128)(2,1)S(1)}, bf16[1024,1536]{1,0:T(8,128)(2,1)S(1)}, bf16[1024,3072]{1,0:T(8,128)(2,1)}) custom-call(s32[1]{0:T(128)} %bitcast.chip_ref, bf16[2048,1024]{1,0:T(8,128)(2,1)} %bitcast.125, bf16[1024,1024]{1,0:T(8,128)(2,1)S(1)} %fusion.17.p0_ref, ...), custom_call_target="tpu_custom_call" | custom-call | tf_op jit(solution)/shard_map/feed/pallas_call | solution.py:459
  206.2 2.1 copy-done.2
  209.6 1.7 copy-done.16
  211.3 4.8 %fusion.20 = bf16[1536,1024]{1,0:T(8,128)(2,1)} fusion(bf16[1024,1536]{1,0:T(8,128)(2,1)S(1)} %get-tuple-element.66, bf16[1024,1024]{1,0:T(8,128)(2,1)S(1)} %bitcast.101), kind=kOutput, calls=%fused_computation.74 | convolution fusion | flops 3221225472 | bytes 8388608 | tf_op jit(solution)/shard_map/dot_general | solution.py:51
  216.5 1.6 copy-done.8
  218.1 11.8 %feed_back.1 = (bf16[1024,3072]{1,0:T(8,128)(2,1)}, bf16[1536,1024]{1,0:T(8,128)(2,1)S(1)}) custom-call(s32[1]{0:T(128)} %bitcast.21.core_ref, bf16[1024,3072]{1,0:T(8,128)(2,1)} %get-tuple-element.67.gu_ref, bf16[1024,1024]{1,0:T(8,128)(2,1)S(1)} %bitcast.102, bf16[16,2,96,1024]{3,2,1,0:T(8,128)(2,1)} %bitcast.129), custom_call_target="tpu_custom_call" | custom-call | tf_op jit(solution)/shard_map/feed_back/pallas_call | solution.py:511
  229.9 1.7 copy-done.18
  231.6 11.6 %fusion.21 = bf16[1024,3072]{1,0:T(8,128)(2,1)} fusion(bf16[1024,1024]{1,0:T(8,128)(2,1)S(1)} %copy-done.23, bf16[1024,3072]{1,0:T(8,128)(2,1)} %get-tuple-element.71), kind=kOutput, calls=%fused_computation.75 | convolution fusion | flops 6442450944 | bytes 14680064 | tf_op jit(solution)/shard_map/dot_general | solution.py:51
  243.3 10.9 %fusion.s0_ref = bf16[1024,1024]{1,0:T(8,128)(2,1)S(1)} fusion(bf16[1024,3072]{1,0:T(8,128)(2,1)} %get-tuple-element.71, bf16[1024,6272]{1,0:T(8,128)(2,1)} %bitcast.120), kind=kOutput, calls=%fused_computation.1 | convolution fusion | flops 6442450944 | bytes 14680064 | tf_op jit(solution)/shard_map/dot_general | solution.py:51
  254.8 3.6 fusion.18
  261.2 5.3 %middle_back.1 = (bf16[1024,1024]{1,0:T(8,128)(2,1)S(1)}, bf16[1024,1024]{1,0:T(8,128)(2,1)S(1)}, f32[1,1024]{1,0:T(1,128)S(1)}) custom-call(f32[1024,1024]{1,0:T(8,128)S(1)} %copy-done.3, bf16[1024,1024]{1,0:T(8,128)(2,1)S(1)} %fusion.s0_ref, bf16[1024,1024]{1,0:T(8,128)(2,1)S(1)} %collective-permute-done.3.s1_ref, bf16[1024,1024]{1,0:T(8,128)(2,1)S(1)} %bitcast.103, ...), custom_call_target="tpu_custom_call" | custom-call | tf_op jit(solution)/shard_map/middle_back/pallas_call | solution.py:550
  266.5 2.5 fusion.19
  270.6 3.0 fusion.4
  273.7 4.8 %collective-permute-start.5 = (bf16[256,1024]{1,0:T(8,128)(2,1)S(1)}, bf16[256,1024]{1,0:T(8,128)(2,1)S(1)}, u32[]{:S(2)}, u32[]{:S(2)}) collective-permute-start(bf16[256,1024]{1,0:T(8,128)(2,1)S(1)} %get-tuple-element.114), channel_id=1, source_target_pairs={{0,4},{1,5},{2,6},{3,7},{4,0},{5,1},{6,2},{7,3},{8,12},{9,13},{10,... | collective-permute-start | bytes 1572872 | tf_op jit(solution)/shard_map/ppermute | solution.py:1033
  279.5 1.9 collective-permute-start.7
  281.5 1.5 collective-permute-start.8
  284.2 1.4 copy-done.27
  285.7 56.9 %attend_back.1 = (bf16[1024,1024]{1,0:T(8,128)(2,1)S(1)}, bf16[2048,512]{1,0:T(8,128)(2,1)S(1)}, bf16[2048,512]{1,0:T(8,128)(2,1)}, f32[1,128]{1,0:T(1,128)S(1)}, f32[1,128]{1,0:T(1,128)S(1)}) custom-call(s32[8]{0:T(128)S(1)} %dynamic_slice.54.ids_ref, s32[16]{0:T(128)S(1)} %select_reduce_fusion.order_ref, bf16[1024,1024]{1,0:T(8,128)(2,1)} %copy-done.20, ...), custom_call_target="tpu_custom_call" | custom-call | flops 10737418240 | bytes 16777216 | tf_op jit(solution)/shard_map/attend_back/pallas_call | solution.py:292
  342.6 1.4 copy-done.4
  346.2 1.6 copy-done.5
  347.8 13.4 %project_back.1 = (bf16[2048,1024]{1,0:T(8,128)(2,1)}, f32[1,1024]{1,0:T(1,128)S(1)}) custom-call(s32[1]{0:T(128)} %bitcast.chip_ref, bf16[1024,1024]{1,0:T(8,128)(2,1)S(1)} %get-tuple-element.85.dq_ref.dq_hbm, bf16[2048,512]{1,0:T(8,128)(2,1)S(1)} %copy-done.5, bf16[2048,512]{1,0:T(8,128)(2,1)} %get-tuple-element.87.dv_ref.dv_hbm, ...), custom_call_target="tpu_custom_call" | custom-call | tf_op jit(solution)/shard_map/project_back/pallas_call | solution.py:402
  361.5 2.0 fusion.8
  363.5 88.8 %reduce.27 = (bf16[32,4224]{1,0:T(8,128)(2,1)S(1)}, bf16[64,1024]{1,0:T(8,128)(2,1)S(1)}, bf16[2,256,1024]{2,1,0:T(8,128)(2,1)S(1)}) custom-call(bf16[2048,1024]{1,0:T(8,128)(2,1)} %get-tuple-element.84.h_hbm, bf16[1024,1024]{1,0:T(8,128)(2,1)S(1)} %get-tuple-element.85.dq_ref.dq_hbm, bf16[2048,512]{1,0:T(8,128)(2,1)} %copy-done.4, ...), custom_call_target="tpu_custom_call" | custom-call | bytes 300000000 | tf_op jit(solution)/shard_map/reduce/pallas_call | solution.py:959
  459.0 2.2 fusion.5
  461.9 1.4 reshape.196
  463.9 1.4 reshape.197
  (176 shorter events, 34.1 us)
Async XLA Ops:
  8.0 131.4 %copy-start = (s32[2,2048]{1,0:T(2,128)S(1)}, s32[2,2048]{1,0:T(2,128)}, u32[]{:S(2)}) copy-start(s32[2,2048]{1,0:T(2,128)} %param.18) | copy-start | bytes 49156
  8.0 208.5 %all-gather.2.cloned.1.call-start = ((), (), s32[]{:S(2)}) async-start(), calls=%async_computation.3 | async-start | bytes 6488064 | tf_op jit(solution)/shard_map/all_gather | solution.py:1089
  9.3 2.5 copy-start.34
  9.6 2.5 copy-start.37
  9.6 2.6 copy-start.38
  136.2 137.4 %reduce-scatter.4.cloned.1.call-start = ((), (), s32[]{:S(2)}) async-start(), calls=%async_computation.4 | async-start | bytes 3932160 | tf_op jit(solution)/shard_map/reduce_scatter | solution.py:1137
  139.4 43.9 %collective-permute-start = (bf16[8,64,1024]{2,1,0:T(8,128)(2,1)}, bf16[8,64,1024]{2,1,0:T(8,128)(2,1)S(1)}, u32[]{:S(2)}, u32[]{:S(2)}) collective-permute-start(bf16[8,64,1024]{2,1,0:T(8,128)(2,1)} %get-tuple-element.112), channel_id=1, source_target_pairs={{0,1},{1,0},{2,3},{3,2},{4,5},{5,4},{6,7},{7,6},{8,9},{9,8},{10,11... | collective-permute-start | bytes 3145736 | tf_op jit(solution)/shard_map/ppermute | solution.py:1032
  141.9 14.6 %copy-start.24 = (f32[2048,128]{1,0:T(8,128)S(1)}, f32[2048,128]{1,0:T(8,128)}, u32[]{:S(2)}) copy-start(f32[2048,128]{1,0:T(8,128)} %constant.135.clone.cos_ref) | copy-start | bytes 3145732
  141.9 14.6 %copy-start.26 = (f32[2048,128]{1,0:T(8,128)S(1)}, f32[2048,128]{1,0:T(8,128)}, u32[]{:S(2)}) copy-start(f32[2048,128]{1,0:T(8,128)} %constant.136.clone.sin_ref) | copy-start | bytes 3145732
  187.0 4.4 collective-permute-start.1
  191.5 19.9 %copy-start.7 = (bf16[2,2,256,1024]{3,2,1,0:T(8,128)(2,1)S(1)}, bf16[2,2,256,1024]{3,2,1,0:T(8,128)(2,1)}, u32[]{:S(2)}) copy-start(bf16[2,2,256,1024]{3,2,1,0:T(8,128)(2,1)} %copy-done.6) | copy-start | bytes 6291460
  216.2 129.5 %reduce-scatter.6.cloned.1.call-start = ((), (), s32[]{:S(2)}) async-start(), calls=%async_computation.5 | async-start | bytes 7864320 | tf_op jit(solution)/shard_map/reduce_scatter | solution.py:1137
  218.1 13.5 %copy-start.23 = (bf16[1024,1024]{1,0:T(8,128)(2,1)S(1)}, bf16[1024,1024]{1,0:T(8,128)(2,1)}, u32[]{:S(2)}) copy-start(bf16[1024,1024]{1,0:T(8,128)(2,1)} %copy-done.22) | copy-start | bytes 6291460
  243.3 212.2 %reduce-scatter.8.cloned.1.call-start = ((), (), s32[]{:S(2)}) async-start(), calls=%async_computation.6 | async-start | bytes 1966080 | tf_op jit(solution)/shard_map/reduce_scatter | solution.py:1138
  243.3 11.5 %copy-start.17 = (bf16[1024,1536]{1,0:T(8,128)(2,1)S(1)}, bf16[1024,1536]{1,0:T(8,128)(2,1)}, u32[]{:S(2)}) copy-start(bf16[1024,1536]{1,0:T(8,128)(2,1)} %copy-done.16) | copy-start | bytes 9437188
  243.3 11.5 %copy-start.19 = (bf16[1536,1024]{1,0:T(8,128)(2,1)S(1)}, bf16[1536,1024]{1,0:T(8,128)(2,1)}, u32[]{:S(2)}) copy-start(bf16[1536,1024]{1,0:T(8,128)(2,1)} %copy-done.18) | copy-start | bytes 9437188
  254.3 5.3 %collective-permute-start.3 = (bf16[1024,1024]{1,0:T(8,128)(2,1)S(1)}, bf16[1024,1024]{1,0:T(8,128)(2,1)S(1)}, u32[]{:S(2)}, u32[]{:S(2)}) collective-permute-start(bf16[1024,1024]{1,0:T(8,128)(2,1)S(1)} %fusion.s0_ref), channel_id=1, source_target_pairs={{0,1},{1,0},{2,3},{3,2},{4,5},{5,4},{6,7},{7,6},{8,9},{9,8},{10,11... | collective-permute-start | bytes 6291464 | tf_op jit(solution)/shard_map/ppermute | solution.py:1032
  254.8 5.3 %copy-start.3 = (f32[1024,1024]{1,0:T(8,128)S(1)}, f32[1024,1024]{1,0:T(8,128)}, u32[]{:S(2)}) copy-start(f32[1024,1024]{1,0:T(8,128)} %copy-done.2) | copy-start | bytes 12582916
  258.4 2.7 copy-start.9
  259.5 11.1 %collective-permute-start.2 = (bf16[512,1024]{1,0:T(8,128)(2,1)}, bf16[512,1024]{1,0:T(8,128)(2,1)}, u32[]{:S(2)}, u32[]{:S(2)}) collective-permute-start(bf16[512,1024]{1,0:T(8,128)(2,1)} %dynamic-slice_bitcast_fusion.1), channel_id=1, source_target_pairs={{0,1},{1,0},{2,3},{3,2},{4,5},{5,4},{6,7},{7,6},{8,9},{9,8},{10,11... | collective-permute-start | bytes 3145736 | tf_op jit(solution)/shard_map/ppermute | solution.py:1032
  261.2 5.4 %copy-start.29 = (bf16[1024,1024]{1,0:T(8,128)(2,1)S(1)}, bf16[1024,1024]{1,0:T(8,128)(2,1)}, u32[]{:S(2)}) copy-start(bf16[1024,1024]{1,0:T(8,128)(2,1)} %copy-done.28) | copy-start | bytes 6291460
  266.5 2.5 copy-start.10
  266.5 2.5 copy-start.21
  270.5 3.1 collective-permute-start.4
  273.6 4.9 %copy-start.32 = (bf16[384,1024]{1,0:T(8,128)(2,1)S(1)}, bf16[384,1024]{1,0:T(8,128)(2,1)}, u32[]{:S(2)}) copy-start(bf16[384,1024]{1,0:T(8,128)(2,1)} %reduce-scatter.4.cloned.1.call-done) | copy-start | bytes 2359300
  273.7 70.2 %collective-permute-start.5 = (bf16[256,1024]{1,0:T(8,128)(2,1)S(1)}, bf16[256,1024]{1,0:T(8,128)(2,1)S(1)}, u32[]{:S(2)}, u32[]{:S(2)}) collective-permute-start(bf16[256,1024]{1,0:T(8,128)(2,1)S(1)} %get-tuple-element.114), channel_id=1, source_target_pairs={{0,4},{1,5},{2,6},{3,7},{4,0},{5,1},{6,2},{7,3},{8,12},{9,13},{10,... | collective-permute-start | bytes 1572872 | tf_op jit(solution)/shard_map/ppermute | solution.py:1033
  278.5 66.5 %collective-permute-start.6 = (bf16[96,1024]{1,0:T(8,128)(2,1)S(1)}, bf16[96,1024]{1,0:T(8,128)(2,1)S(1)}, u32[]{:S(2)}, u32[]{:S(2)}) collective-permute-start(bf16[96,1024]{1,0:T(8,128)(2,1)S(1)} %get-tuple-element.117), channel_id=1, source_target_pairs={{0,2},{1,3},{2,0},{3,1},{4,6},{5,7},{6,4},{7,5},{8,10},{9,11},{10,... | collective-permute-start | bytes 589832 | tf_op jit(solution)/shard_map/ppermute | solution.py:1153
  279.5 65.6 %collective-permute-start.7 = (bf16[96,1024]{1,0:T(8,128)(2,1)S(1)}, bf16[96,1024]{1,0:T(8,128)(2,1)S(1)}, u32[]{:S(2)}, u32[]{:S(2)}) collective-permute-start(bf16[96,1024]{1,0:T(8,128)(2,1)S(1)} %get-tuple-element.116), channel_id=1, source_target_pairs={{0,4},{1,5},{2,6},{3,7},{4,0},{5,1},{6,2},{7,3},{8,12},{9,13},{10,... | collective-permute-start | bytes 589832 | tf_op jit(solution)/shard_map/ppermute | solution.py:1153
  281.5 64.3 %collective-permute-start.8 = (bf16[96,1024]{1,0:T(8,128)(2,1)S(1)}, bf16[96,1024]{1,0:T(8,128)(2,1)}, u32[]{:S(2)}, u32[]{:S(2)}) collective-permute-start(bf16[96,1024]{1,0:T(8,128)(2,1)S(1)} %get-tuple-element.115), channel_id=1, source_target_pairs={{0,6},{1,7},{2,4},{3,5},{4,2},{5,3},{6,0},{7,1},{8,14},{9,15},{10,... | collective-permute-start | bytes 589832 | tf_op jit(solution)/shard_map/ppermute | solution.py:1153
  456.5 1.8 collective-permute-start.9
  461.9 3.5 copy-start.12
  463.3 3.0 copy-start.1
  (24 other events, 36.6 us)
Sparse Core Ops, SparseCore 0:
  136.3 72.2 all-gather.1
  345.9 42.8 reduce-scatter.7
Sparse Core Ops, SparseCore 1:
  216.3 46.8 reduce-scatter.3
  266.0 70.0 reduce-scatter.5

commit v7 on v6

--- a/solution.py
+++ b/solution.py
@@ -427,7 +427,7 @@
 
 def feed_kernel(chip_ref, x_ref, p0_ref, p1_ref, gain_ref, w_ref, mid_ref, sec_ref, act_ref, gu_ref):
     count = x_ref.shape[0]
-    size = min(ROW_TILE, count)
+    size = min(TOKEN_TILE, count)
     tile = lambda i: pl.ds(pl.multiple_of(i * size, size), size)
 
     @pl.when(pl.program_id(0) == 0)
@@ -487,7 +487,7 @@
 
 def feed_back_kernel(core_ref, gu_ref, go_ref, wd_ref, gg_ref, d_ref):
     count = gu_ref.shape[0]
-    size = min(ROW_TILE, count)
+    size = min(TOKEN_TILE, count)
     unit = wd_ref.shape[2]
     for u in range(FF_TILE // unit):
         d_ref[u * unit : (u + 1) * unit, :] = wd_ref[u, 0]

time: 478 us -> 475 us (level)
  transfers between devices with their start and end apart: 14 -> 14, of which waited for: 1 -> 1; matrix products, arithmetic and copies ran while one was open for 11% -> 11% of each run, Pallas kernels for 49% -> 48%
where the time goes in v7:
time: 475 us; the launch traced here: 471 us
  Pallas kernels  349 us (73%)
  local copies, waits for them, and re-layouts  41 us (9%)
  matrix products  35.8 us (8%)
  between operations  16.5 us (3%)
  starting transfers between devices  12.7 us (3%)
  other arithmetic  12.4 us (3%)
    pallas_call x1, Pallas kernels, gather(): pl.pallas_call(gather_kernel, out_shape=[jax.ShapeDtypeStruct((4, 4, rows...  121 us
    pallas_call x1, Pallas kernels, reduce(): pl.pallas_call(reduce_kernel, out_shape=[jax.ShapeDtypeStruct((rows // 2,...  88.3 us
    pallas_call x1, Pallas kernels, attend_back(): pl.pallas_call(functools.partial(attend_back_kernel, span), out_shape=[ja...  56.7 us
    dot_general x6, matrix products, dot(): return lax.dot_general(a, b, (dims, ((), ())), preferred_element_type=out)  35.8 us
    pallas_call x1, Pallas kernels, attend(): pl.pallas_call(functools.partial(attend_kernel, span), out_shape=[jax.Sha...  26.8 us
    unnamed x87, local copies, waits for them, and re-layouts  23.6 us
    pallas_call x1, Pallas kernels, project_back(): pl.pallas_call(functools.partial(project_back_kernel, own), out_shape=[ja...  13.4 us
    pallas_call x1, Pallas kernels, feed(): pl.pallas_call(feed_kernel, out_shape=[jax.ShapeDtypeStruct((rows, width)...  13.2 us
  transfers between devices with their start and end apart: 14, of which 1 were waited for; matrix products, arithmetic and copies ran while one was open for 11% of the time, Pallas kernels for 48%

profile of v7, /device:TPU:0, one launch (start us, length us, event | category | flops | bytes accessed | tf_op | source)
XLA Modules:
  0.0 471.5 jit_solution(9175270955657802664)
XLA Ops:
  13.4 121.4 %gather.7 = (bf16[4,4,64,6272]{3,2,1,0:T(8,128)(2,1)}, bf16[4,2,256,1024]{3,2,1,0:T(8,128)(2,1)}, bf16[2,2,256,1024]{3,2,1,0:T(8,128)(2,1)S(1)}) custom-call(bf16[2,32,5248]{2,1,0:T(8,128)(2,1)S(1)} %pad_maximum_fusion.pk_ref, bf16[64,1024]{1,0:T(8,128)(2,1)S(1)} %copy-done.15, bf16[2,256,1024]{2,1,0:T(8,128)(2,1)S(1)} %copy-done.13, ...), custom_call_target="tpu_custom_call" | custom-call | bytes 300000000 | tf_op jit(solution)/shard_map/gather/pallas_call | solution.py:702
  136.5 1.8 slice.148
  141.9 12.9 %project.1 = (bf16[2048,1024]{1,0:T(8,128)(2,1)}, bf16[1024,1024]{1,0:T(8,128)(2,1)S(1)}, bf16[2048,1024]{1,0:T(8,128)(2,1)}) custom-call(s32[1]{0:T(128)} %bitcast.chip_ref, bf16[2048,1024]{1,0:T(8,128)(2,1)} %bitcast.124, f32[1,1024]{1,0:T(1,128)S(1)} %bitcast.107, bf16[1024,6272]{1,0:T(8,128)(2,1)} %bitcast.117, bf16[1024,6272]{1,0:T(8,128)(2,1)} %bitcast.118), custom_call_target="tpu_custom_call" | custom-call | tf_op jit(solution)/shard_map/project/pallas_call | solution.py:351
  156.5 26.8 %attend.1 = (bf16[1024,1024]{1,0:T(8,128)(2,1)S(1)}, f32[4,8,1,256]{3,2,1,0:T(1,128)S(1)}) custom-call(s32[8]{0:T(128)S(1)} %dynamic_slice.54.ids_ref, s32[16]{0:T(128)S(1)} %select_reduce_fusion.order_ref, bf16[1024,1024]{1,0:T(8,128)(2,1)} %copy-done.20, bf16[2048,1024]{1,0:T(8,128)(2,1)} %get-tuple-element.63.k_ref.v_ref, ...), custom_call_target="tpu_custom_call" | custom-call | flops 8589934592 | bytes 8388608 | tf_op jit(solution)/shard_map/attend/pallas_call | solution.py:168
  184.7 2.4 fusion.17.p0_ref
  187.6 3.9 collective-permute-done.1.p1_ref
  191.5 13.2 %feed.1 = (f32[1024,1024]{1,0:T(8,128)S(1)}, bf16[1024,1024]{1,0:T(8,128)(2,1)S(1)}, bf16[1024,1536]{1,0:T(8,128)(2,1)S(1)}, bf16[1024,3072]{1,0:T(8,128)(2,1)}) custom-call(s32[1]{0:T(128)} %bitcast.chip_ref, bf16[2048,1024]{1,0:T(8,128)(2,1)} %bitcast.125, bf16[1024,1024]{1,0:T(8,128)(2,1)S(1)} %fusion.17.p0_ref, ...), custom_call_target="tpu_custom_call" | custom-call | tf_op jit(solution)/shard_map/feed/pallas_call | solution.py:459
  204.6 2.1 copy-done.2
  206.7 1.4 copy-done.22
  208.1 1.7 copy-done.16
  209.8 4.8 %fusion.20 = bf16[1536,1024]{1,0:T(8,128)(2,1)} fusion(bf16[1024,1536]{1,0:T(8,128)(2,1)S(1)} %get-tuple-element.66, bf16[1024,1024]{1,0:T(8,128)(2,1)S(1)} %bitcast.101), kind=kOutput, calls=%fused_computation.74 | convolution fusion | flops 3221225472 | bytes 8388608 | tf_op jit(solution)/shard_map/dot_general | solution.py:51
  215.2 1.6 copy-done.8
  216.8 10.8 %feed_back.1 = (bf16[1024,3072]{1,0:T(8,128)(2,1)}, bf16[1536,1024]{1,0:T(8,128)(2,1)S(1)}) custom-call(s32[1]{0:T(128)} %bitcast.21.core_ref, bf16[1024,3072]{1,0:T(8,128)(2,1)} %get-tuple-element.67.gu_ref, bf16[1024,1024]{1,0:T(8,128)(2,1)S(1)} %bitcast.102, bf16[16,2,96,1024]{3,2,1,0:T(8,128)(2,1)} %bitcast.129), custom_call_target="tpu_custom_call" | custom-call | tf_op jit(solution)/shard_map/feed_back/pallas_call | solution.py:511
  227.6 1.7 copy-done.18
  229.3 11.6 %fusion.21 = bf16[1024,3072]{1,0:T(8,128)(2,1)} fusion(bf16[1024,1024]{1,0:T(8,128)(2,1)S(1)} %copy-done.23, bf16[1024,3072]{1,0:T(8,128)(2,1)} %get-tuple-element.71), kind=kOutput, calls=%fused_computation.75 | convolution fusion | flops 6442450944 | bytes 14680064 | tf_op jit(solution)/shard_map/dot_general | solution.py:51
  241.0 10.9 %fusion.s0_ref = bf16[1024,1024]{1,0:T(8,128)(2,1)S(1)} fusion(bf16[1024,3072]{1,0:T(8,128)(2,1)} %get-tuple-element.71, bf16[1024,6272]{1,0:T(8,128)(2,1)} %bitcast.120), kind=kOutput, calls=%fused_computation.1 | convolution fusion | flops 6442450944 | bytes 14680064 | tf_op jit(solution)/shard_map/dot_general | solution.py:51
  252.6 3.6 fusion.18
  258.9 5.3 %middle_back.1 = (bf16[1024,1024]{1,0:T(8,128)(2,1)S(1)}, bf16[1024,1024]{1,0:T(8,128)(2,1)S(1)}, f32[1,1024]{1,0:T(1,128)S(1)}) custom-call(f32[1024,1024]{1,0:T(8,128)S(1)} %copy-done.3, bf16[1024,1024]{1,0:T(8,128)(2,1)S(1)} %fusion.s0_ref, bf16[1024,1024]{1,0:T(8,128)(2,1)S(1)} %collective-permute-done.3.s1_ref, bf16[1024,1024]{1,0:T(8,128)(2,1)S(1)} %bitcast.103, ...), custom_call_target="tpu_custom_call" | custom-call | tf_op jit(solution)/shard_map/middle_back/pallas_call | solution.py:550
  264.3 2.5 fusion.19
  268.3 2.7 fusion.4
  271.2 5.6 %collective-permute-start.5 = (bf16[256,1024]{1,0:T(8,128)(2,1)S(1)}, bf16[256,1024]{1,0:T(8,128)(2,1)S(1)}, u32[]{:S(2)}, u32[]{:S(2)}) collective-permute-start(bf16[256,1024]{1,0:T(8,128)(2,1)S(1)} %get-tuple-element.114), channel_id=1, source_target_pairs={{0,4},{1,5},{2,6},{3,7},{4,0},{5,1},{6,2},{7,3},{8,12},{9,13},{10,... | collective-permute-start | bytes 1572872 | tf_op jit(solution)/shard_map/ppermute | solution.py:1033
  277.5 1.9 collective-permute-start.7
  279.5 1.8 collective-permute-start.8
  283.9 56.7 %attend_back.1 = (bf16[1024,1024]{1,0:T(8,128)(2,1)S(1)}, bf16[2048,512]{1,0:T(8,128)(2,1)S(1)}, bf16[2048,512]{1,0:T(8,128)(2,1)}, f32[1,128]{1,0:T(1,128)S(1)}, f32[1,128]{1,0:T(1,128)S(1)}) custom-call(s32[8]{0:T(128)S(1)} %dynamic_slice.54.ids_ref, s32[16]{0:T(128)S(1)} %select_reduce_fusion.order_ref, bf16[1024,1024]{1,0:T(8,128)(2,1)} %copy-done.20, ...), custom_call_target="tpu_custom_call" | custom-call | flops 10737418240 | bytes 16777216 | tf_op jit(solution)/shard_map/attend_back/pallas_call | solution.py:292
  340.6 1.4 copy-done.4
  344.2 1.6 copy-done.5
  345.8 13.4 %project_back.1 = (bf16[2048,1024]{1,0:T(8,128)(2,1)}, f32[1,1024]{1,0:T(1,128)S(1)}) custom-call(s32[1]{0:T(128)} %bitcast.chip_ref, bf16[1024,1024]{1,0:T(8,128)(2,1)S(1)} %get-tuple-element.85.dq_ref.dq_hbm, bf16[2048,512]{1,0:T(8,128)(2,1)S(1)} %copy-done.5, bf16[2048,512]{1,0:T(8,128)(2,1)} %get-tuple-element.87.dv_ref.dv_hbm, ...), custom_call_target="tpu_custom_call" | custom-call | tf_op jit(solution)/shard_map/project_back/pallas_call | solution.py:402
  359.5 2.0 fusion.8
  361.5 88.3 %reduce.27 = (bf16[32,4224]{1,0:T(8,128)(2,1)S(1)}, bf16[64,1024]{1,0:T(8,128)(2,1)S(1)}, bf16[2,256,1024]{2,1,0:T(8,128)(2,1)S(1)}) custom-call(bf16[2048,1024]{1,0:T(8,128)(2,1)} %get-tuple-element.84.h_hbm, bf16[1024,1024]{1,0:T(8,128)(2,1)S(1)} %get-tuple-element.85.dq_ref.dq_hbm, bf16[2048,512]{1,0:T(8,128)(2,1)} %copy-done.4, ...), custom_call_target="tpu_custom_call" | custom-call | bytes 300000000 | tf_op jit(solution)/shard_map/reduce/pallas_call | solution.py:959
  456.5 2.2 fusion.5
  459.4 1.4 reshape.196
  461.4 1.4 reshape.197
  (176 shorter events, 34.0 us)
Async XLA Ops:
  8.0 131.4 %copy-start = (s32[2,2048]{1,0:T(2,128)S(1)}, s32[2,2048]{1,0:T(2,128)}, u32[]{:S(2)}) copy-start(s32[2,2048]{1,0:T(2,128)} %param.18) | copy-start | bytes 49156
  8.0 207.1 %all-gather.2.cloned.1.call-start = ((), (), s32[]{:S(2)}) async-start(), calls=%async_computation.3 | async-start | bytes 6488064 | tf_op jit(solution)/shard_map/all_gather | solution.py:1089
  9.3 2.5 copy-start.34
  9.6 2.5 copy-start.37
  9.6 2.6 copy-start.38
  136.2 134.8 %reduce-scatter.4.cloned.1.call-start = ((), (), s32[]{:S(2)}) async-start(), calls=%async_computation.4 | async-start | bytes 3932160 | tf_op jit(solution)/shard_map/reduce_scatter | solution.py:1137
  139.4 43.9 %collective-permute-start = (bf16[8,64,1024]{2,1,0:T(8,128)(2,1)}, bf16[8,64,1024]{2,1,0:T(8,128)(2,1)S(1)}, u32[]{:S(2)}, u32[]{:S(2)}) collective-permute-start(bf16[8,64,1024]{2,1,0:T(8,128)(2,1)} %get-tuple-element.112), channel_id=1, source_target_pairs={{0,1},{1,0},{2,3},{3,2},{4,5},{5,4},{6,7},{7,6},{8,9},{9,8},{10,11... | collective-permute-start | bytes 3145736 | tf_op jit(solution)/shard_map/ppermute | solution.py:1032
  141.9 14.6 %copy-start.24 = (f32[2048,128]{1,0:T(8,128)S(1)}, f32[2048,128]{1,0:T(8,128)}, u32[]{:S(2)}) copy-start(f32[2048,128]{1,0:T(8,128)} %constant.135.clone.cos_ref) | copy-start | bytes 3145732
  141.9 14.6 %copy-start.26 = (f32[2048,128]{1,0:T(8,128)S(1)}, f32[2048,128]{1,0:T(8,128)}, u32[]{:S(2)}) copy-start(f32[2048,128]{1,0:T(8,128)} %constant.136.clone.sin_ref) | copy-start | bytes 3145732
  187.0 4.5 collective-permute-start.1
  191.5 18.3 %copy-start.7 = (bf16[2,2,256,1024]{3,2,1,0:T(8,128)(2,1)S(1)}, bf16[2,2,256,1024]{3,2,1,0:T(8,128)(2,1)}, u32[]{:S(2)}) copy-start(bf16[2,2,256,1024]{3,2,1,0:T(8,128)(2,1)} %copy-done.6) | copy-start | bytes 6291460
  214.7 129.1 %reduce-scatter.6.cloned.1.call-start = ((), (), s32[]{:S(2)}) async-start(), calls=%async_computation.5 | async-start | bytes 7864320 | tf_op jit(solution)/shard_map/reduce_scatter | solution.py:1137
  216.8 12.5 %copy-start.23 = (bf16[1024,1024]{1,0:T(8,128)(2,1)S(1)}, bf16[1024,1024]{1,0:T(8,128)(2,1)}, u32[]{:S(2)}) copy-start(bf16[1024,1024]{1,0:T(8,128)(2,1)} %copy-done.22) | copy-start | bytes 6291460
  240.9 212.0 %reduce-scatter.8.cloned.1.call-start = ((), (), s32[]{:S(2)}) async-start(), calls=%async_computation.6 | async-start | bytes 1966080 | tf_op jit(solution)/shard_map/reduce_scatter | solution.py:1138
  241.0 11.6 %copy-start.17 = (bf16[1024,1536]{1,0:T(8,128)(2,1)S(1)}, bf16[1024,1536]{1,0:T(8,128)(2,1)}, u32[]{:S(2)}) copy-start(bf16[1024,1536]{1,0:T(8,128)(2,1)} %copy-done.16) | copy-start | bytes 9437188
  241.0 11.5 %copy-start.19 = (bf16[1536,1024]{1,0:T(8,128)(2,1)S(1)}, bf16[1536,1024]{1,0:T(8,128)(2,1)}, u32[]{:S(2)}) copy-start(bf16[1536,1024]{1,0:T(8,128)(2,1)} %copy-done.18) | copy-start | bytes 9437188
  251.9 5.3 %collective-permute-start.3 = (bf16[1024,1024]{1,0:T(8,128)(2,1)S(1)}, bf16[1024,1024]{1,0:T(8,128)(2,1)S(1)}, u32[]{:S(2)}, u32[]{:S(2)}) collective-permute-start(bf16[1024,1024]{1,0:T(8,128)(2,1)S(1)} %fusion.s0_ref), channel_id=1, source_target_pairs={{0,1},{1,0},{2,3},{3,2},{4,5},{5,4},{6,7},{7,6},{8,9},{9,8},{10,11... | collective-permute-start | bytes 6291464 | tf_op jit(solution)/shard_map/ppermute | solution.py:1032
  252.6 5.3 %copy-start.3 = (f32[1024,1024]{1,0:T(8,128)S(1)}, f32[1024,1024]{1,0:T(8,128)}, u32[]{:S(2)}) copy-start(f32[1024,1024]{1,0:T(8,128)} %copy-done.2) | copy-start | bytes 12582916
  256.2 2.7 copy-start.9
  257.2 11.1 %collective-permute-start.2 = (bf16[512,1024]{1,0:T(8,128)(2,1)}, bf16[512,1024]{1,0:T(8,128)(2,1)}, u32[]{:S(2)}, u32[]{:S(2)}) collective-permute-start(bf16[512,1024]{1,0:T(8,128)(2,1)} %dynamic-slice_bitcast_fusion.1), channel_id=1, source_target_pairs={{0,1},{1,0},{2,3},{3,2},{4,5},{5,4},{6,7},{7,6},{8,9},{9,8},{10,11... | collective-permute-start | bytes 3145736 | tf_op jit(solution)/shard_map/ppermute | solution.py:1032
  258.9 5.3 %copy-start.29 = (bf16[1024,1024]{1,0:T(8,128)(2,1)S(1)}, bf16[1024,1024]{1,0:T(8,128)(2,1)}, u32[]{:S(2)}) copy-start(bf16[1024,1024]{1,0:T(8,128)(2,1)} %copy-done.28) | copy-start | bytes 6291460
  264.2 2.5 copy-start.10
  264.3 2.5 copy-start.21
  268.2 2.8 collective-permute-start.4
  271.1 5.7 %copy-start.32 = (bf16[384,1024]{1,0:T(8,128)(2,1)S(1)}, bf16[384,1024]{1,0:T(8,128)(2,1)}, u32[]{:S(2)}) copy-start(bf16[384,1024]{1,0:T(8,128)(2,1)} %reduce-scatter.4.cloned.1.call-done) | copy-start | bytes 2359300
  271.2 70.8 %collective-permute-start.5 = (bf16[256,1024]{1,0:T(8,128)(2,1)S(1)}, bf16[256,1024]{1,0:T(8,128)(2,1)S(1)}, u32[]{:S(2)}, u32[]{:S(2)}) collective-permute-start(bf16[256,1024]{1,0:T(8,128)(2,1)S(1)} %get-tuple-element.114), channel_id=1, source_target_pairs={{0,4},{1,5},{2,6},{3,7},{4,0},{5,1},{6,2},{7,3},{8,12},{9,13},{10,... | collective-permute-start | bytes 1572872 | tf_op jit(solution)/shard_map/ppermute | solution.py:1033
  276.8 66.2 %collective-permute-start.6 = (bf16[96,1024]{1,0:T(8,128)(2,1)S(1)}, bf16[96,1024]{1,0:T(8,128)(2,1)S(1)}, u32[]{:S(2)}, u32[]{:S(2)}) collective-permute-start(bf16[96,1024]{1,0:T(8,128)(2,1)S(1)} %get-tuple-element.117), channel_id=1, source_target_pairs={{0,2},{1,3},{2,0},{3,1},{4,6},{5,7},{6,4},{7,5},{8,10},{9,11},{10,... | collective-permute-start | bytes 589832 | tf_op jit(solution)/shard_map/ppermute | solution.py:1153
  277.5 65.5 %collective-permute-start.7 = (bf16[96,1024]{1,0:T(8,128)(2,1)S(1)}, bf16[96,1024]{1,0:T(8,128)(2,1)S(1)}, u32[]{:S(2)}, u32[]{:S(2)}) collective-permute-start(bf16[96,1024]{1,0:T(8,128)(2,1)S(1)} %get-tuple-element.116), channel_id=1, source_target_pairs={{0,4},{1,5},{2,6},{3,7},{4,0},{5,1},{6,2},{7,3},{8,12},{9,13},{10,... | collective-permute-start | bytes 589832 | tf_op jit(solution)/shard_map/ppermute | solution.py:1153
  279.5 64.3 %collective-permute-start.8 = (bf16[96,1024]{1,0:T(8,128)(2,1)S(1)}, bf16[96,1024]{1,0:T(8,128)(2,1)}, u32[]{:S(2)}, u32[]{:S(2)}) collective-permute-start(bf16[96,1024]{1,0:T(8,128)(2,1)S(1)} %get-tuple-element.115), channel_id=1, source_target_pairs={{0,6},{1,7},{2,4},{3,5},{4,2},{5,3},{6,0},{7,1},{8,14},{9,15},{10,... | collective-permute-start | bytes 589832 | tf_op jit(solution)/shard_map/ppermute | solution.py:1153
  454.0 1.8 collective-permute-start.9
  459.4 3.5 copy-start.12
  460.8 3.0 copy-start.1
  (24 other events, 36.5 us)
Sparse Core Ops, SparseCore 0:
  136.3 72.2 all-gather.1
  343.9 41.9 reduce-scatter.7
Sparse Core Ops, SparseCore 1:
  214.8 46.8 reduce-scatter.3
  264.5 70.0 reduce-scatter.5

commit v8 on v7

--- a/solution.py
+++ b/solution.py
@@ -487,7 +487,7 @@
 
 def feed_back_kernel(core_ref, gu_ref, go_ref, wd_ref, gg_ref, d_ref):
     count = gu_ref.shape[0]
-    size = min(TOKEN_TILE, count)
+    size = min(2 * TOKEN_TILE, count)
     unit = wd_ref.shape[2]
     for u in range(FF_TILE // unit):
         d_ref[u * unit : (u + 1) * unit, :] = wd_ref[u, 0]

time: 475 us -> 475 us (level)
  no operation moved by 1% of the time
where the time goes in v8:
time: 475 us; the launch traced here: 471 us
  Pallas kernels  349 us (73%)
  local copies, waits for them, and re-layouts  40.9 us (9%)
  matrix products  35.8 us (8%)
  between operations  16.5 us (3%)
  starting transfers between devices  12.7 us (3%)
  other arithmetic  12.4 us (3%)
    pallas_call x1, Pallas kernels, gather(): pl.pallas_call(gather_kernel, out_shape=[jax.ShapeDtypeStruct((4, 4, rows...  121 us
    pallas_call x1, Pallas kernels, reduce(): pl.pallas_call(reduce_kernel, out_shape=[jax.ShapeDtypeStruct((rows // 2,...  88.7 us
    pallas_call x1, Pallas kernels, attend_back(): pl.pallas_call(functools.partial(attend_back_kernel, span), out_shape=[ja...  56.7 us
    dot_general x6, matrix products, dot(): return lax.dot_general(a, b, (dims, ((), ())), preferred_element_type=out)  35.8 us
    pallas_call x1, Pallas kernels, attend(): pl.pallas_call(functools.partial(attend_kernel, span), out_shape=[jax.Sha...  26.8 us
    unnamed x87, local copies, waits for them, and re-layouts  23.5 us
    pallas_call x1, Pallas kernels, project_back(): pl.pallas_call(functools.partial(project_back_kernel, own), out_shape=[ja...  13.4 us
    pallas_call x1, Pallas kernels, feed(): pl.pallas_call(feed_kernel, out_shape=[jax.ShapeDtypeStruct((rows, width)...  13.2 us
  transfers between devices with their start and end apart: 14, of which 1 were waited for; matrix products, arithmetic and copies ran while one was open for 11% of the time, Pallas kernels for 48%

profile of v8, /device:TPU:0, one launch (start us, length us, event | category | flops | bytes accessed | tf_op | source)
XLA Modules:
  0.0 471.1 jit_solution(7356718994716448691)
XLA Ops:
  13.4 121.4 %gather.7 = (bf16[4,4,64,6272]{3,2,1,0:T(8,128)(2,1)}, bf16[4,2,256,1024]{3,2,1,0:T(8,128)(2,1)}, bf16[2,2,256,1024]{3,2,1,0:T(8,128)(2,1)S(1)}) custom-call(bf16[2,32,5248]{2,1,0:T(8,128)(2,1)S(1)} %pad_maximum_fusion.pk_ref, bf16[64,1024]{1,0:T(8,128)(2,1)S(1)} %copy-done.15, bf16[2,256,1024]{2,1,0:T(8,128)(2,1)S(1)} %copy-done.13, ...), custom_call_target="tpu_custom_call" | custom-call | bytes 300000000 | tf_op jit(solution)/shard_map/gather/pallas_call | solution.py:702
  136.5 1.8 slice.148
  141.9 12.9 %project.1 = (bf16[2048,1024]{1,0:T(8,128)(2,1)}, bf16[1024,1024]{1,0:T(8,128)(2,1)S(1)}, bf16[2048,1024]{1,0:T(8,128)(2,1)}) custom-call(s32[1]{0:T(128)} %bitcast.chip_ref, bf16[2048,1024]{1,0:T(8,128)(2,1)} %bitcast.124, f32[1,1024]{1,0:T(1,128)S(1)} %bitcast.107, bf16[1024,6272]{1,0:T(8,128)(2,1)} %bitcast.117, bf16[1024,6272]{1,0:T(8,128)(2,1)} %bitcast.118), custom_call_target="tpu_custom_call" | custom-call | tf_op jit(solution)/shard_map/project/pallas_call | solution.py:351
  156.5 26.8 %attend.1 = (bf16[1024,1024]{1,0:T(8,128)(2,1)S(1)}, f32[4,8,1,256]{3,2,1,0:T(1,128)S(1)}) custom-call(s32[8]{0:T(128)S(1)} %dynamic_slice.54.ids_ref, s32[16]{0:T(128)S(1)} %select_reduce_fusion.order_ref, bf16[1024,1024]{1,0:T(8,128)(2,1)} %copy-done.20, bf16[2048,1024]{1,0:T(8,128)(2,1)} %get-tuple-element.63.k_ref.v_ref, ...), custom_call_target="tpu_custom_call" | custom-call | flops 8589934592 | bytes 8388608 | tf_op jit(solution)/shard_map/attend/pallas_call | solution.py:168
  184.7 2.4 fusion.17.p0_ref
  187.6 3.9 collective-permute-done.1.p1_ref
  191.5 13.2 %feed.1 = (f32[1024,1024]{1,0:T(8,128)S(1)}, bf16[1024,1024]{1,0:T(8,128)(2,1)S(1)}, bf16[1024,1536]{1,0:T(8,128)(2,1)S(1)}, bf16[1024,3072]{1,0:T(8,128)(2,1)}) custom-call(s32[1]{0:T(128)} %bitcast.chip_ref, bf16[2048,1024]{1,0:T(8,128)(2,1)} %bitcast.125, bf16[1024,1024]{1,0:T(8,128)(2,1)S(1)} %fusion.17.p0_ref, ...), custom_call_target="tpu_custom_call" | custom-call | tf_op jit(solution)/shard_map/feed/pallas_call | solution.py:459
  204.6 2.1 copy-done.2
  206.7 1.4 copy-done.22
  208.1 1.7 copy-done.16
  209.8 4.8 %fusion.20 = bf16[1536,1024]{1,0:T(8,128)(2,1)} fusion(bf16[1024,1536]{1,0:T(8,128)(2,1)S(1)} %get-tuple-element.66, bf16[1024,1024]{1,0:T(8,128)(2,1)S(1)} %bitcast.101), kind=kOutput, calls=%fused_computation.74 | convolution fusion | flops 3221225472 | bytes 8388608 | tf_op jit(solution)/shard_map/dot_general | solution.py:51
  215.2 1.6 copy-done.8
  216.8 10.3 %feed_back.1 = (bf16[1024,3072]{1,0:T(8,128)(2,1)}, bf16[1536,1024]{1,0:T(8,128)(2,1)S(1)}) custom-call(s32[1]{0:T(128)} %bitcast.21.core_ref, bf16[1024,3072]{1,0:T(8,128)(2,1)} %get-tuple-element.67.gu_ref, bf16[1024,1024]{1,0:T(8,128)(2,1)S(1)} %bitcast.102, bf16[16,2,96,1024]{3,2,1,0:T(8,128)(2,1)} %bitcast.129), custom_call_target="tpu_custom_call" | custom-call | tf_op jit(solution)/shard_map/feed_back/pallas_call | solution.py:511
  227.0 1.7 copy-done.18
  228.7 11.6 %fusion.21 = bf16[1024,3072]{1,0:T(8,128)(2,1)} fusion(bf16[1024,1024]{1,0:T(8,128)(2,1)S(1)} %copy-done.23, bf16[1024,3072]{1,0:T(8,128)(2,1)} %get-tuple-element.71), kind=kOutput, calls=%fused_computation.75 | convolution fusion | flops 6442450944 | bytes 14680064 | tf_op jit(solution)/shard_map/dot_general | solution.py:51
  240.4 10.9 %fusion.s0_ref = bf16[1024,1024]{1,0:T(8,128)(2,1)S(1)} fusion(bf16[1024,3072]{1,0:T(8,128)(2,1)} %get-tuple-element.71, bf16[1024,6272]{1,0:T(8,128)(2,1)} %bitcast.120), kind=kOutput, calls=%fused_computation.1 | convolution fusion | flops 6442450944 | bytes 14680064 | tf_op jit(solution)/shard_map/dot_general | solution.py:51
  251.8 3.6 fusion.18
  258.2 5.3 %middle_back.1 = (bf16[1024,1024]{1,0:T(8,128)(2,1)S(1)}, bf16[1024,1024]{1,0:T(8,128)(2,1)S(1)}, f32[1,1024]{1,0:T(1,128)S(1)}) custom-call(f32[1024,1024]{1,0:T(8,128)S(1)} %copy-done.3, bf16[1024,1024]{1,0:T(8,128)(2,1)S(1)} %fusion.s0_ref, bf16[1024,1024]{1,0:T(8,128)(2,1)S(1)} %collective-permute-done.3.s1_ref, bf16[1024,1024]{1,0:T(8,128)(2,1)S(1)} %bitcast.103, ...), custom_call_target="tpu_custom_call" | custom-call | tf_op jit(solution)/shard_map/middle_back/pallas_call | solution.py:550
  263.5 2.5 fusion.19
  267.6 2.7 fusion.4
  270.5 5.7 %collective-permute-start.5 = (bf16[256,1024]{1,0:T(8,128)(2,1)S(1)}, bf16[256,1024]{1,0:T(8,128)(2,1)S(1)}, u32[]{:S(2)}, u32[]{:S(2)}) collective-permute-start(bf16[256,1024]{1,0:T(8,128)(2,1)S(1)} %get-tuple-element.114), channel_id=1, source_target_pairs={{0,4},{1,5},{2,6},{3,7},{4,0},{5,1},{6,2},{7,3},{8,12},{9,13},{10,... | collective-permute-start | bytes 1572872 | tf_op jit(solution)/shard_map/ppermute | solution.py:1033
  277.2 1.9 collective-permute-start.7
  279.2 1.5 collective-permute-start.8
  283.1 56.7 %attend_back.1 = (bf16[1024,1024]{1,0:T(8,128)(2,1)S(1)}, bf16[2048,512]{1,0:T(8,128)(2,1)S(1)}, bf16[2048,512]{1,0:T(8,128)(2,1)}, f32[1,128]{1,0:T(1,128)S(1)}, f32[1,128]{1,0:T(1,128)S(1)}) custom-call(s32[8]{0:T(128)S(1)} %dynamic_slice.54.ids_ref, s32[16]{0:T(128)S(1)} %select_reduce_fusion.order_ref, bf16[1024,1024]{1,0:T(8,128)(2,1)} %copy-done.20, ...), custom_call_target="tpu_custom_call" | custom-call | flops 10737418240 | bytes 16777216 | tf_op jit(solution)/shard_map/attend_back/pallas_call | solution.py:292
  339.8 1.4 copy-done.4
  343.4 1.6 copy-done.5
  345.0 13.4 %project_back.1 = (bf16[2048,1024]{1,0:T(8,128)(2,1)}, f32[1,1024]{1,0:T(1,128)S(1)}) custom-call(s32[1]{0:T(128)} %bitcast.chip_ref, bf16[1024,1024]{1,0:T(8,128)(2,1)S(1)} %get-tuple-element.85.dq_ref.dq_hbm, bf16[2048,512]{1,0:T(8,128)(2,1)S(1)} %copy-done.5, bf16[2048,512]{1,0:T(8,128)(2,1)} %get-tuple-element.87.dv_ref.dv_hbm, ...), custom_call_target="tpu_custom_call" | custom-call | tf_op jit(solution)/shard_map/project_back/pallas_call | solution.py:402
  358.7 2.0 fusion.8
  360.7 88.7 %reduce.27 = (bf16[32,4224]{1,0:T(8,128)(2,1)S(1)}, bf16[64,1024]{1,0:T(8,128)(2,1)S(1)}, bf16[2,256,1024]{2,1,0:T(8,128)(2,1)S(1)}) custom-call(bf16[2048,1024]{1,0:T(8,128)(2,1)} %get-tuple-element.84.h_hbm, bf16[1024,1024]{1,0:T(8,128)(2,1)S(1)} %get-tuple-element.85.dq_ref.dq_hbm, bf16[2048,512]{1,0:T(8,128)(2,1)} %copy-done.4, ...), custom_call_target="tpu_custom_call" | custom-call | bytes 300000000 | tf_op jit(solution)/shard_map/reduce/pallas_call | solution.py:959
  456.1 2.2 fusion.5
  458.9 1.4 reshape.196
  461.0 1.4 reshape.197
  (176 shorter events, 34.2 us)
Async XLA Ops:
  8.0 131.4 %copy-start = (s32[2,2048]{1,0:T(2,128)S(1)}, s32[2,2048]{1,0:T(2,128)}, u32[]{:S(2)}) copy-start(s32[2,2048]{1,0:T(2,128)} %param.18) | copy-start | bytes 49156
  8.0 207.1 %all-gather.2.cloned.1.call-start = ((), (), s32[]{:S(2)}) async-start(), calls=%async_computation.3 | async-start | bytes 6488064 | tf_op jit(solution)/shard_map/all_gather | solution.py:1089
  9.3 2.5 copy-start.34
  9.6 2.5 copy-start.37
  9.6 2.6 copy-start.38
  136.2 134.1 %reduce-scatter.4.cloned.1.call-start = ((), (), s32[]{:S(2)}) async-start(), calls=%async_computation.4 | async-start | bytes 3932160 | tf_op jit(solution)/shard_map/reduce_scatter | solution.py:1137
  139.4 43.9 %collective-permute-start = (bf16[8,64,1024]{2,1,0:T(8,128)(2,1)}, bf16[8,64,1024]{2,1,0:T(8,128)(2,1)S(1)}, u32[]{:S(2)}, u32[]{:S(2)}) collective-permute-start(bf16[8,64,1024]{2,1,0:T(8,128)(2,1)} %get-tuple-element.112), channel_id=1, source_target_pairs={{0,1},{1,0},{2,3},{3,2},{4,5},{5,4},{6,7},{7,6},{8,9},{9,8},{10,11... | collective-permute-start | bytes 3145736 | tf_op jit(solution)/shard_map/ppermute | solution.py:1032
  141.9 14.6 %copy-start.24 = (f32[2048,128]{1,0:T(8,128)S(1)}, f32[2048,128]{1,0:T(8,128)}, u32[]{:S(2)}) copy-start(f32[2048,128]{1,0:T(8,128)} %constant.135.clone.cos_ref) | copy-start | bytes 3145732
  141.9 14.6 %copy-start.26 = (f32[2048,128]{1,0:T(8,128)S(1)}, f32[2048,128]{1,0:T(8,128)}, u32[]{:S(2)}) copy-start(f32[2048,128]{1,0:T(8,128)} %constant.136.clone.sin_ref) | copy-start | bytes 3145732
  187.0 4.5 collective-permute-start.1
  191.5 18.3 %copy-start.7 = (bf16[2,2,256,1024]{3,2,1,0:T(8,128)(2,1)S(1)}, bf16[2,2,256,1024]{3,2,1,0:T(8,128)(2,1)}, u32[]{:S(2)}) copy-start(bf16[2,2,256,1024]{3,2,1,0:T(8,128)(2,1)} %copy-done.6) | copy-start | bytes 6291460
  214.7 128.3 %reduce-scatter.6.cloned.1.call-start = ((), (), s32[]{:S(2)}) async-start(), calls=%async_computation.5 | async-start | bytes 7864320 | tf_op jit(solution)/shard_map/reduce_scatter | solution.py:1137
  216.8 12.0 %copy-start.23 = (bf16[1024,1024]{1,0:T(8,128)(2,1)S(1)}, bf16[1024,1024]{1,0:T(8,128)(2,1)}, u32[]{:S(2)}) copy-start(bf16[1024,1024]{1,0:T(8,128)(2,1)} %copy-done.22) | copy-start | bytes 6291460
  240.4 212.1 %reduce-scatter.8.cloned.1.call-start = ((), (), s32[]{:S(2)}) async-start(), calls=%async_computation.6 | async-start | bytes 1966080 | tf_op jit(solution)/shard_map/reduce_scatter | solution.py:1138
  240.4 11.4 %copy-start.17 = (bf16[1024,1536]{1,0:T(8,128)(2,1)S(1)}, bf16[1024,1536]{1,0:T(8,128)(2,1)}, u32[]{:S(2)}) copy-start(bf16[1024,1536]{1,0:T(8,128)(2,1)} %copy-done.16) | copy-start | bytes 9437188
  240.4 11.4 %copy-start.19 = (bf16[1536,1024]{1,0:T(8,128)(2,1)S(1)}, bf16[1536,1024]{1,0:T(8,128)(2,1)}, u32[]{:S(2)}) copy-start(bf16[1536,1024]{1,0:T(8,128)(2,1)} %copy-done.18) | copy-start | bytes 9437188
  251.3 5.3 %collective-permute-start.3 = (bf16[1024,1024]{1,0:T(8,128)(2,1)S(1)}, bf16[1024,1024]{1,0:T(8,128)(2,1)S(1)}, u32[]{:S(2)}, u32[]{:S(2)}) collective-permute-start(bf16[1024,1024]{1,0:T(8,128)(2,1)S(1)} %fusion.s0_ref), channel_id=1, source_target_pairs={{0,1},{1,0},{2,3},{3,2},{4,5},{5,4},{6,7},{7,6},{8,9},{9,8},{10,11... | collective-permute-start | bytes 6291464 | tf_op jit(solution)/shard_map/ppermute | solution.py:1032
  251.8 5.3 %copy-start.3 = (f32[1024,1024]{1,0:T(8,128)S(1)}, f32[1024,1024]{1,0:T(8,128)}, u32[]{:S(2)}) copy-start(f32[1024,1024]{1,0:T(8,128)} %copy-done.2) | copy-start | bytes 12582916
  255.4 2.8 copy-start.9
  256.5 11.1 %collective-permute-start.2 = (bf16[512,1024]{1,0:T(8,128)(2,1)}, bf16[512,1024]{1,0:T(8,128)(2,1)}, u32[]{:S(2)}, u32[]{:S(2)}) collective-permute-start(bf16[512,1024]{1,0:T(8,128)(2,1)} %dynamic-slice_bitcast_fusion.1), channel_id=1, source_target_pairs={{0,1},{1,0},{2,3},{3,2},{4,5},{5,4},{6,7},{7,6},{8,9},{9,8},{10,11... | collective-permute-start | bytes 3145736 | tf_op jit(solution)/shard_map/ppermute | solution.py:1032
  258.2 5.3 %copy-start.29 = (bf16[1024,1024]{1,0:T(8,128)(2,1)S(1)}, bf16[1024,1024]{1,0:T(8,128)(2,1)}, u32[]{:S(2)}) copy-start(bf16[1024,1024]{1,0:T(8,128)(2,1)} %copy-done.28) | copy-start | bytes 6291460
  263.5 2.5 copy-start.10
  263.5 2.5 copy-start.21
  267.5 2.8 collective-permute-start.4
  270.4 5.8 %copy-start.32 = (bf16[384,1024]{1,0:T(8,128)(2,1)S(1)}, bf16[384,1024]{1,0:T(8,128)(2,1)}, u32[]{:S(2)}) copy-start(bf16[384,1024]{1,0:T(8,128)(2,1)} %reduce-scatter.4.cloned.1.call-done) | copy-start | bytes 2359300
  270.5 70.7 %collective-permute-start.5 = (bf16[256,1024]{1,0:T(8,128)(2,1)S(1)}, bf16[256,1024]{1,0:T(8,128)(2,1)S(1)}, u32[]{:S(2)}, u32[]{:S(2)}) collective-permute-start(bf16[256,1024]{1,0:T(8,128)(2,1)S(1)} %get-tuple-element.114), channel_id=1, source_target_pairs={{0,4},{1,5},{2,6},{3,7},{4,0},{5,1},{6,2},{7,3},{8,12},{9,13},{10,... | collective-permute-start | bytes 1572872 | tf_op jit(solution)/shard_map/ppermute | solution.py:1033
  276.2 66.1 %collective-permute-start.6 = (bf16[96,1024]{1,0:T(8,128)(2,1)S(1)}, bf16[96,1024]{1,0:T(8,128)(2,1)S(1)}, u32[]{:S(2)}, u32[]{:S(2)}) collective-permute-start(bf16[96,1024]{1,0:T(8,128)(2,1)S(1)} %get-tuple-element.117), channel_id=1, source_target_pairs={{0,2},{1,3},{2,0},{3,1},{4,6},{5,7},{6,4},{7,5},{8,10},{9,11},{10,... | collective-permute-start | bytes 589832 | tf_op jit(solution)/shard_map/ppermute | solution.py:1153
  277.2 65.1 %collective-permute-start.7 = (bf16[96,1024]{1,0:T(8,128)(2,1)S(1)}, bf16[96,1024]{1,0:T(8,128)(2,1)S(1)}, u32[]{:S(2)}, u32[]{:S(2)}) collective-permute-start(bf16[96,1024]{1,0:T(8,128)(2,1)S(1)} %get-tuple-element.116), channel_id=1, source_target_pairs={{0,4},{1,5},{2,6},{3,7},{4,0},{5,1},{6,2},{7,3},{8,12},{9,13},{10,... | collective-permute-start | bytes 589832 | tf_op jit(solution)/shard_map/ppermute | solution.py:1153
  279.2 63.8 %collective-permute-start.8 = (bf16[96,1024]{1,0:T(8,128)(2,1)S(1)}, bf16[96,1024]{1,0:T(8,128)(2,1)}, u32[]{:S(2)}, u32[]{:S(2)}) collective-permute-start(bf16[96,1024]{1,0:T(8,128)(2,1)S(1)} %get-tuple-element.115), channel_id=1, source_target_pairs={{0,6},{1,7},{2,4},{3,5},{4,2},{5,3},{6,0},{7,1},{8,14},{9,15},{10,... | collective-permute-start | bytes 589832 | tf_op jit(solution)/shard_map/ppermute | solution.py:1153
  453.6 1.8 collective-permute-start.9
  458.9 3.5 copy-start.12
  460.4 3.0 copy-start.1
  (24 other events, 36.4 us)
Sparse Core Ops, SparseCore 0:
  136.3 72.2 all-gather.1
  343.1 42.5 reduce-scatter.7
Sparse Core Ops, SparseCore 1:
  214.8 46.8 reduce-scatter.3
  264.5 70.0 reduce-scatter.5
